TPU v7x, 32 devices: a whole 2x2x4 slice. The times are simulated.
32 devices in a mesh: dp: 8 (over y, x, core), head: 4 (over z).
Axes of the slice: x: 2, y: 2, z: 4, core: 2. Of those that a mesh axis runs over, the one named last changes fastest.
Arguments:
- layer_entries: bfloat16 [8192, 1024], P(('dp', 'head')), may hold values from -6 to 6
- triple_projection_matrix: bfloat16 [1024, 3072], P('dp', 'head'), may hold values from -0.1875 to 0.1875
- attention_exit_matrix: bfloat16 [1024, 1024], P('dp', 'head'), may hold values from -1.5 to 1.5
- expand_matrix: bfloat16 [1024, 4096], P('dp', 'head'), may hold values from -0.1875 to 0.1875
- contract_matrix: bfloat16 [4096, 1024], P('dp', 'head'), may hold values from -0.09375 to 0.09375
- nested_projector: bfloat16 [1024, 288], P('dp', 'head'), may hold values from -0.1875 to 0.1875
- offset_model_width: bfloat16 [5, 1024], P(None, ('dp', 'head')), may hold values from -3 to 3
- offset_expanded: bfloat16 [4096], P(('dp', 'head')), may hold values from -3 to 3
- standardize_factor: bfloat16 [2, 1024], P(None, ('dp', 'head')), may hold values from 0.5 to 1.5
- standardize_offset: bfloat16 [2, 1024], P(None, ('dp', 'head')), may hold values from -3 to 3
- logarithmic_warmth: float32 [1], replicated, may hold values from -3.9 to -3
- passage_lengths_each: int32 [24], P('dp'), may hold values from 50 to 256, as said below
- question_lengths: int32 [64], P('dp'), may hold values from 8 to 32, as said below
- relevant_passage: int32 [64], P('dp'), may hold values from 0 to 2
Outputs:
- outputs: bfloat16 [8192, 1024], P(('dp', 'head'))
- loss: float32 [1], replicated
- grad_tokens: float32 [8192, 1024], P(('dp', 'head'))
- grad_w_qkv: float32 [1024, 3072], P('dp', 'head')
- grad_w_out: float32 [1024, 1024], P('dp', 'head')
- grad_w_up: float32 [1024, 4096], P('dp', 'head')
- grad_w_down: float32 [4096, 1024], P('dp', 'head')
- grad_w_heads: float32 [1024, 288], P('dp', 'head')
- grad_bias_d: float32 [5, 1024], P(None, ('dp', 'head'))
- grad_bias_up: float32 [4096], P(('dp', 'head'))
- grad_norm_gain: float32 [2, 1024], P(None, ('dp', 'head'))
- grad_norm_shift: float32 [2, 1024], P(None, ('dp', 'head'))
- grad_log_temp: float32 [1], replicated
Inputs may be any that keep to these rules, and one draw needn't show every extreme that they name: `passage_lengths_each`: tokens of each document; in every draw some document has exactly 256. `question_lengths`: real tokens of each query; in every draw some query has exactly 32.
All inputs are finite; a program needn't handle non-finite values.
Results may differ from a plain program's by a relative error of at most 0.024.
Values may be sent and summed in bfloat16 or wider, within the bound.
No kernel may reach another device: no remote copies, remote signals or barrier semaphores. Data moves between devices by JAX's collectives and lax.ppermute only.
A program may use at most 128 MiB of HBM per device.

v0:
```python
import jax
import jax.numpy as jnp
from jax import lax
from jax.sharding import PartitionSpec as P

D = 1024
HEADS = 16
HEAD_DIM = 64
EMB = 128
EMB_MID = 96
EMB_SMALL = 64
QLEN = 32
ROW_BLOCK = 256


EPS_NORM = 1e-05
EPS_UNIT = 1e-06
SHARPNESS = 0.05
ROPE_BASE = 10000.0
MASKED = -1000000000.0
SQRT_HALF = 0.7071067811865476
GAUSS_SCALE = 0.3989422804014327


def rope_tables(positions):
    halfway = HEAD_DIM // 2
    powers = jnp.arange(halfway, dtype=jnp.float32) * (2.0 / HEAD_DIM)
    angles = positions.astype(jnp.float32)[:, None] * (ROPE_BASE ** (-powers))[None, :]
    return (jnp.cos(angles)[:, None, :], jnp.sin(angles)[:, None, :])


def rotate(vectors, cosines, sines):
    halfway = vectors.shape[-1] // 2
    first_half = vectors[..., :halfway]
    second_half = vectors[..., halfway:]
    return jnp.concatenate(
        [first_half * cosines - second_half * sines, second_half * cosines + first_half * sines],
        axis=-1,
    )


def unrotate(grads, cosines, sines):
    halfway = grads.shape[-1] // 2
    first_half = grads[..., :halfway]
    second_half = grads[..., halfway:]
    return jnp.concatenate(
        [first_half * cosines + second_half * sines, second_half * cosines - first_half * sines],
        axis=-1,
    )


def norm_forward(values, gain, shift):
    centred = values - jnp.mean(values, axis=-1, keepdims=True)
    variance = jnp.mean(centred * centred, axis=-1, keepdims=True)
    inverse = lax.rsqrt(variance + EPS_NORM)
    scaled = centred * inverse
    return (scaled * gain + shift, scaled, inverse)


def norm_backward(grad_out, scaled, inverse, gain):
    grad_scaled = grad_out * gain
    grad_in = inverse * (
        grad_scaled
        - jnp.mean(grad_scaled, axis=-1, keepdims=True)
        - scaled * jnp.mean(grad_scaled * scaled, axis=-1, keepdims=True)
    )
    return (grad_in, jnp.sum(grad_out * scaled, axis=0), jnp.sum(grad_out, axis=0))


def head_windows(projector_matrix):
    starts = (0, 0, EMB, EMB + EMB_MID)
    widths = (EMB, EMB, EMB_MID, EMB_SMALL)
    padded = jnp.concatenate(
        [projector_matrix, jnp.zeros((projector_matrix.shape[0], EMB), projector_matrix.dtype)],
        axis=1,
    )
    columns = jnp.arange(EMB)
    return [
        padded[:, starts[member] : starts[member] + EMB]
        * (columns < widths[member]).astype(projector_matrix.dtype)[None, :]
        for member in range(4)
    ]


def pairing_objective(
    mapped_vectors,
    participant_number,
    passage_lengths_each,
    question_lengths,
    relevant_passage,
    logarithmic_warmth,
):
    docs_group = passage_lengths_each.shape[0]
    row_count = mapped_vectors.shape[0] // (docs_group + 1)
    queries_here = question_lengths.shape[0]
    row_ids = jnp.arange(row_count, dtype=jnp.int32)
    inverse = lax.rsqrt(jnp.sum(mapped_vectors * mapped_vectors, axis=-1, keepdims=True) + EPS_UNIT)
    unit = mapped_vectors * inverse
    unit_low = unit.astype(jnp.bfloat16)
    query_unit = unit_low[:row_count]
    doc_unit = unit_low[row_count:]
    doc_valid = (row_ids[None, :] < passage_lengths_each[:, None]).reshape(1, -1)
    similar = (
        jnp.einsum("te,se->ts", query_unit, doc_unit, preferred_element_type=jnp.float32)
        / SHARPNESS
    )
    similar = jnp.where(doc_valid, similar, MASKED).reshape(row_count, docs_group, row_count)
    top_score = jnp.max(similar, axis=-1)
    raised = jnp.exp(similar - top_score[..., None])
    raised_total = jnp.sum(raised, axis=-1)
    soft_max = SHARPNESS * (top_score + jnp.log(raised_total))
    query_valid = (row_ids % QLEN < jnp.repeat(question_lengths, QLEN)).astype(jnp.float32)
    lengths = question_lengths.astype(jnp.float32)
    pairing_ratings = (
        jnp.sum((soft_max * query_valid[:, None]).reshape(queries_here, QLEN, docs_group), axis=1)
        / lengths[:, None]
    )
    smoothing_warmth = jnp.exp(logarithmic_warmth[0])
    similarity_entries = pairing_ratings / smoothing_warmth
    top_logit = jnp.max(similarity_entries, axis=-1)
    logit_exp = jnp.exp(similarity_entries - top_logit[:, None])
    logit_total = jnp.sum(logit_exp, axis=-1)
    onehot = (relevant_passage[:, None] == jnp.arange(docs_group, dtype=jnp.int32)[None, :]).astype(
        jnp.float32
    )
    losses = top_logit + jnp.log(logit_total) - jnp.sum(similarity_entries * onehot, axis=-1)
    query_ids = jnp.arange(queries_here, dtype=jnp.int32)
    chosen = (
        (participant_number >= 2) | (query_ids // (queries_here // 2) == participant_number)
    ).astype(jnp.float32)
    local_loss = jnp.sum(chosen * losses) / queries_here
    derivative_similarity_lines = (chosen / queries_here)[:, None] * (
        logit_exp / logit_total[:, None] - onehot
    )
    grad_temp = -jnp.sum(derivative_similarity_lines * similarity_entries)
    derivative_rating_lines = derivative_similarity_lines / smoothing_warmth
    grad_soft = (
        jnp.repeat(derivative_rating_lines / lengths[:, None], QLEN, axis=0) * query_valid[:, None]
    )
    grad_similar = (
        (grad_soft[:, :, None] * (raised / raised_total[..., None]))
        .reshape(row_count, docs_group * row_count)
        .astype(jnp.bfloat16)
    )
    grad_query = jnp.einsum("ts,se->te", grad_similar, doc_unit, preferred_element_type=jnp.float32)
    grad_doc = jnp.einsum("ts,te->se", grad_similar, query_unit, preferred_element_type=jnp.float32)
    grad_unit = jnp.concatenate([grad_query, grad_doc], axis=0)
    grad_proj = inverse * (grad_unit - unit * jnp.sum(grad_unit * unit, axis=-1, keepdims=True))
    return (local_loss, grad_temp, grad_proj.astype(jnp.bfloat16))


def on_device(
    layer_entries,
    triple_projection_matrix,
    attention_exit_matrix,
    expand_matrix,
    contract_matrix,
    nested_projector,
    offset_model_width,
    offset_expanded,
    standardize_factor,
    standardize_offset,
    logarithmic_warmth,
    passage_lengths_each,
    question_lengths,
    relevant_passage,
):
    column_parts = (
        lax.all_gather(triple_projection_matrix, "head", axis=1, tiled=True),
        lax.all_gather(attention_exit_matrix, "head", axis=1, tiled=True),
        lax.all_gather(expand_matrix, "head", axis=1, tiled=True),
        lax.all_gather(contract_matrix, "head", axis=1, tiled=True),
        lax.all_gather(nested_projector, "head", axis=1, tiled=True),
    )
    wqkv_full, wout_full, wup_full, wdown_full, heads_full = (
        lax.all_gather(column_parts[0], "dp", axis=0, tiled=True),
        lax.all_gather(column_parts[1], "dp", axis=0, tiled=True),
        lax.all_gather(column_parts[2], "dp", axis=0, tiled=True),
        lax.all_gather(column_parts[3], "dp", axis=0, tiled=True),
        lax.all_gather(column_parts[4], "dp", axis=0, tiled=True),
    )
    biases_full, bias_mid_full, gains_full, shifts_full = (
        lax.all_gather(offset_model_width, ("dp", "head"), axis=1, tiled=True),
        lax.all_gather(offset_expanded, ("dp", "head"), axis=0, tiled=True),
        lax.all_gather(standardize_factor, ("dp", "head"), axis=1, tiled=True),
        lax.all_gather(standardize_offset, ("dp", "head"), axis=1, tiled=True),
    )
    row_count = layer_entries.shape[0]
    members = lax.axis_size("head")
    participant_number = lax.axis_index("head")
    head_cols = EMB + EMB_MID + EMB_SMALL
    row_ids = jnp.arange(row_count, dtype=jnp.int32)
    is_query = participant_number == 0
    doc_here = passage_lengths_each[jnp.maximum(participant_number - 1, 0)]
    valid = jnp.where(
        is_query, row_ids % QLEN < jnp.repeat(question_lengths, QLEN), row_ids < doc_here
    )
    segment = jnp.where(is_query, row_ids // QLEN, 0)
    position = jnp.where(is_query, row_ids % QLEN, row_ids)
    cosines, sines = rope_tables(position)
    score_scale = HEAD_DIM ** (-0.5)
    block_count = row_count // ROW_BLOCK
    inputs_wide = layer_entries.astype(jnp.float32)
    bias_qkv = biases_full[:3].reshape(3 * D).astype(jnp.float32)
    qkv = (
        jnp.dot(layer_entries, wqkv_full, preferred_element_type=jnp.float32) + bias_qkv
    ).reshape(row_count, 3, HEADS, HEAD_DIM)
    queries = rotate(qkv[:, 0], cosines, sines).astype(jnp.bfloat16)
    keys = rotate(qkv[:, 1], cosines, sines).astype(jnp.bfloat16)
    values = qkv[:, 2].astype(jnp.bfloat16)

    def block_scores(query_block, segment_block):
        raw_scores = (
            jnp.einsum("rhd,thd->hrt", query_block, keys, preferred_element_type=jnp.float32)
            * score_scale
        )
        allowed = (segment_block[:, None] == segment[None, :]) & valid[None, :]
        return jnp.where(allowed[None], raw_scores, MASKED)

    def attend(arguments_given):
        query_block, segment_block = arguments_given
        pairing_ratings = block_scores(query_block, segment_block)
        top_score = jnp.max(pairing_ratings, axis=-1, keepdims=True)
        raised = jnp.exp(pairing_ratings - top_score)
        raised_total = jnp.sum(raised, axis=-1, keepdims=True)
        probs_low = (raised / raised_total).astype(jnp.bfloat16)
        return (
            jnp.einsum("hrt,thd->rhd", probs_low, values, preferred_element_type=jnp.float32),
            top_score,
            raised_total,
        )

    query_blocks = queries.reshape(block_count, ROW_BLOCK, HEADS, HEAD_DIM)
    segment_blocks = segment.reshape(block_count, ROW_BLOCK)
    attended, top_scores, raised_totals = lax.map(attend, (query_blocks, segment_blocks))
    attended = attended.reshape(row_count, D).astype(jnp.bfloat16)
    branch = jnp.dot(attended, wout_full, preferred_element_type=jnp.float32) + biases_full[
        3
    ].astype(jnp.float32)
    normed, scaled_one, inverse_one = norm_forward(
        inputs_wide + branch, gains_full[0].astype(jnp.float32), shifts_full[0].astype(jnp.float32)
    )
    normed_low = normed.astype(jnp.bfloat16)
    pre_act = jnp.dot(
        normed_low, wup_full, preferred_element_type=jnp.float32
    ) + bias_mid_full.astype(jnp.float32)
    hidden = (0.5 * pre_act * (1.0 + jax.scipy.special.erf(pre_act * SQRT_HALF))).astype(
        jnp.bfloat16
    )
    branch_two = jnp.dot(hidden, wdown_full, preferred_element_type=jnp.float32) + biases_full[
        4
    ].astype(jnp.float32)
    final, scaled_two, inverse_two = norm_forward(
        normed + branch_two, gains_full[1].astype(jnp.float32), shifts_full[1].astype(jnp.float32)
    )
    outputs = final.astype(jnp.bfloat16)
    again_parts = (
        lax.all_gather(triple_projection_matrix, "head", axis=1, tiled=True),
        lax.all_gather(attention_exit_matrix, "head", axis=1, tiled=True),
        lax.all_gather(expand_matrix, "head", axis=1, tiled=True),
        lax.all_gather(contract_matrix, "head", axis=1, tiled=True),
        lax.all_gather(nested_projector, "head", axis=1, tiled=True),
    )
    wqkv_back, wout_back, wup_back, wdown_back, heads_back = (
        lax.all_gather(again_parts[0], "dp", axis=0, tiled=True),
        lax.all_gather(again_parts[1], "dp", axis=0, tiled=True),
        lax.all_gather(again_parts[2], "dp", axis=0, tiled=True),
        lax.all_gather(again_parts[3], "dp", axis=0, tiled=True),
        lax.all_gather(again_parts[4], "dp", axis=0, tiled=True),
    )
    all_windows = jnp.concatenate(head_windows(heads_full), axis=1)
    own_proj = jnp.dot(outputs, all_windows, preferred_element_type=jnp.float32).reshape(
        row_count, members, EMB
    )
    mapped_vectors = (
        lax.all_to_all(
            own_proj.astype(jnp.bfloat16), "head", split_axis=1, concat_axis=0, tiled=True
        )
        .astype(own_proj.dtype)
        .reshape(members * row_count, EMB)
    )
    local_loss, grad_temp, grad_proj = pairing_objective(
        mapped_vectors,
        participant_number,
        passage_lengths_each,
        question_lengths,
        relevant_passage,
        logarithmic_warmth,
    )
    grad_back = lax.all_to_all(
        grad_proj.reshape(members * row_count, 1, EMB),
        "head",
        split_axis=0,
        concat_axis=1,
        tiled=True,
    ).reshape(row_count, members * EMB)
    back_all = jnp.concatenate(head_windows(heads_back), axis=1)
    grad_final = jnp.einsum("te,de->td", grad_back, back_all, preferred_element_type=jnp.float32)
    grad_all = jnp.einsum("td,te->de", outputs, grad_back, preferred_element_type=jnp.float32)
    starts = (0, 0, EMB, EMB + EMB_MID)
    widths = (EMB, EMB, EMB_MID, EMB_SMALL)
    grad_heads = jnp.zeros((D, head_cols), jnp.float32)
    for member in range(4):
        grad_heads = grad_heads.at[:, starts[member] : starts[member] + widths[member]].add(
            grad_all[:, member * EMB : member * EMB + widths[member]]
        )
    grad_two, gain_grad_two, shift_grad_two = norm_backward(
        grad_final, scaled_two, inverse_two, gains_full[1].astype(jnp.float32)
    )
    grad_branch_two = grad_two.astype(jnp.bfloat16)
    grad_w_down = jnp.einsum(
        "tf,td->fd", hidden, grad_branch_two, preferred_element_type=jnp.float32
    )
    grad_hidden = jnp.einsum(
        "td,fd->tf", grad_branch_two, wdown_back, preferred_element_type=jnp.float32
    )
    slope = (
        0.5 * (1.0 + jax.scipy.special.erf(pre_act * SQRT_HALF))
        + pre_act * jnp.exp(-0.5 * pre_act * pre_act) * GAUSS_SCALE
    )
    grad_pre = (grad_hidden * slope).astype(jnp.bfloat16)
    grad_w_up = jnp.einsum("td,tf->df", normed_low, grad_pre, preferred_element_type=jnp.float32)
    grad_normed = grad_two + jnp.einsum(
        "tf,df->td", grad_pre, wup_back, preferred_element_type=jnp.float32
    )
    grad_one, gain_grad_one, shift_grad_one = norm_backward(
        grad_normed, scaled_one, inverse_one, gains_full[0].astype(jnp.float32)
    )
    grad_branch = grad_one.astype(jnp.bfloat16)
    grad_w_out = jnp.einsum("tc,td->cd", attended, grad_branch, preferred_element_type=jnp.float32)
    grad_attended = (
        jnp.einsum("td,cd->tc", grad_branch, wout_back, preferred_element_type=jnp.float32)
        .astype(jnp.bfloat16)
        .reshape(block_count, ROW_BLOCK, HEADS, HEAD_DIM)
    )

    def attend_back(carry, arguments_given):
        grad_keys, grad_values = carry
        query_block, segment_block, top_score, raised_total, grad_block = arguments_given
        probs = jnp.exp(block_scores(query_block, segment_block) - top_score) / raised_total
        grad_probs = jnp.einsum(
            "rhd,thd->hrt", grad_block, values, preferred_element_type=jnp.float32
        )
        derivative_rating_lines = (
            probs * (grad_probs - jnp.sum(probs * grad_probs, axis=-1, keepdims=True))
        ).astype(jnp.bfloat16)
        grad_query = (
            jnp.einsum(
                "hrt,thd->rhd", derivative_rating_lines, keys, preferred_element_type=jnp.float32
            )
            * score_scale
        )
        grad_keys = (
            grad_keys
            + jnp.einsum(
                "hrt,rhd->thd",
                derivative_rating_lines,
                query_block,
                preferred_element_type=jnp.float32,
            )
            * score_scale
        )
        grad_values = grad_values + jnp.einsum(
            "hrt,rhd->thd",
            probs.astype(jnp.bfloat16),
            grad_block,
            preferred_element_type=jnp.float32,
        )
        return ((grad_keys, grad_values), grad_query)

    zeros_rows = jnp.zeros((row_count, HEADS, HEAD_DIM), jnp.float32)
    (grad_keys, grad_values), grad_queries = lax.scan(
        attend_back,
        (zeros_rows, zeros_rows),
        (query_blocks, segment_blocks, top_scores, raised_totals, grad_attended),
    )
    grad_queries = grad_queries.reshape(row_count, HEADS, HEAD_DIM)
    grad_qkv = (
        jnp.stack(
            [
                unrotate(grad_queries, cosines, sines),
                unrotate(grad_keys, cosines, sines),
                grad_values,
            ],
            axis=1,
        )
        .reshape(row_count, 3 * D)
        .astype(jnp.bfloat16)
    )
    grad_w_qkv = jnp.einsum(
        "tc,tk->ck", layer_entries, grad_qkv, preferred_element_type=jnp.float32
    )
    grad_tokens = grad_one + jnp.einsum(
        "tk,ck->tc", grad_qkv, wqkv_back, preferred_element_type=jnp.float32
    )
    gradient_bias_query_key_value = jnp.sum(grad_qkv, axis=0, dtype=jnp.float32).reshape(3, D)
    grad_bias_d = jnp.concatenate(
        [
            gradient_bias_query_key_value,
            jnp.sum(grad_branch, axis=0, dtype=jnp.float32)[None, :],
            jnp.sum(grad_branch_two, axis=0, dtype=jnp.float32)[None, :],
        ],
        axis=0,
    )
    grad_bias_up = jnp.sum(grad_pre, axis=0, dtype=jnp.float32)
    grad_gain = jnp.stack([gain_grad_one, gain_grad_two])
    grad_shift = jnp.stack([shift_grad_one, shift_grad_two])
    row_summed = (
        lax.psum_scatter(grad_w_qkv, "dp", scatter_dimension=0, tiled=True),
        lax.psum_scatter(grad_w_out, "dp", scatter_dimension=0, tiled=True),
        lax.psum_scatter(grad_w_up, "dp", scatter_dimension=0, tiled=True),
        lax.psum_scatter(grad_w_down, "dp", scatter_dimension=0, tiled=True),
        lax.psum_scatter(grad_heads, "dp", scatter_dimension=0, tiled=True),
    )
    summed = (
        lax.psum_scatter(
            row_summed[0].astype(jnp.bfloat16), "head", scatter_dimension=1, tiled=True
        ).astype(jnp.float32),
        lax.psum_scatter(
            row_summed[1].astype(jnp.bfloat16), "head", scatter_dimension=1, tiled=True
        ).astype(jnp.float32),
        lax.psum_scatter(
            row_summed[2].astype(jnp.bfloat16), "head", scatter_dimension=1, tiled=True
        ).astype(jnp.float32),
        lax.psum_scatter(
            row_summed[3].astype(jnp.bfloat16), "head", scatter_dimension=1, tiled=True
        ).astype(jnp.float32),
        lax.psum_scatter(
            row_summed[4].astype(jnp.bfloat16), "head", scatter_dimension=1, tiled=True
        ).astype(jnp.float32),
    )
    vector_summed = (
        lax.psum_scatter(grad_bias_d, ("dp", "head"), scatter_dimension=1, tiled=True),
        lax.psum_scatter(grad_bias_up, ("dp", "head"), scatter_dimension=0, tiled=True),
        lax.psum_scatter(grad_gain, ("dp", "head"), scatter_dimension=1, tiled=True),
        lax.psum_scatter(grad_shift, ("dp", "head"), scatter_dimension=1, tiled=True),
    )
    loss_total, temp_total = lax.psum((local_loss, grad_temp), ("dp", "head"))
    return (
        outputs,
        loss_total.reshape(1),
        grad_tokens,
        summed[0],
        summed[1],
        summed[2],
        summed[3],
        summed[4],
        vector_summed[0],
        vector_summed[1],
        vector_summed[2],
        vector_summed[3],
        temp_total.reshape(1),
    )


def solution(mesh):
    return jax.shard_map(
        on_device,
        mesh=mesh,
        in_specs=(
            P(("dp", "head"), None),
            P("dp", "head"),
            P("dp", "head"),
            P("dp", "head"),
            P("dp", "head"),
            P("dp", "head"),
            P(None, ("dp", "head")),
            P(("dp", "head")),
            P(None, ("dp", "head")),
            P(None, ("dp", "head")),
            P(),
            P("dp"),
            P("dp"),
            P("dp"),
        ),
        out_specs=(
            P(("dp", "head"), None),
            P(),
            P(("dp", "head"), None),
            P("dp", "head"),
            P("dp", "head"),
            P("dp", "head"),
            P("dp", "head"),
            P("dp", "head"),
            P(None, ("dp", "head")),
            P(("dp", "head")),
            P(None, ("dp", "head")),
            P(None, ("dp", "head")),
            P(),
        ),
        check_vma=False,
    )
```

profile of v0, /device:TPU:0, one launch (start us, length us, event | category | flops | bytes accessed | tf_op | source)
XLA Modules:
  0.0 1416.7 jit_solution(12120307907434827334)
XLA Ops:
  8.8 27.2 %all_gather.52 = bf16[128,3072]{1,0:T(8,128)(2,1)} all-gather(bf16[128,768]{1,0:T(8,128)(2,1)} %param.23), channel_id=1, replica_groups=mesh['dp'=8,'head'=4] {'head'}, dimensions={1}, use_global_device_ids=true | all-gather | bytes 983040 | tf_op jit(solution)/shard_map/all_gather | solution.py:169
  36.1 17.9 %all_gather.55 = bf16[128,1024]{1,0:T(8,128)(2,1)} all-gather(bf16[128,256]{1,0:T(8,128)(2,1)} %param.24), channel_id=1, replica_groups=mesh['dp'=8,'head'=4] {'head'}, dimensions={1}, use_global_device_ids=true | all-gather | bytes 327680 | tf_op jit(solution)/shard_map/all_gather | solution.py:170
  54.6 26.4 %all-gather.19.cloned.1.call-done = bf16[512,1024]{1,0:T(8,128)(2,1)} async-done(((bf16[512,256]{1,0:T(8,128)(2,1)}), bf16[512,1024]{1,0:T(8,128)(2,1)}) %all-gather.19.cloned.1.call-update) | async-done | bytes 1048592 | tf_op jit(solution)/shard_map/all_gather | solution.py:172
  81.1 67.3 %all-gather = bf16[32,32,5]{1,2,0:T(8,128)(2,1)S(1)} all-gather(bf16[1,32,5]{1,2,0:T(8,128)(2,1)S(1)} %bitcast.206), channel_id=1, replica_groups=mesh['dp'=8,'head'=4] {'dp','head'}, dimensions={0}, use_global_device_ids=true | all-gather | bytes 10560 | tf_op jit(solution)/shard_map/all_gather | solution.py:183
  148.5 63.1 %all-gather.3 = bf16[32,1,128]{2,1,0:T(2,128)(2,1)S(1)} all-gather(bf16[1,1,128]{2,1,0:T(2,128)(2,1)S(1)} %bitcast.207), channel_id=1, replica_groups=mesh['dp'=8,'head'=4] {'dp','head'}, dimensions={0}, use_global_device_ids=true | all-gather | bytes 8448 | tf_op jit(solution)/shard_map/all_gather | solution.py:184
  212.4 65.2 %all-gather.2 = bf16[32,32,2]{1,2,0:T(2,128)(2,1)S(1)} all-gather(bf16[1,32,2]{1,2,0:T(2,128)(2,1)S(1)} %bitcast.208), channel_id=1, replica_groups=mesh['dp'=8,'head'=4] {'dp','head'}, dimensions={0}, use_global_device_ids=true | all-gather | bytes 4224 | tf_op jit(solution)/shard_map/all_gather | solution.py:186
  277.7 63.0 %all-gather.1 = bf16[32,32,2]{1,2,0:T(2,128)(2,1)S(1)} all-gather(bf16[1,32,2]{1,2,0:T(2,128)(2,1)S(1)} %bitcast.209), channel_id=1, replica_groups=mesh['dp'=8,'head'=4] {'dp','head'}, dimensions={0}, use_global_device_ids=true | all-gather | bytes 4224 | tf_op jit(solution)/shard_map/all_gather | solution.py:185
  342.8 13.1 all_gather.64
  355.9 8.8 all_gather.65
  368.5 6.3 convolution_add_fusion.1
  390.7 7.8 convolution_add_fusion
  398.5 7.2 fusion.80
  412.6 8.9 all-to-all-done
  447.4 5.7 all-to-all-done.1
  462.1 6.8 convert_reduce_fusion
  489.4 6.3 convolution_bitcast_fusion
  495.7 10.0 fusion.73
  505.8 11.1 fusion.66
  522.3 29.0 %reduce-scatter.26.cloned.1.call-done = f32[128,1024]{1,0:T(8,128)} async-done(((f32[1024,1024]{1,0:T(8,128)}), f32[128,1024]{1,0:T(8,128)}) %reduce-scatter.26.cloned.1.call-update) | async-done | bytes 524304 | tf_op jit(solution)/shard_map/reduce_scatter | solution.py:410
  553.1 94.1 %reduce-scatter.22.cloned.1.call-done = f32[128,3072]{0,1:T(8,128)} async-done(((f32[1024,3072]{0,1:T(8,128)}), f32[128,3072]{0,1:T(8,128)}) %reduce-scatter.22.cloned.1.call-update) | async-done | bytes 1572880 | tf_op jit(solution)/shard_map/reduce_scatter | solution.py:409
  649.7 116.9 %reduce-scatter.30.cloned.1.call-done = f32[128,4096]{1,0:T(8,128)} async-done(((f32[1024,4096]{1,0:T(8,128)}), f32[128,4096]{1,0:T(8,128)}) %reduce-scatter.30.cloned.1.call-update) | async-done | bytes 2097168 | tf_op jit(solution)/shard_map/reduce_scatter | solution.py:411
  769.3 116.8 %reduce-scatter.34.cloned.1.call-done = f32[512,1024]{1,0:T(8,128)} async-done(((f32[4096,1024]{1,0:T(8,128)}), f32[512,1024]{1,0:T(8,128)}) %reduce-scatter.34.cloned.1.call-update) | async-done | bytes 2097168 | tf_op jit(solution)/shard_map/reduce_scatter | solution.py:412
  891.4 41.0 %all-reduce.4 = (f32[1]{0:T(128)}, f32[4096]{0:T(1024)S(1)}, f32[1]{0:T(128)}) all-reduce(f32[1]{0:T(128)} %bitcast.30, f32[4096]{0:T(1024)S(1)} %get-tuple-element.241, f32[1]{0:T(128)} %bitcast.56), channel_id=1, replica_groups=mesh['dp'=8,'head'=4] {'dp','head'}, use_global_device_ids=true, to_apply=%region_14.15 | all-reduce | flops 4098 | bytes 32784 | tf_op jit(solution)/shard_map/psum | solution.py:438
  933.0 5.6 convolution_add_fusion.3
  938.6 84.5 %reduce-scatter.42.cloned.1.call-done = f32[32,2]{1,0:T(8,128)} async-done(((f32[1024,2]{1,0:T(8,128)}), f32[32,2]{1,0:T(8,128)}) %reduce-scatter.42.cloned.1.call-update) | async-done | bytes 272
  1024.5 131.3 %reduce-scatter.44.cloned.1.call-done = f32[32,2]{1,0:T(8,128)} async-done(((f32[1024,2]{1,0:T(8,128)}), f32[32,2]{1,0:T(8,128)}) %reduce-scatter.44.cloned.1.call-update) | async-done | bytes 272
  1157.1 131.7 %reduce-scatter.40.cloned.1.call-done = f32[32,5]{1,0:T(8,128)} async-done(((f32[1024,5]{1,0:T(8,128)}), f32[32,5]{1,0:T(8,128)}) %reduce-scatter.40.cloned.1.call-update) | async-done | bytes 656
  1290.2 16.5 %reduce-scatter.46.cloned.1.call-done = bf16[128,72]{0,1:T(8,128)(2,1)} async-done(((bf16[128,288]{0,1:T(8,128)(2,1)}), bf16[128,72]{0,1:T(8,128)(2,1)}) %reduce-scatter.46.cloned.1.call-update) | async-done | bytes 18448
  1308.1 19.2 %reduce-scatter.28.cloned.1.call-done = bf16[128,256]{1,0:T(8,128)(2,1)} async-done(((bf16[128,1024]{1,0:T(8,128)(2,1)}), bf16[128,256]{1,0:T(8,128)(2,1)}) %reduce-scatter.28.cloned.1.call-update) | async-done | bytes 65552 | tf_op jit(solution)/shard_map/reduce_scatter | solution.py:419
  1328.8 22.4 %reduce-scatter.24.cloned.1.call-done = bf16[128,768]{0,1:T(8,128)(2,1)} async-done(((bf16[128,3072]{0,1:T(8,128)(2,1)}), bf16[128,768]{0,1:T(8,128)(2,1)}) %reduce-scatter.24.cloned.1.call-update) | async-done | bytes 196624 | tf_op jit(solution)/shard_map/reduce_scatter | solution.py:416
  1352.9 26.9 %reduce-scatter.32.cloned.1.call-done = bf16[128,1024]{1,0:T(8,128)(2,1)} async-done(((bf16[128,4096]{1,0:T(8,128)(2,1)}), bf16[128,1024]{1,0:T(8,128)(2,1)}) %reduce-scatter.32.cloned.1.call-update) | async-done | bytes 262160 | tf_op jit(solution)/shard_map/reduce_scatter | solution.py:422
  1381.6 26.3 %reduce-scatter.36.cloned.1.call-done = bf16[512,256]{1,0:T(8,128)(2,1)} async-done(((bf16[512,1024]{1,0:T(8,128)(2,1)}), bf16[512,256]{1,0:T(8,128)(2,1)}) %reduce-scatter.36.cloned.1.call-update) | async-done | bytes 262160 | tf_op jit(solution)/shard_map/reduce_scatter | solution.py:425
  (248 shorter events, 115.2 us)
Async XLA Ops:
  7.2 73.9 %copy-start.28 = (bf16[5,32]{1,0:T(8,128)(2,1)S(1)}, bf16[5,32]{1,0:T(8,128)(2,1)}, u32[]{:S(2)}) copy-start(bf16[5,32]{1,0:T(8,128)(2,1)} %param.28) | copy-start | bytes 964
  7.2 141.3 %copy-start.30 = (bf16[128]{0:T(256)(128)(2,1)S(1)}, bf16[128]{0:T(256)(128)(2,1)}, u32[]{:S(2)}) copy-start(bf16[128]{0:T(256)(128)(2,1)} %param.29) | copy-start | bytes 772
  7.2 205.0 %copy-start.24 = (s32[8]{0:T(128)S(1)}, s32[8]{0:T(128)}, u32[]{:S(2)}) copy-start(s32[8]{0:T(128)} %param.34) | copy-start | bytes 100
  7.2 205.2 %copy-start.31 = (bf16[2,32]{1,0:T(2,128)(2,1)S(1)}, bf16[2,32]{1,0:T(2,128)(2,1)}, u32[]{:S(2)}) copy-start(bf16[2,32]{1,0:T(2,128)(2,1)} %param.31) | copy-start | bytes 388
  7.2 270.5 %copy-start.32 = (bf16[2,32]{1,0:T(2,128)(2,1)S(1)}, bf16[2,32]{1,0:T(2,128)(2,1)}, u32[]{:S(2)}) copy-start(bf16[2,32]{1,0:T(2,128)(2,1)} %param.30) | copy-start | bytes 388
  7.2 334.3 %copy-start.33 = (s32[3]{0:T(128)S(1)}, s32[3]{0:T(128)}, u32[]{:S(2)}) copy-start(s32[3]{0:T(128)} %param.33) | copy-start | bytes 40
  7.2 335.5 %copy-start.20 = (bf16[128,72]{0,1:T(8,128)(2,1)S(1)}, bf16[128,72]{0,1:T(8,128)(2,1)}, u32[]{:S(2)}) copy-start(bf16[128,72]{0,1:T(8,128)(2,1)} %param.27) | copy-start | bytes 55300
  7.3 361.3 %copy-start.5 = (bf16[256,1024]{1,0:T(8,128)(2,1)S(1)}, bf16[256,1024]{1,0:T(8,128)(2,1)}, u32[]{:S(2)}) copy-start(bf16[256,1024]{1,0:T(8,128)(2,1)} %param.22) | copy-start | bytes 1572868
  7.3 46.8 %all-gather.15.cloned.1.call-start = ((), (), s32[]{:S(2)}) async-start(), calls=%async_computation.17 | async-start | bytes 1310720 | tf_op jit(solution)/shard_map/all_gather | solution.py:171
  8.0 73.1 %all-gather.19.cloned.1.call-start = ((), (), s32[]{:S(2)}) async-start(), calls=%async_computation.19 | async-start | bytes 1310720 | tf_op jit(solution)/shard_map/all_gather | solution.py:172
  8.7 359.8 %all-gather.11.cloned.1.call-start = ((), (), s32[]{:S(2)}) async-start(), calls=%async_computation.15 | async-start | bytes 7077888 | tf_op jit(solution)/shard_map/all_gather | solution.py:176
  36.0 351.7 %all-gather.13.cloned.1.call-start = ((), (), s32[]{:S(2)}) async-start(), calls=%async_computation.16 | async-start | bytes 2359296 | tf_op jit(solution)/shard_map/all_gather | solution.py:177
  54.0 336.6 %all-gather.17.cloned.1.call-start = ((), (), s32[]{:S(2)}) async-start(), calls=%async_computation.18 | async-start | bytes 9437184 | tf_op jit(solution)/shard_map/all_gather | solution.py:178
  54.6 343.9 %all-gather.21.cloned.1.call-start = ((), (), s32[]{:S(2)}) async-start(), calls=%async_computation.20 | async-start | bytes 9437184 | tf_op jit(solution)/shard_map/all_gather | solution.py:179
  406.0 16.0 %copy-start.26 = (pred[768]{0:T(1024)(128)(4,1)S(1)}, pred[768]{0:T(1024)(128)(4,1)}, u32[]{:S(2)}) copy-start(pred[768]{0:T(1024)(128)(4,1)} %lt.95) | copy-start | bytes 2308
  408.3 13.2 all-to-all-start
  442.6 10.4 all-to-all-start.1
  446.1 74.6 %reduce-scatter.38.cloned.1.call-start = ((), (), s32[]{:S(2)}) async-start(), calls=%async_computation.29 | async-start | bytes 1327104 | tf_op jit(solution)/shard_map/reduce_scatter | solution.py:413
  460.3 91.0 %reduce-scatter.26.cloned.1.call-start = ((), (), s32[]{:S(2)}) async-start(), calls=%async_computation.23 | async-start | bytes 4718592 | tf_op jit(solution)/shard_map/reduce_scatter | solution.py:410
  474.8 172.4 %reduce-scatter.22.cloned.1.call-start = ((), (), s32[]{:S(2)}) async-start(), calls=%async_computation.21 | async-start | bytes 14155776 | tf_op jit(solution)/shard_map/reduce_scatter | solution.py:409
  495.7 270.9 %reduce-scatter.30.cloned.1.call-start = ((), (), s32[]{:S(2)}) async-start(), calls=%async_computation.25 | async-start | bytes 18874368 | tf_op jit(solution)/shard_map/reduce_scatter | solution.py:411
  505.8 380.4 %reduce-scatter.34.cloned.1.call-start = ((), (), s32[]{:S(2)}) async-start(), calls=%async_computation.27 | async-start | bytes 18874368 | tf_op jit(solution)/shard_map/reduce_scatter | solution.py:412
  516.9 506.2 %reduce-scatter.42.cloned.1.call-start = ((), (), s32[]{:S(2)}) async-start(), calls=%async_computation.31 | async-start | bytes 540672
  518.0 637.7 %reduce-scatter.44.cloned.1.call-start = ((), (), s32[]{:S(2)}) async-start(), calls=%async_computation.32 | async-start | bytes 540672
  519.2 769.6 %reduce-scatter.40.cloned.1.call-start = ((), (), s32[]{:S(2)}) async-start(), calls=%async_computation.30 | async-start | bytes 540672
  520.4 786.4 %reduce-scatter.46.cloned.1.call-start = ((), (), s32[]{:S(2)}) async-start(), calls=%async_computation.33 | async-start | bytes 92160
  522.3 805.0 %reduce-scatter.28.cloned.1.call-start = ((), (), s32[]{:S(2)}) async-start(), calls=%async_computation.24 | async-start | bytes 327680 | tf_op jit(solution)/shard_map/reduce_scatter | solution.py:419
  553.1 798.1 %reduce-scatter.24.cloned.1.call-start = ((), (), s32[]{:S(2)}) async-start(), calls=%async_computation.22 | async-start | bytes 983040 | tf_op jit(solution)/shard_map/reduce_scatter | solution.py:416
  649.6 239.2 %copy-start.29 = (s32[8]{0:T(128)S(1)}, s32[8]{0:T(128)}, u32[]{:S(2)}) copy-start(s32[8]{0:T(128)} %param.35) | copy-start | bytes 100
  649.6 283.3 %copy-start.3 = (bf16[256,3,16,64]{0,3,2,1:T(8,128)(2,1)S(1)}, bf16[256,3,16,64]{0,3,2,1:T(8,128)(2,1)}, u32[]{:S(2)}) copy-start(bf16[256,3,16,64]{0,3,2,1:T(8,128)(2,1)} %copy-done.2) | copy-start | bytes 4718596
  649.7 730.1 %reduce-scatter.32.cloned.1.call-start = ((), (), s32[]{:S(2)}) async-start(), calls=%async_computation.26 | async-start | bytes 1310720 | tf_op jit(solution)/shard_map/reduce_scatter | solution.py:422
  769.3 638.6 %reduce-scatter.36.cloned.1.call-start = ((), (), s32[]{:S(2)}) async-start(), calls=%async_computation.28 | async-start | bytes 1310720 | tf_op jit(solution)/shard_map/reduce_scatter | solution.py:425
  (25 other events, 115.4 us)
Sparse Core Ops, SparseCore 0:
  9.7 39.6 all-gather.14
  51.0 30.0 all-gather.18
  83.0 43.9 all-gather.10
  128.7 27.8 all-gather.12
  158.4 54.4 all-gather.16
  214.6 54.4 all-gather.20
  460.4 35.7 reduce-scatter.37
  499.9 51.2 reduce-scatter.25
  554.8 92.3 reduce-scatter.21
  650.6 115.9 reduce-scatter.29
  770.2 115.9 reduce-scatter.33
  888.8 134.3 reduce-scatter.41
  1025.5 130.2 reduce-scatter.43
  1158.4 130.3 reduce-scatter.39
  1291.6 15.0 reduce-scatter.45
  1309.4 17.8 reduce-scatter.27
  1329.5 21.5 reduce-scatter.23
  1353.4 26.3 reduce-scatter.31
  1382.1 25.7 reduce-scatter.35
where the time goes:
time: 1430 us; the launch traced here: 1420 us
  waiting for transfers between devices  859 us (60%)
  blocking collectives  367 us (26%)
  matrix products  91.1 us (6%)
  other arithmetic  41.6 us (3%)
  local copies, waits for them, and re-layouts  33 us (2%)
  between operations  17.3 us (1%)
    unnamed x23, waiting for transfers between devices  366 us
    reduce_scatter x1, waiting for transfers between devices, on_device(): lax.psum_scatter(grad_w_up, 'dp', scatter_dimension=0, tiled=True)  117 us
    reduce_scatter x1, waiting for transfers between devices, on_device(): lax.psum_scatter(grad_w_down, 'dp', scatter_dimension=0, tiled=True)  117 us
    reduce_scatter x1, waiting for transfers between devices, on_device(): lax.psum_scatter(grad_w_qkv, 'dp', scatter_dimension=0, tiled=True)  94.1 us
    all_gather x1, blocking collectives, on_device(): lax.all_gather(offset_model_width, ('dp', 'head'), axis=1, tiled=True)  67.3 us
    all_gather x1, blocking collectives, on_device(): lax.all_gather(standardize_offset, ('dp', 'head'), axis=1, tiled=True)  65.2 us
    all_gather x1, blocking collectives, on_device(): lax.all_gather(offset_expanded, ('dp', 'head'), axis=0, tiled=True)  63.1 us
    all_gather x1, blocking collectives, on_device(): lax.all_gather(standardize_factor, ('dp', 'head'), axis=1, tiled=True)  63 us
  transfers between devices with their start and end apart: 21, of which 15 were waited for; matrix products, arithmetic and copies ran while one was open for 9% of the time, Pallas kernels for 0%

commit v1 on v0

v1 whole, which is shorter than its diff:
```python
import jax
import jax.numpy as jnp
from jax import lax
from jax.sharding import PartitionSpec as P

D = 1024
HEADS = 16
HEAD_DIM = 64
FF = 4096
EMB = 128
EMB_MID = 96
EMB_SMALL = 64
QLEN = 32

EPS_NORM = 1e-05
EPS_UNIT = 1e-06
SHARPNESS = 0.05
ROPE_BASE = 10000.0
MASKED = -1000000000.0
SQRT_HALF = 0.7071067811865476
GAUSS_SCALE = 0.3989422804014327

BF = jnp.bfloat16
F32 = jnp.float32
STARTS = (0, EMB, EMB + EMB_MID)
WIDTHS = (EMB, EMB_MID, EMB_SMALL)
SLOTS = 3
QUADS = 4
GROUP = 128
HIDE = FF // 8


def mm(a, b):
    return jnp.dot(a, b, preferred_element_type=F32)


def mm_tn(a, b):
    return lax.dot_general(a, b, (((0,), (0,)), ((), ())), preferred_element_type=F32)


def mm_nt(a, b):
    return lax.dot_general(a, b, (((1,), (1,)), ((), ())), preferred_element_type=F32)


def norm_forward(values, gain, shift):
    centred = values - jnp.mean(values, axis=-1, keepdims=True)
    variance = jnp.mean(centred * centred, axis=-1, keepdims=True)
    inverse = lax.rsqrt(variance + EPS_NORM)
    scaled = centred * inverse
    return (scaled * gain + shift, scaled, inverse)


def norm_backward(grad_out, scaled, inverse, gain):
    grad_scaled = grad_out * gain
    grad_in = inverse * (
        grad_scaled
        - jnp.mean(grad_scaled, axis=-1, keepdims=True)
        - scaled * jnp.mean(grad_scaled * scaled, axis=-1, keepdims=True)
    )
    return (grad_in, jnp.sum(grad_out * scaled, axis=0), jnp.sum(grad_out, axis=0))


def rope_tables(positions):
    halfway = HEAD_DIM // 2
    powers = jnp.arange(halfway, dtype=F32) * (2.0 / HEAD_DIM)
    angles = positions.astype(F32)[:, None] * (ROPE_BASE ** (-powers))[None, :]
    return (jnp.cos(angles)[:, None, :], jnp.sin(angles)[:, None, :])


def rotate(vectors, cosines, sines):
    halfway = vectors.shape[-1] // 2
    first = vectors[..., :halfway]
    second = vectors[..., halfway:]
    return jnp.concatenate(
        [first * cosines - second * sines, second * cosines + first * sines], axis=-1
    )


def pad_windows(matrix):
    columns = [
        jnp.pad(matrix[:, s : s + w], ((0, 0), (0, EMB - w))) for s, w in zip(STARTS, WIDTHS)
    ]
    return jnp.concatenate(columns, axis=1)


def soft_maxsim(all_proj, place, doc_lens, query_lens, targets, temp_log):
    docs = doc_lens.shape[0]
    rows = all_proj.shape[0] // (docs + 1)
    queries = query_lens.shape[0]
    own_doc = jnp.maximum(place - 1, 0)
    row_ids = jnp.arange(rows, dtype=jnp.int32)
    doc_valid = (row_ids[None, :] < doc_lens[:, None]).reshape(1, -1)
    query_valid = (row_ids % QLEN < jnp.repeat(query_lens, QLEN)).astype(F32)
    lengths = query_lens.astype(F32)
    warmth = jnp.exp(temp_log[0])
    onehot = (targets[:, None] == jnp.arange(docs, dtype=jnp.int32)[None, :]).astype(F32)
    loss = jnp.zeros((), F32)
    grad_temp = jnp.zeros((), F32)
    grads = []
    for slot in range(SLOTS):
        mapped = all_proj[:, slot * EMB : (slot + 1) * EMB].astype(F32)
        inverse = lax.rsqrt(jnp.sum(mapped * mapped, axis=-1, keepdims=True) + EPS_UNIT)
        unit = mapped * inverse
        low = unit.astype(BF)
        query_unit, doc_unit = low[:rows], low[rows:]
        similar = jnp.where(doc_valid, mm_nt(query_unit, doc_unit) / SHARPNESS, MASKED)
        similar = similar.reshape(rows, docs, rows)
        top = jnp.max(similar, axis=-1)
        raised = jnp.exp(similar - top[..., None])
        total = jnp.sum(raised, axis=-1)
        soft = SHARPNESS * (top + jnp.log(total))
        ratings = (
            jnp.sum((soft * query_valid[:, None]).reshape(queries, QLEN, docs), axis=1)
            / lengths[:, None]
        )
        logits = ratings / warmth
        top_logit = jnp.max(logits, axis=-1)
        logit_exp = jnp.exp(logits - top_logit[:, None])
        logit_total = jnp.sum(logit_exp, axis=-1)
        losses = top_logit + jnp.log(logit_total) - jnp.sum(logits * onehot, axis=-1)
        loss = loss + jnp.sum(losses) / queries
        grad_logits = (logit_exp / logit_total[:, None] - onehot) / queries
        grad_temp = grad_temp - jnp.sum(grad_logits * logits)
        grad_soft = (
            jnp.repeat(grad_logits / warmth / lengths[:, None], QLEN, axis=0)
            * query_valid[:, None]
        )
        grad_similar = (
            (grad_soft[:, :, None] * (raised / total[..., None]))
            .reshape(rows, docs * rows)
            .astype(BF)
        )
        own_similar = lax.dynamic_slice(grad_similar, (0, own_doc * rows), (rows, rows))
        grad_unit = jnp.where(
            place == 0, mm(grad_similar, doc_unit), mm_tn(own_similar, query_unit)
        )
        own_unit = lax.dynamic_slice(unit, (place * rows, 0), (rows, EMB))
        own_inverse = lax.dynamic_slice(inverse, (place * rows, 0), (rows, 1))
        grads.append(
            own_inverse
            * (grad_unit - own_unit * jnp.sum(grad_unit * own_unit, axis=-1, keepdims=True))
        )
    return loss, grad_temp, jnp.concatenate(grads, axis=1).astype(BF)


def on_device(
    layer_entries,
    triple_projection_matrix,
    attention_exit_matrix,
    expand_matrix,
    contract_matrix,
    nested_projector,
    offset_model_width,
    offset_expanded,
    standardize_factor,
    standardize_offset,
    logarithmic_warmth,
    passage_lengths_each,
    question_lengths,
    relevant_passage,
):
    n_dp = lax.axis_size("dp")
    n_hd = lax.axis_size("head")
    n_all = n_dp * n_hd
    dp = lax.axis_index("dp")
    hd = lax.axis_index("head")
    low_span = n_dp // 8
    quad = dp // (2 * low_span)
    core = (dp // low_span) % 2
    pair_mask = low_span
    x_mask = 2 * low_span
    y_mask = 4 * low_span

    def swap(a, dp_mask=0, hd_mask=0):
        pairs = [
            (d * n_hd + h, (d ^ dp_mask) * n_hd + (h ^ hd_mask))
            for d in range(n_dp)
            for h in range(n_hd)
        ]
        return lax.ppermute(a, ("dp", "head"), pairs)

    def joined(bit, own, other):
        return jnp.where(
            bit == 0, jnp.concatenate([own, other], 0), jnp.concatenate([other, own], 0)
        )

    def gather_low(a):
        span = 1
        while span < low_span:
            a = joined((dp // span) % 2, a, swap(a, span))
            span *= 2
        return a

    def gather_head(a):
        span = 1
        while span < n_hd:
            a = joined((hd // span) % 2, a, swap(a, 0, span))
            span *= 2
        return a

    def scatter_low(a):
        span = low_span // 2
        while span >= 1:
            half = a.shape[0] // 2
            bit = (dp // span) % 2
            give = lax.dynamic_slice_in_dim(a, (1 - bit) * half, half, 0)
            keep = lax.dynamic_slice_in_dim(a, bit * half, half, 0)
            a = (keep.astype(F32) + swap(give, span).astype(F32)).astype(BF)
            span //= 2
        return a

    rows = layer_entries.shape[0]

    wup_low = gather_low(expand_matrix)
    wdown_low = gather_low(contract_matrix)
    up_rows = wup_low.shape[0]
    col_blocks = wup_low.shape[1] // 256
    packed_mlp = jnp.concatenate(
        [wup_low[:, i * 256 : (i + 1) * 256] for i in range(col_blocks)] + [wdown_low], axis=0
    )
    if low_span > 1:
        dp_groups = [
            [((q * 2 + k) * low_span + s) for q in range(QUADS) for k in range(2)]
            for s in range(low_span)
        ]
        mlp_all = lax.all_gather(
            lax.all_gather(packed_mlp, "head"), "dp", axis_index_groups=dp_groups
        )
        mlp_all = mlp_all.reshape((8, n_hd) + packed_mlp.shape)
    else:
        mlp_all = lax.all_gather(packed_mlp, ("dp", "head")).reshape(
            (8, n_hd) + packed_mlp.shape
        )
    heads_all = lax.all_gather(nested_projector, "head", axis=1, tiled=True)
    wide = offset_model_width.shape[1]
    vectors = jnp.concatenate(
        [
            offset_model_width,
            standardize_factor,
            standardize_offset,
            offset_expanded.reshape(FF // D, wide),
        ],
        axis=0,
    )
    vectors = lax.all_gather(lax.all_gather(vectors, "head"), "dp").reshape(n_all, 13, wide)

    partner_rows = swap(layer_entries, pair_mask)
    lens_own = jnp.concatenate([passage_lengths_each, question_lengths])
    lens_partner = swap(lens_own, pair_mask)
    both = jnp.concatenate([layer_entries, partner_rows], axis=0)

    wqkv_low = gather_low(triple_projection_matrix)
    k_rows = wqkv_low.shape[0]
    by_parity = wqkv_low.reshape(k_rows, -1, 2, GROUP)
    keep = lax.dynamic_index_in_dim(by_parity, core, 2, False).reshape(k_rows, -1)
    give = lax.dynamic_index_in_dim(by_parity, 1 - core, 2, False).reshape(k_rows, -1)
    wqkv_own = joined(core, keep, swap(give, pair_mask))
    wout_low = gather_low(attention_exit_matrix)
    halves = wout_low.shape[1] // GROUP
    wout_own = jnp.concatenate(
        [wout_low[:, i * GROUP : (i + 1) * GROUP] for i in range(halves)], axis=0
    )
    qkv_cols = wqkv_own.shape[1]
    out_shape = (wout_low.shape[0], halves)
    packed = jnp.concatenate([wqkv_own, wout_own], axis=1)
    shard = packed.shape
    packed = gather_head(packed[None])
    half = shard[0] // 2
    first, second = packed[:, :half], packed[:, half:]
    y_bit, x_bit = quad // 2, quad % 2
    first = joined(x_bit, first[None], swap(first, x_mask)[None])
    second = joined(y_bit, second[None], swap(second, y_mask)[None])
    first = joined(y_bit, first[None], swap(first, y_mask)[None])
    second = joined(x_bit, second[None], swap(second, x_mask)[None])
    second = jnp.swapaxes(second, 0, 1)
    packed = jnp.concatenate([first, second], axis=3).reshape((QUADS, n_hd) + shard)
    wqkv = packed[..., :qkv_cols].transpose(0, 2, 1, 3).reshape(D, n_hd * qkv_cols)
    wout = (
        packed[..., qkv_cols:]
        .reshape(QUADS, n_hd, halves, out_shape[0], GROUP)
        .transpose(0, 3, 1, 2, 4)
        .reshape(D // 2, D)
    )

    biases = vectors[:, :5].transpose(1, 0, 2).reshape(5, D).astype(F32)
    gains = vectors[:, 5:7].transpose(1, 0, 2).reshape(2, D).astype(F32)
    shifts = vectors[:, 7:9].transpose(1, 0, 2).reshape(2, D).astype(F32)
    bias_mid = vectors[:, 9:].reshape(FF).astype(F32)
    bias_qkv = biases[:3].reshape(-1, 2, GROUP)
    bias_qkv = lax.dynamic_index_in_dim(bias_qkv, core, 1, False).reshape(-1)
    bias_up = lax.dynamic_index_in_dim(
        bias_mid.reshape(-1, 2, HIDE), core, 1, False
    ).reshape(-1)

    row_ids = jnp.arange(rows, dtype=jnp.int32)
    is_query = hd == 0
    docs = passage_lengths_each.shape[0]

    def valid_of(lens):
        doc_here = lens[jnp.maximum(hd - 1, 0)]
        return jnp.where(is_query, row_ids % QLEN < jnp.repeat(lens[docs:], QLEN), row_ids < doc_here)

    valid = jnp.stack([valid_of(lens_own), valid_of(lens_partner)])
    segment = jnp.where(is_query, row_ids // QLEN, 0)
    position = jnp.where(is_query, row_ids % QLEN, row_ids)
    allowed = (segment[:, None] == segment[None, :])[None] & valid[:, None, :]
    cosines, sines = rope_tables(position)
    score_scale = HEAD_DIM ** (-0.5)
    heads_here = HEADS // 2

    qkv = (mm(both, wqkv) + bias_qkv).reshape(2, rows, 3, heads_here, HEAD_DIM)
    queries = rotate(qkv[:, :, 0], cosines, sines).astype(BF)
    keys = rotate(qkv[:, :, 1], cosines, sines).astype(BF)
    values = qkv[:, :, 2].astype(BF)
    scores = (
        jnp.einsum("brhd,bthd->bhrt", queries, keys, preferred_element_type=F32) * score_scale
    )
    scores = jnp.where(allowed[:, None], scores, MASKED)
    raised = jnp.exp(scores - jnp.max(scores, axis=-1, keepdims=True))
    probs = raised / jnp.sum(raised, axis=-1, keepdims=True)
    probs_low = probs.astype(BF)
    attended = (
        jnp.einsum("bhrt,bthd->brhd", probs_low, values, preferred_element_type=F32)
        .reshape(2 * rows, D // 2)
        .astype(BF)
    )
    part = mm(attended, wout)
    branch = part[:rows] + swap(part[rows:], pair_mask) + biases[3]
    normed, scaled_one, inverse_one = norm_forward(
        layer_entries.astype(F32) + branch, gains[0], shifts[0]
    )
    normed_own = normed.astype(BF)
    normed_low = jnp.concatenate([normed_own, swap(normed_own, pair_mask)], axis=0)

    order = [quad ^ r for r in range(QUADS)]
    up_all = mlp_all[:, :, : col_blocks * up_rows].reshape(8, n_hd, col_blocks, up_rows, 256)
    up_all = up_all.reshape(8, n_hd, -1, 2, HIDE // 256, up_rows, 256)
    up_all = lax.dynamic_index_in_dim(up_all, core, 3, False)
    wup = (
        up_all.transpose(1, 2, 0, 4, 3, 5)
        .reshape(QUADS, D, HIDE)
    )
    wup = jnp.concatenate(
        [lax.dynamic_index_in_dim(wup, order[r], 0, False) for r in range(QUADS)], axis=1
    )
    down_all = mlp_all[:, :, col_blocks * up_rows :].reshape(QUADS, 2, n_hd, HIDE, D // n_hd)
    down_all = lax.dynamic_index_in_dim(down_all, core, 1, False)
    wdown = jnp.concatenate(
        [lax.dynamic_index_in_dim(down_all, order[r], 0, False) for r in range(QUADS)], axis=1
    )
    wdown = wdown.transpose(1, 0, 2).reshape(QUADS * HIDE, D)
    bias_up_rel = jnp.concatenate(
        [lax.dynamic_slice(bias_up, (order[r] * HIDE,), (HIDE,)) for r in range(QUADS)]
    )
    pre_act = mm(normed_low, wup) + bias_up_rel
    gate = 0.5 * (1.0 + lax.erf(pre_act * SQRT_HALF))
    hidden = (pre_act * gate).astype(BF)
    part = mm(hidden, wdown)
    branch_two = part[:rows] + swap(part[rows:], pair_mask) + biases[4]
    final, scaled_two, inverse_two = norm_forward(normed + branch_two, gains[1], shifts[1])
    outputs = final.astype(BF)

    windows = pad_windows(lax.all_gather(heads_all, "dp", axis=0, tiled=True))
    own_proj = mm(outputs, windows).astype(BF)
    all_proj = lax.all_gather(own_proj, "head", axis=0, tiled=True)
    loss, grad_temp, grad_proj = soft_maxsim(
        all_proj, hd, passage_lengths_each, question_lengths, relevant_passage, logarithmic_warmth
    )

    grad_final = mm_nt(grad_proj, windows)
    grad_all = mm_tn(outputs, grad_proj)
    grad_heads = jnp.concatenate(
        [grad_all[:, i * EMB : i * EMB + w] for i, w in enumerate(WIDTHS)], axis=1
    )
    grad_two, gain_two, shift_two = norm_backward(grad_final, scaled_two, inverse_two, gains[1])
    branch_two_own = grad_two.astype(BF)
    branch_two_both = jnp.concatenate([branch_two_own, swap(branch_two_own, pair_mask)], axis=0)

    def in_order(a):
        width = a.shape[1] // QUADS
        return [lax.dynamic_slice(a, (0, order[r] * width), (a.shape[0], width)) for r in range(QUADS)]

    def blocks_of(a):
        width = a.shape[1] // QUADS
        return [a[:, r * width : (r + 1) * width] for r in range(QUADS)]

    def reduce_quads(lhs, rhs, first_mask, second_mask):
        away = {x_mask: 1, y_mask: 2}
        a, b = away[first_mask], away[second_mask]
        width = lhs[0].shape[1]
        send = mm_tn(jnp.concatenate([lhs[a], lhs[3]], axis=1), rhs).astype(BF)
        got = swap(send, first_mask).astype(F32)
        send = (mm_tn(lhs[b], rhs) + got[width:]).astype(BF)
        kept = mm_tn(lhs[0], rhs) + got[:width]
        return (kept + swap(send, second_mask).astype(F32)).astype(BF)

    def over_head(a):
        return lax.psum_scatter(a, "head", scatter_dimension=1, tiled=True)

    def finish_split(a, group):
        a = over_head(a)
        count = a.shape[0] // 2
        give = lax.dynamic_slice_in_dim(a, (1 - core) * count, count, 0)
        keep = lax.dynamic_slice_in_dim(a, core * count, count, 0)
        other = swap(give, pair_mask)
        keep = keep.reshape(count, -1, 1, group)
        other = other.reshape(count, -1, 1, group)
        whole = jnp.where(
            core == 0,
            jnp.concatenate([keep, other], axis=2),
            jnp.concatenate([other, keep], axis=2),
        ).reshape(count, -1)
        return scatter_low(whole).astype(F32)

    grad_w_heads = lax.psum_scatter(
        lax.psum_scatter(grad_heads, "dp", scatter_dimension=0, tiled=True),
        "head", scatter_dimension=1, tiled=True,
    )

    grad_w_down = scatter_low(
        over_head(reduce_quads(blocks_of(hidden), branch_two_both, x_mask, y_mask))
    ).astype(F32)
    slope = gate + pre_act * jnp.exp(-0.5 * pre_act * pre_act) * GAUSS_SCALE
    grad_pre_rel = (mm_nt(branch_two_both, wdown) * slope).astype(BF)
    bias_up_grad = jnp.sum(grad_pre_rel.astype(F32), axis=0)
    part = mm_nt(grad_pre_rel, wup)
    grad_pre = jnp.concatenate(
        [lax.dynamic_slice(grad_pre_rel, (0, order[r] * HIDE), (2 * rows, HIDE)) for r in range(QUADS)],
        axis=1,
    )
    grad_w_up = finish_split(
        reduce_quads(in_order(normed_low), grad_pre, y_mask, x_mask), HIDE
    )
    grad_normed = grad_two + part[:rows] + swap(part[rows:], pair_mask)
    grad_one, gain_one, shift_one = norm_backward(grad_normed, scaled_one, inverse_one, gains[0])
    branch_own = grad_one.astype(BF)
    branch_both = jnp.concatenate([branch_own, swap(branch_own, pair_mask)], axis=0)
    grad_w_out = scatter_low(
        over_head(reduce_quads(in_order(attended), branch_both, y_mask, x_mask))
    ).astype(F32)
    grad_attended = (
        mm_nt(branch_both, wout).astype(BF).reshape(2, rows, heads_here, HEAD_DIM)
    )
    grad_values = jnp.einsum("bhrt,brhd->bthd", probs_low, grad_attended, preferred_element_type=F32)
    grad_probs = jnp.einsum("brhd,bthd->bhrt", grad_attended, values, preferred_element_type=F32)
    grad_scores = (
        probs * (grad_probs - jnp.sum(probs * grad_probs, axis=-1, keepdims=True))
    ).astype(BF)
    grad_queries = (
        jnp.einsum("bhrt,bthd->brhd", grad_scores, keys, preferred_element_type=F32) * score_scale
    )
    grad_keys = (
        jnp.einsum("bhrt,brhd->bthd", grad_scores, queries, preferred_element_type=F32)
        * score_scale
    )
    grad_qkv = (
        jnp.stack(
            [rotate(grad_queries, cosines, -sines), rotate(grad_keys, cosines, -sines), grad_values],
            axis=2,
        )
        .reshape(2 * rows, 3 * D // 2)
        .astype(BF)
    )
    both_rel = in_order(both)
    split = 3 * D // 4
    kept = jnp.concatenate(
        [
            reduce_quads(both_rel, grad_qkv[:, :split], x_mask, y_mask),
            reduce_quads(both_rel, grad_qkv[:, split:], y_mask, x_mask),
        ],
        axis=1,
    )
    grad_w_qkv = finish_split(kept, GROUP)
    part = mm_nt(grad_qkv, wqkv)
    grad_tokens = grad_one + part[:rows] + swap(part[rows:], pair_mask)

    own_core = (jnp.arange(2) == core).astype(F32)
    qkv_bias = (
        jnp.sum(grad_qkv.astype(F32), axis=0).reshape(-1, 1, GROUP) * own_core[None, :, None]
    ).reshape(3, D)
    up_bias = jnp.zeros((QUADS, HIDE), F32)
    up_bias = jnp.stack(
        [lax.dynamic_slice(bias_up_grad, (order[r] * HIDE,), (HIDE,)) for r in range(QUADS)]
    )
    up_bias = (up_bias[:, None, :] * own_core[None, :, None]).reshape(FF)
    small = jnp.concatenate(
        [
            qkv_bias,
            jnp.sum(branch_own.astype(F32), axis=0)[None],
            jnp.sum(branch_two_own.astype(F32), axis=0)[None],
            jnp.stack([gain_one, gain_two, shift_one, shift_two]),
        ],
        axis=0,
    )
    once = (hd == 0).astype(F32)
    scalars = jnp.broadcast_to(jnp.stack([loss, grad_temp]) * once, (n_all, 2))
    small = jnp.concatenate(
        [
            small.reshape(9, n_all, wide).transpose(1, 0, 2).reshape(n_all, 9 * wide),
            up_bias.reshape(n_all, FF // n_all),
            scalars,
        ],
        axis=1,
    )
    summed = lax.psum_scatter(small.reshape(n_dp, -1), "dp", scatter_dimension=0, tiled=True)
    summed = lax.psum_scatter(summed.reshape(n_hd, -1), "head", scatter_dimension=0, tiled=True)
    summed = summed.reshape(-1)
    mat = summed[: 9 * wide].reshape(9, wide)
    end = 9 * wide + FF // n_all
    return (
        outputs,
        summed[end : end + 1],
        grad_tokens,
        grad_w_qkv,
        grad_w_out,
        grad_w_up,
        grad_w_down,
        grad_w_heads,
        mat[:5],
        summed[9 * wide : end],
        mat[5:7],
        mat[7:9],
        summed[end + 1 : end + 2],
    )


def solution(mesh):
    return jax.shard_map(
        on_device,
        mesh=mesh,
        in_specs=(
            P(("dp", "head"), None),
            P("dp", "head"),
            P("dp", "head"),
            P("dp", "head"),
            P("dp", "head"),
            P("dp", "head"),
            P(None, ("dp", "head")),
            P(("dp", "head")),
            P(None, ("dp", "head")),
            P(None, ("dp", "head")),
            P(),
            P("dp"),
            P("dp"),
            P("dp"),
        ),
        out_specs=(
            P(("dp", "head"), None),
            P(),
            P(("dp", "head"), None),
            P("dp", "head"),
            P("dp", "head"),
            P("dp", "head"),
            P("dp", "head"),
            P("dp", "head"),
            P(None, ("dp", "head")),
            P(("dp", "head")),
            P(None, ("dp", "head")),
            P(None, ("dp", "head")),
            P(),
        ),
        check_vma=False,
    )
```

time: 1430 us -> 695 us (0.49)
  waiting for transfers between devices: 859 us -> 220 us
  blocking collectives: 367 us -> 99.6 us
  local copies, waits for them, and re-layouts: 33 us -> 184 us
  other arithmetic: 41.6 us -> 62.1 us
  starting transfers between devices: 8.36 us -> 23 us
    reduce_scatter x8 -> x3, waiting for transfers between devices: 451 us -> 0.01 us  [over_head(): return lax.psum_scatter(a, 'head', scatter_dimension=1, tiled=True)]
    unnamed x23 -> x9, waiting for transfers between devices: 366 us -> 0.12 us
    all_gather x8 -> x5, blocking collectives: 326 us -> 64 us  [the longest x1 18.2 us: on_device(): all_proj = lax.all_gather(own_proj, 'head', axis=0, tiled=True)]
    ppermute x0 -> x28, waiting for transfers between devices: none -> 220 us  [swap(): return lax.ppermute(a, ('dp', 'head'), pairs)]
    slice x0 -> x28, local copies, waits for them, and re-layouts: none -> 46.5 us  [the longest x2 23.8 us: on_device(): mlp_all[:, :, col_blocks * up_rows:]]
    psum x1 -> x0, blocking collectives: 41 us -> none  [on_device(): loss_total, temp_total = lax.psum((local_loss, grad_temp), ('dp', 'head'))]
    unnamed x0 -> x2, blocking collectives: none -> 35.6 us
    all_gather x6 -> x1, waiting for transfers between devices: 26.5 us -> 0.01 us  [on_device(): lax.all_gather(packed_mlp, ('dp', 'head'))]
  transfers between devices with their start and end apart: 21 -> 35, of which waited for: 15 -> 16; matrix products, arithmetic and copies ran while one was open for 9% -> 32% of each run, Pallas kernels for 0% -> 0%
where the time goes in v1:
time: 695 us; the launch traced here: 687 us
  waiting for transfers between devices  220 us (32%)
  local copies, waits for them, and re-layouts  184 us (26%)
  blocking collectives  99.6 us (14%)
  matrix products  77.1 us (11%)
  other arithmetic  62.1 us (9%)
  starting transfers between devices  23 us (3%)
  between operations  21.4 us (3%)
    ppermute x28, waiting for transfers between devices, swap(): return lax.ppermute(a, ('dp', 'head'), pairs)  220 us
    unnamed x341, local copies, waits for them, and re-layouts  39.2 us
    unnamed x2, blocking collectives  35.6 us
    dot_general x19, matrix products, mm_tn(): lax.dot_general(a, b, (((0,), (0,)), ((), ())), preferred_element_type=F32)  32.5 us
    slice x2, local copies, waits for them, and re-layouts, on_device(): mlp_all[:, :, col_blocks * up_rows:]  23.8 us
    ppermute x28, starting transfers between devices, swap(): return lax.ppermute(a, ('dp', 'head'), pairs)  22.7 us
    all_gather x1, blocking collectives, on_device(): all_proj = lax.all_gather(own_proj, 'head', axis=0, tiled=True)  18.2 us
    dot_general x8, matrix products, mm_nt(): lax.dot_general(a, b, (((1,), (1,)), ((), ())), preferred_element_type=F32)  17.8 us
  transfers between devices with their start and end apart: 35, of which 16 were waited for; matrix products, arithmetic and copies ran while one was open for 32% of the time, Pallas kernels for 0%

profile of v1, /device:TPU:0, one launch (start us, length us, event | category | flops | bytes accessed | tf_op | source)
XLA Modules:
  0.0 686.9 jit_solution(3419633342567953692)
XLA Ops:
  21.0 13.4 %all-gather.3 = bf16[4,13,32]{2,1,0:T(8,128)(2,1)S(1)} all-gather(bf16[1,13,32]{2,1,0:T(8,128)(2,1)S(1)} %maximum_bitcast_fusion.5), channel_id=2, replica_groups=mesh['dp'=8,'head'=4] {'head'}, dimensions={0}, use_global_device_ids=true | all-gather | bytes 4160 | tf_op jit(solution)/shard_map/all_gather | solution.py:245
  34.4 9.2 %all-gather.1 = bf16[32,13,32]{2,1,0:T(8,128)(2,1)S(1)} all-gather(bf16[4,13,32]{2,1,0:T(8,128)(2,1)S(1)} %all-gather.3), channel_id=3, replica_groups=mesh['dp'=8,'head'=4] {'dp'}, dimensions={0}, use_global_device_ids=true | all-gather | bytes 29952 | tf_op jit(solution)/shard_map/all_gather | solution.py:245
  44.5 48.1 %collective-permute-done.3 = bf16[2,256,512]{1,2,0:T(8,128)(2,1)S(1)} collective-permute-done((bf16[2,256,512]{1,2,0:T(8,128)(2,1)S(1)}, bf16[2,256,512]{1,2,0:T(8,128)(2,1)S(1)}, u32[]{:S(2)}, u32[]{:S(2)}) %collective-permute-start.3) | collective-permute-done | bytes 524320 | tf_op jit(solution)/shard_map/ppermute | solution.py:180
  100.9 18.4 %collective-permute-done.4 = bf16[4,128,512]{1,2,0:T(8,128)(2,1)S(1)} collective-permute-done((bf16[4,128,512]{1,2,0:T(8,128)(2,1)}, bf16[4,128,512]{1,2,0:T(8,128)(2,1)S(1)}, u32[]{:S(2)}, u32[]{:S(2)}) %collective-permute-start.4) | collective-permute-done | bytes 524320 | tf_op jit(solution)/shard_map/ppermute | solution.py:180
  126.1 36.4 %collective-permute-done.5 = bf16[2,4,128,512]{2,3,1,0:T(8,128)(2,1)S(1)} collective-permute-done((bf16[2,4,128,512]{2,3,1,0:T(8,128)(2,1)S(1)}, bf16[2,4,128,512]{2,3,1,0:T(8,128)(2,1)S(1)}, u32[]{:S(2)}, u32[]{:S(2)}) %collective-permute-start.5) | collective-permute-done | bytes 1048608 | tf_op jit(solution)/shard_map/ppermute | solution.py:180
  165.8 7.5 %copy.147 = bf16[2,2,4,256,512]{4,3,2,1,0:T(8,128)(2,1)} copy(bf16[2,2,4,256,512]{3,4,2,0,1:T(8,128)(2,1)} %pad_maximum_fusion) | data formatting | bytes 8388608 | tf_op jit(solution)/shard_map/concatenate | solution.py:276
  182.5 3.5 convolution_add_fusion
  186.0 5.5 reshape.862
  194.2 3.9 fusion.170
  205.0 4.7 fusion.176
  225.3 11.6 %fusion.169 = (bf16[8,4,512,256]{3,2,1,0:T(8,128)(2,1)}, bf16[8,4,512,256]{3,2,1,0:T(8,128)(2,1)}) fusion(bf16[8,4,1024,256]{3,2,1,0:T(8,128)(2,1)} %bitcast.185), kind=kLoop, calls=%fused_computation.416 | loop fusion | bytes 33554432 | tf_op jit(solution)/shard_map/slice | solution.py:346
  236.8 12.2 %copy.158 = bf16[8,4,512,256]{2,3,1,0:T(8,128)(2,1)} copy(bf16[8,4,512,256]{3,2,1,0:T(8,128)(2,1)} %get-tuple-element.103) | data formatting | bytes 16777216 | tf_op jit(solution)/shard_map/slice | solution.py:346
  249.0 4.7 constant_dynamic-slice_fusion.13
  253.8 7.5 %copy.210 = bf16[8,4,1,1,2,128,256]{5,0,6,4,1,3,2:T(8,128)(2,1)} copy(bf16[8,4,1,1,2,128,256]{6,5,4,3,1,0,2:T(8,128)(2,1)} %constant_dynamic-slice_fusion.13) | data formatting | bytes 8388608
  261.3 7.3 %reshape.829 = bf16[4,1024,512]{1,2,0:T(8,128)(2,1)} reshape(bf16[4,1,8,128,2,256]{3,2,5,4,0,1:T(8,128)(2,1)} %bitcast.188) | data formatting | bytes 8388608 | tf_op jit(solution)/shard_map/reshape | solution.py:341
  271.3 4.0 dynamic-slice_bitcast_fusion.3
  276.0 4.8 multiply_convert_fusion.1
  284.5 13.2 %all_gather.33 = bf16[128,288]{0,1:T(8,128)(2,1)S(1)} all-gather(bf16[128,72]{0,1:T(8,128)(2,1)S(1)} %copy-done.102), channel_id=1, replica_groups=mesh['dp'=8,'head'=4] {'head'}, dimensions={1}, use_global_device_ids=true | all-gather | bytes 92160 | tf_op jit(solution)/shard_map/all_gather | solution.py:234
  297.7 10.0 %all_gather.34 = bf16[1024,288]{0,1:T(8,128)(2,1)S(1)} all-gather(bf16[128,288]{0,1:T(8,128)(2,1)S(1)} %all_gather.33), channel_id=1, replica_groups=mesh['dp'=8,'head'=4] {'dp'}, dimensions={0}, use_global_device_ids=true | all-gather | bytes 663552 | tf_op jit(solution)/shard_map/all_gather | solution.py:363
  323.2 18.2 %all_gather.35 = bf16[1024,384]{1,0:T(8,128)(2,1)S(1)} all-gather(bf16[256,384]{1,0:T(8,128)(2,1)S(1)} %convolution_convert_fusion.7), channel_id=1, replica_groups=mesh['dp'=8,'head'=4] {'head'}, dimensions={0}, use_global_device_ids=true | all-gather | bytes 983040 | tf_op jit(solution)/shard_map/all_gather | solution.py:365
  406.7 5.9 convert_reduce_fusion
  451.1 29.3 %collective-permute-done.23 = bf16[512,2048]{1,0:T(8,128)(2,1)} collective-permute-done((bf16[512,2048]{1,0:T(8,128)(2,1)}, bf16[512,2048]{1,0:T(8,128)(2,1)}, u32[]{:S(2)}, u32[]{:S(2)}) %collective-permute-start.23) | collective-permute-done | bytes 2097184 | tf_op jit(solution)/shard_map/ppermute | solution.py:180
  486.5 12.3 %collective-permute-done.18 = bf16[512,768]{1,0:T(8,128)(2,1)} collective-permute-done((bf16[512,768]{1,0:T(8,128)(2,1)}, bf16[512,768]{1,0:T(8,128)(2,1)}, u32[]{:S(2)}, u32[]{:S(2)}) %collective-permute-start.18) | collective-permute-done | bytes 786464 | tf_op jit(solution)/shard_map/ppermute | solution.py:180
  506.8 5.8 collective-permute-done.19
  522.1 13.1 %collective-permute-done.24 = bf16[256,2048]{1,0:T(8,128)(2,1)} collective-permute-done((bf16[256,2048]{1,0:T(8,128)(2,1)}, bf16[256,2048]{1,0:T(8,128)(2,1)}, u32[]{:S(2)}, u32[]{:S(2)}) %collective-permute-start.24) | collective-permute-done | bytes 1048608 | tf_op jit(solution)/shard_map/ppermute | solution.py:180
  542.4 35.2 %collective-permute-done.26 = bf16[1024,1024]{1,0:T(8,128)(2,1)} collective-permute-done((bf16[1024,1024]{1,0:T(8,128)(2,1)}, bf16[1024,1024]{1,0:T(8,128)(2,1)}, u32[]{:S(2)}, u32[]{:S(2)}) %collective-permute-start.26) | collective-permute-done | bytes 2097184 | tf_op jit(solution)/shard_map/ppermute | solution.py:180
  589.2 6.1 collective-permute-done.22
  598.0 7.8 %collective-permute-done.27 = bf16[512,1024]{1,0:T(8,128)(2,1)} collective-permute-done((bf16[512,1024]{1,0:T(8,128)(2,1)}, bf16[512,1024]{1,0:T(8,128)(2,1)}, u32[]{:S(2)}, u32[]{:S(2)}) %collective-permute-start.27) | collective-permute-done | bytes 1048608 | tf_op jit(solution)/shard_map/ppermute | solution.py:180
  605.8 4.1 fusion.13
  617.8 3.7 fusion.179
  624.6 25.4 %all-reduce.2 = f32[8,1672]{1,0:T(8,128)S(1)} all-reduce(f32[8,1672]{1,0:T(8,128)S(1)} %reshape.842), channel_id=5, replica_groups=mesh['dp'=8,'head'=4] {'dp'}, use_global_device_ids=true, to_apply=%region_49.50.clone | all-reduce | flops 13376 | bytes 107008
  650.8 10.2 %all-reduce.3 = f32[4,418]{1,0:T(4,128)S(1)} all-reduce(f32[4,418]{1,0:T(4,128)S(1)} %reshape.843), channel_id=6, replica_groups=mesh['dp'=8,'head'=4] {'head'}, use_global_device_ids=true, to_apply=%region_50.51.clone | all-reduce | flops 1672 | bytes 13376
  (658 shorter events, 262.6 us)
Async XLA Ops:
  7.3 218.0 %all-gather.6.cloned.1.call-start = ((), (), s32[]{:S(2)}) async-start(), calls=%async_computation.10 | async-start | bytes 17301504 | tf_op jit(solution)/shard_map/all_gather | solution.py:231
  12.6 605.1 %reduce-scatter.17.cloned.1.call-start = ((), (), s32[]{:S(2)}) async-start(), calls=%async_computation.9 | async-start | bytes 1327104 | tf_op jit(solution)/shard_map/reduce_scatter | solution.py:416
  15.4 28.2 %collective-permute-start.2 = (bf16[1,256,512]{1,2,0:T(8,128)(2,1)S(1)}, bf16[1,256,512]{1,2,0:T(8,128)(2,1)S(1)}, u32[]{:S(2)}, u32[]{:S(2)}) collective-permute-start(bf16[1,256,512]{1,2,0:T(8,128)(2,1)S(1)} %maximum_bitcast_fusion.4), channel_id=1, source_target_pairs={{0,1},{1,0},{2,3},{3,2},{4,5},{5,4},{6,7},{7,6},{8,9},{9,8},{10,11... | collective-permute-start | bytes 786440 | tf_op jit(solution)/shard_map/ppermute | solution.py:180
  18.4 106.2 %collective-permute-start = (bf16[256,1024]{1,0:T(8,128)(2,1)S(1)}, bf16[256,1024]{1,0:T(8,128)(2,1)}, u32[]{:S(2)}, u32[]{:S(2)}) collective-permute-start(bf16[256,1024]{1,0:T(8,128)(2,1)S(1)} %copy-done.26), channel_id=1, source_target_pairs={{0,4},{1,5},{2,6},{3,7},{4,0},{5,1},{6,2},{7,3},{8,12},{9,13},{10,... | collective-permute-start | bytes 1572872 | tf_op jit(solution)/shard_map/ppermute | solution.py:180
  19.0 79.8 %collective-permute-start.8 = (s32[11]{0:T(128)}, s32[11]{0:T(128)}, u32[]{:S(2)}, u32[]{:S(2)}) collective-permute-start(s32[11]{0:T(128)} %pad_add_fusion.1), channel_id=1, source_target_pairs={{0,4},{1,5},{2,6},{3,7},{4,0},{5,1},{6,2},{7,3},{8,12},{9,13},{10,... | collective-permute-start | bytes 140 | tf_op jit(solution)/shard_map/ppermute | solution.py:180
  43.7 48.9 %collective-permute-start.3 = (bf16[2,256,512]{1,2,0:T(8,128)(2,1)S(1)}, bf16[2,256,512]{1,2,0:T(8,128)(2,1)S(1)}, u32[]{:S(2)}, u32[]{:S(2)}) collective-permute-start(bf16[2,256,512]{1,2,0:T(8,128)(2,1)S(1)} %maximum_select_fusion.6), channel_id=1, source_target_pairs={{0,2},{1,3},{2,0},{3,1},{4,6},{5,7},{6,4},{7,5},{8,10},{9,11},{10,... | collective-permute-start | bytes 1572872 | tf_op jit(solution)/shard_map/ppermute | solution.py:180
  94.5 24.8 %collective-permute-start.4 = (bf16[4,128,512]{1,2,0:T(8,128)(2,1)}, bf16[4,128,512]{1,2,0:T(8,128)(2,1)S(1)}, u32[]{:S(2)}, u32[]{:S(2)}) collective-permute-start(bf16[4,128,512]{1,2,0:T(8,128)(2,1)} %get-tuple-element.139), channel_id=1, source_target_pairs={{0,8},{1,9},{2,10},{3,11},{4,12},{5,13},{6,14},{7,15},{8,0},{9,1},... | collective-permute-start | bytes 1572872 | tf_op jit(solution)/shard_map/ppermute | solution.py:180
  96.7 25.7 %collective-permute-start.6 = (bf16[4,128,512]{1,2,0:T(8,128)(2,1)}, bf16[4,128,512]{1,2,0:T(8,128)(2,1)S(1)}, u32[]{:S(2)}, u32[]{:S(2)}) collective-permute-start(bf16[4,128,512]{1,2,0:T(8,128)(2,1)} %get-tuple-element.138), channel_id=1, source_target_pairs={{0,16},{1,17},{2,18},{3,19},{4,20},{5,21},{6,22},{7,23},{8,24},{9,... | collective-permute-start | bytes 1572872 | tf_op jit(solution)/shard_map/ppermute | solution.py:180
  120.7 41.8 %collective-permute-start.5 = (bf16[2,4,128,512]{2,3,1,0:T(8,128)(2,1)S(1)}, bf16[2,4,128,512]{2,3,1,0:T(8,128)(2,1)S(1)}, u32[]{:S(2)}, u32[]{:S(2)}) collective-permute-start(bf16[2,4,128,512]{2,3,1,0:T(8,128)(2,1)S(1)} %maximum_select_fusion.3), channel_id=1, source_target_pairs={{0,16},{1,17},{2,18},{3,19},{4,20},{5,21},{6,22},{7,23},{8,24},{9,... | collective-permute-start | bytes 3145736 | tf_op jit(solution)/shard_map/ppermute | solution.py:180
  122.5 40.3 %collective-permute-start.7 = (bf16[2,4,128,512]{2,3,1,0:T(8,128)(2,1)S(1)}, bf16[2,4,128,512]{2,3,1,0:T(8,128)(2,1)S(1)}, u32[]{:S(2)}, u32[]{:S(2)}) collective-permute-start(bf16[2,4,128,512]{2,3,1,0:T(8,128)(2,1)S(1)} %maximum_select_fusion.5), channel_id=1, source_target_pairs={{0,8},{1,9},{2,10},{3,11},{4,12},{5,13},{6,14},{7,15},{8,0},{9,1},... | collective-permute-start | bytes 3145736 | tf_op jit(solution)/shard_map/ppermute | solution.py:180
  225.1 50.8 %collective-permute-start.10 = (bf16[256,1024]{1,0:T(8,128)(2,1)S(1)}, bf16[256,1024]{1,0:T(8,128)(2,1)S(1)}, u32[]{:S(2)}, u32[]{:S(2)}) collective-permute-start(bf16[256,1024]{1,0:T(8,128)(2,1)S(1)} %fusion.49), channel_id=1, source_target_pairs={{0,4},{1,5},{2,6},{3,7},{4,0},{5,1},{6,2},{7,3},{8,12},{9,13},{10,... | collective-permute-start | bytes 1572872 | tf_op jit(solution)/shard_map/ppermute | solution.py:180
  283.3 36.4 %collective-permute-start.11 = (f32[256,1024]{1,0:T(8,128)S(1)}, f32[256,1024]{1,0:T(8,128)S(1)}, u32[]{:S(2)}, u32[]{:S(2)}) collective-permute-start(f32[256,1024]{1,0:T(8,128)S(1)} %slice.381), channel_id=1, source_target_pairs={{0,4},{1,5},{2,6},{3,7},{4,0},{5,1},{6,2},{7,3},{8,12},{9,13},{10,... | collective-permute-start | bytes 3145736 | tf_op jit(solution)/shard_map/ppermute | solution.py:180
  417.8 3.0 collective-permute-start.13
  424.5 5.5 collective-permute-start.14
  428.4 52.0 %collective-permute-start.23 = (bf16[512,2048]{1,0:T(8,128)(2,1)}, bf16[512,2048]{1,0:T(8,128)(2,1)}, u32[]{:S(2)}, u32[]{:S(2)}) collective-permute-start(bf16[512,2048]{1,0:T(8,128)(2,1)} %convolution_convert_fusion), channel_id=1, source_target_pairs={{0,16},{1,17},{2,18},{3,19},{4,20},{5,21},{6,22},{7,23},{8,24},{9,... | collective-permute-start | bytes 6291464 | tf_op jit(solution)/shard_map/ppermute | solution.py:180
  444.6 37.9 %collective-permute-start.16 = (bf16[512,768]{1,0:T(8,128)(2,1)}, bf16[512,768]{1,0:T(8,128)(2,1)}, u32[]{:S(2)}, u32[]{:S(2)}) collective-permute-start(bf16[512,768]{1,0:T(8,128)(2,1)} %convolution_convert_fusion.3), channel_id=1, source_target_pairs={{0,8},{1,9},{2,10},{3,11},{4,12},{5,13},{6,14},{7,15},{8,0},{9,1},... | collective-permute-start | bytes 2359304 | tf_op jit(solution)/shard_map/ppermute | solution.py:180
  446.6 52.2 %collective-permute-start.18 = (bf16[512,768]{1,0:T(8,128)(2,1)}, bf16[512,768]{1,0:T(8,128)(2,1)}, u32[]{:S(2)}, u32[]{:S(2)}) collective-permute-start(bf16[512,768]{1,0:T(8,128)(2,1)} %convolution_convert_fusion.2), channel_id=1, source_target_pairs={{0,16},{1,17},{2,18},{3,19},{4,20},{5,21},{6,22},{7,23},{8,24},{9,... | collective-permute-start | bytes 2359304 | tf_op jit(solution)/shard_map/ppermute | solution.py:180
  451.0 215.8 %reduce-scatter.19.cloned.1.call-start = ((), (), s32[]{:S(2)}) async-start(), calls=%async_computation.11 | async-start | bytes 983040
  484.9 21.4 %collective-permute-start.17 = (bf16[256,768]{1,0:T(8,128)(2,1)S(1)}, bf16[256,768]{1,0:T(8,128)(2,1)S(1)}, u32[]{:S(2)}, u32[]{:S(2)}) collective-permute-start(bf16[256,768]{1,0:T(8,128)(2,1)S(1)} %fusion.29), channel_id=1, source_target_pairs={{0,16},{1,17},{2,18},{3,19},{4,20},{5,21},{6,22},{7,23},{8,24},{9,... | collective-permute-start | bytes 1179656 | tf_op jit(solution)/shard_map/ppermute | solution.py:180
  500.5 12.1 %collective-permute-start.19 = (bf16[256,768]{1,0:T(8,128)(2,1)S(1)}, bf16[256,768]{1,0:T(8,128)(2,1)S(1)}, u32[]{:S(2)}, u32[]{:S(2)}) collective-permute-start(bf16[256,768]{1,0:T(8,128)(2,1)S(1)} %fusion.31), channel_id=1, source_target_pairs={{0,8},{1,9},{2,10},{3,11},{4,12},{5,13},{6,14},{7,15},{8,0},{9,1},... | collective-permute-start | bytes 1179656 | tf_op jit(solution)/shard_map/ppermute | solution.py:180
  503.9 31.3 %collective-permute-start.24 = (bf16[256,2048]{1,0:T(8,128)(2,1)}, bf16[256,2048]{1,0:T(8,128)(2,1)}, u32[]{:S(2)}, u32[]{:S(2)}) collective-permute-start(bf16[256,2048]{1,0:T(8,128)(2,1)} %fusion.10), channel_id=1, source_target_pairs={{0,8},{1,9},{2,10},{3,11},{4,12},{5,13},{6,14},{7,15},{8,0},{9,1},... | collective-permute-start | bytes 3145736 | tf_op jit(solution)/shard_map/ppermute | solution.py:180
  516.4 152.0 %reduce-scatter.13.cloned.1.call-start = ((), (), s32[]{:S(2)}) async-start(), calls=%async_computation.7 | async-start | bytes 1310720 | tf_op jit(solution)/shard_map/reduce_scatter | solution.py:398
  520.5 57.0 %collective-permute-start.26 = (bf16[1024,1024]{1,0:T(8,128)(2,1)}, bf16[1024,1024]{1,0:T(8,128)(2,1)}, u32[]{:S(2)}, u32[]{:S(2)}) collective-permute-start(bf16[1024,1024]{1,0:T(8,128)(2,1)} %convolution_convert_fusion.1), channel_id=1, source_target_pairs={{0,8},{1,9},{2,10},{3,11},{4,12},{5,13},{6,14},{7,15},{8,0},{9,1},... | collective-permute-start | bytes 6291464 | tf_op jit(solution)/shard_map/ppermute | solution.py:180
  538.3 134.1 %reduce-scatter.11.cloned.1.call-start = ((), (), s32[]{:S(2)}) async-start(), calls=%async_computation.6 | async-start | bytes 327680 | tf_op jit(solution)/shard_map/reduce_scatter | solution.py:398
  540.9 43.5 %collective-permute-start.21 = (bf16[256,1024]{1,0:T(8,128)(2,1)}, bf16[256,1024]{1,0:T(8,128)(2,1)}, u32[]{:S(2)}, u32[]{:S(2)}) collective-permute-start(bf16[256,1024]{1,0:T(8,128)(2,1)} %convolution_convert_fusion.4), channel_id=1, source_target_pairs={{0,16},{1,17},{2,18},{3,19},{4,20},{5,21},{6,22},{7,23},{8,24},{9,... | collective-permute-start | bytes 1572872 | tf_op jit(solution)/shard_map/ppermute | solution.py:180
  582.8 23.0 %collective-permute-start.27 = (bf16[512,1024]{1,0:T(8,128)(2,1)}, bf16[512,1024]{1,0:T(8,128)(2,1)}, u32[]{:S(2)}, u32[]{:S(2)}) collective-permute-start(bf16[512,1024]{1,0:T(8,128)(2,1)} %fusion.11), channel_id=1, source_target_pairs={{0,16},{1,17},{2,18},{3,19},{4,20},{5,21},{6,22},{7,23},{8,24},{9,... | collective-permute-start | bytes 3145736 | tf_op jit(solution)/shard_map/ppermute | solution.py:180
  588.7 6.6 collective-permute-start.22
  597.9 78.0 %reduce-scatter.15.cloned.1.call-start = ((), (), s32[]{:S(2)}) async-start(), calls=%async_computation.8 | async-start | bytes 1310720 | tf_op jit(solution)/shard_map/reduce_scatter | solution.py:398
  609.9 70.0 %reduce-scatter.21.cloned.1.call-start = ((), (), s32[]{:S(2)}) async-start(), calls=%async_computation.12 | async-start | bytes 184320
  623.9 46.1 %collective-permute-start.15 = (f32[256,1024]{1,0:T(8,128)}, f32[256,1024]{1,0:T(8,128)}, u32[]{:S(2)}, u32[]{:S(2)}) collective-permute-start(f32[256,1024]{1,0:T(8,128)} %slice.404), channel_id=1, source_target_pairs={{0,4},{1,5},{2,6},{3,7},{4,0},{5,1},{6,2},{7,3},{8,12},{9,13},{10,... | collective-permute-start | bytes 3145736 | tf_op jit(solution)/shard_map/ppermute | solution.py:180
  668.4 5.5 collective-permute-start.20
  669.4 8.3 %collective-permute-start.25 = (bf16[128,512]{1,0:T(8,128)(2,1)S(1)}, bf16[128,512]{1,0:T(8,128)(2,1)}, u32[]{:S(2)}, u32[]{:S(2)}) collective-permute-start(bf16[128,512]{1,0:T(8,128)(2,1)S(1)} %get-tuple-element.153), channel_id=1, source_target_pairs={{0,4},{1,5},{2,6},{3,7},{4,0},{5,1},{6,2},{7,3},{8,12},{9,13},{10,... | collective-permute-start | bytes 393224 | tf_op jit(solution)/shard_map/ppermute | solution.py:180
  (160 other events, 1450.8 us)
Sparse Core Ops, SparseCore 0:
  12.8 167.1 all-gather.5
  451.2 40.0 reduce-scatter.16
  516.5 21.9 reduce-scatter.18
  540.8 26.3 reduce-scatter.12
  597.8 18.1 reduce-scatter.10
  618.3 25.4 reduce-scatter.14
  646.6 17.9 reduce-scatter.20

commit v2 on v1

v2 whole, which is shorter than its diff:
```python
import jax
import jax.numpy as jnp
from jax import lax
from jax.experimental import pallas as pl
from jax.experimental.pallas import tpu as pltpu
from jax.sharding import PartitionSpec as P

D = 1024
HEADS = 16
HEAD_DIM = 64
FF = 4096
EMB = 128
EMB_MID = 96
EMB_SMALL = 64
QLEN = 32

EPS_NORM = 1e-05
EPS_UNIT = 1e-06
SHARPNESS = 0.05
ROPE_BASE = 10000.0
MASKED = -1000000000.0
SQRT_HALF = 0.7071067811865476
GAUSS_SCALE = 0.3989422804014327

BF = jnp.bfloat16
F32 = jnp.float32
STARTS = (0, EMB, EMB + EMB_MID)
WIDTHS = (EMB, EMB_MID, EMB_SMALL)
SLOTS = 3
QUADS = 4
GROUP = 128
HIDE = FF // 8


PAIRS = 4
VMEM_SPEC = pl.BlockSpec(memory_space=pltpu.VMEM)
SMEM_SPEC = pl.BlockSpec(memory_space=pltpu.SMEM)


def dot_nn(a, b):
    return lax.dot_general(a, b, (((1,), (0,)), ((), ())), preferred_element_type=F32)


def dot_tn(a, b):
    return lax.dot_general(a, b, (((0,), (0,)), ((), ())), preferred_element_type=F32)


def dot_nt(a, b):
    return lax.dot_general(a, b, (((1,), (1,)), ((), ())), preferred_element_type=F32)


def params(mib):
    return pltpu.CompilerParams(vmem_limit_bytes=58 << 20)


TIME_UNIT = 1150000000


def cost(micros):
    return pl.CostEstimate(flops=int(micros * TIME_UNIT), bytes_accessed=1, transcendentals=0)


def whole(a):
    zeros = (0,) * len(a.shape)
    return pl.BlockSpec(a.shape, lambda i: zeros, pipeline_mode=pl.Buffered(1))


def call(kernel, outs, args, n_smem, mib, estimate, name, scratch=()):
    return pl.pallas_call(
        kernel,
        out_shape=outs,
        grid=(1,),
        in_specs=[SMEM_SPEC] * n_smem + [whole(a) for a in args[n_smem:]],
        out_specs=[whole(a) for a in outs],
        scratch_shapes=list(scratch),
        compiler_params=params(mib),
        cost_estimate=estimate,
        name=name,
    )(*args)


def norm_parts(values):
    centred = values - jnp.mean(values, axis=-1, keepdims=True)
    variance = jnp.mean(centred * centred, axis=-1, keepdims=True)
    inverse = lax.rsqrt(variance + EPS_NORM)
    return centred * inverse, inverse


def norm_back(grad_out, scaled, inverse, gain):
    grad_scaled = grad_out * gain
    return inverse * (
        grad_scaled
        - jnp.mean(grad_scaled, axis=-1, keepdims=True)
        - scaled * jnp.mean(grad_scaled * scaled, axis=-1, keepdims=True)
    )


def pieces_of(a0, ax, ay, b0, by, bx):
    def piece(rq, rz):
        at = rz // 2
        if rz % 2 == 0:
            return [a0.at[at], ax.at[at], ay.at[0, at], ay.at[1, at]][rq]
        return [b0.at[at], bx.at[0, at], by.at[at], bx.at[1, at]][rq]

    return piece


def lanes_at(index, width=GROUP):
    return pl.ds(pl.multiple_of(index * width, width), width)


def turn(x, cos, sin_a, sin_b):
    return x * cos + pltpu.roll(x, 96, 1) * sin_a + pltpu.roll(x, 32, 1) * sin_b


def head_mask(h, shape):
    lane = lax.broadcasted_iota(jnp.int32, shape, 1)
    return (lane < HEAD_DIM) if h == 0 else (lane >= HEAD_DIM)


def softmax_rows(q, k, allowed):
    s = jnp.where(allowed, dot_nt(q, k), MASKED)
    raised = jnp.exp(s - jnp.max(s, axis=-1, keepdims=True))
    return raised * (1.0 / jnp.sum(raised, axis=-1, keepdims=True))


def attention_forward(
    place, x, a0, ax, ay, b0, by, bx, cos, sin_a, sin_b, mask, qkv, att, part, vec
):
    quad, hd, core = place[0], place[1], place[5]
    piece = pieces_of(a0, ax, ay, b0, by, bx)
    rows = cos.shape[0]
    for rq in range(4):
        for c in range(2):
            at = slice(c * GROUP, (c + 1) * GROUP)
            total = piece(rq, 0)[256:272, at].astype(F32)
            for rz in range(1, 4):
                total += piece(rq, rz)[256:272, at].astype(F32)
            vec[:, lanes_at(2 * (quad ^ rq) + c)] = total
    for rz in range(4):
        z = hd ^ rz
        acc = dot_nn(x[0], piece(0, rz)[0:256, 0:384])
        for rq in range(1, 4):
            acc += dot_nn(x[rq], piece(rq, rz)[0:256, 0:384])
        for j in range(3):
            i = 3 * z + j
            scale = jnp.where(i < PAIRS, HEAD_DIM**-0.5, 1.0).astype(F32)
            near = vec[0:8, lanes_at(2 * (i % 4) + core)]
            row = lax.broadcasted_iota(jnp.int32, near.shape, 0)
            bias = jnp.sum(jnp.where(row == i // 4, near, 0.0), axis=0, keepdims=True)
            for b in range(2):
                here = acc[b * rows : (b + 1) * rows, j * GROUP : (j + 1) * GROUP]
                here = here + bias
                turned = turn(here, cos[...], sin_a[...], sin_b[...])
                here = jnp.where(i < 2 * PAIRS, turned, here) * scale
                qkv[b * rows : (b + 1) * rows, lanes_at(i)] = here.astype(BF)

    def one(it, carry):
        b, r = it // PAIRS, it % PAIRS
        i = quad ^ r
        row = pl.ds(pl.multiple_of(b * rows, rows), rows)
        q = qkv[row, pl.ds(pl.multiple_of(i * GROUP, GROUP), GROUP)]
        k = qkv[row, pl.ds(pl.multiple_of((PAIRS + i) * GROUP, GROUP), GROUP)]
        v = qkv[row, pl.ds(pl.multiple_of((2 * PAIRS + i) * GROUP, GROUP), GROUP)]
        allowed = mask[b] > 0
        got = []
        for h in range(2):
            qh = jnp.where(head_mask(h, q.shape), q, jnp.zeros_like(q))
            probs = softmax_rows(qh, k, allowed)
            got.append(dot_nn(probs.astype(BF), v))
        att[r, row, :] = jnp.where(head_mask(0, q.shape), got[0], got[1]).astype(BF)
        return carry

    lax.fori_loop(0, 2 * PAIRS, one, 0)
    for rz in range(4):
        for half in range(2):
            sel = slice(half * GROUP, (half + 1) * GROUP)
            acc = dot_nn(att[0], piece(0, rz)[sel, 384:512])
            for rq in range(1, 4):
                acc += dot_nn(att[rq], piece(rq, rz)[sel, 384:512])
            part[:, lanes_at(2 * (hd ^ rz) + half)] = acc


def attention_backward(
    place, own, other, qkv, a0, ax, ay, b0, by, bx, cos, sin_a, sin_b, mask,
    grad_qkv, gx_own, gx_other, sums, ga,
):
    quad, hd = place[0], place[1]
    piece = pieces_of(a0, ax, ay, b0, by, bx)
    rows = cos.shape[0]
    for b, grad in ((0, own), (1, other)):
        for rq in range(4):
            acc = None
            for rz in range(4):
                for half in range(2):
                    w = piece(rq, rz)[half * GROUP : (half + 1) * GROUP, 384:512]
                    term = dot_nt(grad[:, lanes_at(2 * (hd ^ rz) + half)], w)
                    acc = term if acc is None else acc + term
            ga[rq, b * rows : (b + 1) * rows, :] = acc.astype(BF)

    def one(it, carry):
        b, r = it // PAIRS, it % PAIRS
        i = quad ^ r
        row = pl.ds(pl.multiple_of(b * rows, rows), rows)
        at_q = pl.ds(pl.multiple_of(i * GROUP, GROUP), GROUP)
        at_k = pl.ds(pl.multiple_of((PAIRS + i) * GROUP, GROUP), GROUP)
        at_v = pl.ds(pl.multiple_of((2 * PAIRS + i) * GROUP, GROUP), GROUP)
        q, k, v = qkv[row, at_q], qkv[row, at_k], qkv[row, at_v]
        grad_out = ga[r, row, :]
        allowed = mask[b] > 0
        zero = jnp.zeros_like(q)
        gq = gk = gv = None
        for h in range(2):
            sel = head_mask(h, q.shape)
            qh = jnp.where(sel, q, zero)
            kh = jnp.where(sel, k, zero)
            goh = jnp.where(sel, grad_out, zero)
            probs = softmax_rows(qh, k, allowed)
            gp = dot_nt(goh, v)
            gs = probs * (gp - jnp.sum(probs * gp, axis=-1, keepdims=True))
            gs = gs.astype(BF)
            tq, tk, tv = dot_nn(gs, kh), dot_tn(gs, qh), dot_tn(probs.astype(BF), goh)
            gq = tq if gq is None else gq + tq
            gk = tk if gk is None else gk + tk
            gv = tv if gv is None else gv + tv
        c, sa, sb = cos[...], -sin_a[...], -sin_b[...]
        grad_qkv[row, at_q] = turn(gq * (HEAD_DIM**-0.5), c, sa, sb).astype(BF)
        grad_qkv[row, at_k] = turn(gk, c, sa, sb).astype(BF)
        grad_qkv[row, at_v] = gv.astype(BF)
        return carry

    lax.fori_loop(0, 2 * PAIRS, one, 0)
    for rq in range(4):
        at = pl.ds(pl.multiple_of((quad ^ rq) * 256, 256), 256)
        acc = None
        for rz in range(4):
            cols = pl.ds(pl.multiple_of((hd ^ rz) * 384, GROUP), 384)
            term = dot_nt(grad_qkv[:, cols], piece(rq, rz)[0:256, 0:384])
            acc = term if acc is None else acc + term
        gx_own[:, at] = acc[:rows]
        gx_other[:, at] = acc[rows:]
    sums[...] = jnp.sum(grad_qkv[...].astype(F32), axis=0, keepdims=True)


def feed_forward(
    place, x, part, recv, vec, wup, wdown,
    scaled_out, inv_out, rel_out, hidden_out, slope_out, own_out, other_out, low,
):
    r = pl.program_id(0)
    rows = scaled_out.shape[0]

    @pl.when(r == 0)
    def _():
        for b in range(2):
            sel = slice(b * rows, (b + 1) * rows)
            swapped = slice((1 - b) * rows, (2 - b) * rows)
            h = x[sel, :].astype(F32) + part[sel, :] + recv[swapped, :] + vec[3:4, :]
            scaled, inverse = norm_parts(h)
            low[sel, :] = (scaled * vec[5:6, :] + vec[7:8, :]).astype(BF)
            if b == 0:
                scaled_out[...] = scaled
                inv_out[...] = inverse
        for q in range(QUADS):
            at = pl.ds(pl.multiple_of((place[0] ^ q) * 256, 256), 256)
            rel_out[q, :, :] = low[:, at]
        own_out[...] = jnp.zeros_like(own_out)
        other_out[...] = jnp.zeros_like(other_out)

    for cb in range(2):
        cols = slice(cb * 256, (cb + 1) * 256)
        w = wup[:, 0, cb * 128 : (cb + 1) * 128, :].reshape(D, 256)
        bias = [
            vec[9 + 2 * cb + k : 10 + 2 * cb + k, lanes_at(2 * (place[0] ^ r) + place[1])]
            for k in range(2)
        ]
        pre = dot_nn(low[...], w) + jnp.concatenate(bias, axis=1)
        gate = 0.5 * (1.0 + lax.erf(pre * SQRT_HALF))
        hidden_out[0, :, cols] = (pre * gate).astype(BF)
        slope_out[0, :, cols] = (
            gate + pre * jnp.exp(-0.5 * pre * pre) * GAUSS_SCALE
        ).astype(BF)
    for z in range(4):
        cols = slice(z * 256, (z + 1) * 256)
        acc = dot_nn(hidden_out[0], wdown[0, z])
        own_out[:, cols] += acc[:rows]
        other_out[:, cols] += acc[rows:]


def feed_forward_back(
    place, own, other, slope, wup, wdown, pre_out, own_out, other_out, sums, both
):
    r = pl.program_id(0)
    rows = own.shape[0]

    @pl.when(r == 0)
    def _():
        both[0:rows, :] = own[...]
        both[rows:, :] = other[...]
        own_out[...] = jnp.zeros_like(own_out)
        other_out[...] = jnp.zeros_like(other_out)

    acc = dot_nt(both[:, 0:256], wdown[0, 0])
    for z in range(1, 4):
        acc += dot_nt(both[:, z * 256 : (z + 1) * 256], wdown[0, z])
    grad = (acc * slope[0].astype(F32)).astype(BF)
    pre_out[...] = grad
    sums[...] = jnp.sum(grad.astype(F32), axis=0, keepdims=True)
    total = None
    for cb in range(2):
        w = wup[:, 0, cb * 128 : (cb + 1) * 128, :].reshape(D, 256)
        term = dot_nt(pre_out[:, cb * 256 : (cb + 1) * 256], w)
        total = term if total is None else total + term
    own_out[...] += total[:rows]
    other_out[...] += total[rows:]


def final_norm(scaled_one, part, recv, vec, windows, out, scaled_out, inv_out, proj):
    h = scaled_one[...] * vec[5:6, :] + vec[7:8, :] + part[...] + recv[...] + vec[4:5, :]
    scaled, inverse = norm_parts(h)
    scaled_out[...] = scaled
    inv_out[...] = inverse
    low = (scaled * vec[6:7, :] + vec[8:9, :]).astype(BF)
    out[...] = low
    proj[...] = dot_nn(low, windows[...]).astype(BF)


def soft_maxsim(
    place, temp, lanes, projs, windows, out, scaled, inverse_two, vec,
    grad_two, low_two, grad_heads, sums, scalars, gproj, units, shares, similar_low,
):
    hd = place[1]
    rows = out.shape[0]
    docs = projs.shape[0] - 1
    row = lax.broadcasted_iota(jnp.int32, (rows, GROUP), 0)
    lane = lax.broadcasted_iota(jnp.int32, (rows, GROUP), 1)
    member = (row // QLEN == lane).astype(F32)
    lens = lanes[0:1, :]
    len_row = jnp.sum(member * lens, axis=1, keepdims=True)
    valid = (row % QLEN).astype(F32) < len_row
    queries = rows // QLEN
    used = lax.broadcasted_iota(jnp.int32, (1, GROUP), 1) < queries
    weight = jnp.where(valid, member, 0.0) / jnp.where(used, lens, 1.0)
    warmth = jnp.exp(jnp.full((1, GROUP), temp[0], F32))
    key = lax.broadcasted_iota(jnp.int32, (rows, rows), 1)
    loss = jnp.zeros((1, GROUP), F32)
    grad_temp = jnp.zeros((1, GROUP), F32)
    for slot in range(SLOTS):
        cols = slice(slot * EMB, (slot + 1) * EMB)

        def unit_of(block):
            mapped = projs[block, :, cols].astype(F32)
            inverse = lax.rsqrt(jnp.sum(mapped * mapped, axis=-1, keepdims=True) + EPS_UNIT)
            return mapped * inverse, inverse

        for block in range(docs + 1):
            units[block * rows : (block + 1) * rows, :] = unit_of(block)[0].astype(BF)
        logits = []
        for d in range(docs):
            doc = slice((d + 1) * rows, (d + 2) * rows)
            similar = dot_nt(units[0:rows, :], units[doc, :]) * (1.0 / SHARPNESS)
            similar = jnp.where(key < place[2 + d], similar, MASKED)
            top = jnp.max(similar, axis=-1, keepdims=True)
            raised = jnp.exp(similar - top)
            total = jnp.sum(raised, axis=-1, keepdims=True)
            soft = SHARPNESS * (top + jnp.log(total))
            shares[:, d * rows : (d + 1) * rows] = raised * (1.0 / total)
            logits.append(jnp.sum(soft * weight, axis=0, keepdims=True) / warmth)
        top_logit = jnp.maximum(jnp.maximum(logits[0], logits[1]), logits[2])
        exps = [jnp.exp(x - top_logit) for x in logits]
        total = exps[0] + exps[1] + exps[2]
        hits = [(lanes[1:2, :] == float(d)).astype(F32) for d in range(docs)]
        picked = logits[0] * hits[0] + logits[1] * hits[1] + logits[2] * hits[2]
        loss += jnp.where(used, top_logit + jnp.log(total) - picked, 0.0) / queries
        for d in range(docs):
            grad = jnp.where(used, exps[d] / total - hits[d], 0.0) / queries
            grad_temp -= grad * logits[d]
            grad_soft = jnp.sum(weight * (grad / warmth), axis=1, keepdims=True)
            at = slice(d * rows, (d + 1) * rows)
            similar_low[:, at] = (grad_soft * shares[:, at]).astype(BF)

        own = jnp.maximum(hd - 1, 0)
        at = pl.ds(pl.multiple_of(own * rows, rows), rows)
        from_docs = dot_nn(similar_low[...], units[rows:, :])
        from_queries = dot_tn(similar_low[:, at], units[0:rows, :])
        grad = jnp.where(hd == 0, from_docs, from_queries)
        unit, inverse = unit_of(hd)
        gproj[:, cols] = (
            inverse * (grad - unit * jnp.sum(grad * unit, axis=-1, keepdims=True))
        ).astype(BF)

    scalars[0:1, :] = loss
    scalars[1:2, :] = grad_temp
    grad_final = dot_nt(gproj[...], windows[...])
    xhat = scaled[...]
    grad = norm_back(grad_final, xhat, inverse_two[...], vec[6:7, :])
    grad_two[...] = grad
    low_two[...] = grad.astype(BF)
    sums[0:1, :] = jnp.sum(grad_final * xhat, axis=0, keepdims=True)
    sums[1:2, :] = jnp.sum(grad_final, axis=0, keepdims=True)
    sums[2:3, :] = jnp.sum(low_two[...].astype(F32), axis=0, keepdims=True)
    grad_heads[...] = dot_tn(out[...], gproj[...])


def first_norm_back(grad_two, own, recv, scaled, inverse, vec, grad_one, low_one, sums):
    grad_out = grad_two[...] + own[...] + recv[...]
    xhat = scaled[...]
    grad = norm_back(grad_out, xhat, inverse[...], vec[5:6, :])
    grad_one[...] = grad
    low_one[...] = grad.astype(BF)
    sums[0:1, :] = jnp.sum(grad_out * xhat, axis=0, keepdims=True)
    sums[1:2, :] = jnp.sum(grad_out, axis=0, keepdims=True)
    sums[2:3, :] = jnp.sum(low_one[...].astype(F32), axis=0, keepdims=True)


def weight_grad(spot, lhs, rhs, blocks, places, adds, name, micros, kind=BF):
    tokens, width = lhs.shape[1:]
    whole_cols = places is None
    places = (None,) if whole_cols else places
    count = len(places)
    tile = rhs[0].shape[1] // (1 if whole_cols else 4)
    step = (blocks[1] - blocks[0]) if len(blocks) > 1 else 0
    parts = len(rhs)
    span = tokens // parts
    n_add = len(adds)

    def column(s, place):
        return 0 if place is None else s[2] ^ place

    def kernel(spot_ref, lhs_ref, *refs):
        out = refs[-1]
        for k in range(count):
            total = None
            for p in range(parts):
                term = dot_tn(lhs_ref[0, p * span : (p + 1) * span, :], refs[k * parts + p][...])
                total = term if total is None else total + term
            for add in refs[count * parts + k * n_add : count * parts + (k + 1) * n_add]:
                total += add[0].astype(F32)
            out[k] = total.astype(kind)

    specs = [pl.BlockSpec((1, tokens, width), lambda i, s: (blocks[0] + step * i, 0, 0))]
    for place in places:
        specs += [pl.BlockSpec((span, tile), lambda i, s, c=place: (0, column(s, c)))] * parts
    for place in places:
        for _, at, aligned in adds:
            if aligned:
                index = lambda i, s, at=at, c=place: (at, 0, column(s, c))
            else:
                index = lambda i, s, at=at: (at, 0, 0)
            specs.append(pl.BlockSpec((1, width, tile), index))
    return pl.pallas_call(
        kernel,
        out_shape=jax.ShapeDtypeStruct((len(blocks) * count, width, tile), kind),
        grid_spec=pltpu.PrefetchScalarGridSpec(
            num_scalar_prefetch=1,
            grid=(len(blocks),),
            in_specs=specs,
            out_specs=pl.BlockSpec((count, width, tile), lambda i, s: (i, 0, 0)),
        ),
        compiler_params=params(24),
        cost_estimate=cost(micros),
        name=name,
    )(spot, lhs, *(list(rhs) * count), *([a for a, _, _ in adds] * count))


def tail_grad(spot, x, grad_qkv, att, own, other, halves, blocks, places, adds, name, micros, kind=BF):
    tokens = x.shape[1]
    whole_cols = places is None
    places = (None,) if whole_cols else places
    count = len(places)
    heads = 4 if whole_cols else 1
    step = (blocks[1] - blocks[0]) if len(blocks) > 1 else 0
    n_half = len(halves)
    rows = tokens // 2
    n_add = len(adds)
    per = n_add // n_half
    lane_blocks = 1 if whole_cols else n_half

    def column(s, place):
        return 0 if place is None else s[2] ^ place

    def kernel(spot_ref, x_ref, att_ref, *refs):
        out = refs[-1]
        at_add = count * (1 + 2 * lane_blocks)
        for c in range(count):
            qkv_ref, *pair = refs[c * (1 + 2 * lane_blocks) : (c + 1) * (1 + 2 * lane_blocks)]
            for k, half in enumerate(halves):
                left_all = dot_tn(x_ref[0, :, half * GROUP : (half + 1) * GROUP], qkv_ref[...])
                for z in range(heads):
                    if whole_cols:
                        lanes = slice((2 * z + half) * GROUP, (2 * z + half + 1) * GROUP)
                        up, down = pair[0][:, lanes], pair[1][:, lanes]
                    else:
                        up, down = pair[2 * k][...], pair[2 * k + 1][...]
                    right = dot_tn(att_ref[0, 0:rows, :], up) + dot_tn(att_ref[0, rows:, :], down)
                    left = left_all[:, z * 384 : (z + 1) * 384]
                    first = at_add + c * n_add + k * per
                    lo = z * 512
                    for add in refs[first : first + per]:
                        left += add[0, 0, :, lo : lo + 384].astype(F32)
                        right += add[0, 0, :, lo + 384 : lo + 512].astype(F32)
                    out[c, k, :, lo : lo + 384] = left.astype(kind)
                    out[c, k, :, lo + 384 : lo + 512] = right.astype(kind)

    specs = [
        pl.BlockSpec((1, tokens, 256), lambda i, s: (blocks[0] + step * i, 0, 0)),
        pl.BlockSpec((1, tokens, GROUP), lambda i, s: (blocks[0] + step * i, 0, 0)),
    ]
    inputs = []
    for place in places:
        specs.append(pl.BlockSpec((tokens, 384 * heads), lambda i, s, c=place: (0, column(s, c))))
        inputs.append(grad_qkv)
        for half in halves[:lane_blocks]:
            if whole_cols:
                index = lambda i, s: (0, 0)
            else:
                index = lambda i, s, c=place, half=half: (0, 2 * column(s, c) + half)
            specs += [pl.BlockSpec((rows, D if whole_cols else GROUP), index)] * 2
            inputs += [own, other]
    for place in places:
        for a, at, k, aligned in adds:
            if aligned:
                index = lambda i, s, at=at, k=k, c=place: (at, k, 0, column(s, c))
            else:
                index = lambda i, s, at=at, k=k: (at, k, 0, 0)
            specs.append(pl.BlockSpec((1, 1, GROUP, 512 * heads), index))
            inputs.append(a)
    return pl.pallas_call(
        kernel,
        out_shape=jax.ShapeDtypeStruct((len(blocks) * count, n_half, GROUP, 512 * heads), kind),
        grid_spec=pltpu.PrefetchScalarGridSpec(
            num_scalar_prefetch=1,
            grid=(len(blocks),),
            in_specs=specs,
            out_specs=pl.BlockSpec(
                (count, n_half, GROUP, 512 * heads), lambda i, s: (i, 0, 0, 0)
            ),
        ),
        compiler_params=params(24),
        cost_estimate=cost(micros),
        name=name,
    )(spot, x, att, *inputs)


def pack_sums(spot, two, one, up, qkv, scalars, out):
    core, hd = spot[1], spot[2]
    out[...] = jnp.zeros_like(out)
    for i in range(3 * PAIRS):
        out[2 * (i % 4) + core, i // 4 : i // 4 + 1, :] = qkv[0:1, i * GROUP : (i + 1) * GROUP]
    for i in range(4 * QUADS):
        out[2 * (i // 4) + core, 9 + i % 4 : 10 + i % 4, :] = up[
            0:1, i * GROUP : (i + 1) * GROUP
        ]
    once = jnp.where(hd == 0, 1.0, 0.0).astype(F32)
    totals = [jnp.sum(scalars[k : k + 1, :], axis=1, keepdims=True) * once for k in range(2)]
    for t in range(2 * QUADS):
        at = slice(t * GROUP, (t + 1) * GROUP)
        out[t, 3:4, :] = one[2:3, at]
        out[t, 4:5, :] = two[2:3, at]
        out[t, 5:6, :] = one[0:1, at]
        out[t, 6:7, :] = two[0:1, at]
        out[t, 7:8, :] = one[1:2, at]
        out[t, 8:9, :] = two[1:2, at]
        for k in range(2):
            out[t, 13 + k : 14 + k, :] = jnp.broadcast_to(totals[k], (1, GROUP))


def make_windows(tiles, windows):
    lane = lax.broadcasted_iota(jnp.int32, (GROUP // 2, GROUP), 1)
    for dp in range(2 * QUADS):
        for half in range(2):
            first_row = dp * GROUP + half * (GROUP // 2)
            at = slice(first_row, first_row + GROUP // 2)
            t = [
                tiles[dp, z, :, half * GROUP : (half + 1) * GROUP].astype(F32) for z in range(4)
            ]
            second = pltpu.roll(t[1], 72, 1)
            first = jnp.where(lane < 72, t[0], second)
            middle = jnp.where(lane < 16, second, pltpu.roll(t[2], 16, 1))
            middle = jnp.where(lane < 88, middle, pltpu.roll(t[3], 88, 1))
            windows[at, 0:128] = first.astype(BF)
            windows[at, 128:256] = jnp.where(lane < 96, middle, 0.0).astype(BF)
            windows[at, 256:384] = jnp.where(lane < 64, pltpu.roll(t[3], 120, 1), 0.0).astype(BF)


def on_device(
    layer_entries,
    triple_projection_matrix,
    attention_exit_matrix,
    expand_matrix,
    contract_matrix,
    nested_projector,
    offset_model_width,
    offset_expanded,
    standardize_factor,
    standardize_offset,
    logarithmic_warmth,
    passage_lengths_each,
    question_lengths,
    relevant_passage,
):
    n_dp = lax.axis_size("dp")
    n_hd = lax.axis_size("head")
    n_all = n_dp * n_hd
    dp = lax.axis_index("dp")
    hd = lax.axis_index("head")
    low_span = n_dp // 8
    quad = dp // (2 * low_span)
    core = (dp // low_span) % 2
    pair_mask = low_span
    x_mask = 2 * low_span
    y_mask = 4 * low_span

    def swap(a, dp_mask=0, hd_mask=0):
        pairs = [
            (d * n_hd + h, (d ^ dp_mask) * n_hd + (h ^ hd_mask))
            for d in range(n_dp)
            for h in range(n_hd)
        ]
        return lax.ppermute(a, ("dp", "head"), pairs)

    def after(value, *others):
        return lax.optimization_barrier((value, *others))[0]

    def joined(bit, own, other):
        return jnp.where(
            bit == 0, jnp.concatenate([own, other], 0), jnp.concatenate([other, own], 0)
        )

    def gather_low(a):
        span = 1
        while span < low_span:
            a = joined((dp // span) % 2, a, swap(a, span))
            span *= 2
        return a

    def scatter_low(a):
        span = low_span // 2
        while span >= 1:
            half = a.shape[0] // 2
            bit = (dp // span) % 2
            give = lax.dynamic_slice_in_dim(a, (1 - bit) * half, half, 0)
            keep = lax.dynamic_slice_in_dim(a, bit * half, half, 0)
            a = (keep.astype(F32) + swap(give, span).astype(F32)).astype(BF)
            span //= 2
        return a

    rows = layer_entries.shape[0]
    docs = passage_lengths_each.shape[0]

    wup_low = gather_low(expand_matrix)
    col_blocks = wup_low.shape[1] // 256
    heads_low = gather_low(nested_projector)
    head_cols = heads_low.shape[1]
    heads_low = jnp.pad(heads_low, ((0, 0), (0, GROUP - head_cols)))
    packed_mlp = jnp.concatenate(
        [wup_low[:, i * 256 : (i + 1) * 256] for i in range(col_blocks)]
        + [
            gather_low(contract_matrix),
            jnp.concatenate([heads_low[: GROUP // 2], heads_low[GROUP // 2 :]], axis=1),
        ],
        axis=0,
    )
    if low_span > 1:
        dp_groups = [
            [((q * 2 + k) * low_span + s) for q in range(QUADS) for k in range(2)]
            for s in range(low_span)
        ]
        mlp_all = lax.all_gather(
            lax.all_gather(packed_mlp, "head"), "dp", axis_index_groups=dp_groups
        )
    else:
        mlp_all = lax.all_gather(packed_mlp, ("dp", "head"))
    mlp_all = mlp_all.reshape((8, n_hd) + packed_mlp.shape)

    partner_rows = swap(layer_entries, pair_mask)
    lens_own = jnp.concatenate([passage_lengths_each, question_lengths])
    lens_partner = swap(lens_own, pair_mask)
    both = jnp.concatenate([layer_entries, partner_rows], axis=0)
    order = [quad ^ r for r in range(QUADS)]
    both_rel = jnp.stack(
        [lax.dynamic_slice(both, (0, order[r] * 256), (2 * rows, 256)) for r in range(QUADS)]
    )

    wide = offset_model_width.shape[1]
    mine = (jnp.arange(n_hd) == hd).astype(BF)
    vectors = jnp.concatenate([offset_model_width, standardize_factor, standardize_offset], axis=0)
    n_vec = vectors.shape[0]
    vectors = gather_low(vectors[None]).transpose(1, 0, 2)
    vectors = (vectors[:, :, None, :] * mine[None, None, :, None]).reshape(n_vec, GROUP)
    middle = gather_low(offset_expanded[None])
    middle = (middle[:, None, :] * mine[None, :, None]).reshape(4, GROUP)
    vectors = jnp.concatenate([vectors, middle, jnp.zeros((16 - n_vec - 4, GROUP), BF)], axis=0)

    wqkv_low = gather_low(triple_projection_matrix)
    parts = wqkv_low.reshape(wqkv_low.shape[0], -1, 2, GROUP)
    keep, give = (
        lax.dynamic_index_in_dim(parts, k, 2, False).reshape(wqkv_low.shape[0], -1)
        for k in (core, 1 - core)
    )
    qkv_cols = keep.shape[1]
    k_rows = keep.shape[0]
    other = jnp.pad(vectors, ((0, 0), (0, qkv_cols - GROUP)))
    other = swap(jnp.concatenate([give, other], axis=0), pair_mask)
    wout_low = gather_low(attention_exit_matrix)
    wout_own = jnp.concatenate([wout_low[:, :GROUP], wout_low[:, GROUP:]], axis=0)
    vectors = jnp.where(
        core == 0,
        jnp.concatenate([vectors, other[k_rows:, :GROUP]], axis=1),
        jnp.concatenate([other[k_rows:, :GROUP], vectors], axis=1),
    )
    packed = jnp.concatenate(
        [
            jnp.concatenate([joined(core, keep, other[:k_rows]), wout_own], axis=1),
            jnp.pad(vectors, ((0, 0), (0, qkv_cols + GROUP - 2 * GROUP))),
        ],
        axis=0,
    )[None]

    a0 = jnp.concatenate([packed, swap(packed, 0, 2)], axis=0)
    b0 = swap(a0, 0, 1)
    ax = swap(a0, x_mask)
    by = swap(b0, y_mask)
    ay = swap(jnp.stack([a0, ax]), y_mask)
    bx = swap(jnp.stack([b0, by]), x_mask)
    attn_pieces = (a0, ax, ay, b0, by, bx)
    spot = jnp.stack([quad, core, hd]).astype(jnp.int32)

    row_ids = jnp.arange(rows, dtype=jnp.int32)
    is_query = hd == 0

    def valid_of(lens):
        doc_here = lens[jnp.maximum(hd - 1, 0)]
        return jnp.where(
            is_query, row_ids % QLEN < jnp.repeat(lens[docs:], QLEN), row_ids < doc_here
        )

    valid = jnp.stack([valid_of(lens_own), valid_of(lens_partner)])
    segment = jnp.where(is_query, row_ids // QLEN, 0)
    position = jnp.where(is_query, row_ids % QLEN, row_ids)
    mask = ((segment[:, None] == segment[None, :])[None] & valid[:, None, :]).astype(F32)
    halfway = HEAD_DIM // 2
    powers = jnp.arange(halfway, dtype=F32) * (2.0 / HEAD_DIM)
    angles = position.astype(F32)[:, None] * (ROPE_BASE ** (-powers))[None, :]
    cosine, sine = jnp.cos(angles), jnp.sin(angles)
    none = jnp.zeros_like(sine)
    cos = jnp.concatenate([cosine] * 4, axis=1)
    sin_a = jnp.concatenate([-sine, none] * 2, axis=1)
    sin_b = jnp.concatenate([none, sine] * 2, axis=1)
    place = jnp.concatenate(
        [
            jnp.stack([quad, hd]).astype(jnp.int32),
            passage_lengths_each,
            core.reshape(1).astype(jnp.int32),
        ]
    ).astype(jnp.int32)
    tokens = 2 * rows

    qkv, att, part, vec = call(
        attention_forward,
        [
            jax.ShapeDtypeStruct((tokens, 3 * D // 2), BF),
            jax.ShapeDtypeStruct((PAIRS, tokens, GROUP), BF),
            jax.ShapeDtypeStruct((tokens, D), F32),
            jax.ShapeDtypeStruct((16, D), F32),
        ],
        [place, both_rel, *attn_pieces, cos, sin_a, sin_b, mask],
        1, 40, cost(0.1), "attention_forward",
    )
    recv = swap(part, pair_mask)
    def up_map(r, s):
        return (0, s[0] ^ r, s[1], 0)

    def down_map(r, s):
        return (2 * (s[0] ^ r) + s[1], 0, 1, 0)

    def const2(r, s):
        return (0, 0)

    up_spec = pl.BlockSpec((8, 1, 256, 256), up_map)
    down_spec = pl.BlockSpec((1, 4, HIDE, 256), down_map)
    scaled_one, inv_one, low_rel, hidden, slope, out_own, out_other = pl.pallas_call(
        feed_forward,
        out_shape=[
            jax.ShapeDtypeStruct((rows, D), F32),
            jax.ShapeDtypeStruct((rows, 1), F32),
            jax.ShapeDtypeStruct((QUADS, tokens, 256), BF),
            jax.ShapeDtypeStruct((QUADS, tokens, HIDE), BF),
            jax.ShapeDtypeStruct((QUADS, tokens, HIDE), BF),
            jax.ShapeDtypeStruct((rows, D), F32),
            jax.ShapeDtypeStruct((rows, D), F32),
        ],
        grid_spec=pltpu.PrefetchScalarGridSpec(
            num_scalar_prefetch=1,
            grid=(QUADS,),
            in_specs=[
                pl.BlockSpec((tokens, D), const2),
                pl.BlockSpec((tokens, D), const2),
                pl.BlockSpec((tokens, D), const2),
                pl.BlockSpec((16, D), const2),
                up_spec,
                down_spec,
            ],
            out_specs=[
                pl.BlockSpec((rows, D), const2),
                pl.BlockSpec((rows, 1), const2),
                pl.BlockSpec((QUADS, tokens, 256), lambda r, s: (0, 0, 0)),
                pl.BlockSpec((1, tokens, HIDE), lambda r, s: (r, 0, 0)),
                pl.BlockSpec((1, tokens, HIDE), lambda r, s: (r, 0, 0)),
                pl.BlockSpec((rows, D), const2),
                pl.BlockSpec((rows, D), const2),
            ],
            scratch_shapes=[pltpu.VMEM((tokens, D), BF)],
        ),
        compiler_params=params(48),
        cost_estimate=cost(12),
        name="feed_forward",
    )(spot, both, part, recv, vec, mlp_all, mlp_all)
    windows = pl.pallas_call(
        make_windows,
        out_shape=jax.ShapeDtypeStruct((D, SLOTS * EMB), BF),
        grid=(1,),
        in_specs=[pl.BlockSpec((8, 4, GROUP // 2, 256), lambda i: (0, 0, 16, 0))],
        out_specs=pl.BlockSpec((D, SLOTS * EMB), lambda i: (0, 0)),
        compiler_params=params(16),
        cost_estimate=cost(1),
        name="make_windows",
    )(mlp_all)
    recv = swap(out_other, pair_mask)
    outputs, scaled_two, inv_two, own_proj = call(
        final_norm,
        [
            jax.ShapeDtypeStruct((rows, D), BF),
            jax.ShapeDtypeStruct((rows, D), F32),
            jax.ShapeDtypeStruct((rows, 1), F32),
            jax.ShapeDtypeStruct((rows, SLOTS * EMB), BF),
        ],
        [scaled_one, out_own, recv, vec, windows],
        0, 16, cost(2.6), "final_norm",
    )
    projs = lax.all_gather(own_proj, "head")
    lanes = jnp.stack(
        [
            jnp.pad(question_lengths.astype(F32), (0, GROUP - question_lengths.shape[0])),
            jnp.pad(relevant_passage.astype(F32), (0, GROUP - relevant_passage.shape[0])),
        ]
    )
    grad_two, low_two, grad_heads, sums_two, scalars = call(
        soft_maxsim,
        [
            jax.ShapeDtypeStruct((rows, D), F32),
            jax.ShapeDtypeStruct((rows, D), BF),
            jax.ShapeDtypeStruct((D, SLOTS * EMB), F32),
            jax.ShapeDtypeStruct((3, D), F32),
            jax.ShapeDtypeStruct((2, GROUP), F32),
        ],
        [place, logarithmic_warmth, lanes, projs, windows, outputs, scaled_two, inv_two, vec],
        2, 24, cost(4.3), "soft_maxsim", [
            pltpu.VMEM((rows, SLOTS * EMB), BF),
            pltpu.VMEM(((docs + 1) * rows, EMB), BF),
            pltpu.VMEM((rows, docs * rows), F32),
            pltpu.VMEM((rows, docs * rows), BF),
        ],
    )

    low_two_other = swap(low_two, pair_mask)

    def swap_head(a, mask):
        return swap(a, 0, mask)

    def finish_split(a, group):
        count = a.shape[0] // 2
        give = lax.dynamic_slice_in_dim(a, (1 - core) * count, count, 0)
        keep = lax.dynamic_slice_in_dim(a, core * count, count, 0)
        other = swap(give, pair_mask)
        keep = keep.reshape(count, -1, 1, group)
        other = other.reshape(count, -1, 1, group)
        whole = jnp.where(
            core == 0,
            jnp.concatenate([keep, other], axis=2),
            jnp.concatenate([other, keep], axis=2),
        ).reshape(count, -1)
        return scatter_low(whole).astype(F32)

    grad_w_heads = jnp.concatenate(
        [grad_heads[:, i * EMB : i * EMB + w] for i, w in enumerate(WIDTHS)], axis=1
    )
    low_two, grad_w_heads = lax.optimization_barrier((low_two, grad_w_heads))
    down_far = weight_grad(
        spot, hidden, (low_two, low_two_other), (1, 3), None, (), "down_far", 0.1
    )
    down_got = swap(down_far, x_mask)
    low_two_next = after(low_two, down_far)
    grad_pre, gn_own, gn_other, bias_up_grad = pl.pallas_call(
        feed_forward_back,
        out_shape=[
            jax.ShapeDtypeStruct((tokens, QUADS * HIDE), BF),
            jax.ShapeDtypeStruct((rows, D), F32),
            jax.ShapeDtypeStruct((rows, D), F32),
            jax.ShapeDtypeStruct((1, QUADS * HIDE), F32),
        ],
        grid_spec=pltpu.PrefetchScalarGridSpec(
            num_scalar_prefetch=1,
            grid=(QUADS,),
            in_specs=[
                pl.BlockSpec((rows, D), const2),
                pl.BlockSpec((rows, D), const2),
                pl.BlockSpec((1, tokens, HIDE), lambda r, s: (r, 0, 0)),
                up_spec,
                down_spec,
            ],
            out_specs=[
                pl.BlockSpec((tokens, HIDE), lambda r, s: (0, s[0] ^ r)),
                pl.BlockSpec((rows, D), const2),
                pl.BlockSpec((rows, D), const2),
                pl.BlockSpec((1, HIDE), lambda r, s: (0, s[0] ^ r)),
            ],
            scratch_shapes=[pltpu.VMEM((tokens, D), BF)],
        ),
        compiler_params=params(40),
        cost_estimate=cost(0.1),
        name="feed_forward_back",
    )(spot, low_two_next, low_two_other, slope, mlp_all, mlp_all)
    up_far = weight_grad(spot, low_rel, (grad_pre,), (2, 3), None, (), "up_far", 0.1)
    up_got = swap(up_far, y_mask)
    recv = swap(gn_other, pair_mask)
    grad_one, low_one, sums_one = call(
        first_norm_back,
        [
            jax.ShapeDtypeStruct((rows, D), F32),
            jax.ShapeDtypeStruct((rows, D), BF),
            jax.ShapeDtypeStruct((3, D), F32),
        ],
        [grad_two, after(gn_own, up_far), recv, scaled_one, inv_one, vec],
        0, 16, cost(0.1), "first_norm_back",
    )
    low_one_other = swap(low_one, pair_mask)
    grad_qkv, gx_own, gx_other, bias_qkv_grad = call(
        attention_backward,
        [
            jax.ShapeDtypeStruct((tokens, 3 * D // 2), BF),
            jax.ShapeDtypeStruct((rows, D), F32),
            jax.ShapeDtypeStruct((rows, D), F32),
            jax.ShapeDtypeStruct((1, 3 * D // 2), F32),
        ],
        [place, low_one, low_one_other, qkv, *attn_pieces, cos, sin_a, sin_b, mask],
        1, 40, cost(0.1), "attention_backward", [pltpu.VMEM((PAIRS, tokens, GROUP), BF)],
    )
    sums = pl.pallas_call(
        pack_sums,
        out_shape=jax.ShapeDtypeStruct((2 * QUADS, 16, GROUP), F32),
        in_specs=[SMEM_SPEC] + [VMEM_SPEC] * 5,
        out_specs=VMEM_SPEC,
        cost_estimate=cost(0.1),
        name="pack_sums",
    )(spot, sums_two, sums_one, bias_up_grad, bias_qkv_grad, scalars)

    def tail(after_this, halves, blocks, places, adds, name, micros, kind=BF):
        return tail_grad(
            spot, both_rel, after(grad_qkv, *after_this), att, low_one, low_one_other,
            halves, blocks, places, adds, name, micros, kind,
        )

    def second(value, *others):
        return (after(value, *others), low_two_other)

    tail_a = tail((), (0,), (1, 3), None, (), "tail_a_far", 0.1)
    a_got = swap(tail_a, x_mask)
    tail_b = tail((tail_a,), (1,), (2, 3), None, (), "tail_b_far", 0.1)
    b_got = swap(tail_b, y_mask)

    down_near = weight_grad(
        spot, hidden, second(low_two, tail_b), (2,), None, ((down_got, 1, True),), "down_near", 12
    )
    down_last = swap(down_near, y_mask)
    up_near = weight_grad(
        spot, low_rel, (after(grad_pre, down_near),), (1,), None, ((up_got, 1, True),), "up_near", 16
    )
    up_last = swap(up_near, x_mask)
    a_near = tail((up_near,), (0,), (2,), None, ((a_got, 1, 0, True),), "tail_a_near", 10)
    a_last = swap(a_near, y_mask)
    b_near = tail((a_near,), (1,), (1,), None, ((b_got, 1, 0, True),), "tail_b_near", 10)
    b_last = swap(b_near, x_mask)

    down_adds = ((down_got, 0, True), (down_last, 0, True))
    up_adds = ((up_got, 0, True), (up_last, 0, True))
    a_adds = ((a_got, 0, 0, True), (a_last, 0, 0, True))
    b_adds = ((b_got, 0, 0, True), (b_last, 0, 0, True))
    down_z = weight_grad(
        spot, hidden, second(low_two, b_near), (0,), (1, 3), down_adds, "down_head", 10
    )
    down_z1 = swap_head(down_z, 1)
    up_z = weight_grad(
        spot, low_rel, (after(grad_pre, down_z),), (0,), (1, 3), up_adds, "up_head", 10
    )
    up_z1 = swap_head(up_z, 1)
    tail_z = tail((up_z,), (0, 1), (0,), (1, 3), a_adds + b_adds, "tail_head", 10)
    tail_z1 = swap_head(tail_z, 1)
    down_zz = weight_grad(
        spot, hidden, second(low_two, tail_z), (0,), (2,),
        down_adds + ((down_z1, 1, False),), "down_head_near", 8,
    )
    down_z2 = swap_head(down_zz, 2)
    up_zz = weight_grad(
        spot, low_rel, (after(grad_pre, down_zz),), (0,), (2,),
        up_adds + ((up_z1, 1, False),), "up_head_near", 8,
    )
    up_z2 = swap_head(up_zz, 2)
    tail_zz = tail(
        (up_zz,), (0, 1), (0,), (2,),
        a_adds + ((tail_z1, 1, 0, False),) + b_adds + ((tail_z1, 1, 1, False),),
        "tail_head_near", 8,
    )
    tail_z2 = swap_head(tail_zz, 2)
    exact = BF if low_span > 1 else F32
    grad_w_down = weight_grad(
        spot, hidden, second(low_two, tail_zz), (0,), (0,),
        down_adds + ((down_z1, 0, False), (down_z2, 0, False)), "down_own", 4, exact,
    )[0]
    up_own = weight_grad(
        spot, low_rel, (after(grad_pre, grad_w_down),), (0,), (0,),
        up_adds + ((up_z1, 0, False), (up_z2, 0, False)), "up_own", 4,
    )[0]
    kept = tail(
        (up_own,), (0, 1), (0,), (0,),
        a_adds + ((tail_z1, 0, 0, False), (tail_z2, 0, 0, False))
        + b_adds + ((tail_z1, 0, 1, False), (tail_z2, 0, 1, False)),
        "tail_own", 4,
    ).reshape(256, 512)
    grad_w_down = scatter_low(grad_w_down).astype(F32)
    grad_w_up = finish_split(up_own, HIDE)
    grad_w_qkv = finish_split(kept[:, :qkv_cols], GROUP)
    kept_out = kept[:, qkv_cols:]
    grad_w_out = scatter_low(
        jnp.concatenate([kept_out[:GROUP], kept_out[GROUP:]], axis=1)
    ).astype(F32)
    head_rows = D // n_dp
    sums = jnp.pad(sums, ((0, 0), (0, 0), (0, n_hd * head_cols - GROUP)))
    sums = jnp.repeat(sums, low_span, axis=0)
    mixed = jnp.concatenate([grad_w_heads.reshape(n_dp, head_rows, -1), sums], axis=1)
    mixed = mixed.reshape(n_dp * (head_rows + 16), -1)
    mixed = lax.psum_scatter(mixed, "dp", scatter_dimension=0, tiled=True)
    sums = mixed[head_rows:, :GROUP].reshape(16, 2, GROUP // 2).transpose(1, 0, 2)
    sums = jnp.pad(sums.reshape(32, GROUP // 2), ((0, 0), (0, head_cols - GROUP // 2)))
    mixed = mixed[:head_rows].reshape(head_rows, n_hd, head_cols).transpose(1, 0, 2)
    mixed = jnp.concatenate([mixed, jnp.broadcast_to(sums, (n_hd,) + sums.shape)], axis=1)
    mixed = lax.psum_scatter(
        mixed.reshape(n_hd * (head_rows + 32), head_cols), "head", scatter_dimension=0, tiled=True
    )
    grad_w_heads = mixed[:head_rows]
    sums = mixed[head_rows:, : GROUP // 2].reshape(2, 16, GROUP // 2).transpose(1, 0, 2)
    sums = sums.reshape(16, GROUP)
    grad_tokens = grad_one + gx_own + swap(gx_other, pair_mask)

    place_in = (dp % low_span) * n_hd + hd
    mat = lax.dynamic_slice(sums[:9], (0, place_in * wide), (9, wide))
    mid = FF // n_all
    up_sum = lax.dynamic_slice(sums[9:13].reshape(-1), (place_in * mid,), (mid,))
    return (
        outputs,
        sums[13, 0:1],
        grad_tokens,
        grad_w_qkv,
        grad_w_out,
        grad_w_up,
        grad_w_down,
        grad_w_heads,
        mat[:5],
        up_sum,
        mat[5:7],
        mat[7:9],
        sums[14, 0:1],
    )


def solution(mesh):
    return jax.shard_map(
        on_device,
        mesh=mesh,
        in_specs=(
            P(("dp", "head"), None),
            P("dp", "head"),
            P("dp", "head"),
            P("dp", "head"),
            P("dp", "head"),
            P("dp", "head"),
            P(None, ("dp", "head")),
            P(("dp", "head")),
            P(None, ("dp", "head")),
            P(None, ("dp", "head")),
            P(),
            P("dp"),
            P("dp"),
            P("dp"),
        ),
        out_specs=(
            P(("dp", "head"), None),
            P(),
            P(("dp", "head"), None),
            P("dp", "head"),
            P("dp", "head"),
            P("dp", "head"),
            P("dp", "head"),
            P("dp", "head"),
            P(None, ("dp", "head")),
            P(("dp", "head")),
            P(None, ("dp", "head")),
            P(None, ("dp", "head")),
            P(),
        ),
        check_vma=False,
    )
```

time: 695 us -> 433 us (0.62)
  local copies, waits for them, and re-layouts: 184 us -> 34.6 us
  Pallas kernels: 0 us -> 142 us
  blocking collectives: 99.6 us -> 22.3 us
  matrix products: 77.1 us -> 0 us
  other arithmetic: 62.1 us -> 14.8 us
  waiting for transfers between devices: 220 us -> 173 us
  starting transfers between devices: 23 us -> 30 us
    pallas_call x0 -> x26, Pallas kernels: none -> 142 us  [the longest x5 48.2 us: call(): pl.pallas_call(kernel, out_shape=outs, grid=(1,), in_specs=[SMEM_SPEC] *...]
    dot_general x40 -> x0, matrix products: 72.4 us -> none  [the longest x19 32.5 us: mm_tn(): lax.dot_general(a, b, (((0,), (0,)), ((), ())), preferred_element_type=F32)]
    ppermute x28 -> x31, waiting for transfers between devices: 220 us -> 159 us  [swap(): return lax.ppermute(a, ('dp', 'head'), pairs)]
    all_gather x5 -> x1, blocking collectives: 64 us -> 22.3 us  [on_device(): projs = lax.all_gather(own_proj, 'head')]
    slice x23 -> x18, local copies, waits for them, and re-layouts: 43.1 us -> 7.23 us  [the longest x2 2.37 us: on_device(): grad_heads[:, i * EMB:i * EMB + w]]
    unnamed x2 -> x0, blocking collectives: 35.6 us -> none
    unnamed x341 -> x80, local copies, waits for them, and re-layouts: 39.2 us -> 21.6 us
    convert_element_type x18 -> x5, other arithmetic: 18.9 us -> 1.51 us  [the longest x1 0.84 us: on_device(): ((segment[:, None] == segment[None, :])[None] & valid[:, None, :]).astype...]
  transfers between devices with their start and end apart: 35 -> 34, of which waited for: 16 -> 18; matrix products, arithmetic and copies ran while one was open for 32% -> 7% of each run, Pallas kernels for 0% -> 25%
where the time goes in v2:
time: 433 us; the launch traced here: 432 us
  waiting for transfers between devices  173 us (40%)
  Pallas kernels  142 us (33%)
  local copies, waits for them, and re-layouts  34.6 us (8%)
  starting transfers between devices  30 us (7%)
  blocking collectives  22.3 us (5%)
  between operations  15 us (3%)
  other arithmetic  14.8 us (3%)
    ppermute x31, waiting for transfers between devices, swap(): return lax.ppermute(a, ('dp', 'head'), pairs)  159 us
    pallas_call x5, Pallas kernels, call(): pl.pallas_call(kernel, out_shape=outs, grid=(1,), in_specs=[SMEM_SPEC] *...  48.2 us
    pallas_call x10, Pallas kernels, weight_grad(): pl.pallas_call(kernel, out_shape=jax.ShapeDtypeStruct((len(blocks) * coun...  37.7 us
    ppermute x31, starting transfers between devices, swap(): return lax.ppermute(a, ('dp', 'head'), pairs)  29.6 us
    pallas_call x7, Pallas kernels, tail_grad(): pl.pallas_call(kernel, out_shape=jax.ShapeDtypeStruct((len(blocks) * coun...  27.5 us
    all_gather x1, blocking collectives, on_device(): projs = lax.all_gather(own_proj, 'head')  22.3 us
    unnamed x80, local copies, waits for them, and re-layouts  21.6 us
    all_gather x1, waiting for transfers between devices, on_device(): mlp_all = lax.all_gather(packed_mlp, ('dp', 'head'))  14.4 us
  transfers between devices with their start and end apart: 34, of which 18 were waited for; matrix products, arithmetic and copies ran while one was open for 7% of the time, Pallas kernels for 25%

profile of v2, /device:TPU:0, one launch (start us, length us, event | category | flops | bytes accessed | tf_op | source)
XLA Modules:
  0.0 431.8 jit_solution(1549889688851197024)
XLA Ops:
  16.0 4.0 collective-permute-start.2
  21.3 21.3 %collective-permute-done.2 = bf16[1,272,512]{2,1,0:T(8,128)(2,1)S(1)} collective-permute-done((bf16[1,272,512]{2,1,0:T(8,128)(2,1)S(1)}, bf16[1,272,512]{2,1,0:T(8,128)(2,1)S(1)}, u32[]{:S(2)}, u32[]{:S(2)}) %collective-permute-start.2) | collective-permute-done | bytes 278560 | tf_op jit(solution)/shard_map/ppermute | solution.py:619
  49.6 19.8 %collective-permute-done.5.b0 = bf16[2,272,512]{2,1,0:T(8,128)(2,1)S(1)} collective-permute-done((bf16[2,272,512]{2,1,0:T(8,128)(2,1)S(1)}, bf16[2,272,512]{2,1,0:T(8,128)(2,1)S(1)}, u32[]{:S(2)}, u32[]{:S(2)}) %collective-permute-start.5) | collective-permute-done | bytes 557088 | tf_op jit(solution)/shard_map/ppermute | solution.py:619
  73.4 11.6 %collective-permute-done.6.by = bf16[2,272,512]{2,1,0:T(8,128)(2,1)S(1)} collective-permute-done((bf16[2,272,512]{2,1,0:T(8,128)(2,1)S(1)}, bf16[2,272,512]{2,1,0:T(8,128)(2,1)S(1)}, u32[]{:S(2)}, u32[]{:S(2)}) %collective-permute-start.6) | collective-permute-done | bytes 557088 | tf_op jit(solution)/shard_map/ppermute | solution.py:619
  93.0 24.7 %collective-permute-done.4.ay = bf16[2,2,272,512]{3,2,1,0:T(8,128)(2,1)} collective-permute-done((bf16[2,2,272,512]{3,2,1,0:T(8,128)(2,1)}, bf16[2,2,272,512]{3,2,1,0:T(8,128)(2,1)}, u32[]{:S(2)}, u32[]{:S(2)}) %collective-permute-start.4) | collective-permute-done | bytes 1114144 | tf_op jit(solution)/shard_map/ppermute | solution.py:619
  117.7 6.8 %collective-permute-done.7.bx = bf16[2,2,272,512]{3,2,1,0:T(8,128)(2,1)S(1)} collective-permute-done((bf16[2,2,272,512]{3,2,1,0:T(8,128)(2,1)}, bf16[2,2,272,512]{3,2,1,0:T(8,128)(2,1)S(1)}, u32[]{:S(2)}, u32[]{:S(2)}) %collective-permute-start.7) | collective-permute-done | bytes 1114144 | tf_op jit(solution)/shard_map/ppermute | solution.py:619
  125.6 15.8 %attention_forward.1 = (bf16[512,1536]{1,0:T(8,128)(2,1)}, bf16[4,512,128]{2,1,0:T(8,128)(2,1)}, f32[512,1024]{1,0:T(8,128)}, f32[16,1024]{1,0:T(8,128)}) custom-call(s32[6]{0:T(128)} %pad_add_fusion.2.place, bf16[4,512,256]{2,1,0:T(8,128)(2,1)} %pad_maximum_fusion.3.x.x_ref, bf16[2,272,512]{2,1,0:T(8,128)(2,1)} %copy-done, bf16[2,272,512]{2,1,0:T(8,128)(2,1)} %copy-done.2, ...), custom_call_target="tpu_custom_call" | custom-call | flops 115000000 | bytes 1 | tf_op jit(solution)/shard_map/attention_forward/pallas_call | solution.py:69
  141.9 3.8 collective-permute-done.9.recv
  145.7 14.4 %all-gather.4.cloned.1.call-done = bf16[34816,256]{1,0:T(8,128)(2,1)} async-done(((bf16[1088,256]{1,0:T(8,128)(2,1)}), bf16[34816,256]{1,0:T(8,128)(2,1)}) %all-gather.4.cloned.1.call-update) | async-done | bytes 17825808 | tf_op jit(solution)/shard_map/all_gather | solution.py:672
  160.1 14.2 %feed_forward.1 = (f32[256,1024]{1,0:T(8,128)}, f32[256,1]{1,0:T(8,128)}, bf16[4,512,256]{2,1,0:T(8,128)(2,1)}, bf16[4,512,512]{2,1,0:T(8,128)(2,1)}, bf16[4,512...) custom-call(s32[3]{0:T(128)} %pad_add_fusion.1.place.spot_ref.spot, bf16[512,1024]{1,0:T(8,128)(2,1)} %copy-done.6, ...), custom_call_target="tpu_custom_call" | custom-call | flops 13799999488 | bytes 1 | tf_op jit(solution)/shard_map/feed_forward/pallas_call | solution.py:781
  179.3 3.9 final_norm.1
  183.2 22.3 %all-gather.1 = bf16[1024,384]{1,0:T(8,128)(2,1)} all-gather(bf16[256,384]{1,0:T(8,128)(2,1)} %get-tuple-element.67), channel_id=3, replica_groups=mesh['dp'=8,'head'=4] {'head'}, dimensions={0}, use_global_device_ids=true | all-gather | bytes 983040 | tf_op jit(solution)/shard_map/all_gather | solution.py:840
  205.6 7.3 %soft_maxsim.1 = (f32[256,1024]{1,0:T(8,128)}, bf16[256,1024]{1,0:T(8,128)(2,1)}, f32[1024,384]{1,0:T(8,128)}, f32[3,1024]{1,0:T(4,128)}, f32[2,128]{1,0:T(2,128)}) custom-call(s32[6]{0:T(128)} %pad_add_fusion.2.place, f32[1]{0:T(128)S(6)} %copy.96.temp, f32[2,128]{1,0:T(2,128)} %pad_maximum_fusion.12.lanes, bf16[4,256,384]{2,1,0:T(8,128)(2,1)} %bitcast.70, ...), custom_call_target="tpu_custom_call" | custom-call | flops 4944999936 | bytes 1 | tf_op jit(solution)/shard_map/soft_maxsim/pallas_call | solution.py:69
  216.4 4.5 %down_far.1 = bf16[2,512,1024]{2,1,0:T(8,128)(2,1)} custom-call(s32[3]{0:T(128)} %pad_add_fusion.1.place.spot_ref.spot, bf16[4,512,512]{2,1,0:T(8,128)(2,1)} %get-tuple-element.76.lhs_ref, bf16[256,1024]{1,0:T(8,128)(2,1)} %get-tuple-element.107.refs_0_.own.refs_2_, bf16[256,1024]{1,0:T(8,128)(2,1)} %copy-done.7), custom_call_target="tpu_custom_call" | custom-call | flops 115000000 | bytes 1 | tf_op jit(solution)/shard_map/down_far/pallas_call | solution.py:450
  222.1 10.1 %feed_forward_back.1 = (bf16[512,2048]{1,0:T(8,128)(2,1)}, f32[256,1024]{1,0:T(8,128)}, f32[256,1024]{1,0:T(8,128)}, f32[1,2048]{1,0:T(1,128)}) custom-call(s32[3]{0:T(128)} %pad_add_fusion.1.place.spot_ref.spot, bf16[256,1024]{1,0:T(8,128)(2,1)} %get-tuple-element.107.refs_0_.own.refs_2_, bf16[256,1024]{1,0:T(8,128)(2,1)} %copy-done.7, ...), custom_call_target="tpu_custom_call" | custom-call | flops 115000000 | bytes 1 | tf_op jit(solution)/shard_map/feed_forward_back/pallas_call | solution.py:893
  232.6 4.8 %up_far.1 = bf16[2,256,2048]{2,1,0:T(8,128)(2,1)} custom-call(s32[3]{0:T(128)} %pad_add_fusion.1.place.spot_ref.spot, bf16[4,512,256]{2,1,0:T(8,128)(2,1)} %get-tuple-element.80.lhs_ref, bf16[512,2048]{1,0:T(8,128)(2,1)} %get-tuple-element.108.refs_0_.refs_1_), custom_call_target="tpu_custom_call" | custom-call | flops 115000000 | bytes 1 | tf_op jit(solution)/shard_map/up_far/pallas_call | solution.py:450
  240.0 4.0 first_norm_back.1
  247.0 17.2 %attention_backward.1 = (bf16[512,1536]{1,0:T(8,128)(2,1)}, f32[256,1024]{1,0:T(8,128)}, f32[256,1024]{1,0:T(8,128)}, f32[1,1536]{1,0:T(1,128)}) custom-call(s32[6]{0:T(128)} %pad_add_fusion.2.place, bf16[256,1024]{1,0:T(8,128)(2,1)} %get-tuple-element.87.own.refs_1_.refs_3_.refs_6_.refs_8_, bf16[256,1024]{1,0:T(8,128)(2,1)} %copy-done.4, ...), custom_call_target="tpu_custom_call" | custom-call | flops 115000000 | bytes 1 | tf_op jit(solution)/shard_map/attention_backward/pallas_call | solution.py:69
  264.2 4.4 %tail_a_far.1 = bf16[2,1,128,2048]{3,2,1,0:T(8,128)(2,1)} custom-call(s32[3]{0:T(128)} %pad_add_fusion.1.place.spot_ref.spot, bf16[4,512,256]{2,1,0:T(8,128)(2,1)} %pad_maximum_fusion.3.x.x_ref, bf16[4,512,128]{2,1,0:T(8,128)(2,1)} %get-tuple-element.94.att_ref, bf16[512,1536]{1,0:T(8,128)(2,1)} %get-tuple-element.106.refs_0_.refs_5_, ...), custom_call_target="tpu_custom_call" | custom-call | flops 115000000 | bytes 1 | tf_op jit(solution)/shard_map/tail_a_far/pallas_call | solution.py:527
  269.7 4.4 %tail_b_far.1 = bf16[2,1,128,2048]{3,2,1,0:T(8,128)(2,1)} custom-call(s32[3]{0:T(128)} %pad_add_fusion.1.place.spot_ref.spot, bf16[4,512,256]{2,1,0:T(8,128)(2,1)} %pad_maximum_fusion.3.x.x_ref, bf16[4,512,128]{2,1,0:T(8,128)(2,1)} %get-tuple-element.94.att_ref, bf16[512,1536]{1,0:T(8,128)(2,1)} %get-tuple-element.106.refs_0_.refs_5_, ...), custom_call_target="tpu_custom_call" | custom-call | flops 115000000 | bytes 1 | tf_op jit(solution)/shard_map/tail_b_far/pallas_call | solution.py:527
  278.3 4.1 down_near.1
  286.2 4.5 %up_near.1 = bf16[1,256,2048]{2,1,0:T(8,128)(2,1)} custom-call(s32[3]{0:T(128)} %pad_add_fusion.1.place.spot_ref.spot, bf16[4,512,256]{2,1,0:T(8,128)(2,1)} %get-tuple-element.80.lhs_ref, bf16[512,2048]{1,0:T(8,128)(2,1)} %get-tuple-element.108.refs_0_.refs_1_, bf16[2,256,2048]{2,1,0:T(8,128)(2,1)} %collective-permute-done.17.refs_1_.refs_2_.refs_4_), custom_call_target="tpu_custom_call" | custom-call | flops 18400000000 | bytes 1 | tf_op jit(solution)/shard_map/up_near/pallas_call | solution.py:450
  294.9 4.0 tail_a_near.1
  298.9 14.5 %collective-permute-done.19.refs_3_.refs_12_.refs_16_.refs_8_.refs_9_ = bf16[2,1,128,2048]{3,2,1,0:T(8,128)(2,1)} collective-permute-done((bf16[2,1,128,2048]{3,2,1,0:T(8,128)(2,1)}, bf16[2,1,128,2048]{3,2,1,0:T(8,128)(2,1)}, u32[]{:S(2)}, u32[]{:S(2)}) %collective-permute-start.19) | collective-permute-done | bytes 1048608 | tf_op jit(solution)/shard_map/ppermute | solution.py:619
  313.4 4.0 tail_b_near.1
  321.4 16.8 %collective-permute-done.20.refs_5_.refs_7_.refs_3_ = bf16[1,512,1024]{2,1,0:T(8,128)(2,1)} collective-permute-done((bf16[1,512,1024]{2,1,0:T(8,128)(2,1)}, bf16[1,512,1024]{2,1,0:T(8,128)(2,1)}, u32[]{:S(2)}, u32[]{:S(2)}) %collective-permute-start.20) | collective-permute-done | bytes 1048608 | tf_op jit(solution)/shard_map/ppermute | solution.py:619
  338.2 3.6 down_head.1
  343.0 3.6 up_head.1
  350.0 3.9 tail_head.1
  363.6 18.2 %collective-permute-done.25.refs_3_ = bf16[2,256,512]{2,1,0:T(8,128)(2,1)S(1)} collective-permute-done((bf16[2,256,512]{2,1,0:T(8,128)(2,1)}, bf16[2,256,512]{2,1,0:T(8,128)(2,1)S(1)}, u32[]{:S(2)}, u32[]{:S(2)}) %collective-permute-start.25) | collective-permute-done | bytes 524320 | tf_op jit(solution)/shard_map/ppermute | solution.py:619
  386.1 4.7 %collective-permute-done.23.refs_7_.refs_10_.refs_11_ = bf16[2,2,128,512]{3,2,1,0:T(8,128)(2,1)S(1)} collective-permute-done((bf16[2,2,128,512]{3,2,1,0:T(8,128)(2,1)}, bf16[2,2,128,512]{3,2,1,0:T(8,128)(2,1)S(1)}, u32[]{:S(2)}, u32[]{:S(2)}) %collective-permute-start.23) | collective-permute-done | bytes 524320 | tf_op jit(solution)/shard_map/ppermute | solution.py:619
  400.4 7.8 %collective-permute-done.26.refs_8_.refs_12_ = bf16[1,2,128,512]{3,2,1,0:T(8,128)(2,1)S(1)} collective-permute-done((bf16[1,2,128,512]{3,2,1,0:T(8,128)(2,1)}, bf16[1,2,128,512]{3,2,1,0:T(8,128)(2,1)S(1)}, u32[]{:S(2)}, u32[]{:S(2)}) %collective-permute-start.26) | collective-permute-done | bytes 262176 | tf_op jit(solution)/shard_map/ppermute | solution.py:619
  (237 shorter events, 107.7 us)
Async XLA Ops:
  7.2 152.9 %all-gather.4.cloned.1.call-start = ((), (), s32[]{:S(2)}) async-start(), calls=%async_computation.3 | async-start | bytes 18382848 | tf_op jit(solution)/shard_map/all_gather | solution.py:672
  13.5 340.5 %reduce-scatter.5.cloned.1.call-start = ((), (), s32[]{:S(2)}) async-start(), calls=%async_computation.2 | async-start | bytes 1990656 | tf_op jit(solution)/shard_map/reduce_scatter | solution.py:1041
  16.0 26.7 %collective-permute-start.2 = (bf16[1,272,512]{2,1,0:T(8,128)(2,1)S(1)}, bf16[1,272,512]{2,1,0:T(8,128)(2,1)S(1)}, u32[]{:S(2)}, u32[]{:S(2)}) collective-permute-start(bf16[1,272,512]{2,1,0:T(8,128)(2,1)S(1)} %fusion.2), channel_id=1, source_target_pairs={{0,2},{1,3},{2,0},{3,1},{4,6},{5,7},{6,4},{7,5},{8,10},{9,11},{10,... | collective-permute-start | bytes 835592 | tf_op jit(solution)/shard_map/ppermute | solution.py:619
  20.0 71.6 %collective-permute-start = (bf16[256,1024]{1,0:T(8,128)(2,1)}, bf16[256,1024]{1,0:T(8,128)(2,1)S(1)}, u32[]{:S(2)}, u32[]{:S(2)}) collective-permute-start(bf16[256,1024]{1,0:T(8,128)(2,1)} %param.14), channel_id=1, source_target_pairs={{0,4},{1,5},{2,6},{3,7},{4,0},{5,1},{6,2},{7,3},{8,12},{9,13},{10,... | collective-permute-start | bytes 1572872 | tf_op jit(solution)/shard_map/ppermute | solution.py:619
  20.1 69.2 %collective-permute-start.8 = (s32[11]{0:T(128)S(1)}, s32[11]{0:T(128)S(1)}, u32[]{:S(2)}, u32[]{:S(2)}) collective-permute-start(s32[11]{0:T(128)S(1)} %pad_add_fusion.3), channel_id=1, source_target_pairs={{0,4},{1,5},{2,6},{3,7},{4,0},{5,1},{6,2},{7,3},{8,12},{9,13},{10,... | collective-permute-start | bytes 140 | tf_op jit(solution)/shard_map/ppermute | solution.py:619
  42.7 26.6 %collective-permute-start.5 = (bf16[2,272,512]{2,1,0:T(8,128)(2,1)S(1)}, bf16[2,272,512]{2,1,0:T(8,128)(2,1)S(1)}, u32[]{:S(2)}, u32[]{:S(2)}) collective-permute-start(bf16[2,272,512]{2,1,0:T(8,128)(2,1)S(1)} %get-tuple-element.153.a0), channel_id=1, source_target_pairs={{0,1},{1,0},{2,3},{3,2},{4,5},{5,4},{6,7},{7,6},{8,9},{9,8},{10,11... | collective-permute-start | bytes 1671176 | tf_op jit(solution)/shard_map/ppermute | solution.py:619
  47.3 24.4 %collective-permute-start.3 = (bf16[2,272,512]{2,1,0:T(8,128)(2,1)S(1)}, bf16[2,272,512]{2,1,0:T(8,128)(2,1)S(1)}, u32[]{:S(2)}, u32[]{:S(2)}) collective-permute-start(bf16[2,272,512]{2,1,0:T(8,128)(2,1)S(1)} %get-tuple-element.153.a0), channel_id=1, source_target_pairs={{0,8},{1,9},{2,10},{3,11},{4,12},{5,13},{6,14},{7,15},{8,0},{9,1},... | collective-permute-start | bytes 1671176 | tf_op jit(solution)/shard_map/ppermute | solution.py:619
  69.4 15.6 %collective-permute-start.6 = (bf16[2,272,512]{2,1,0:T(8,128)(2,1)S(1)}, bf16[2,272,512]{2,1,0:T(8,128)(2,1)S(1)}, u32[]{:S(2)}, u32[]{:S(2)}) collective-permute-start(bf16[2,272,512]{2,1,0:T(8,128)(2,1)S(1)} %collective-permute-done.5.b0), channel_id=1, source_target_pairs={{0,16},{1,17},{2,18},{3,19},{4,20},{5,21},{6,22},{7,23},{8,24},{9,... | collective-permute-start | bytes 1671176 | tf_op jit(solution)/shard_map/ppermute | solution.py:619
  72.9 44.8 %collective-permute-start.4 = (bf16[2,2,272,512]{3,2,1,0:T(8,128)(2,1)}, bf16[2,2,272,512]{3,2,1,0:T(8,128)(2,1)}, u32[]{:S(2)}, u32[]{:S(2)}) collective-permute-start(bf16[2,2,272,512]{3,2,1,0:T(8,128)(2,1)} %pad_maximum_fusion.1), channel_id=1, source_target_pairs={{0,16},{1,17},{2,18},{3,19},{4,20},{5,21},{6,22},{7,23},{8,24},{9,... | collective-permute-start | bytes 3342344 | tf_op jit(solution)/shard_map/ppermute | solution.py:619
  86.1 38.5 %collective-permute-start.7 = (bf16[2,2,272,512]{3,2,1,0:T(8,128)(2,1)}, bf16[2,2,272,512]{3,2,1,0:T(8,128)(2,1)S(1)}, u32[]{:S(2)}, u32[]{:S(2)}) collective-permute-start(bf16[2,2,272,512]{3,2,1,0:T(8,128)(2,1)} %pad_maximum_fusion.2), channel_id=1, source_target_pairs={{0,8},{1,9},{2,10},{3,11},{4,12},{5,13},{6,14},{7,15},{8,0},{9,1},... | collective-permute-start | bytes 3342344 | tf_op jit(solution)/shard_map/ppermute | solution.py:619
  141.4 4.4 %collective-permute-start.9 = (f32[512,1024]{1,0:T(8,128)}, f32[512,1024]{1,0:T(8,128)S(1)}, u32[]{:S(2)}, u32[]{:S(2)}) collective-permute-start(f32[512,1024]{1,0:T(8,128)} %get-tuple-element.61.part), channel_id=1, source_target_pairs={{0,4},{1,5},{2,6},{3,7},{4,0},{5,1},{6,2},{7,3},{8,12},{9,13},{10,... | collective-permute-start | bytes 6291464 | tf_op jit(solution)/shard_map/ppermute | solution.py:619
  174.3 4.1 collective-permute-start.10
  212.8 2.7 collective-permute-start.11
  220.9 57.3 %collective-permute-start.16 = (bf16[2,512,1024]{2,1,0:T(8,128)(2,1)}, bf16[2,512,1024]{2,1,0:T(8,128)(2,1)}, u32[]{:S(2)}, u32[]{:S(2)}) collective-permute-start(bf16[2,512,1024]{2,1,0:T(8,128)(2,1)} %down_far.1), channel_id=1, source_target_pairs={{0,8},{1,9},{2,10},{3,11},{4,12},{5,13},{6,14},{7,15},{8,0},{9,1},... | collective-permute-start | bytes 6291464 | tf_op jit(solution)/shard_map/ppermute | solution.py:619
  232.3 6.8 %collective-permute-start.12 = (f32[256,1024]{1,0:T(8,128)}, f32[256,1024]{1,0:T(8,128)S(1)}, u32[]{:S(2)}, u32[]{:S(2)}) collective-permute-start(f32[256,1024]{1,0:T(8,128)} %get-tuple-element.83), channel_id=1, source_target_pairs={{0,4},{1,5},{2,6},{3,7},{4,0},{5,1},{6,2},{7,3},{8,12},{9,13},{10,... | collective-permute-start | bytes 3145736 | tf_op jit(solution)/shard_map/ppermute | solution.py:619
  237.4 48.8 %collective-permute-start.17 = (bf16[2,256,2048]{2,1,0:T(8,128)(2,1)}, bf16[2,256,2048]{2,1,0:T(8,128)(2,1)}, u32[]{:S(2)}, u32[]{:S(2)}) collective-permute-start(bf16[2,256,2048]{2,1,0:T(8,128)(2,1)} %up_far.1), channel_id=1, source_target_pairs={{0,16},{1,17},{2,18},{3,19},{4,20},{5,21},{6,22},{7,23},{8,24},{9,... | collective-permute-start | bytes 6291464 | tf_op jit(solution)/shard_map/ppermute | solution.py:619
  244.0 2.1 collective-permute-start.13
  268.6 26.3 %collective-permute-start.15 = (bf16[2,1,128,2048]{3,2,1,0:T(8,128)(2,1)}, bf16[2,1,128,2048]{3,2,1,0:T(8,128)(2,1)}, u32[]{:S(2)}, u32[]{:S(2)}) collective-permute-start(bf16[2,1,128,2048]{3,2,1,0:T(8,128)(2,1)} %tail_a_far.1), channel_id=1, source_target_pairs={{0,8},{1,9},{2,10},{3,11},{4,12},{5,13},{6,14},{7,15},{8,0},{9,1},... | collective-permute-start | bytes 3145736 | tf_op jit(solution)/shard_map/ppermute | solution.py:619
  274.2 39.2 %collective-permute-start.19 = (bf16[2,1,128,2048]{3,2,1,0:T(8,128)(2,1)}, bf16[2,1,128,2048]{3,2,1,0:T(8,128)(2,1)}, u32[]{:S(2)}, u32[]{:S(2)}) collective-permute-start(bf16[2,1,128,2048]{3,2,1,0:T(8,128)(2,1)} %tail_b_far.1), channel_id=1, source_target_pairs={{0,16},{1,17},{2,18},{3,19},{4,20},{5,21},{6,22},{7,23},{8,24},{9,... | collective-permute-start | bytes 3145736 | tf_op jit(solution)/shard_map/ppermute | solution.py:619
  274.2 45.9 %collective-permute-start.14 = (f32[256,1024]{1,0:T(8,128)}, f32[256,1024]{1,0:T(8,128)S(1)}, u32[]{:S(2)}, u32[]{:S(2)}) collective-permute-start(f32[256,1024]{1,0:T(8,128)} %get-tuple-element.93), channel_id=1, source_target_pairs={{0,4},{1,5},{2,6},{3,7},{4,0},{5,1},{6,2},{7,3},{8,12},{9,13},{10,... | collective-permute-start | bytes 3145736 | tf_op jit(solution)/shard_map/ppermute | solution.py:619
  278.0 117.5 %reduce-scatter.7.cloned.1.call-start = ((), (), s32[]{:S(2)}) async-start(), calls=%async_computation.4 | async-start | bytes 409600 | tf_op jit(solution)/shard_map/reduce_scatter | solution.py:1046
  282.4 55.9 %collective-permute-start.20 = (bf16[1,512,1024]{2,1,0:T(8,128)(2,1)}, bf16[1,512,1024]{2,1,0:T(8,128)(2,1)}, u32[]{:S(2)}, u32[]{:S(2)}) collective-permute-start(bf16[1,512,1024]{2,1,0:T(8,128)(2,1)} %down_near.1), channel_id=1, source_target_pairs={{0,16},{1,17},{2,18},{3,19},{4,20},{5,21},{6,22},{7,23},{8,24},{9,... | collective-permute-start | bytes 3145736 | tf_op jit(solution)/shard_map/ppermute | solution.py:619
  290.6 51.4 %collective-permute-start.21 = (bf16[1,256,2048]{2,1,0:T(8,128)(2,1)}, bf16[1,256,2048]{2,1,0:T(8,128)(2,1)S(1)}, u32[]{:S(2)}, u32[]{:S(2)}) collective-permute-start(bf16[1,256,2048]{2,1,0:T(8,128)(2,1)} %up_near.1), channel_id=1, source_target_pairs={{0,8},{1,9},{2,10},{3,11},{4,12},{5,13},{6,14},{7,15},{8,0},{9,1},... | collective-permute-start | bytes 3145736 | tf_op jit(solution)/shard_map/ppermute | solution.py:619
  317.4 31.0 %collective-permute-start.22 = (bf16[1,1,128,2048]{3,2,1,0:T(8,128)(2,1)}, bf16[1,1,128,2048]{3,2,1,0:T(8,128)(2,1)S(1)}, u32[]{:S(2)}, u32[]{:S(2)}) collective-permute-start(bf16[1,1,128,2048]{3,2,1,0:T(8,128)(2,1)} %tail_b_near.1), channel_id=1, source_target_pairs={{0,8},{1,9},{2,10},{3,11},{4,12},{5,13},{6,14},{7,15},{8,0},{9,1},... | collective-permute-start | bytes 1572872 | tf_op jit(solution)/shard_map/ppermute | solution.py:619
  318.1 30.6 %collective-permute-start.18 = (bf16[1,1,128,2048]{3,2,1,0:T(8,128)(2,1)}, bf16[1,1,128,2048]{3,2,1,0:T(8,128)(2,1)S(1)}, u32[]{:S(2)}, u32[]{:S(2)}) collective-permute-start(bf16[1,1,128,2048]{3,2,1,0:T(8,128)(2,1)} %tail_a_near.1), channel_id=1, source_target_pairs={{0,16},{1,17},{2,18},{3,19},{4,20},{5,21},{6,22},{7,23},{8,24},{9,... | collective-permute-start | bytes 1572872 | tf_op jit(solution)/shard_map/ppermute | solution.py:619
  341.8 15.2 %collective-permute-start.24 = (bf16[2,512,256]{2,1,0:T(8,128)(2,1)}, bf16[2,512,256]{2,1,0:T(8,128)(2,1)S(1)}, u32[]{:S(2)}, u32[]{:S(2)}) collective-permute-start(bf16[2,512,256]{2,1,0:T(8,128)(2,1)} %down_head.1), channel_id=1, source_target_pairs={{0,1},{1,0},{2,3},{3,2},{4,5},{5,4},{6,7},{7,6},{8,9},{9,8},{10,11... | collective-permute-start | bytes 1572872 | tf_op jit(solution)/shard_map/ppermute | solution.py:619
  346.6 35.2 %collective-permute-start.25 = (bf16[2,256,512]{2,1,0:T(8,128)(2,1)}, bf16[2,256,512]{2,1,0:T(8,128)(2,1)S(1)}, u32[]{:S(2)}, u32[]{:S(2)}) collective-permute-start(bf16[2,256,512]{2,1,0:T(8,128)(2,1)} %up_head.1), channel_id=1, source_target_pairs={{0,1},{1,0},{2,3},{3,2},{4,5},{5,4},{6,7},{7,6},{8,9},{9,8},{10,11... | collective-permute-start | bytes 1572872 | tf_op jit(solution)/shard_map/ppermute | solution.py:619
  353.9 37.0 %collective-permute-start.23 = (bf16[2,2,128,512]{3,2,1,0:T(8,128)(2,1)}, bf16[2,2,128,512]{3,2,1,0:T(8,128)(2,1)S(1)}, u32[]{:S(2)}, u32[]{:S(2)}) collective-permute-start(bf16[2,2,128,512]{3,2,1,0:T(8,128)(2,1)} %tail_head.1), channel_id=1, source_target_pairs={{0,1},{1,0},{2,3},{3,2},{4,5},{5,4},{6,7},{7,6},{8,9},{9,8},{10,11... | collective-permute-start | bytes 1572872 | tf_op jit(solution)/shard_map/ppermute | solution.py:619
  360.9 51.4 %collective-permute-start.28 = (bf16[1,512,256]{2,1,0:T(8,128)(2,1)}, bf16[1,512,256]{2,1,0:T(8,128)(2,1)S(1)}, u32[]{:S(2)}, u32[]{:S(2)}) collective-permute-start(bf16[1,512,256]{2,1,0:T(8,128)(2,1)} %down_head_near.1), channel_id=1, source_target_pairs={{0,2},{1,3},{2,0},{3,1},{4,6},{5,7},{6,4},{7,5},{8,10},{9,11},{10,... | collective-permute-start | bytes 786440 | tf_op jit(solution)/shard_map/ppermute | solution.py:619
  385.7 30.7 %collective-permute-start.29 = (bf16[1,256,512]{2,1,0:T(8,128)(2,1)}, bf16[1,256,512]{2,1,0:T(8,128)(2,1)S(1)}, u32[]{:S(2)}, u32[]{:S(2)}) collective-permute-start(bf16[1,256,512]{2,1,0:T(8,128)(2,1)} %up_head_near.1), channel_id=1, source_target_pairs={{0,2},{1,3},{2,0},{3,1},{4,6},{5,7},{6,4},{7,5},{8,10},{9,11},{10,... | collective-permute-start | bytes 786440 | tf_op jit(solution)/shard_map/ppermute | solution.py:619
  395.0 13.2 %collective-permute-start.26 = (bf16[1,2,128,512]{3,2,1,0:T(8,128)(2,1)}, bf16[1,2,128,512]{3,2,1,0:T(8,128)(2,1)S(1)}, u32[]{:S(2)}, u32[]{:S(2)}) collective-permute-start(bf16[1,2,128,512]{3,2,1,0:T(8,128)(2,1)} %tail_head_near.1), channel_id=1, source_target_pairs={{0,2},{1,3},{2,0},{3,1},{4,6},{5,7},{6,4},{7,5},{8,10},{9,11},{10,... | collective-permute-start | bytes 786440 | tf_op jit(solution)/shard_map/ppermute | solution.py:619
  421.3 2.7 collective-permute-start.30
  (35 other events, 216.8 us)
Sparse Core Ops, SparseCore 0:
  13.6 146.4 all-gather.3
  278.1 46.6 reduce-scatter.4
  357.1 24.7 reduce-scatter.6

commit v3 on v2

--- a/solution.py
+++ b/solution.py
@@ -50,7 +50,7 @@
 
 
 def params(mib):
-    return pltpu.CompilerParams(vmem_limit_bytes=58 << 20)
+    return pltpu.CompilerParams(vmem_limit_bytes=mib << 20)
 
 
 TIME_UNIT = 1150000000
@@ -118,8 +118,23 @@
     return (lane < HEAD_DIM) if h == 0 else (lane >= HEAD_DIM)
 
 
-def softmax_rows(q, k, allowed):
-    s = jnp.where(allowed, dot_nt(q, k), MASKED)
+def stacked(a):
+    zero = jnp.zeros_like(a)
+    return jnp.concatenate(
+        [jnp.where(head_mask(0, a.shape), a, zero), jnp.where(head_mask(1, a.shape), a, zero)],
+        axis=0,
+    )
+
+
+def unstacked(a):
+    half = a.shape[0] // 2
+    top = a[:half]
+    return jnp.where(head_mask(0, top.shape), top, a[half:])
+
+
+def softmax_rows(q, k, mask):
+    mask = jnp.concatenate([mask, mask], axis=0)
+    s = jnp.where(mask > 0, dot_nt(q, k), MASKED)
     raised = jnp.exp(s - jnp.max(s, axis=-1, keepdims=True))
     return raised * (1.0 / jnp.sum(raised, axis=-1, keepdims=True))
 
@@ -162,13 +177,9 @@
         q = qkv[row, pl.ds(pl.multiple_of(i * GROUP, GROUP), GROUP)]
         k = qkv[row, pl.ds(pl.multiple_of((PAIRS + i) * GROUP, GROUP), GROUP)]
         v = qkv[row, pl.ds(pl.multiple_of((2 * PAIRS + i) * GROUP, GROUP), GROUP)]
-        allowed = mask[b] > 0
-        got = []
-        for h in range(2):
-            qh = jnp.where(head_mask(h, q.shape), q, jnp.zeros_like(q))
-            probs = softmax_rows(qh, k, allowed)
-            got.append(dot_nn(probs.astype(BF), v))
-        att[r, row, :] = jnp.where(head_mask(0, q.shape), got[0], got[1]).astype(BF)
+        probs = softmax_rows(stacked(q), k, mask[b])
+        both = dot_nn(probs.astype(BF), v)
+        att[r, row, :] = unstacked(both).astype(BF)
         return carry
 
     lax.fori_loop(0, 2 * PAIRS, one, 0)
@@ -206,23 +217,14 @@
         at_k = pl.ds(pl.multiple_of((PAIRS + i) * GROUP, GROUP), GROUP)
         at_v = pl.ds(pl.multiple_of((2 * PAIRS + i) * GROUP, GROUP), GROUP)
         q, k, v = qkv[row, at_q], qkv[row, at_k], qkv[row, at_v]
-        grad_out = ga[r, row, :]
-        allowed = mask[b] > 0
-        zero = jnp.zeros_like(q)
-        gq = gk = gv = None
-        for h in range(2):
-            sel = head_mask(h, q.shape)
-            qh = jnp.where(sel, q, zero)
-            kh = jnp.where(sel, k, zero)
-            goh = jnp.where(sel, grad_out, zero)
-            probs = softmax_rows(qh, k, allowed)
-            gp = dot_nt(goh, v)
-            gs = probs * (gp - jnp.sum(probs * gp, axis=-1, keepdims=True))
-            gs = gs.astype(BF)
-            tq, tk, tv = dot_nn(gs, kh), dot_tn(gs, qh), dot_tn(probs.astype(BF), goh)
-            gq = tq if gq is None else gq + tq
-            gk = tk if gk is None else gk + tk
-            gv = tv if gv is None else gv + tv
+        q_pair, grad_pair = stacked(q), stacked(ga[r, row, :])
+        probs = softmax_rows(q_pair, k, mask[b])
+        gp = dot_nt(grad_pair, v)
+        gs = probs * (gp - jnp.sum(probs * gp, axis=-1, keepdims=True))
+        gs = gs.astype(BF)
+        gq = unstacked(dot_nn(gs, k))
+        gk = dot_tn(gs, q_pair)
+        gv = dot_tn(probs.astype(BF), grad_pair)
         c, sa, sb = cos[...], -sin_a[...], -sin_b[...]
         grad_qkv[row, at_q] = turn(gq * (HEAD_DIM**-0.5), c, sa, sb).astype(BF)
         grad_qkv[row, at_k] = turn(gk, c, sa, sb).astype(BF)
@@ -321,16 +323,17 @@
     inv_out[...] = inverse
     low = (scaled * vec[6:7, :] + vec[8:9, :]).astype(BF)
     out[...] = low
-    proj[...] = dot_nn(low, windows[...]).astype(BF)
+    proj[...] = dot_nt(windows[...], low).astype(BF)
 
 
 def soft_maxsim(
-    place, temp, lanes, projs, windows, out, scaled, inverse_two, vec,
+    place, temp, lanes, proj_0, proj_1, proj_2, proj_3, windows, out, scaled, inverse_two, vec,
     grad_two, low_two, grad_heads, sums, scalars, gproj, units, shares, similar_low,
 ):
     hd = place[1]
     rows = out.shape[0]
-    docs = projs.shape[0] - 1
+    projs = (proj_0, proj_1, proj_2, proj_3)
+    docs = len(projs) - 1
     row = lax.broadcasted_iota(jnp.int32, (rows, GROUP), 0)
     lane = lax.broadcasted_iota(jnp.int32, (rows, GROUP), 1)
     member = (row // QLEN == lane).astype(F32)
@@ -345,19 +348,20 @@
     loss = jnp.zeros((1, GROUP), F32)
     grad_temp = jnp.zeros((1, GROUP), F32)
     for slot in range(SLOTS):
-        cols = slice(slot * EMB, (slot + 1) * EMB)
-
-        def unit_of(block):
-            mapped = projs[block, :, cols].astype(F32)
-            inverse = lax.rsqrt(jnp.sum(mapped * mapped, axis=-1, keepdims=True) + EPS_UNIT)
+        width = WIDTHS[slot]
+        cols = slice(STARTS[slot], STARTS[slot] + width)
+
+        def unit_of(away):
+            mapped = projs[away][cols, :].astype(F32)
+            inverse = lax.rsqrt(jnp.sum(mapped * mapped, axis=0, keepdims=True) + EPS_UNIT)
             return mapped * inverse, inverse
 
-        for block in range(docs + 1):
-            units[block * rows : (block + 1) * rows, :] = unit_of(block)[0].astype(BF)
+        for away in range(docs + 1):
+            units[0:width, lanes_at(hd ^ away, rows)] = unit_of(away)[0].astype(BF)
         logits = []
         for d in range(docs):
             doc = slice((d + 1) * rows, (d + 2) * rows)
-            similar = dot_nt(units[0:rows, :], units[doc, :]) * (1.0 / SHARPNESS)
+            similar = dot_tn(units[0:width, 0:rows], units[0:width, doc]) * (1.0 / SHARPNESS)
             similar = jnp.where(key < place[2 + d], similar, MASKED)
             top = jnp.max(similar, axis=-1, keepdims=True)
             raised = jnp.exp(similar - top)
@@ -380,17 +384,17 @@
 
         own = jnp.maximum(hd - 1, 0)
         at = pl.ds(pl.multiple_of(own * rows, rows), rows)
-        from_docs = dot_nn(similar_low[...], units[rows:, :])
-        from_queries = dot_tn(similar_low[:, at], units[0:rows, :])
+        from_docs = dot_nt(units[0:width, rows:], similar_low[...])
+        from_queries = dot_nn(units[0:width, 0:rows], similar_low[:, at])
         grad = jnp.where(hd == 0, from_docs, from_queries)
-        unit, inverse = unit_of(hd)
-        gproj[:, cols] = (
-            inverse * (grad - unit * jnp.sum(grad * unit, axis=-1, keepdims=True))
+        unit, inverse = unit_of(0)
+        gproj[cols, :] = (
+            inverse * (grad - unit * jnp.sum(grad * unit, axis=0, keepdims=True))
         ).astype(BF)
 
     scalars[0:1, :] = loss
     scalars[1:2, :] = grad_temp
-    grad_final = dot_nt(gproj[...], windows[...])
+    grad_final = dot_tn(gproj[...], windows[...])
     xhat = scaled[...]
     grad = norm_back(grad_final, xhat, inverse_two[...], vec[6:7, :])
     grad_two[...] = grad
@@ -398,7 +402,9 @@
     sums[0:1, :] = jnp.sum(grad_final * xhat, axis=0, keepdims=True)
     sums[1:2, :] = jnp.sum(grad_final, axis=0, keepdims=True)
     sums[2:3, :] = jnp.sum(low_two[...].astype(F32), axis=0, keepdims=True)
-    grad_heads[...] = dot_tn(out[...], gproj[...])
+    heads = dot_nn(gproj[...], out[...])
+    for t in range(2 * QUADS):
+        grad_heads[t] = heads[:, t * GROUP : (t + 1) * GROUP]
 
 
 def first_norm_back(grad_two, own, recv, scaled, inverse, vec, grad_one, low_one, sums):
@@ -440,12 +446,13 @@
     specs = [pl.BlockSpec((1, tokens, width), lambda i, s: (blocks[0] + step * i, 0, 0))]
     for place in places:
         specs += [pl.BlockSpec((span, tile), lambda i, s, c=place: (0, column(s, c)))] * parts
-    for place in places:
-        for _, at, aligned in adds:
+    for k, place in enumerate(places):
+        for _, at, per_block, per_place, aligned in adds:
+            at += per_place * k
             if aligned:
-                index = lambda i, s, at=at, c=place: (at, 0, column(s, c))
+                index = lambda i, s, at=at, n=per_block, c=place: (at + n * i, 0, column(s, c))
             else:
-                index = lambda i, s, at=at: (at, 0, 0)
+                index = lambda i, s, at=at, n=per_block: (at + n * i, 0, 0)
             specs.append(pl.BlockSpec((1, width, tile), index))
     return pl.pallas_call(
         kernel,
@@ -459,7 +466,7 @@
         compiler_params=params(24),
         cost_estimate=cost(micros),
         name=name,
-    )(spot, lhs, *(list(rhs) * count), *([a for a, _, _ in adds] * count))
+    )(spot, lhs, *(list(rhs) * count), *([add[0] for add in adds] * count))
 
 
 def tail_grad(spot, x, grad_qkv, att, own, other, halves, blocks, places, adds, name, micros, kind=BF):
@@ -541,6 +548,42 @@
     )(spot, x, att, *inputs)
 
 
+def tail_pair(x, grad_qkv, att, own, other, jobs, adds, name, micros):
+    tokens = x.shape[1]
+    rows = tokens // 2
+
+    def kernel(x_ref, qkv_ref, att_ref, own_ref, other_ref, *refs):
+        for n, blocks in enumerate(jobs):
+            out = refs[len(adds) + n]
+            for k, (r, half) in enumerate(blocks):
+                left_all = dot_tn(x_ref[r, :, half * GROUP : (half + 1) * GROUP], qkv_ref[...])
+                for z in range(4):
+                    lanes = slice((2 * z + half) * GROUP, (2 * z + half + 1) * GROUP)
+                    right = dot_tn(att_ref[r, 0:rows, :], own_ref[:, lanes])
+                    right += dot_tn(att_ref[r, rows:, :], other_ref[:, lanes])
+                    left = left_all[:, z * 384 : (z + 1) * 384]
+                    lo = z * 512
+                    if adds:
+                        left += refs[n][0, 0, :, lo : lo + 384].astype(F32)
+                        right += refs[n][0, 0, :, lo + 384 : lo + 512].astype(F32)
+                    out[k, 0, :, lo : lo + 384] = left.astype(BF)
+                    out[k, 0, :, lo + 384 : lo + 512] = right.astype(BF)
+
+    outs = [jax.ShapeDtypeStruct((len(blocks), 1, GROUP, 2048), BF) for blocks in jobs]
+    specs = [whole(a) for a in (x, grad_qkv, att, own, other)]
+    specs += [pl.BlockSpec((1, 1, GROUP, 2048), lambda i: (1, 0, 0, 0))] * len(adds)
+    return pl.pallas_call(
+        kernel,
+        out_shape=outs,
+        grid=(1,),
+        in_specs=specs,
+        out_specs=[whole(a) for a in outs],
+        compiler_params=params(40),
+        cost_estimate=cost(micros),
+        name=name,
+    )(x, grad_qkv, att, own, other, *adds)
+
+
 def pack_sums(spot, two, one, up, qkv, scalars, out):
     core, hd = spot[1], spot[2]
     out[...] = jnp.zeros_like(out)
@@ -564,22 +607,16 @@
             out[t, 13 + k : 14 + k, :] = jnp.broadcast_to(totals[k], (1, GROUP))
 
 
-def make_windows(tiles, windows):
-    lane = lax.broadcasted_iota(jnp.int32, (GROUP // 2, GROUP), 1)
+def make_windows(tiles, windows, wide):
+    cols = windows.shape[0] // 4
     for dp in range(2 * QUADS):
-        for half in range(2):
-            first_row = dp * GROUP + half * (GROUP // 2)
-            at = slice(first_row, first_row + GROUP // 2)
-            t = [
-                tiles[dp, z, :, half * GROUP : (half + 1) * GROUP].astype(F32) for z in range(4)
-            ]
-            second = pltpu.roll(t[1], 72, 1)
-            first = jnp.where(lane < 72, t[0], second)
-            middle = jnp.where(lane < 16, second, pltpu.roll(t[2], 16, 1))
-            middle = jnp.where(lane < 88, middle, pltpu.roll(t[3], 88, 1))
-            windows[at, 0:128] = first.astype(BF)
-            windows[at, 128:256] = jnp.where(lane < 96, middle, 0.0).astype(BF)
-            windows[at, 256:384] = jnp.where(lane < 64, pltpu.roll(t[3], 120, 1), 0.0).astype(BF)
+        at = slice(dp * GROUP, (dp + 1) * GROUP)
+        for z in range(4):
+            lo = z * cols
+            wide[lo : lo + 64, at] = tiles[dp, z, :, 0:GROUP].astype(F32)
+            rest = tiles[dp, z, 0:16, GROUP:].astype(F32)
+            wide[lo + 64 : lo + cols, at] = rest[0 : cols - 64, :]
+    windows[...] = wide[...].astype(BF)
 
 
 def on_device(
@@ -651,12 +688,12 @@
     col_blocks = wup_low.shape[1] // 256
     heads_low = gather_low(nested_projector)
     head_cols = heads_low.shape[1]
-    heads_low = jnp.pad(heads_low, ((0, 0), (0, GROUP - head_cols)))
+    heads_low = jnp.pad(heads_low.T, ((0, GROUP - head_cols), (0, 0)))
     packed_mlp = jnp.concatenate(
         [wup_low[:, i * 256 : (i + 1) * 256] for i in range(col_blocks)]
         + [
             gather_low(contract_matrix),
-            jnp.concatenate([heads_low[: GROUP // 2], heads_low[GROUP // 2 :]], axis=1),
+            jnp.concatenate([heads_low[:64], heads_low[64:]], axis=1),
         ],
         axis=0,
     )
@@ -764,7 +801,7 @@
             jax.ShapeDtypeStruct((16, D), F32),
         ],
         [place, both_rel, *attn_pieces, cos, sin_a, sin_b, mask],
-        1, 40, cost(0.1), "attention_forward",
+        1, 58, cost(0.1), "attention_forward",
     )
     recv = swap(part, pair_mask)
     def up_map(r, s):
@@ -811,17 +848,19 @@
             ],
             scratch_shapes=[pltpu.VMEM((tokens, D), BF)],
         ),
-        compiler_params=params(48),
+        compiler_params=params(58),
         cost_estimate=cost(12),
         name="feed_forward",
     )(spot, both, part, recv, vec, mlp_all, mlp_all)
+    all_cols = n_hd * head_cols
     windows = pl.pallas_call(
         make_windows,
-        out_shape=jax.ShapeDtypeStruct((D, SLOTS * EMB), BF),
+        out_shape=jax.ShapeDtypeStruct((all_cols, D), BF),
         grid=(1,),
-        in_specs=[pl.BlockSpec((8, 4, GROUP // 2, 256), lambda i: (0, 0, 16, 0))],
-        out_specs=pl.BlockSpec((D, SLOTS * EMB), lambda i: (0, 0)),
-        compiler_params=params(16),
+        in_specs=[pl.BlockSpec((8, 4, 64, 256), lambda i: (0, 0, 16, 0))],
+        out_specs=pl.BlockSpec((all_cols, D), lambda i: (0, 0)),
+        scratch_shapes=[pltpu.VMEM((all_cols, D), F32)],
+        compiler_params=params(58),
         cost_estimate=cost(1),
         name="make_windows",
     )(mlp_all)
@@ -832,12 +871,12 @@
             jax.ShapeDtypeStruct((rows, D), BF),
             jax.ShapeDtypeStruct((rows, D), F32),
             jax.ShapeDtypeStruct((rows, 1), F32),
-            jax.ShapeDtypeStruct((rows, SLOTS * EMB), BF),
+            jax.ShapeDtypeStruct((all_cols, rows), BF),
         ],
         [scaled_one, out_own, recv, vec, windows],
         0, 16, cost(2.6), "final_norm",
     )
-    projs = lax.all_gather(own_proj, "head")
+    projs = [own_proj] + [swap(own_proj, 0, k) for k in range(1, n_hd)]
     lanes = jnp.stack(
         [
             jnp.pad(question_lengths.astype(F32), (0, GROUP - question_lengths.shape[0])),
@@ -849,14 +888,14 @@
         [
             jax.ShapeDtypeStruct((rows, D), F32),
             jax.ShapeDtypeStruct((rows, D), BF),
-            jax.ShapeDtypeStruct((D, SLOTS * EMB), F32),
+            jax.ShapeDtypeStruct((2 * QUADS, all_cols, GROUP), F32),
             jax.ShapeDtypeStruct((3, D), F32),
             jax.ShapeDtypeStruct((2, GROUP), F32),
         ],
-        [place, logarithmic_warmth, lanes, projs, windows, outputs, scaled_two, inv_two, vec],
+        [place, logarithmic_warmth, lanes, *projs, windows, outputs, scaled_two, inv_two, vec],
         2, 24, cost(4.3), "soft_maxsim", [
-            pltpu.VMEM((rows, SLOTS * EMB), BF),
-            pltpu.VMEM(((docs + 1) * rows, EMB), BF),
+            pltpu.VMEM((all_cols, rows), BF),
+            pltpu.VMEM((EMB, (docs + 1) * rows), BF),
             pltpu.VMEM((rows, docs * rows), F32),
             pltpu.VMEM((rows, docs * rows), BF),
         ],
@@ -881,10 +920,6 @@
         ).reshape(count, -1)
         return scatter_low(whole).astype(F32)
 
-    grad_w_heads = jnp.concatenate(
-        [grad_heads[:, i * EMB : i * EMB + w] for i, w in enumerate(WIDTHS)], axis=1
-    )
-    low_two, grad_w_heads = lax.optimization_barrier((low_two, grad_w_heads))
     down_far = weight_grad(
         spot, hidden, (low_two, low_two_other), (1, 3), None, (), "down_far", 0.1
     )
@@ -916,7 +951,7 @@
             ],
             scratch_shapes=[pltpu.VMEM((tokens, D), BF)],
         ),
-        compiler_params=params(40),
+        compiler_params=params(58),
         cost_estimate=cost(0.1),
         name="feed_forward_back",
     )(spot, low_two_next, low_two_other, slope, mlp_all, mlp_all)
@@ -943,7 +978,7 @@
             jax.ShapeDtypeStruct((1, 3 * D // 2), F32),
         ],
         [place, low_one, low_one_other, qkv, *attn_pieces, cos, sin_a, sin_b, mask],
-        1, 40, cost(0.1), "attention_backward", [pltpu.VMEM((PAIRS, tokens, GROUP), BF)],
+        1, 58, cost(0.1), "attention_backward", [pltpu.VMEM((PAIRS, tokens, GROUP), BF)],
     )
     sums = pl.pallas_call(
         pack_sums,
@@ -963,46 +998,52 @@
     def second(value, *others):
         return (after(value, *others), low_two_other)
 
-    tail_a = tail((), (0,), (1, 3), None, (), "tail_a_far", 0.1)
+    tail_args = (both_rel, grad_qkv, att, low_one, low_one_other)
+    tail_a, tail_b = tail_pair(
+        *tail_args, (((1, 0), (3, 0)), ((2, 1), (3, 1))), (), "tail_far", 0.1
+    )
     a_got = swap(tail_a, x_mask)
-    tail_b = tail((tail_a,), (1,), (2, 3), None, (), "tail_b_far", 0.1)
     b_got = swap(tail_b, y_mask)
 
-    down_near = weight_grad(
-        spot, hidden, second(low_two, tail_b), (2,), None, ((down_got, 1, True),), "down_near", 12
-    )
-    down_last = swap(down_near, y_mask)
+    down_z = weight_grad(
+        spot, hidden, second(low_two, tail_b), (0, 2), (1, 3),
+        ((down_got, 0, 1, 0, True),), "down_head", 12,
+    )
+    down_z1 = swap_head(down_z, 1)
     up_near = weight_grad(
-        spot, low_rel, (after(grad_pre, down_near),), (1,), None, ((up_got, 1, True),), "up_near", 16
+        spot, low_rel, (after(grad_pre, down_z),), (1,), None,
+        ((up_got, 1, 0, 0, True),), "up_near", 16,
     )
     up_last = swap(up_near, x_mask)
-    a_near = tail((up_near,), (0,), (2,), None, ((a_got, 1, 0, True),), "tail_a_near", 10)
+    down_zz = weight_grad(
+        spot, hidden, second(low_two, up_near), (0, 2), (2,),
+        ((down_got, 0, 1, 0, True), (down_z1, 1, 2, 0, False)), "down_head_near", 10,
+    )
+    down_z2 = swap_head(down_zz, 2)
+    a_near, b_near = tail_pair(
+        both_rel, after(grad_qkv, down_zz), att, low_one, low_one_other,
+        (((2, 0),), ((1, 1),)), (a_got, b_got), "tail_near", 10,
+    )
     a_last = swap(a_near, y_mask)
-    b_near = tail((a_near,), (1,), (1,), None, ((b_got, 1, 0, True),), "tail_b_near", 10)
     b_last = swap(b_near, x_mask)
-
-    down_adds = ((down_got, 0, True), (down_last, 0, True))
-    up_adds = ((up_got, 0, True), (up_last, 0, True))
+    up_adds = ((up_got, 0, 0, 0, True), (up_last, 0, 0, 0, True))
+    up_z = weight_grad(
+        spot, low_rel, (after(grad_pre, b_near),), (0,), (1, 3), up_adds, "up_head", 10
+    )
+    up_z1 = swap_head(up_z, 1)
     a_adds = ((a_got, 0, 0, True), (a_last, 0, 0, True))
     b_adds = ((b_got, 0, 0, True), (b_last, 0, 0, True))
-    down_z = weight_grad(
-        spot, hidden, second(low_two, b_near), (0,), (1, 3), down_adds, "down_head", 10
-    )
-    down_z1 = swap_head(down_z, 1)
-    up_z = weight_grad(
-        spot, low_rel, (after(grad_pre, down_z),), (0,), (1, 3), up_adds, "up_head", 10
-    )
-    up_z1 = swap_head(up_z, 1)
     tail_z = tail((up_z,), (0, 1), (0,), (1, 3), a_adds + b_adds, "tail_head", 10)
     tail_z1 = swap_head(tail_z, 1)
-    down_zz = weight_grad(
-        spot, hidden, second(low_two, tail_z), (0,), (2,),
-        down_adds + ((down_z1, 1, False),), "down_head_near", 8,
-    )
-    down_z2 = swap_head(down_zz, 2)
+    down_y = weight_grad(
+        spot, hidden, second(low_two, tail_z), (2,), (0,),
+        ((down_got, 1, 0, 0, True), (down_z1, 2, 0, 0, False), (down_z2, 1, 0, 0, False)),
+        "down_near", 8,
+    )
+    down_last = swap(down_y, y_mask)
     up_zz = weight_grad(
-        spot, low_rel, (after(grad_pre, down_zz),), (0,), (2,),
-        up_adds + ((up_z1, 1, False),), "up_head_near", 8,
+        spot, low_rel, (after(grad_pre, down_y),), (0,), (2,),
+        up_adds + ((up_z1, 1, 0, 0, False),), "up_head_near", 8,
     )
     up_z2 = swap_head(up_zz, 2)
     tail_zz = tail(
@@ -1014,11 +1055,15 @@
     exact = BF if low_span > 1 else F32
     grad_w_down = weight_grad(
         spot, hidden, second(low_two, tail_zz), (0,), (0,),
-        down_adds + ((down_z1, 0, False), (down_z2, 0, False)), "down_own", 4, exact,
+        (
+            (down_got, 0, 0, 0, True), (down_z1, 0, 0, 0, False),
+            (down_z2, 0, 0, 0, False), (down_last, 0, 0, 0, False),
+        ),
+        "down_own", 4, exact,
     )[0]
     up_own = weight_grad(
         spot, low_rel, (after(grad_pre, grad_w_down),), (0,), (0,),
-        up_adds + ((up_z1, 0, False), (up_z2, 0, False)), "up_own", 4,
+        up_adds + ((up_z1, 0, 0, 0, False), (up_z2, 0, 0, 0, False)), "up_own", 4,
     )[0]
     kept = tail(
         (up_own,), (0, 1), (0,), (0,),
@@ -1033,22 +1078,23 @@
     grad_w_out = scatter_low(
         jnp.concatenate([kept_out[:GROUP], kept_out[GROUP:]], axis=1)
     ).astype(F32)
+    mixed = jnp.concatenate([grad_heads, sums], axis=1)
+    mixed = jnp.repeat(mixed, low_span, axis=0) if low_span > 1 else mixed
+    mixed = lax.psum_scatter(
+        mixed.reshape(n_dp * (all_cols + 16), GROUP), "dp", scatter_dimension=0, tiled=True
+    )
+    shard = (head_cols + 16 + 31) // 32 * 32
+    sums = jnp.pad(mixed[all_cols:], ((0, shard - head_cols - 16), (0, 0)))
+    sums = jnp.broadcast_to(sums, (n_hd,) + sums.shape)
+    mixed = jnp.concatenate([mixed[:all_cols].reshape(n_hd, head_cols, GROUP), sums], axis=1)
+    mixed = lax.psum_scatter(
+        mixed.reshape(n_hd * shard, GROUP), "head", scatter_dimension=0, tiled=True
+    )
     head_rows = D // n_dp
-    sums = jnp.pad(sums, ((0, 0), (0, 0), (0, n_hd * head_cols - GROUP)))
-    sums = jnp.repeat(sums, low_span, axis=0)
-    mixed = jnp.concatenate([grad_w_heads.reshape(n_dp, head_rows, -1), sums], axis=1)
-    mixed = mixed.reshape(n_dp * (head_rows + 16), -1)
-    mixed = lax.psum_scatter(mixed, "dp", scatter_dimension=0, tiled=True)
-    sums = mixed[head_rows:, :GROUP].reshape(16, 2, GROUP // 2).transpose(1, 0, 2)
-    sums = jnp.pad(sums.reshape(32, GROUP // 2), ((0, 0), (0, head_cols - GROUP // 2)))
-    mixed = mixed[:head_rows].reshape(head_rows, n_hd, head_cols).transpose(1, 0, 2)
-    mixed = jnp.concatenate([mixed, jnp.broadcast_to(sums, (n_hd,) + sums.shape)], axis=1)
-    mixed = lax.psum_scatter(
-        mixed.reshape(n_hd * (head_rows + 32), head_cols), "head", scatter_dimension=0, tiled=True
-    )
-    grad_w_heads = mixed[:head_rows]
-    sums = mixed[head_rows:, : GROUP // 2].reshape(2, 16, GROUP // 2).transpose(1, 0, 2)
-    sums = sums.reshape(16, GROUP)
+    grad_w_heads = lax.dynamic_slice(
+        mixed, (0, (dp % low_span) * head_rows), (head_cols, head_rows)
+    ).T
+    sums = mixed[head_cols : head_cols + 16]
     grad_tokens = grad_one + gx_own + swap(gx_other, pair_mask)
 
     place_in = (dp % low_span) * n_hd + hd

time: 433 us -> 389 us (0.90)
  Pallas kernels: 142 us -> 106 us
  blocking collectives: 22.3 us -> 0 us
  starting transfers between devices: 30 us -> 41.1 us
  local copies, waits for them, and re-layouts: 34.6 us -> 40.6 us
    all_gather x1 -> x0, blocking collectives: 22.3 us -> none  [on_device(): projs = lax.all_gather(own_proj, 'head')]
    pallas_call x7 -> x3, Pallas kernels: 27.5 us -> 8.38 us  [tail_grad(): pl.pallas_call(kernel, out_shape=jax.ShapeDtypeStruct((len(blocks) * coun...]
    pallas_call x5, Pallas kernels: 48.2 us -> 36 us  [call(): pl.pallas_call(kernel, out_shape=outs, grid=(1,), in_specs=[SMEM_SPEC] *...]
    ppermute x31 -> x34, starting transfers between devices: 29.6 us -> 40.9 us  [swap(): return lax.ppermute(a, ('dp', 'head'), pairs)]
    pallas_call x10, Pallas kernels: 37.7 us -> 28.1 us  [weight_grad(): pl.pallas_call(kernel, out_shape=jax.ShapeDtypeStruct((len(blocks) * coun...]
    unnamed x80 -> x167, local copies, waits for them, and re-layouts: 21.6 us -> 27.8 us
    pallas_call x1 -> x3, Pallas kernels: 2.48 us -> 7.96 us  [the longest x2 5.7 us: tail_pair(): pl.pallas_call(kernel, out_shape=outs, grid=(1,), in_specs=specs, out_spe...]
    ppermute x31 -> x34, waiting for transfers between devices: 159 us -> 154 us  [swap(): return lax.ppermute(a, ('dp', 'head'), pairs)]
  transfers between devices with their start and end apart: 34 -> 37, of which waited for: 18 -> 21; matrix products, arithmetic and copies ran while one was open for 7% -> 7% of each run, Pallas kernels for 25% -> 21%
where the time goes in v3:
time: 389 us; the launch traced here: 387 us
  waiting for transfers between devices  169 us (43%)
  Pallas kernels  106 us (27%)
  starting transfers between devices  41.1 us (11%)
  local copies, waits for them, and re-layouts  40.6 us (10%)
  between operations  15.3 us (4%)
  other arithmetic  14.5 us (4%)
    ppermute x34, waiting for transfers between devices, swap(): return lax.ppermute(a, ('dp', 'head'), pairs)  154 us
    ppermute x34, starting transfers between devices, swap(): return lax.ppermute(a, ('dp', 'head'), pairs)  40.9 us
    pallas_call x5, Pallas kernels, call(): pl.pallas_call(kernel, out_shape=outs, grid=(1,), in_specs=[SMEM_SPEC] *...  36 us
    pallas_call x10, Pallas kernels, weight_grad(): pl.pallas_call(kernel, out_shape=jax.ShapeDtypeStruct((len(blocks) * coun...  28.1 us
    unnamed x167, local copies, waits for them, and re-layouts  27.8 us
    all_gather x1, waiting for transfers between devices, on_device(): mlp_all = lax.all_gather(packed_mlp, ('dp', 'head'))  14.8 us
    pallas_call x1, Pallas kernels, on_device(): pl.pallas_call(feed_forward, out_shape=[jax.ShapeDtypeStruct((rows, D), F...  14.1 us
    pallas_call x1, Pallas kernels, on_device(): pl.pallas_call(feed_forward_back, out_shape=[jax.ShapeDtypeStruct((tokens...  10.2 us
  transfers between devices with their start and end apart: 37, of which 21 were waited for; matrix products, arithmetic and copies ran while one was open for 7% of the time, Pallas kernels for 21%

profile of v3, /device:TPU:0, one launch (start us, length us, event | category | flops | bytes accessed | tf_op | source)
XLA Modules:
  0.0 386.9 jit_solution(12552286676111149031)
XLA Ops:
  15.8 4.0 %collective-permute-start.2 = (bf16[1,272,512]{2,1,0:T(8,128)(2,1)S(1)}, bf16[1,272,512]{2,1,0:T(8,128)(2,1)S(1)}, u32[]{:S(2)}, u32[]{:S(2)}) collective-permute-start(bf16[1,272,512]{2,1,0:T(8,128)(2,1)S(1)} %fusion.2), channel_id=1, source_target_pairs={{0,2},{1,3},{2,0},{3,1},{4,6},{5,7},{6,4},{7,5},{8,10},{9,11},{10,... | collective-permute-start | bytes 835592 | tf_op jit(solution)/shard_map/ppermute | solution.py:656
  21.1 21.3 %collective-permute-done.2 = bf16[1,272,512]{2,1,0:T(8,128)(2,1)S(1)} collective-permute-done((bf16[1,272,512]{2,1,0:T(8,128)(2,1)S(1)}, bf16[1,272,512]{2,1,0:T(8,128)(2,1)S(1)}, u32[]{:S(2)}, u32[]{:S(2)}) %collective-permute-start.2) | collective-permute-done | bytes 278560 | tf_op jit(solution)/shard_map/ppermute | solution.py:656
  42.5 3.0 collective-permute-start.5
  49.4 19.9 %collective-permute-done.5.b0 = bf16[2,272,512]{2,1,0:T(8,128)(2,1)S(1)} collective-permute-done((bf16[2,272,512]{2,1,0:T(8,128)(2,1)S(1)}, bf16[2,272,512]{2,1,0:T(8,128)(2,1)S(1)}, u32[]{:S(2)}, u32[]{:S(2)}) %collective-permute-start.5) | collective-permute-done | bytes 557088 | tf_op jit(solution)/shard_map/ppermute | solution.py:656
  73.3 11.6 %collective-permute-done.6.by = bf16[2,272,512]{2,1,0:T(8,128)(2,1)S(1)} collective-permute-done((bf16[2,272,512]{2,1,0:T(8,128)(2,1)S(1)}, bf16[2,272,512]{2,1,0:T(8,128)(2,1)S(1)}, u32[]{:S(2)}, u32[]{:S(2)}) %collective-permute-start.6) | collective-permute-done | bytes 557088 | tf_op jit(solution)/shard_map/ppermute | solution.py:656
  92.9 24.6 %collective-permute-done.4.ay = bf16[2,2,272,512]{3,2,1,0:T(8,128)(2,1)S(1)} collective-permute-done((bf16[2,2,272,512]{3,2,1,0:T(8,128)(2,1)}, bf16[2,2,272,512]{3,2,1,0:T(8,128)(2,1)S(1)}, u32[]{:S(2)}, u32[]{:S(2)}) %collective-permute-start.4) | collective-permute-done | bytes 1114144 | tf_op jit(solution)/shard_map/ppermute | solution.py:656
  117.5 7.0 %collective-permute-done.7.bx = bf16[2,2,272,512]{3,2,1,0:T(8,128)(2,1)} collective-permute-done((bf16[2,2,272,512]{3,2,1,0:T(8,128)(2,1)}, bf16[2,2,272,512]{3,2,1,0:T(8,128)(2,1)}, u32[]{:S(2)}, u32[]{:S(2)}) %collective-permute-start.7) | collective-permute-done | bytes 1114144 | tf_op jit(solution)/shard_map/ppermute | solution.py:656
  124.5 13.8 %attention_forward.1 = (bf16[512,1536]{1,0:T(8,128)(2,1)}, bf16[4,512,128]{2,1,0:T(8,128)(2,1)}, f32[512,1024]{1,0:T(8,128)}, f32[16,1024]{1,0:T(8,128)}) custom-call(s32[6]{0:T(128)} %pad_add_fusion.2.place, bf16[4,512,256]{2,1,0:T(8,128)(2,1)} %pad_maximum_fusion.3.x.x_ref, bf16[2,272,512]{2,1,0:T(8,128)(2,1)} %copy-done.59, ...), custom_call_target="tpu_custom_call" | custom-call | flops 115000000 | bytes 1 | tf_op jit(solution)/shard_map/attention_forward/pallas_call | solution.py:69
  138.9 4.8 %collective-permute-done.9.recv = f32[512,1024]{1,0:T(8,128)S(1)} collective-permute-done((f32[512,1024]{1,0:T(8,128)}, f32[512,1024]{1,0:T(8,128)S(1)}, u32[]{:S(2)}, u32[]{:S(2)}) %collective-permute-start.9) | collective-permute-done | bytes 2097184 | tf_op jit(solution)/shard_map/ppermute | solution.py:656
  143.7 14.8 %all-gather.3.cloned.1.call-done = bf16[34816,256]{1,0:T(8,128)(2,1)} async-done(((bf16[1088,256]{1,0:T(8,128)(2,1)}), bf16[34816,256]{1,0:T(8,128)(2,1)}) %all-gather.3.cloned.1.call-update) | async-done | bytes 17825808 | tf_op jit(solution)/shard_map/all_gather | solution.py:709
  158.5 14.1 %feed_forward.1 = (f32[256,1024]{1,0:T(8,128)}, f32[256,1]{1,0:T(8,128)}, bf16[4,512,256]{2,1,0:T(8,128)(2,1)}, bf16[4,512,512]{2,1,0:T(8,128)(2,1)}, bf16[4,512...) custom-call(s32[3]{0:T(128)} %pad_add_fusion.1.place.spot_ref.spot, bf16[512,1024]{1,0:T(8,128)(2,1)} %copy-done.64, ...), custom_call_target="tpu_custom_call" | custom-call | flops 13799999488 | bytes 1 | tf_op jit(solution)/shard_map/feed_forward/pallas_call | solution.py:818
  178.0 6.6 %collective-permute-start.11 = (bf16[288,256]{1,0:T(8,128)(2,1)S(1)}, bf16[288,256]{1,0:T(8,128)(2,1)S(1)}, u32[]{:S(2)}, u32[]{:S(2)}) collective-permute-start(bf16[288,256]{1,0:T(8,128)(2,1)S(1)} %get-tuple-element.67.proj_0), channel_id=1, source_target_pairs={{0,1},{1,0},{2,3},{3,2},{4,5},{5,4},{6,7},{7,6},{8,9},{9,8},{10,11... | collective-permute-start | bytes 442376 | tf_op jit(solution)/shard_map/ppermute | solution.py:656
  188.1 3.3 collective-permute-done.11.proj_1
  191.4 7.1 %collective-permute-done.12.proj_2 = bf16[288,256]{1,0:T(8,128)(2,1)S(1)} collective-permute-done((bf16[288,256]{1,0:T(8,128)(2,1)S(1)}, bf16[288,256]{1,0:T(8,128)(2,1)S(1)}, u32[]{:S(2)}, u32[]{:S(2)}) %collective-permute-start.12) | collective-permute-done | bytes 147488 | tf_op jit(solution)/shard_map/ppermute | solution.py:656
  199.6 4.1 %soft_maxsim.1 = (f32[256,1024]{1,0:T(8,128)S(1)}, bf16[256,1024]{1,0:T(8,128)(2,1)S(1)}, f32[8,288,128]{2,1,0:T(8,128)S(1)}, f32[3,1024]{1,0:T(4,128)S(1)}, f32[2,128]{1,0:T(2,128)S(1)}) custom-call(s32[6]{0:T(128)S(1)} %copy-done.47, f32[1]{0:T(128)S(6)} %copy.64.temp, f32[2,128]{1,0:T(2,128)S(1)} %pad_maximum_fusion.11.lanes, ...), custom_call_target="tpu_custom_call" | custom-call | flops 4944999936 | bytes 1 | tf_op jit(solution)/shard_map/soft_maxsim/pallas_call | solution.py:69
  206.6 3.1 down_far.1
  210.6 10.2 %feed_forward_back.1 = (bf16[512,2048]{1,0:T(8,128)(2,1)}, f32[256,1024]{1,0:T(8,128)}, f32[256,1024]{1,0:T(8,128)}, f32[1,2048]{1,0:T(1,128)}) custom-call(s32[3]{0:T(128)} %pad_add_fusion.1.place.spot_ref.spot, bf16[256,1024]{1,0:T(8,128)(2,1)} %copy-done.1, bf16[256,1024]{1,0:T(8,128)(2,1)} %copy-done.3, bf16[4,512,512]{2,1,0:T(8,128)(2,1)} %get-tuple-element.76.slope, ...), custom_call_target="tpu_custom_call" | custom-call | flops 115000000 | bytes 1 | tf_op jit(solution)/shard_map/feed_forward_back/pallas_call | solution.py:928
  222.5 3.0 up_far.1
  231.6 16.0 %attention_backward.1 = (bf16[512,1536]{1,0:T(8,128)(2,1)}, f32[256,1024]{1,0:T(8,128)}, f32[256,1024]{1,0:T(8,128)}, f32[1,1536]{1,0:T(1,128)}) custom-call(s32[6]{0:T(128)} %pad_add_fusion.2.place, bf16[256,1024]{1,0:T(8,128)(2,1)} %copy-done.14, bf16[256,1024]{1,0:T(8,128)(2,1)} %copy-done.17, bf16[512,1536]{1,0:T(8,128)(2,1)} %get-tuple-element.86.qkv, ...), custom_call_target="tpu_custom_call" | custom-call | flops 115000000 | bytes 1 | tf_op jit(solution)/shard_map/attention_backward/pallas_call | solution.py:69
  261.9 3.0 down_head.1
  267.8 6.5 %collective-permute-done.20.refs_1_.refs_2_.refs_4_ = bf16[2,256,2048]{2,1,0:T(8,128)(2,1)} collective-permute-done((bf16[2,256,2048]{2,1,0:T(8,128)(2,1)}, bf16[2,256,2048]{2,1,0:T(8,128)(2,1)}, u32[]{:S(2)}, u32[]{:S(2)}) %collective-permute-start.20) | collective-permute-done | bytes 2097184 | tf_op jit(solution)/shard_map/ppermute | solution.py:656
  279.4 12.2 %collective-permute-done.21.refs_3_ = bf16[4,512,256]{2,1,0:T(8,128)(2,1)S(1)} collective-permute-done((bf16[4,512,256]{2,1,0:T(8,128)(2,1)S(1)}, bf16[4,512,256]{2,1,0:T(8,128)(2,1)S(1)}, u32[]{:S(2)}, u32[]{:S(2)}) %collective-permute-start.21) | collective-permute-done | bytes 1048608 | tf_op jit(solution)/shard_map/ppermute | solution.py:656
  291.6 3.0 down_head_near.1
  294.6 6.6 %collective-permute-done.22.refs_1_.refs_12_.refs_16_.refs_8_.refs_9_ = bf16[2,1,128,2048]{3,2,1,0:T(8,128)(2,1)} collective-permute-done((bf16[2,1,128,2048]{3,2,1,0:T(8,128)(2,1)}, bf16[2,1,128,2048]{3,2,1,0:T(8,128)(2,1)}, u32[]{:S(2)}, u32[]{:S(2)}) %collective-permute-start.22) | collective-permute-done | bytes 1048608 | tf_op jit(solution)/shard_map/ppermute | solution.py:656
  301.2 3.0 tail_near.1
  305.2 4.6 %collective-permute-start.27 = (bf16[2,512,256]{2,1,0:T(8,128)(2,1)}, bf16[2,512,256]{2,1,0:T(8,128)(2,1)}, u32[]{:S(2)}, u32[]{:S(2)}) collective-permute-start(bf16[2,512,256]{2,1,0:T(8,128)(2,1)} %down_head_near.1), channel_id=1, source_target_pairs={{0,2},{1,3},{2,0},{3,1},{4,6},{5,7},{6,4},{7,5},{8,10},{9,11},{10,... | collective-permute-start | bytes 1572872 | tf_op jit(solution)/shard_map/ppermute | solution.py:656
  316.6 6.5 %collective-permute-done.23.refs_11_.refs_15_.refs_6_ = bf16[1,1,128,2048]{3,2,1,0:T(8,128)(2,1)} collective-permute-done((bf16[1,1,128,2048]{3,2,1,0:T(8,128)(2,1)}, bf16[1,1,128,2048]{3,2,1,0:T(8,128)(2,1)}, u32[]{:S(2)}, u32[]{:S(2)}) %collective-permute-start.23) | collective-permute-done | bytes 524320 | tf_op jit(solution)/shard_map/ppermute | solution.py:656
  325.5 3.3 tail_head.1
  328.9 6.1 %collective-permute-done.27.refs_4_ = bf16[2,512,256]{2,1,0:T(8,128)(2,1)} collective-permute-done((bf16[2,512,256]{2,1,0:T(8,128)(2,1)}, bf16[2,512,256]{2,1,0:T(8,128)(2,1)}, u32[]{:S(2)}, u32[]{:S(2)}) %collective-permute-start.27) | collective-permute-done | bytes 524320 | tf_op jit(solution)/shard_map/ppermute | solution.py:656
  339.3 3.6 collective-permute-done.28.refs_3_
  349.1 8.5 %collective-permute-done.26.refs_7_.refs_10_.refs_11_ = bf16[2,2,128,512]{3,2,1,0:T(8,128)(2,1)} collective-permute-done((bf16[2,2,128,512]{3,2,1,0:T(8,128)(2,1)}, bf16[2,2,128,512]{3,2,1,0:T(8,128)(2,1)}, u32[]{:S(2)}, u32[]{:S(2)}) %collective-permute-start.26) | collective-permute-done | bytes 524320 | tf_op jit(solution)/shard_map/ppermute | solution.py:656
  363.1 3.1 down_own.1
  (313 shorter events, 109.4 us)
Async XLA Ops:
  7.2 151.3 %all-gather.3.cloned.1.call-start = ((), (), s32[]{:S(2)}) async-start(), calls=%async_computation.4 | async-start | bytes 18382848 | tf_op jit(solution)/shard_map/all_gather | solution.py:709
  13.3 300.9 %reduce-scatter.3.cloned.1.call-start = ((), (), s32[]{:S(2)}) async-start(), calls=%async_computation.2 | async-start | bytes 1400832 | tf_op jit(solution)/shard_map/reduce_scatter | solution.py:1083
  15.8 26.7 %collective-permute-start.2 = (bf16[1,272,512]{2,1,0:T(8,128)(2,1)S(1)}, bf16[1,272,512]{2,1,0:T(8,128)(2,1)S(1)}, u32[]{:S(2)}, u32[]{:S(2)}) collective-permute-start(bf16[1,272,512]{2,1,0:T(8,128)(2,1)S(1)} %fusion.2), channel_id=1, source_target_pairs={{0,2},{1,3},{2,0},{3,1},{4,6},{5,7},{6,4},{7,5},{8,10},{9,11},{10,... | collective-permute-start | bytes 835592 | tf_op jit(solution)/shard_map/ppermute | solution.py:656
  19.8 70.7 %collective-permute-start = (bf16[256,1024]{1,0:T(8,128)(2,1)S(1)}, bf16[256,1024]{1,0:T(8,128)(2,1)}, u32[]{:S(2)}, u32[]{:S(2)}) collective-permute-start(bf16[256,1024]{1,0:T(8,128)(2,1)S(1)} %copy-done.67), channel_id=1, source_target_pairs={{0,4},{1,5},{2,6},{3,7},{4,0},{5,1},{6,2},{7,3},{8,12},{9,13},{10,... | collective-permute-start | bytes 1572872 | tf_op jit(solution)/shard_map/ppermute | solution.py:656
  19.9 68.2 %collective-permute-start.8 = (s32[11]{0:T(128)S(1)}, s32[11]{0:T(128)S(1)}, u32[]{:S(2)}, u32[]{:S(2)}) collective-permute-start(s32[11]{0:T(128)S(1)} %pad_add_fusion.3), channel_id=1, source_target_pairs={{0,4},{1,5},{2,6},{3,7},{4,0},{5,1},{6,2},{7,3},{8,12},{9,13},{10,... | collective-permute-start | bytes 140 | tf_op jit(solution)/shard_map/ppermute | solution.py:656
  42.5 26.7 %collective-permute-start.5 = (bf16[2,272,512]{2,1,0:T(8,128)(2,1)S(1)}, bf16[2,272,512]{2,1,0:T(8,128)(2,1)S(1)}, u32[]{:S(2)}, u32[]{:S(2)}) collective-permute-start(bf16[2,272,512]{2,1,0:T(8,128)(2,1)S(1)} %get-tuple-element.140.a0), channel_id=1, source_target_pairs={{0,1},{1,0},{2,3},{3,2},{4,5},{5,4},{6,7},{7,6},{8,9},{9,8},{10,11... | collective-permute-start | bytes 1671176 | tf_op jit(solution)/shard_map/ppermute | solution.py:656
  47.1 24.4 %collective-permute-start.3 = (bf16[2,272,512]{2,1,0:T(8,128)(2,1)S(1)}, bf16[2,272,512]{2,1,0:T(8,128)(2,1)S(1)}, u32[]{:S(2)}, u32[]{:S(2)}) collective-permute-start(bf16[2,272,512]{2,1,0:T(8,128)(2,1)S(1)} %get-tuple-element.140.a0), channel_id=1, source_target_pairs={{0,8},{1,9},{2,10},{3,11},{4,12},{5,13},{6,14},{7,15},{8,0},{9,1},... | collective-permute-start | bytes 1671176 | tf_op jit(solution)/shard_map/ppermute | solution.py:656
  69.3 15.6 %collective-permute-start.6 = (bf16[2,272,512]{2,1,0:T(8,128)(2,1)S(1)}, bf16[2,272,512]{2,1,0:T(8,128)(2,1)S(1)}, u32[]{:S(2)}, u32[]{:S(2)}) collective-permute-start(bf16[2,272,512]{2,1,0:T(8,128)(2,1)S(1)} %collective-permute-done.5.b0), channel_id=1, source_target_pairs={{0,16},{1,17},{2,18},{3,19},{4,20},{5,21},{6,22},{7,23},{8,24},{9,... | collective-permute-start | bytes 1671176 | tf_op jit(solution)/shard_map/ppermute | solution.py:656
  72.7 44.8 %collective-permute-start.4 = (bf16[2,2,272,512]{3,2,1,0:T(8,128)(2,1)}, bf16[2,2,272,512]{3,2,1,0:T(8,128)(2,1)S(1)}, u32[]{:S(2)}, u32[]{:S(2)}) collective-permute-start(bf16[2,2,272,512]{3,2,1,0:T(8,128)(2,1)} %pad_maximum_fusion.1), channel_id=1, source_target_pairs={{0,16},{1,17},{2,18},{3,19},{4,20},{5,21},{6,22},{7,23},{8,24},{9,... | collective-permute-start | bytes 3342344 | tf_op jit(solution)/shard_map/ppermute | solution.py:656
  86.1 38.5 %collective-permute-start.7 = (bf16[2,2,272,512]{3,2,1,0:T(8,128)(2,1)}, bf16[2,2,272,512]{3,2,1,0:T(8,128)(2,1)}, u32[]{:S(2)}, u32[]{:S(2)}) collective-permute-start(bf16[2,2,272,512]{3,2,1,0:T(8,128)(2,1)} %pad_maximum_fusion.2), channel_id=1, source_target_pairs={{0,8},{1,9},{2,10},{3,11},{4,12},{5,13},{6,14},{7,15},{8,0},{9,1},... | collective-permute-start | bytes 3342344 | tf_op jit(solution)/shard_map/ppermute | solution.py:656
  138.4 5.4 %collective-permute-start.9 = (f32[512,1024]{1,0:T(8,128)}, f32[512,1024]{1,0:T(8,128)S(1)}, u32[]{:S(2)}, u32[]{:S(2)}) collective-permute-start(f32[512,1024]{1,0:T(8,128)} %get-tuple-element.61.part), channel_id=1, source_target_pairs={{0,4},{1,5},{2,6},{3,7},{4,0},{5,1},{6,2},{7,3},{8,12},{9,13},{10,... | collective-permute-start | bytes 6291464 | tf_op jit(solution)/shard_map/ppermute | solution.py:656
  172.6 2.9 collective-permute-start.10
  178.0 13.5 %collective-permute-start.11 = (bf16[288,256]{1,0:T(8,128)(2,1)S(1)}, bf16[288,256]{1,0:T(8,128)(2,1)S(1)}, u32[]{:S(2)}, u32[]{:S(2)}) collective-permute-start(bf16[288,256]{1,0:T(8,128)(2,1)S(1)} %get-tuple-element.67.proj_0), channel_id=1, source_target_pairs={{0,1},{1,0},{2,3},{3,2},{4,5},{5,4},{6,7},{7,6},{8,9},{9,8},{10,11... | collective-permute-start | bytes 442376 | tf_op jit(solution)/shard_map/ppermute | solution.py:656
  184.5 13.9 %collective-permute-start.12 = (bf16[288,256]{1,0:T(8,128)(2,1)S(1)}, bf16[288,256]{1,0:T(8,128)(2,1)S(1)}, u32[]{:S(2)}, u32[]{:S(2)}) collective-permute-start(bf16[288,256]{1,0:T(8,128)(2,1)S(1)} %get-tuple-element.67.proj_0), channel_id=1, source_target_pairs={{0,2},{1,3},{2,0},{3,1},{4,6},{5,7},{6,4},{7,5},{8,10},{9,11},{10,... | collective-permute-start | bytes 442376 | tf_op jit(solution)/shard_map/ppermute | solution.py:656
  186.0 12.5 %collective-permute-start.13 = (bf16[288,256]{1,0:T(8,128)(2,1)S(1)}, bf16[288,256]{1,0:T(8,128)(2,1)S(1)}, u32[]{:S(2)}, u32[]{:S(2)}) collective-permute-start(bf16[288,256]{1,0:T(8,128)(2,1)S(1)} %get-tuple-element.67.proj_0), channel_id=1, source_target_pairs={{0,3},{1,2},{2,1},{3,0},{4,7},{5,6},{6,5},{7,4},{8,11},{9,10},{10,... | collective-permute-start | bytes 442376 | tf_op jit(solution)/shard_map/ppermute | solution.py:656
  209.7 49.4 %collective-permute-start.19 = (bf16[2,512,1024]{2,1,0:T(8,128)(2,1)}, bf16[2,512,1024]{2,1,0:T(8,128)(2,1)}, u32[]{:S(2)}, u32[]{:S(2)}) collective-permute-start(bf16[2,512,1024]{2,1,0:T(8,128)(2,1)} %down_far.1), channel_id=1, source_target_pairs={{0,8},{1,9},{2,10},{3,11},{4,12},{5,13},{6,14},{7,15},{8,0},{9,1},... | collective-permute-start | bytes 6291464 | tf_op jit(solution)/shard_map/ppermute | solution.py:656
  220.8 6.4 %collective-permute-start.15 = (f32[256,1024]{1,0:T(8,128)}, f32[256,1024]{1,0:T(8,128)S(1)}, u32[]{:S(2)}, u32[]{:S(2)}) collective-permute-start(f32[256,1024]{1,0:T(8,128)} %get-tuple-element.81), channel_id=1, source_target_pairs={{0,4},{1,5},{2,6},{3,7},{4,0},{5,1},{6,2},{7,3},{8,12},{9,13},{10,... | collective-permute-start | bytes 3145736 | tf_op jit(solution)/shard_map/ppermute | solution.py:656
  225.5 48.7 %collective-permute-start.20 = (bf16[2,256,2048]{2,1,0:T(8,128)(2,1)}, bf16[2,256,2048]{2,1,0:T(8,128)(2,1)}, u32[]{:S(2)}, u32[]{:S(2)}) collective-permute-start(bf16[2,256,2048]{2,1,0:T(8,128)(2,1)} %up_far.1), channel_id=1, source_target_pairs={{0,16},{1,17},{2,18},{3,19},{4,20},{5,21},{6,22},{7,23},{8,24},{9,... | collective-permute-start | bytes 6291464 | tf_op jit(solution)/shard_map/ppermute | solution.py:656
  253.9 47.3 %collective-permute-start.22 = (bf16[2,1,128,2048]{3,2,1,0:T(8,128)(2,1)}, bf16[2,1,128,2048]{3,2,1,0:T(8,128)(2,1)}, u32[]{:S(2)}, u32[]{:S(2)}) collective-permute-start(bf16[2,1,128,2048]{3,2,1,0:T(8,128)(2,1)} %get-tuple-element.95), channel_id=1, source_target_pairs={{0,16},{1,17},{2,18},{3,19},{4,20},{5,21},{6,22},{7,23},{8,24},{9,... | collective-permute-start | bytes 3145736 | tf_op jit(solution)/shard_map/ppermute | solution.py:656
  254.2 40.3 %collective-permute-start.18 = (bf16[2,1,128,2048]{3,2,1,0:T(8,128)(2,1)}, bf16[2,1,128,2048]{3,2,1,0:T(8,128)(2,1)}, u32[]{:S(2)}, u32[]{:S(2)}) collective-permute-start(bf16[2,1,128,2048]{3,2,1,0:T(8,128)(2,1)} %get-tuple-element.94), channel_id=1, source_target_pairs={{0,8},{1,9},{2,10},{3,11},{4,12},{5,13},{6,14},{7,15},{8,0},{9,1},... | collective-permute-start | bytes 3145736 | tf_op jit(solution)/shard_map/ppermute | solution.py:656
  255.5 22.6 %collective-permute-start.17 = (f32[256,1024]{1,0:T(8,128)}, f32[256,1024]{1,0:T(8,128)S(1)}, u32[]{:S(2)}, u32[]{:S(2)}) collective-permute-start(f32[256,1024]{1,0:T(8,128)} %get-tuple-element.91), channel_id=1, source_target_pairs={{0,4},{1,5},{2,6},{3,7},{4,0},{5,1},{6,2},{7,3},{8,12},{9,13},{10,... | collective-permute-start | bytes 3145736 | tf_op jit(solution)/shard_map/ppermute | solution.py:656
  259.1 86.6 %reduce-scatter.5.cloned.1.call-start = ((), (), s32[]{:S(2)}) async-start(), calls=%async_computation.3 | async-start | bytes 245760 | tf_op jit(solution)/shard_map/reduce_scatter | solution.py:1090
  264.9 26.7 %collective-permute-start.21 = (bf16[4,512,256]{2,1,0:T(8,128)(2,1)S(1)}, bf16[4,512,256]{2,1,0:T(8,128)(2,1)S(1)}, u32[]{:S(2)}, u32[]{:S(2)}) collective-permute-start(bf16[4,512,256]{2,1,0:T(8,128)(2,1)S(1)} %down_head.1), channel_id=1, source_target_pairs={{0,1},{1,0},{2,3},{3,2},{4,5},{5,4},{6,7},{7,6},{8,9},{9,8},{10,11... | collective-permute-start | bytes 3145736 | tf_op jit(solution)/shard_map/ppermute | solution.py:656
  276.8 34.5 %collective-permute-start.24 = (bf16[1,256,2048]{2,1,0:T(8,128)(2,1)S(1)}, bf16[1,256,2048]{2,1,0:T(8,128)(2,1)S(1)}, u32[]{:S(2)}, u32[]{:S(2)}) collective-permute-start(bf16[1,256,2048]{2,1,0:T(8,128)(2,1)S(1)} %up_near.1), channel_id=1, source_target_pairs={{0,8},{1,9},{2,10},{3,11},{4,12},{5,13},{6,14},{7,15},{8,0},{9,1},... | collective-permute-start | bytes 3145736 | tf_op jit(solution)/shard_map/ppermute | solution.py:656
  304.1 18.9 %collective-permute-start.25 = (bf16[1,1,128,2048]{3,2,1,0:T(8,128)(2,1)}, bf16[1,1,128,2048]{3,2,1,0:T(8,128)(2,1)}, u32[]{:S(2)}, u32[]{:S(2)}) collective-permute-start(bf16[1,1,128,2048]{3,2,1,0:T(8,128)(2,1)} %get-tuple-element.101), channel_id=1, source_target_pairs={{0,8},{1,9},{2,10},{3,11},{4,12},{5,13},{6,14},{7,15},{8,0},{9,1},... | collective-permute-start | bytes 1572872 | tf_op jit(solution)/shard_map/ppermute | solution.py:656
  305.2 29.8 %collective-permute-start.27 = (bf16[2,512,256]{2,1,0:T(8,128)(2,1)}, bf16[2,512,256]{2,1,0:T(8,128)(2,1)}, u32[]{:S(2)}, u32[]{:S(2)}) collective-permute-start(bf16[2,512,256]{2,1,0:T(8,128)(2,1)} %down_head_near.1), channel_id=1, source_target_pairs={{0,2},{1,3},{2,0},{3,1},{4,6},{5,7},{6,4},{7,5},{8,10},{9,11},{10,... | collective-permute-start | bytes 1572872 | tf_op jit(solution)/shard_map/ppermute | solution.py:656
  309.7 13.3 %collective-permute-start.23 = (bf16[1,1,128,2048]{3,2,1,0:T(8,128)(2,1)}, bf16[1,1,128,2048]{3,2,1,0:T(8,128)(2,1)}, u32[]{:S(2)}, u32[]{:S(2)}) collective-permute-start(bf16[1,1,128,2048]{3,2,1,0:T(8,128)(2,1)} %get-tuple-element.100), channel_id=1, source_target_pairs={{0,16},{1,17},{2,18},{3,19},{4,20},{5,21},{6,22},{7,23},{8,24},{9,... | collective-permute-start | bytes 1572872 | tf_op jit(solution)/shard_map/ppermute | solution.py:656
  314.2 28.8 %collective-permute-start.28 = (bf16[2,256,512]{2,1,0:T(8,128)(2,1)}, bf16[2,256,512]{2,1,0:T(8,128)(2,1)}, u32[]{:S(2)}, u32[]{:S(2)}) collective-permute-start(bf16[2,256,512]{2,1,0:T(8,128)(2,1)} %up_head.1), channel_id=1, source_target_pairs={{0,1},{1,0},{2,3},{3,2},{4,5},{5,4},{6,7},{7,6},{8,9},{9,8},{10,11... | collective-permute-start | bytes 1572872 | tf_op jit(solution)/shard_map/ppermute | solution.py:656
  328.8 28.9 %collective-permute-start.26 = (bf16[2,2,128,512]{3,2,1,0:T(8,128)(2,1)}, bf16[2,2,128,512]{3,2,1,0:T(8,128)(2,1)}, u32[]{:S(2)}, u32[]{:S(2)}) collective-permute-start(bf16[2,2,128,512]{3,2,1,0:T(8,128)(2,1)} %tail_head.1), channel_id=1, source_target_pairs={{0,1},{1,0},{2,3},{3,2},{4,5},{5,4},{6,7},{7,6},{8,9},{9,8},{10,11... | collective-permute-start | bytes 1572872 | tf_op jit(solution)/shard_map/ppermute | solution.py:656
  337.6 25.5 %collective-permute-start.31 = (bf16[1,512,256]{2,1,0:T(8,128)(2,1)}, bf16[1,512,256]{2,1,0:T(8,128)(2,1)}, u32[]{:S(2)}, u32[]{:S(2)}) collective-permute-start(bf16[1,512,256]{2,1,0:T(8,128)(2,1)} %down_near.1), channel_id=1, source_target_pairs={{0,16},{1,17},{2,18},{3,19},{4,20},{5,21},{6,22},{7,23},{8,24},{9,... | collective-permute-start | bytes 786440 | tf_op jit(solution)/shard_map/ppermute | solution.py:656
  345.7 20.6 %collective-permute-start.32 = (bf16[1,256,512]{2,1,0:T(8,128)(2,1)}, bf16[1,256,512]{2,1,0:T(8,128)(2,1)}, u32[]{:S(2)}, u32[]{:S(2)}) collective-permute-start(bf16[1,256,512]{2,1,0:T(8,128)(2,1)} %up_head_near.1), channel_id=1, source_target_pairs={{0,2},{1,3},{2,0},{3,1},{4,6},{5,7},{6,4},{7,5},{8,10},{9,11},{10,... | collective-permute-start | bytes 786440 | tf_op jit(solution)/shard_map/ppermute | solution.py:656
  363.0 11.1 %collective-permute-start.29 = (bf16[1,2,128,512]{3,2,1,0:T(8,128)(2,1)}, bf16[1,2,128,512]{3,2,1,0:T(8,128)(2,1)S(1)}, u32[]{:S(2)}, u32[]{:S(2)}) collective-permute-start(bf16[1,2,128,512]{3,2,1,0:T(8,128)(2,1)} %tail_head_near.1), channel_id=1, source_target_pairs={{0,2},{1,3},{2,0},{3,1},{4,6},{5,7},{6,4},{7,5},{8,10},{9,11},{10,... | collective-permute-start | bytes 786440 | tf_op jit(solution)/shard_map/ppermute | solution.py:656
  (83 other events, 609.7 us)
Sparse Core Ops, SparseCore 0:
  13.4 144.9 all-gather.2
  259.2 43.5 reduce-scatter.2
  316.7 26.8 reduce-scatter.4

commit v4 on v3

--- a/solution.py
+++ b/solution.py
@@ -103,6 +103,16 @@
         return [b0.at[at], bx.at[0, at], by.at[at], bx.at[1, at]][rq]
 
     return piece
+
+
+def exit_tile(piece, rq, rz):
+    return jnp.concatenate(
+        [
+            jnp.concatenate([piece(q, rz)[0:128, 384:512], piece(q, rz)[128:256, 384:512]], axis=1)
+            for q in (rq, rq + 1)
+        ],
+        axis=0,
+    )
 
 
 def lanes_at(index, width=GROUP):
@@ -183,13 +193,10 @@
         return carry
 
     lax.fori_loop(0, 2 * PAIRS, one, 0)
+    pairs = [jnp.concatenate([att[0], att[1]], axis=1), jnp.concatenate([att[2], att[3]], axis=1)]
     for rz in range(4):
-        for half in range(2):
-            sel = slice(half * GROUP, (half + 1) * GROUP)
-            acc = dot_nn(att[0], piece(0, rz)[sel, 384:512])
-            for rq in range(1, 4):
-                acc += dot_nn(att[rq], piece(rq, rz)[sel, 384:512])
-            part[:, lanes_at(2 * (hd ^ rz) + half)] = acc
+        acc = dot_nn(pairs[0], exit_tile(piece, 0, rz)) + dot_nn(pairs[1], exit_tile(piece, 2, rz))
+        part[:, lanes_at(hd ^ rz, 256)] = acc
 
 
 def attention_backward(
@@ -199,15 +206,17 @@
     quad, hd = place[0], place[1]
     piece = pieces_of(a0, ax, ay, b0, by, bx)
     rows = cos.shape[0]
-    for b, grad in ((0, own), (1, other)):
-        for rq in range(4):
-            acc = None
-            for rz in range(4):
-                for half in range(2):
-                    w = piece(rq, rz)[half * GROUP : (half + 1) * GROUP, 384:512]
-                    term = dot_nt(grad[:, lanes_at(2 * (hd ^ rz) + half)], w)
-                    acc = term if acc is None else acc + term
-            ga[rq, b * rows : (b + 1) * rows, :] = acc.astype(BF)
+    for rq in (0, 2):
+        sums_of = [None, None]
+        for rz in range(4):
+            w = exit_tile(piece, rq, rz)
+            for b, grad in ((0, own), (1, other)):
+                term = dot_nt(grad[:, lanes_at(hd ^ rz, 256)], w)
+                sums_of[b] = term if sums_of[b] is None else sums_of[b] + term
+        for b in range(2):
+            at = slice(b * rows, (b + 1) * rows)
+            ga[rq, at, :] = sums_of[b][:, 0:GROUP].astype(BF)
+            ga[rq + 1, at, :] = sums_of[b][:, GROUP:].astype(BF)
 
     def one(it, carry):
         b, r = it // PAIRS, it % PAIRS
@@ -244,48 +253,50 @@
     sums[...] = jnp.sum(grad_qkv[...].astype(F32), axis=0, keepdims=True)
 
 
-def feed_forward(
-    place, x, part, recv, vec, wup, wdown,
-    scaled_out, inv_out, rel_out, hidden_out, slope_out, own_out, other_out, low,
-):
-    r = pl.program_id(0)
+def first_norm(place, x, part, recv, vec, scaled_out, inv_out, low, rel_out):
     rows = scaled_out.shape[0]
-
-    @pl.when(r == 0)
+    for b in range(2):
+        sel = slice(b * rows, (b + 1) * rows)
+        swapped = slice((1 - b) * rows, (2 - b) * rows)
+        h = x[sel, :].astype(F32) + part[sel, :] + recv[swapped, :] + vec[3:4, :]
+        scaled, inverse = norm_parts(h)
+        low[sel, :] = (scaled * vec[5:6, :] + vec[7:8, :]).astype(BF)
+        if b == 0:
+            scaled_out[...] = scaled
+            inv_out[...] = inverse
+    for q in range(QUADS):
+        rel_out[q, :, :] = low[:, lanes_at(place[0] ^ q, 256)]
+
+
+def feed_forward(place, low, vec, wup, wdown, hidden_out, slope_out, own_out, other_out, kept):
+    step = pl.program_id(0)
+    rows = own_out.shape[0]
+
+    @pl.when(step < QUADS)
     def _():
-        for b in range(2):
-            sel = slice(b * rows, (b + 1) * rows)
-            swapped = slice((1 - b) * rows, (2 - b) * rows)
-            h = x[sel, :].astype(F32) + part[sel, :] + recv[swapped, :] + vec[3:4, :]
-            scaled, inverse = norm_parts(h)
-            low[sel, :] = (scaled * vec[5:6, :] + vec[7:8, :]).astype(BF)
-            if b == 0:
-                scaled_out[...] = scaled
-                inv_out[...] = inverse
-        for q in range(QUADS):
-            at = pl.ds(pl.multiple_of((place[0] ^ q) * 256, 256), 256)
-            rel_out[q, :, :] = low[:, at]
-        own_out[...] = jnp.zeros_like(own_out)
-        other_out[...] = jnp.zeros_like(other_out)
-
-    for cb in range(2):
-        cols = slice(cb * 256, (cb + 1) * 256)
-        w = wup[:, 0, cb * 128 : (cb + 1) * 128, :].reshape(D, 256)
-        bias = [
-            vec[9 + 2 * cb + k : 10 + 2 * cb + k, lanes_at(2 * (place[0] ^ r) + place[1])]
-            for k in range(2)
-        ]
-        pre = dot_nn(low[...], w) + jnp.concatenate(bias, axis=1)
-        gate = 0.5 * (1.0 + lax.erf(pre * SQRT_HALF))
-        hidden_out[0, :, cols] = (pre * gate).astype(BF)
-        slope_out[0, :, cols] = (
-            gate + pre * jnp.exp(-0.5 * pre * pre) * GAUSS_SCALE
-        ).astype(BF)
-    for z in range(4):
-        cols = slice(z * 256, (z + 1) * 256)
-        acc = dot_nn(hidden_out[0], wdown[0, z])
-        own_out[:, cols] += acc[:rows]
-        other_out[:, cols] += acc[rows:]
+        for cb in range(2):
+            cols = slice(cb * 256, (cb + 1) * 256)
+            w = wup[:, 0, cb * 128 : (cb + 1) * 128, :].reshape(D, 256)
+            bias = [
+                vec[9 + 2 * cb + k : 10 + 2 * cb + k, lanes_at(2 * (place[0] ^ step) + place[1])]
+                for k in range(2)
+            ]
+            pre = dot_nn(low[...], w) + jnp.concatenate(bias, axis=1)
+            gate = 0.5 * (1.0 + lax.erf(pre * SQRT_HALF))
+            hidden = (pre * gate).astype(BF)
+            hidden_out[0, :, cols] = hidden
+            kept[step, :, cols] = hidden
+            slope_out[0, :, cols] = (
+                gate + pre * jnp.exp(-0.5 * pre * pre) * GAUSS_SCALE
+            ).astype(BF)
+
+    @pl.when(step >= QUADS)
+    def _():
+        acc = dot_nn(kept[0], wdown[place[0], 0, 0])
+        for r in range(1, QUADS):
+            acc += dot_nn(kept[r], wdown[place[0] ^ r, 0, 0])
+        own_out[...] = acc[:rows]
+        other_out[...] = acc[rows:]
 
 
 def feed_forward_back(
@@ -404,7 +415,7 @@
     sums[2:3, :] = jnp.sum(low_two[...].astype(F32), axis=0, keepdims=True)
     heads = dot_nn(gproj[...], out[...])
     for t in range(2 * QUADS):
-        grad_heads[t] = heads[:, t * GROUP : (t + 1) * GROUP]
+        grad_heads[t, 0 : heads.shape[0], :] = heads[:, t * GROUP : (t + 1) * GROUP]
 
 
 def first_norm_back(grad_two, own, recv, scaled, inverse, vec, grad_one, low_one, sums):
@@ -542,7 +553,7 @@
                 (count, n_half, GROUP, 512 * heads), lambda i, s: (i, 0, 0, 0)
             ),
         ),
-        compiler_params=params(24),
+        compiler_params=params(58),
         cost_estimate=cost(micros),
         name=name,
     )(spot, x, att, *inputs)
@@ -578,13 +589,13 @@
         grid=(1,),
         in_specs=specs,
         out_specs=[whole(a) for a in outs],
-        compiler_params=params(40),
+        compiler_params=params(24 if adds else 58),
         cost_estimate=cost(micros),
         name=name,
     )(x, grad_qkv, att, own, other, *adds)
 
 
-def pack_sums(spot, two, one, up, qkv, scalars, out):
+def pack_sums(spot, two, one, up, qkv, scalars, heads, out):
     core, hd = spot[1], spot[2]
     out[...] = jnp.zeros_like(out)
     for i in range(3 * PAIRS):
@@ -804,23 +815,37 @@
         1, 58, cost(0.1), "attention_forward",
     )
     recv = swap(part, pair_mask)
-    def up_map(r, s):
-        return (0, s[0] ^ r, s[1], 0)
-
-    def down_map(r, s):
-        return (2 * (s[0] ^ r) + s[1], 0, 1, 0)
+    scaled_one, inv_one, low_both, low_rel = call(
+        first_norm,
+        [
+            jax.ShapeDtypeStruct((rows, D), F32),
+            jax.ShapeDtypeStruct((rows, 1), F32),
+            jax.ShapeDtypeStruct((tokens, D), BF),
+            jax.ShapeDtypeStruct((QUADS, tokens, 256), BF),
+        ],
+        [place, both, part, recv, vec],
+        1, 24, cost(1), "first_norm",
+    )
 
     def const2(r, s):
         return (0, 0)
 
-    up_spec = pl.BlockSpec((8, 1, 256, 256), up_map)
-    down_spec = pl.BlockSpec((1, 4, HIDE, 256), down_map)
-    scaled_one, inv_one, low_rel, hidden, slope, out_own, out_other = pl.pallas_call(
+    def hide(r, s):
+        return s[0] ^ jnp.minimum(r, QUADS - 1)
+
+    def column(r):
+        return jnp.maximum(r - QUADS, 0)
+
+    by_core = mlp_all.reshape((QUADS, 2) + mlp_all.shape[1:])
+    up_spec = pl.BlockSpec((8, 1, 256, 256), lambda r, s: (0, s[0] ^ r, s[1], 0))
+    down_spec = pl.BlockSpec((1, 4, HIDE, 256), lambda r, s: (2 * (s[0] ^ r) + s[1], 0, 1, 0))
+    hidden_spec = pl.BlockSpec(
+        (1, tokens, HIDE), lambda r, s: (jnp.minimum(r, QUADS - 1), 0, 0)
+    )
+    column_spec = pl.BlockSpec((rows, 256), lambda r, s: (0, column(r)))
+    hidden, slope, out_own, out_other = pl.pallas_call(
         feed_forward,
         out_shape=[
-            jax.ShapeDtypeStruct((rows, D), F32),
-            jax.ShapeDtypeStruct((rows, 1), F32),
-            jax.ShapeDtypeStruct((QUADS, tokens, 256), BF),
             jax.ShapeDtypeStruct((QUADS, tokens, HIDE), BF),
             jax.ShapeDtypeStruct((QUADS, tokens, HIDE), BF),
             jax.ShapeDtypeStruct((rows, D), F32),
@@ -828,30 +853,22 @@
         ],
         grid_spec=pltpu.PrefetchScalarGridSpec(
             num_scalar_prefetch=1,
-            grid=(QUADS,),
+            grid=(2 * QUADS,),
             in_specs=[
                 pl.BlockSpec((tokens, D), const2),
-                pl.BlockSpec((tokens, D), const2),
-                pl.BlockSpec((tokens, D), const2),
                 pl.BlockSpec((16, D), const2),
-                up_spec,
-                down_spec,
+                pl.BlockSpec((8, 1, 256, 256), lambda r, s: (0, hide(r, s), s[1], 0)),
+                pl.BlockSpec(
+                    (QUADS, 1, 1, HIDE, 256), lambda r, s: (0, s[1], column(r), 1, 0)
+                ),
             ],
-            out_specs=[
-                pl.BlockSpec((rows, D), const2),
-                pl.BlockSpec((rows, 1), const2),
-                pl.BlockSpec((QUADS, tokens, 256), lambda r, s: (0, 0, 0)),
-                pl.BlockSpec((1, tokens, HIDE), lambda r, s: (r, 0, 0)),
-                pl.BlockSpec((1, tokens, HIDE), lambda r, s: (r, 0, 0)),
-                pl.BlockSpec((rows, D), const2),
-                pl.BlockSpec((rows, D), const2),
-            ],
-            scratch_shapes=[pltpu.VMEM((tokens, D), BF)],
+            out_specs=[hidden_spec, hidden_spec, column_spec, column_spec],
+            scratch_shapes=[pltpu.VMEM((QUADS, tokens, HIDE), BF)],
         ),
         compiler_params=params(58),
         cost_estimate=cost(12),
         name="feed_forward",
-    )(spot, both, part, recv, vec, mlp_all, mlp_all)
+    )(spot, low_both, vec, mlp_all, by_core)
     all_cols = n_hd * head_cols
     windows = pl.pallas_call(
         make_windows,
@@ -888,7 +905,7 @@
         [
             jax.ShapeDtypeStruct((rows, D), F32),
             jax.ShapeDtypeStruct((rows, D), BF),
-            jax.ShapeDtypeStruct((2 * QUADS, all_cols, GROUP), F32),
+            jax.ShapeDtypeStruct((2 * QUADS, all_cols + 16, GROUP), F32),
             jax.ShapeDtypeStruct((3, D), F32),
             jax.ShapeDtypeStruct((2, GROUP), F32),
         ],
@@ -980,14 +997,19 @@
         [place, low_one, low_one_other, qkv, *attn_pieces, cos, sin_a, sin_b, mask],
         1, 58, cost(0.1), "attention_backward", [pltpu.VMEM((PAIRS, tokens, GROUP), BF)],
     )
-    sums = pl.pallas_call(
+    mixed = pl.pallas_call(
         pack_sums,
-        out_shape=jax.ShapeDtypeStruct((2 * QUADS, 16, GROUP), F32),
-        in_specs=[SMEM_SPEC] + [VMEM_SPEC] * 5,
-        out_specs=VMEM_SPEC,
+        out_shape=jax.ShapeDtypeStruct(grad_heads.shape, F32),
+        grid=(1,),
+        in_specs=[SMEM_SPEC]
+        + [whole(a) for a in (sums_two, sums_one, bias_up_grad, bias_qkv_grad, scalars)]
+        + [pl.BlockSpec(memory_space=pl.ANY)],
+        out_specs=pl.BlockSpec((2 * QUADS, 16, GROUP), lambda i: (0, all_cols // 16, 0)),
+        input_output_aliases={6: 0},
+        compiler_params=params(24),
         cost_estimate=cost(0.1),
         name="pack_sums",
-    )(spot, sums_two, sums_one, bias_up_grad, bias_qkv_grad, scalars)
+    )(spot, sums_two, sums_one, bias_up_grad, bias_qkv_grad, scalars, grad_heads)
 
     def tail(after_this, halves, blocks, places, adds, name, micros, kind=BF):
         return tail_grad(
@@ -1007,49 +1029,49 @@
 
     down_z = weight_grad(
         spot, hidden, second(low_two, tail_b), (0, 2), (1, 3),
-        ((down_got, 0, 1, 0, True),), "down_head", 12,
+        ((down_got, 0, 1, 0, True),), "down_head", 6,
     )
     down_z1 = swap_head(down_z, 1)
     up_near = weight_grad(
         spot, low_rel, (after(grad_pre, down_z),), (1,), None,
-        ((up_got, 1, 0, 0, True),), "up_near", 16,
+        ((up_got, 1, 0, 0, True),), "up_near", 8,
     )
     up_last = swap(up_near, x_mask)
     down_zz = weight_grad(
         spot, hidden, second(low_two, up_near), (0, 2), (2,),
-        ((down_got, 0, 1, 0, True), (down_z1, 1, 2, 0, False)), "down_head_near", 10,
+        ((down_got, 0, 1, 0, True), (down_z1, 1, 2, 0, False)), "down_head_near", 5,
     )
     down_z2 = swap_head(down_zz, 2)
     a_near, b_near = tail_pair(
         both_rel, after(grad_qkv, down_zz), att, low_one, low_one_other,
-        (((2, 0),), ((1, 1),)), (a_got, b_got), "tail_near", 10,
+        (((2, 0),), ((1, 1),)), (a_got, b_got), "tail_near", 5,
     )
     a_last = swap(a_near, y_mask)
     b_last = swap(b_near, x_mask)
     up_adds = ((up_got, 0, 0, 0, True), (up_last, 0, 0, 0, True))
     up_z = weight_grad(
-        spot, low_rel, (after(grad_pre, b_near),), (0,), (1, 3), up_adds, "up_head", 10
+        spot, low_rel, (after(grad_pre, b_near),), (0,), (1, 3), up_adds, "up_head", 5
     )
     up_z1 = swap_head(up_z, 1)
+    down_y = weight_grad(
+        spot, hidden, second(low_two, up_z), (2,), (0,),
+        ((down_got, 1, 0, 0, True), (down_z1, 2, 0, 0, False), (down_z2, 1, 0, 0, False)),
+        "down_near", 0.1,
+    )
+    down_last = swap(down_y, y_mask)
     a_adds = ((a_got, 0, 0, True), (a_last, 0, 0, True))
     b_adds = ((b_got, 0, 0, True), (b_last, 0, 0, True))
-    tail_z = tail((up_z,), (0, 1), (0,), (1, 3), a_adds + b_adds, "tail_head", 10)
+    tail_z = tail((down_y,), (0, 1), (0,), (1, 3), a_adds + b_adds, "tail_head", 5)
     tail_z1 = swap_head(tail_z, 1)
-    down_y = weight_grad(
-        spot, hidden, second(low_two, tail_z), (2,), (0,),
-        ((down_got, 1, 0, 0, True), (down_z1, 2, 0, 0, False), (down_z2, 1, 0, 0, False)),
-        "down_near", 8,
-    )
-    down_last = swap(down_y, y_mask)
     up_zz = weight_grad(
-        spot, low_rel, (after(grad_pre, down_y),), (0,), (2,),
-        up_adds + ((up_z1, 1, 0, 0, False),), "up_head_near", 8,
+        spot, low_rel, (after(grad_pre, tail_z),), (0,), (2,),
+        up_adds + ((up_z1, 1, 0, 0, False),), "up_head_near", 4,
     )
     up_z2 = swap_head(up_zz, 2)
     tail_zz = tail(
         (up_zz,), (0, 1), (0,), (2,),
         a_adds + ((tail_z1, 1, 0, False),) + b_adds + ((tail_z1, 1, 1, False),),
-        "tail_head_near", 8,
+        "tail_head_near", 4,
     )
     tail_z2 = swap_head(tail_zz, 2)
     exact = BF if low_span > 1 else F32
@@ -1078,7 +1100,6 @@
     grad_w_out = scatter_low(
         jnp.concatenate([kept_out[:GROUP], kept_out[GROUP:]], axis=1)
     ).astype(F32)
-    mixed = jnp.concatenate([grad_heads, sums], axis=1)
     mixed = jnp.repeat(mixed, low_span, axis=0) if low_span > 1 else mixed
     mixed = lax.psum_scatter(
         mixed.reshape(n_dp * (all_cols + 16), GROUP), "dp", scatter_dimension=0, tiled=True

time: 389 us -> 376 us (0.967)
  waiting for transfers between devices: 169 us -> 155 us
  local copies, waits for them, and re-layouts: 40.6 us -> 35.9 us
  Pallas kernels: 106 us -> 110 us
    ppermute x34, waiting for transfers between devices: 154 us -> 141 us  [swap(): return lax.ppermute(a, ('dp', 'head'), pairs)]
    unnamed x167 -> x135, local copies, waits for them, and re-layouts: 27.8 us -> 22.2 us
    pallas_call x5 -> x6, Pallas kernels: 36 us -> 37.4 us  [call(): pl.pallas_call(kernel, out_shape=outs, grid=(1,), in_specs=[SMEM_SPEC] *...]
  transfers between devices with their start and end apart: 37 -> 37, of which waited for: 21 -> 23; matrix products, arithmetic and copies ran while one was open for 7% -> 7% of each run, Pallas kernels for 21% -> 22%
where the time goes in v4:
time: 376 us; the launch traced here: 374 us
  waiting for transfers between devices  155 us (41%)
  Pallas kernels  110 us (29%)
  starting transfers between devices  44.2 us (12%)
  local copies, waits for them, and re-layouts  35.9 us (10%)
  between operations  15.2 us (4%)
  other arithmetic  13.6 us (4%)
    ppermute x34, waiting for transfers between devices, swap(): return lax.ppermute(a, ('dp', 'head'), pairs)  141 us
    ppermute x34, starting transfers between devices, swap(): return lax.ppermute(a, ('dp', 'head'), pairs)  44.1 us
    pallas_call x6, Pallas kernels, call(): pl.pallas_call(kernel, out_shape=outs, grid=(1,), in_specs=[SMEM_SPEC] *...  37.4 us
    pallas_call x10, Pallas kernels, weight_grad(): pl.pallas_call(kernel, out_shape=jax.ShapeDtypeStruct((len(blocks) * coun...  27.3 us
    unnamed x135, local copies, waits for them, and re-layouts  22.2 us
    pallas_call x1, Pallas kernels, on_device(): pl.pallas_call(feed_forward, out_shape=[jax.ShapeDtypeStruct((QUADS, toke...  13.1 us
    all_gather x1, waiting for transfers between devices, on_device(): mlp_all = lax.all_gather(packed_mlp, ('dp', 'head'))  11.9 us
    pallas_call x3, Pallas kernels, tail_grad(): pl.pallas_call(kernel, out_shape=jax.ShapeDtypeStruct((len(blocks) * coun...  10.8 us
  transfers between devices with their start and end apart: 37, of which 23 were waited for; matrix products, arithmetic and copies ran while one was open for 7% of the time, Pallas kernels for 22%

profile of v4, /device:TPU:0, one launch (start us, length us, event | category | flops | bytes accessed | tf_op | source)
XLA Modules:
  0.0 374.1 jit_solution(11417997244003252607)
XLA Ops:
  15.7 4.0 %collective-permute-start.2 = (bf16[1,272,512]{2,1,0:T(8,128)(2,1)S(1)}, bf16[1,272,512]{2,1,0:T(8,128)(2,1)S(1)}, u32[]{:S(2)}, u32[]{:S(2)}) collective-permute-start(bf16[1,272,512]{2,1,0:T(8,128)(2,1)S(1)} %fusion.2), channel_id=1, source_target_pairs={{0,2},{1,3},{2,0},{3,1},{4,6},{5,7},{6,4},{7,5},{8,10},{9,11},{10,... | collective-permute-start | bytes 835592 | tf_op jit(solution)/shard_map/ppermute | solution.py:667
  21.1 21.3 %collective-permute-done.2 = bf16[1,272,512]{2,1,0:T(8,128)(2,1)S(1)} collective-permute-done((bf16[1,272,512]{2,1,0:T(8,128)(2,1)S(1)}, bf16[1,272,512]{2,1,0:T(8,128)(2,1)S(1)}, u32[]{:S(2)}, u32[]{:S(2)}) %collective-permute-start.2) | collective-permute-done | bytes 278560 | tf_op jit(solution)/shard_map/ppermute | solution.py:667
  42.5 3.0 collective-permute-start.5
  49.4 19.8 %collective-permute-done.5.b0 = bf16[2,272,512]{2,1,0:T(8,128)(2,1)S(1)} collective-permute-done((bf16[2,272,512]{2,1,0:T(8,128)(2,1)S(1)}, bf16[2,272,512]{2,1,0:T(8,128)(2,1)S(1)}, u32[]{:S(2)}, u32[]{:S(2)}) %collective-permute-start.5) | collective-permute-done | bytes 557088 | tf_op jit(solution)/shard_map/ppermute | solution.py:667
  73.2 11.5 %collective-permute-done.6.by = bf16[2,272,512]{2,1,0:T(8,128)(2,1)S(1)} collective-permute-done((bf16[2,272,512]{2,1,0:T(8,128)(2,1)S(1)}, bf16[2,272,512]{2,1,0:T(8,128)(2,1)S(1)}, u32[]{:S(2)}, u32[]{:S(2)}) %collective-permute-start.6) | collective-permute-done | bytes 557088 | tf_op jit(solution)/shard_map/ppermute | solution.py:667
  93.8 23.7 %collective-permute-done.4.ay = bf16[2,2,272,512]{3,2,1,0:T(8,128)(2,1)} collective-permute-done((bf16[2,2,272,512]{3,2,1,0:T(8,128)(2,1)}, bf16[2,2,272,512]{3,2,1,0:T(8,128)(2,1)}, u32[]{:S(2)}, u32[]{:S(2)}) %collective-permute-start.4) | collective-permute-done | bytes 1114144 | tf_op jit(solution)/shard_map/ppermute | solution.py:667
  117.5 6.9 %collective-permute-done.7.bx = bf16[2,2,272,512]{3,2,1,0:T(8,128)(2,1)} collective-permute-done((bf16[2,2,272,512]{3,2,1,0:T(8,128)(2,1)}, bf16[2,2,272,512]{3,2,1,0:T(8,128)(2,1)}, u32[]{:S(2)}, u32[]{:S(2)}) %collective-permute-start.7) | collective-permute-done | bytes 1114144 | tf_op jit(solution)/shard_map/ppermute | solution.py:667
  124.3 13.3 %attention_forward.1 = (bf16[512,1536]{1,0:T(8,128)(2,1)}, bf16[4,512,128]{2,1,0:T(8,128)(2,1)}, f32[512,1024]{1,0:T(8,128)}, f32[16,1024]{1,0:T(8,128)}) custom-call(s32[6]{0:T(128)} %pad_add_fusion.1.place, bf16[4,512,256]{2,1,0:T(8,128)(2,1)} %pad_maximum_fusion.2.x.x_ref, bf16[2,272,512]{2,1,0:T(8,128)(2,1)} %copy-done.47, ...), custom_call_target="tpu_custom_call" | custom-call | flops 115000000 | bytes 1 | tf_op jit(solution)/shard_map/attention_forward/pallas_call | solution.py:69
  138.2 3.8 %collective-permute-done.9.recv = f32[512,1024]{1,0:T(8,128)S(1)} collective-permute-done((f32[512,1024]{1,0:T(8,128)}, f32[512,1024]{1,0:T(8,128)S(1)}, u32[]{:S(2)}, u32[]{:S(2)}) %collective-permute-start.9) | collective-permute-done | bytes 2097184 | tf_op jit(solution)/shard_map/ppermute | solution.py:667
  148.0 11.9 %all-gather.3.cloned.1.call-done = bf16[34816,256]{1,0:T(8,128)(2,1)} async-done(((bf16[1088,256]{1,0:T(8,128)(2,1)}), bf16[34816,256]{1,0:T(8,128)(2,1)}) %all-gather.3.cloned.1.call-update) | async-done | bytes 17825808 | tf_op jit(solution)/shard_map/all_gather | solution.py:720
  159.9 13.1 %feed_forward.1 = (bf16[4,512,512]{2,1,0:T(8,128)(2,1)}, bf16[4,512,512]{2,1,0:T(8,128)(2,1)}, f32[256,1024]{1,0:T(8,128)}, f32[256,1024]{1,0:T(8,128)}) custom-call(s32[3]{0:T(128)} %pad_add_fusion.3.place.spot_ref.spot, bf16[512,1024]{1,0:T(8,128)(2,1)} %copy-done.44, f32[16,1024]{1,0:T(8,128)} %get-tuple-element.63.vec, ...), custom_call_target="tpu_custom_call" | custom-call | flops 13799999488 | bytes 1 | tf_op jit(solution)/shard_map/feed_forward/pallas_call | solution.py:846
  178.3 4.5 %collective-permute-start.11 = (bf16[288,256]{1,0:T(8,128)(2,1)S(1)}, bf16[288,256]{1,0:T(8,128)(2,1)S(1)}, u32[]{:S(2)}, u32[]{:S(2)}) collective-permute-start(bf16[288,256]{1,0:T(8,128)(2,1)S(1)} %get-tuple-element.69.proj_0), channel_id=1, source_target_pairs={{0,1},{1,0},{2,3},{3,2},{4,5},{5,4},{6,7},{7,6},{8,9},{9,8},{10,11... | collective-permute-start | bytes 442376 | tf_op jit(solution)/shard_map/ppermute | solution.py:667
  186.5 3.3 collective-permute-done.11.proj_1
  189.8 7.0 %collective-permute-done.12.proj_2 = bf16[288,256]{1,0:T(8,128)(2,1)S(1)} collective-permute-done((bf16[288,256]{1,0:T(8,128)(2,1)S(1)}, bf16[288,256]{1,0:T(8,128)(2,1)S(1)}, u32[]{:S(2)}, u32[]{:S(2)}) %collective-permute-start.12) | collective-permute-done | bytes 147488 | tf_op jit(solution)/shard_map/ppermute | solution.py:667
  197.9 5.1 %soft_maxsim.1 = (f32[256,1024]{1,0:T(8,128)S(1)}, bf16[256,1024]{1,0:T(8,128)(2,1)S(1)}, f32[8,304,128]{2,1,0:T(8,128)}, f32[3,1024]{1,0:T(4,128)S(1)}, f32[2,128]{1,0:T(2,128)S(1)}) custom-call(s32[6]{0:T(128)S(1)} %copy-done.39, f32[1]{0:T(128)S(6)} %copy.66.temp, f32[2,128]{1,0:T(2,128)S(1)} %pad_maximum_fusion.10.lanes, ...), custom_call_target="tpu_custom_call" | custom-call | flops 4944999936 | bytes 1 | tf_op jit(solution)/shard_map/soft_maxsim/pallas_call | solution.py:69
  204.9 3.1 down_far.1
  209.3 10.2 %feed_forward_back.1 = (bf16[512,2048]{1,0:T(8,128)(2,1)}, f32[256,1024]{1,0:T(8,128)}, f32[256,1024]{1,0:T(8,128)}, f32[1,2048]{1,0:T(1,128)}) custom-call(s32[3]{0:T(128)} %pad_add_fusion.3.place.spot_ref.spot, bf16[256,1024]{1,0:T(8,128)(2,1)} %copy-done.2, bf16[256,1024]{1,0:T(8,128)(2,1)} %copy-done.4, bf16[4,512,512]{2,1,0:T(8,128)(2,1)} %get-tuple-element.77.slope, ...), custom_call_target="tpu_custom_call" | custom-call | flops 115000000 | bytes 1 | tf_op jit(solution)/shard_map/feed_forward_back/pallas_call | solution.py:945
  221.2 3.0 up_far.1
  230.4 15.3 %attention_backward.1 = (bf16[512,1536]{1,0:T(8,128)(2,1)}, f32[256,1024]{1,0:T(8,128)}, f32[256,1024]{1,0:T(8,128)}, f32[1,1536]{1,0:T(1,128)}) custom-call(s32[6]{0:T(128)} %pad_add_fusion.1.place, bf16[256,1024]{1,0:T(8,128)(2,1)} %copy-done.11, bf16[256,1024]{1,0:T(8,128)(2,1)} %copy-done.13, bf16[512,1536]{1,0:T(8,128)(2,1)} %get-tuple-element.87.qkv, ...), custom_call_target="tpu_custom_call" | custom-call | flops 115000000 | bytes 1 | tf_op jit(solution)/shard_map/attention_backward/pallas_call | solution.py:69
  245.7 4.8 %tail_far.1 = (bf16[2,1,128,2048]{3,2,1,0:T(8,128)(2,1)}, bf16[2,1,128,2048]{3,2,1,0:T(8,128)(2,1)}) custom-call(bf16[4,512,256]{2,1,0:T(8,128)(2,1)} %pad_maximum_fusion.2.x.x_ref, bf16[512,1536]{1,0:T(8,128)(2,1)} %get-tuple-element.108.qkv_ref.refs_0_.refs_5_, bf16[4,512,128]{2,1,0:T(8,128)(2,1)} %get-tuple-element.94.att_ref, ...), custom_call_target="tpu_custom_call" | custom-call | flops 115000000 | bytes 1 | tf_op jit(solution)/shard_map/tail_far/pallas_call | solution.py:586
  253.2 3.6 collective-permute-done.19.refs_4_.refs_5_.refs_2_
  262.6 10.4 %collective-permute-done.20.refs_1_.refs_2_.refs_4_ = bf16[2,256,2048]{2,1,0:T(8,128)(2,1)} collective-permute-done((bf16[2,256,2048]{2,1,0:T(8,128)(2,1)}, bf16[2,256,2048]{2,1,0:T(8,128)(2,1)}, u32[]{:S(2)}, u32[]{:S(2)}) %collective-permute-start.20) | collective-permute-done | bytes 2097184 | tf_op jit(solution)/shard_map/ppermute | solution.py:667
  279.0 5.4 %collective-permute-done.21.refs_3_ = bf16[4,512,256]{2,1,0:T(8,128)(2,1)S(1)} collective-permute-done((bf16[4,512,256]{2,1,0:T(8,128)(2,1)S(1)}, bf16[4,512,256]{2,1,0:T(8,128)(2,1)S(1)}, u32[]{:S(2)}, u32[]{:S(2)}) %collective-permute-start.21) | collective-permute-done | bytes 1048608 | tf_op jit(solution)/shard_map/ppermute | solution.py:667
  287.4 3.2 collective-permute-start.25
  290.6 9.5 %collective-permute-done.22.refs_1_.refs_12_.refs_16_.refs_8_.refs_9_ = bf16[2,1,128,2048]{3,2,1,0:T(8,128)(2,1)} collective-permute-done((bf16[2,1,128,2048]{3,2,1,0:T(8,128)(2,1)}, bf16[2,1,128,2048]{3,2,1,0:T(8,128)(2,1)}, u32[]{:S(2)}, u32[]{:S(2)}) %collective-permute-start.22) | collective-permute-done | bytes 1048608 | tf_op jit(solution)/shard_map/ppermute | solution.py:667
  306.1 3.0 up_head.1
  317.7 4.0 %tail_head.1 = bf16[2,2,128,512]{3,2,1,0:T(8,128)(2,1)} custom-call(s32[3]{0:T(128)} %pad_add_fusion.3.place.spot_ref.spot, bf16[4,512,256]{2,1,0:T(8,128)(2,1)} %pad_maximum_fusion.2.x.x_ref, bf16[4,512,128]{2,1,0:T(8,128)(2,1)} %get-tuple-element.94.att_ref, bf16[512,1536]{1,0:T(8,128)(2,1)} %get-tuple-element.108.qkv_ref.refs_0_.refs_5_, ...), custom_call_target="tpu_custom_call" | custom-call | flops 5750000128 | bytes 1 | tf_op jit(solution)/shard_map/tail_head/pallas_call | solution.py:545
  338.9 4.8 %collective-permute-done.27.refs_7_.refs_10_.refs_11_ = bf16[2,2,128,512]{3,2,1,0:T(8,128)(2,1)} collective-permute-done((bf16[2,2,128,512]{3,2,1,0:T(8,128)(2,1)}, bf16[2,2,128,512]{3,2,1,0:T(8,128)(2,1)}, u32[]{:S(2)}, u32[]{:S(2)}) %collective-permute-start.27) | collective-permute-done | bytes 524320 | tf_op jit(solution)/shard_map/ppermute | solution.py:667
  343.7 3.3 tail_head_near.1
  347.1 3.1 down_own.1
  356.2 3.6 collective-permute-done.29.refs_8_.refs_12_
  359.9 3.4 tail_own.1
  (281 shorter events, 112.6 us)
Async XLA Ops:
  7.2 152.7 %all-gather.3.cloned.1.call-start = ((), (), s32[]{:S(2)}) async-start(), calls=%async_computation.4 | async-start | bytes 18382848 | tf_op jit(solution)/shard_map/all_gather | solution.py:720
  13.3 298.6 %reduce-scatter.3.cloned.1.call-start = ((), (), s32[]{:S(2)}) async-start(), calls=%async_computation.2 | async-start | bytes 1400832 | tf_op jit(solution)/shard_map/reduce_scatter | solution.py:1104
  15.7 26.7 %collective-permute-start.2 = (bf16[1,272,512]{2,1,0:T(8,128)(2,1)S(1)}, bf16[1,272,512]{2,1,0:T(8,128)(2,1)S(1)}, u32[]{:S(2)}, u32[]{:S(2)}) collective-permute-start(bf16[1,272,512]{2,1,0:T(8,128)(2,1)S(1)} %fusion.2), channel_id=1, source_target_pairs={{0,2},{1,3},{2,0},{3,1},{4,6},{5,7},{6,4},{7,5},{8,10},{9,11},{10,... | collective-permute-start | bytes 835592 | tf_op jit(solution)/shard_map/ppermute | solution.py:667
  19.7 71.6 %collective-permute-start = (bf16[256,1024]{1,0:T(8,128)(2,1)}, bf16[256,1024]{1,0:T(8,128)(2,1)}, u32[]{:S(2)}, u32[]{:S(2)}) collective-permute-start(bf16[256,1024]{1,0:T(8,128)(2,1)} %param.14), channel_id=1, source_target_pairs={{0,4},{1,5},{2,6},{3,7},{4,0},{5,1},{6,2},{7,3},{8,12},{9,13},{10,... | collective-permute-start | bytes 1572872 | tf_op jit(solution)/shard_map/ppermute | solution.py:667
  19.8 69.2 %collective-permute-start.8 = (s32[11]{0:T(128)S(1)}, s32[11]{0:T(128)S(1)}, u32[]{:S(2)}, u32[]{:S(2)}) collective-permute-start(s32[11]{0:T(128)S(1)} %pad_add_fusion.2), channel_id=1, source_target_pairs={{0,4},{1,5},{2,6},{3,7},{4,0},{5,1},{6,2},{7,3},{8,12},{9,13},{10,... | collective-permute-start | bytes 140 | tf_op jit(solution)/shard_map/ppermute | solution.py:667
  42.5 26.6 %collective-permute-start.5 = (bf16[2,272,512]{2,1,0:T(8,128)(2,1)S(1)}, bf16[2,272,512]{2,1,0:T(8,128)(2,1)S(1)}, u32[]{:S(2)}, u32[]{:S(2)}) collective-permute-start(bf16[2,272,512]{2,1,0:T(8,128)(2,1)S(1)} %get-tuple-element.142.a0), channel_id=1, source_target_pairs={{0,1},{1,0},{2,3},{3,2},{4,5},{5,4},{6,7},{7,6},{8,9},{9,8},{10,11... | collective-permute-start | bytes 1671176 | tf_op jit(solution)/shard_map/ppermute | solution.py:667
  47.0 24.4 %collective-permute-start.3 = (bf16[2,272,512]{2,1,0:T(8,128)(2,1)S(1)}, bf16[2,272,512]{2,1,0:T(8,128)(2,1)S(1)}, u32[]{:S(2)}, u32[]{:S(2)}) collective-permute-start(bf16[2,272,512]{2,1,0:T(8,128)(2,1)S(1)} %get-tuple-element.142.a0), channel_id=1, source_target_pairs={{0,8},{1,9},{2,10},{3,11},{4,12},{5,13},{6,14},{7,15},{8,0},{9,1},... | collective-permute-start | bytes 1671176 | tf_op jit(solution)/shard_map/ppermute | solution.py:667
  69.1 15.6 %collective-permute-start.6 = (bf16[2,272,512]{2,1,0:T(8,128)(2,1)S(1)}, bf16[2,272,512]{2,1,0:T(8,128)(2,1)S(1)}, u32[]{:S(2)}, u32[]{:S(2)}) collective-permute-start(bf16[2,272,512]{2,1,0:T(8,128)(2,1)S(1)} %collective-permute-done.5.b0), channel_id=1, source_target_pairs={{0,16},{1,17},{2,18},{3,19},{4,20},{5,21},{6,22},{7,23},{8,24},{9,... | collective-permute-start | bytes 1671176 | tf_op jit(solution)/shard_map/ppermute | solution.py:667
  72.7 44.8 %collective-permute-start.4 = (bf16[2,2,272,512]{3,2,1,0:T(8,128)(2,1)}, bf16[2,2,272,512]{3,2,1,0:T(8,128)(2,1)}, u32[]{:S(2)}, u32[]{:S(2)}) collective-permute-start(bf16[2,2,272,512]{3,2,1,0:T(8,128)(2,1)} %pad_maximum_fusion), channel_id=1, source_target_pairs={{0,16},{1,17},{2,18},{3,19},{4,20},{5,21},{6,22},{7,23},{8,24},{9,... | collective-permute-start | bytes 3342344 | tf_op jit(solution)/shard_map/ppermute | solution.py:667
  85.9 38.5 %collective-permute-start.7 = (bf16[2,2,272,512]{3,2,1,0:T(8,128)(2,1)}, bf16[2,2,272,512]{3,2,1,0:T(8,128)(2,1)}, u32[]{:S(2)}, u32[]{:S(2)}) collective-permute-start(bf16[2,2,272,512]{3,2,1,0:T(8,128)(2,1)} %pad_maximum_fusion.1), channel_id=1, source_target_pairs={{0,8},{1,9},{2,10},{3,11},{4,12},{5,13},{6,14},{7,15},{8,0},{9,1},... | collective-permute-start | bytes 3342344 | tf_op jit(solution)/shard_map/ppermute | solution.py:667
  137.6 4.4 %collective-permute-start.9 = (f32[512,1024]{1,0:T(8,128)}, f32[512,1024]{1,0:T(8,128)S(1)}, u32[]{:S(2)}, u32[]{:S(2)}) collective-permute-start(f32[512,1024]{1,0:T(8,128)} %get-tuple-element.62.part), channel_id=1, source_target_pairs={{0,4},{1,5},{2,6},{3,7},{4,0},{5,1},{6,2},{7,3},{8,12},{9,13},{10,... | collective-permute-start | bytes 6291464 | tf_op jit(solution)/shard_map/ppermute | solution.py:667
  173.0 2.9 collective-permute-start.10
  178.3 11.4 %collective-permute-start.11 = (bf16[288,256]{1,0:T(8,128)(2,1)S(1)}, bf16[288,256]{1,0:T(8,128)(2,1)S(1)}, u32[]{:S(2)}, u32[]{:S(2)}) collective-permute-start(bf16[288,256]{1,0:T(8,128)(2,1)S(1)} %get-tuple-element.69.proj_0), channel_id=1, source_target_pairs={{0,1},{1,0},{2,3},{3,2},{4,5},{5,4},{6,7},{7,6},{8,9},{9,8},{10,11... | collective-permute-start | bytes 442376 | tf_op jit(solution)/shard_map/ppermute | solution.py:667
  182.9 13.9 %collective-permute-start.12 = (bf16[288,256]{1,0:T(8,128)(2,1)S(1)}, bf16[288,256]{1,0:T(8,128)(2,1)S(1)}, u32[]{:S(2)}, u32[]{:S(2)}) collective-permute-start(bf16[288,256]{1,0:T(8,128)(2,1)S(1)} %get-tuple-element.69.proj_0), channel_id=1, source_target_pairs={{0,2},{1,3},{2,0},{3,1},{4,6},{5,7},{6,4},{7,5},{8,10},{9,11},{10,... | collective-permute-start | bytes 442376 | tf_op jit(solution)/shard_map/ppermute | solution.py:667
  184.3 12.5 %collective-permute-start.13 = (bf16[288,256]{1,0:T(8,128)(2,1)S(1)}, bf16[288,256]{1,0:T(8,128)(2,1)S(1)}, u32[]{:S(2)}, u32[]{:S(2)}) collective-permute-start(bf16[288,256]{1,0:T(8,128)(2,1)S(1)} %get-tuple-element.69.proj_0), channel_id=1, source_target_pairs={{0,3},{1,2},{2,1},{3,0},{4,7},{5,6},{6,5},{7,4},{8,11},{9,10},{10,... | collective-permute-start | bytes 442376 | tf_op jit(solution)/shard_map/ppermute | solution.py:667
  208.0 48.8 %collective-permute-start.19 = (bf16[2,512,1024]{2,1,0:T(8,128)(2,1)}, bf16[2,512,1024]{2,1,0:T(8,128)(2,1)}, u32[]{:S(2)}, u32[]{:S(2)}) collective-permute-start(bf16[2,512,1024]{2,1,0:T(8,128)(2,1)} %down_far.1), channel_id=1, source_target_pairs={{0,8},{1,9},{2,10},{3,11},{4,12},{5,13},{6,14},{7,15},{8,0},{9,1},... | collective-permute-start | bytes 6291464 | tf_op jit(solution)/shard_map/ppermute | solution.py:667
  219.5 6.4 %collective-permute-start.15 = (f32[256,1024]{1,0:T(8,128)}, f32[256,1024]{1,0:T(8,128)S(1)}, u32[]{:S(2)}, u32[]{:S(2)}) collective-permute-start(f32[256,1024]{1,0:T(8,128)} %get-tuple-element.82), channel_id=1, source_target_pairs={{0,4},{1,5},{2,6},{3,7},{4,0},{5,1},{6,2},{7,3},{8,12},{9,13},{10,... | collective-permute-start | bytes 3145736 | tf_op jit(solution)/shard_map/ppermute | solution.py:667
  224.2 48.7 %collective-permute-start.20 = (bf16[2,256,2048]{2,1,0:T(8,128)(2,1)}, bf16[2,256,2048]{2,1,0:T(8,128)(2,1)}, u32[]{:S(2)}, u32[]{:S(2)}) collective-permute-start(bf16[2,256,2048]{2,1,0:T(8,128)(2,1)} %up_far.1), channel_id=1, source_target_pairs={{0,16},{1,17},{2,18},{3,19},{4,20},{5,21},{6,22},{7,23},{8,24},{9,... | collective-permute-start | bytes 6291464 | tf_op jit(solution)/shard_map/ppermute | solution.py:667
  250.5 49.5 %collective-permute-start.22 = (bf16[2,1,128,2048]{3,2,1,0:T(8,128)(2,1)}, bf16[2,1,128,2048]{3,2,1,0:T(8,128)(2,1)}, u32[]{:S(2)}, u32[]{:S(2)}) collective-permute-start(bf16[2,1,128,2048]{3,2,1,0:T(8,128)(2,1)} %get-tuple-element.97), channel_id=1, source_target_pairs={{0,16},{1,17},{2,18},{3,19},{4,20},{5,21},{6,22},{7,23},{8,24},{9,... | collective-permute-start | bytes 3145736 | tf_op jit(solution)/shard_map/ppermute | solution.py:667
  250.9 39.7 %collective-permute-start.18 = (bf16[2,1,128,2048]{3,2,1,0:T(8,128)(2,1)}, bf16[2,1,128,2048]{3,2,1,0:T(8,128)(2,1)}, u32[]{:S(2)}, u32[]{:S(2)}) collective-permute-start(bf16[2,1,128,2048]{3,2,1,0:T(8,128)(2,1)} %get-tuple-element.96), channel_id=1, source_target_pairs={{0,8},{1,9},{2,10},{3,11},{4,12},{5,13},{6,14},{7,15},{8,0},{9,1},... | collective-permute-start | bytes 3145736 | tf_op jit(solution)/shard_map/ppermute | solution.py:667
  251.8 24.7 %collective-permute-start.17 = (f32[256,1024]{1,0:T(8,128)}, f32[256,1024]{1,0:T(8,128)}, u32[]{:S(2)}, u32[]{:S(2)}) collective-permute-start(f32[256,1024]{1,0:T(8,128)} %get-tuple-element.93), channel_id=1, source_target_pairs={{0,4},{1,5},{2,6},{3,7},{4,0},{5,1},{6,2},{7,3},{8,12},{9,13},{10,... | collective-permute-start | bytes 3145736 | tf_op jit(solution)/shard_map/ppermute | solution.py:667
  253.1 82.4 %reduce-scatter.5.cloned.1.call-start = ((), (), s32[]{:S(2)}) async-start(), calls=%async_computation.3 | async-start | bytes 245760 | tf_op jit(solution)/shard_map/reduce_scatter | solution.py:1111
  259.8 24.7 %collective-permute-start.21 = (bf16[4,512,256]{2,1,0:T(8,128)(2,1)S(1)}, bf16[4,512,256]{2,1,0:T(8,128)(2,1)S(1)}, u32[]{:S(2)}, u32[]{:S(2)}) collective-permute-start(bf16[4,512,256]{2,1,0:T(8,128)(2,1)S(1)} %down_head.1), channel_id=1, source_target_pairs={{0,1},{1,0},{2,3},{3,2},{4,5},{5,4},{6,7},{7,6},{8,9},{9,8},{10,11... | collective-permute-start | bytes 3145736 | tf_op jit(solution)/shard_map/ppermute | solution.py:667
  275.5 30.6 %collective-permute-start.24 = (bf16[1,256,2048]{2,1,0:T(8,128)(2,1)S(1)}, bf16[1,256,2048]{2,1,0:T(8,128)(2,1)S(1)}, u32[]{:S(2)}, u32[]{:S(2)}) collective-permute-start(bf16[1,256,2048]{2,1,0:T(8,128)(2,1)S(1)} %up_near.1), channel_id=1, source_target_pairs={{0,8},{1,9},{2,10},{3,11},{4,12},{5,13},{6,14},{7,15},{8,0},{9,1},... | collective-permute-start | bytes 3145736 | tf_op jit(solution)/shard_map/ppermute | solution.py:667
  287.4 26.8 %collective-permute-start.25 = (bf16[2,512,256]{2,1,0:T(8,128)(2,1)}, bf16[2,512,256]{2,1,0:T(8,128)(2,1)}, u32[]{:S(2)}, u32[]{:S(2)}) collective-permute-start(bf16[2,512,256]{2,1,0:T(8,128)(2,1)} %down_head_near.1), channel_id=1, source_target_pairs={{0,2},{1,3},{2,0},{3,1},{4,6},{5,7},{6,4},{7,5},{8,10},{9,11},{10,... | collective-permute-start | bytes 1572872 | tf_op jit(solution)/shard_map/ppermute | solution.py:667
  303.0 14.7 %collective-permute-start.26 = (bf16[1,1,128,2048]{3,2,1,0:T(8,128)(2,1)}, bf16[1,1,128,2048]{3,2,1,0:T(8,128)(2,1)}, u32[]{:S(2)}, u32[]{:S(2)}) collective-permute-start(bf16[1,1,128,2048]{3,2,1,0:T(8,128)(2,1)} %get-tuple-element.103), channel_id=1, source_target_pairs={{0,8},{1,9},{2,10},{3,11},{4,12},{5,13},{6,14},{7,15},{8,0},{9,1},... | collective-permute-start | bytes 1572872 | tf_op jit(solution)/shard_map/ppermute | solution.py:667
  304.0 13.7 %collective-permute-start.23 = (bf16[1,1,128,2048]{3,2,1,0:T(8,128)(2,1)}, bf16[1,1,128,2048]{3,2,1,0:T(8,128)(2,1)}, u32[]{:S(2)}, u32[]{:S(2)}) collective-permute-start(bf16[1,1,128,2048]{3,2,1,0:T(8,128)(2,1)} %get-tuple-element.102), channel_id=1, source_target_pairs={{0,16},{1,17},{2,18},{3,19},{4,20},{5,21},{6,22},{7,23},{8,24},{9,... | collective-permute-start | bytes 1572872 | tf_op jit(solution)/shard_map/ppermute | solution.py:667
  309.1 16.9 %collective-permute-start.28 = (bf16[2,256,512]{2,1,0:T(8,128)(2,1)}, bf16[2,256,512]{2,1,0:T(8,128)(2,1)}, u32[]{:S(2)}, u32[]{:S(2)}) collective-permute-start(bf16[2,256,512]{2,1,0:T(8,128)(2,1)} %up_head.1), channel_id=1, source_target_pairs={{0,1},{1,0},{2,3},{3,2},{4,5},{5,4},{6,7},{7,6},{8,9},{9,8},{10,11... | collective-permute-start | bytes 1572872 | tf_op jit(solution)/shard_map/ppermute | solution.py:667
  321.7 21.9 %collective-permute-start.27 = (bf16[2,2,128,512]{3,2,1,0:T(8,128)(2,1)}, bf16[2,2,128,512]{3,2,1,0:T(8,128)(2,1)}, u32[]{:S(2)}, u32[]{:S(2)}) collective-permute-start(bf16[2,2,128,512]{3,2,1,0:T(8,128)(2,1)} %tail_head.1), channel_id=1, source_target_pairs={{0,1},{1,0},{2,3},{3,2},{4,5},{5,4},{6,7},{7,6},{8,9},{9,8},{10,11... | collective-permute-start | bytes 1572872 | tf_op jit(solution)/shard_map/ppermute | solution.py:667
  324.4 22.7 %collective-permute-start.31 = (bf16[1,512,256]{2,1,0:T(8,128)(2,1)S(1)}, bf16[1,512,256]{2,1,0:T(8,128)(2,1)}, u32[]{:S(2)}, u32[]{:S(2)}) collective-permute-start(bf16[1,512,256]{2,1,0:T(8,128)(2,1)S(1)} %down_near.1), channel_id=1, source_target_pairs={{0,16},{1,17},{2,18},{3,19},{4,20},{5,21},{6,22},{7,23},{8,24},{9,... | collective-permute-start | bytes 786440 | tf_op jit(solution)/shard_map/ppermute | solution.py:667
  331.2 19.1 %collective-permute-start.32 = (bf16[1,256,512]{2,1,0:T(8,128)(2,1)}, bf16[1,256,512]{2,1,0:T(8,128)(2,1)}, u32[]{:S(2)}, u32[]{:S(2)}) collective-permute-start(bf16[1,256,512]{2,1,0:T(8,128)(2,1)} %up_head_near.1), channel_id=1, source_target_pairs={{0,2},{1,3},{2,0},{3,1},{4,6},{5,7},{6,4},{7,5},{8,10},{9,11},{10,... | collective-permute-start | bytes 786440 | tf_op jit(solution)/shard_map/ppermute | solution.py:667
  347.0 12.8 %collective-permute-start.29 = (bf16[1,2,128,512]{3,2,1,0:T(8,128)(2,1)}, bf16[1,2,128,512]{3,2,1,0:T(8,128)(2,1)}, u32[]{:S(2)}, u32[]{:S(2)}) collective-permute-start(bf16[1,2,128,512]{3,2,1,0:T(8,128)(2,1)} %tail_head_near.1), channel_id=1, source_target_pairs={{0,2},{1,3},{2,0},{3,1},{4,6},{5,7},{6,4},{7,5},{8,10},{9,11},{10,... | collective-permute-start | bytes 786440 | tf_op jit(solution)/shard_map/ppermute | solution.py:667
  (67 other events, 532.8 us)
Sparse Core Ops, SparseCore 0:
  13.4 146.4 all-gather.2
  253.2 43.9 reduce-scatter.2
  314.3 21.1 reduce-scatter.4

commit v5 on v4

--- a/solution.py
+++ b/solution.py
@@ -618,6 +618,18 @@
             out[t, 13 + k : 14 + k, :] = jnp.broadcast_to(totals[k], (1, GROUP))
 
 
+def pack_matrices(up, down, heads, out):
+    rows = up.shape[0]
+    groups = up.shape[1] // 256
+    for i in range(groups):
+        out[i * rows : (i + 1) * rows, :] = up[:, i * 256 : (i + 1) * 256]
+    at = groups * rows
+    out[at : at + down.shape[0], :] = down[...]
+    at += down.shape[0]
+    out[at : at + 64, 0:GROUP] = heads[0:64, :]
+    out[at : at + 64, GROUP:] = heads[64:, :]
+
+
 def make_windows(tiles, windows, wide):
     cols = windows.shape[0] // 4
     for dp in range(2 * QUADS):
@@ -700,13 +712,12 @@
     heads_low = gather_low(nested_projector)
     head_cols = heads_low.shape[1]
     heads_low = jnp.pad(heads_low.T, ((0, GROUP - head_cols), (0, 0)))
-    packed_mlp = jnp.concatenate(
-        [wup_low[:, i * 256 : (i + 1) * 256] for i in range(col_blocks)]
-        + [
-            gather_low(contract_matrix),
-            jnp.concatenate([heads_low[:64], heads_low[64:]], axis=1),
-        ],
-        axis=0,
+    wdown_low = gather_low(contract_matrix)
+    (packed_mlp,) = call(
+        pack_matrices,
+        [jax.ShapeDtypeStruct((wup_low.shape[0] * col_blocks + wdown_low.shape[0] + 64, 256), BF)],
+        [wup_low, wdown_low, heads_low],
+        0, 16, cost(0.1), "pack_matrices",
     )
     if low_span > 1:
         dp_groups = [

time: 376 us -> 374 us (level)
    unnamed x135 -> x132, local copies, waits for them, and re-layouts: 22.2 us -> 19 us
    pallas_call x6 -> x7, Pallas kernels: 37.4 us -> 38.3 us  [call(): pl.pallas_call(kernel, out_shape=outs, grid=(1,), in_specs=[SMEM_SPEC] *...]
  transfers between devices with their start and end apart: 37 -> 37, of which waited for: 23 -> 22; matrix products, arithmetic and copies ran while one was open for 7% -> 7% of each run, Pallas kernels for 22% -> 23%
where the time goes in v5:
time: 374 us; the launch traced here: 373 us
  waiting for transfers between devices  155 us (41%)
  Pallas kernels  111 us (30%)
  starting transfers between devices  45.6 us (12%)
  local copies, waits for them, and re-layouts  32.6 us (9%)
  between operations  15.2 us (4%)
  other arithmetic  13.6 us (4%)
    ppermute x34, waiting for transfers between devices, swap(): return lax.ppermute(a, ('dp', 'head'), pairs)  142 us
    ppermute x34, starting transfers between devices, swap(): return lax.ppermute(a, ('dp', 'head'), pairs)  45.5 us
    pallas_call x7, Pallas kernels, call(): pl.pallas_call(kernel, out_shape=outs, grid=(1,), in_specs=[SMEM_SPEC] *...  38.3 us
    pallas_call x10, Pallas kernels, weight_grad(): pl.pallas_call(kernel, out_shape=jax.ShapeDtypeStruct((len(blocks) * coun...  27.3 us
    unnamed x132, local copies, waits for them, and re-layouts  19 us
    pallas_call x1, Pallas kernels, on_device(): pl.pallas_call(feed_forward, out_shape=[jax.ShapeDtypeStruct((QUADS, toke...  13.1 us
    all_gather x1, waiting for transfers between devices, on_device(): mlp_all = lax.all_gather(packed_mlp, ('dp', 'head'))  11.8 us
    pallas_call x3, Pallas kernels, tail_grad(): pl.pallas_call(kernel, out_shape=jax.ShapeDtypeStruct((len(blocks) * coun...  10.8 us
  transfers between devices with their start and end apart: 37, of which 22 were waited for; matrix products, arithmetic and copies ran while one was open for 7% of the time, Pallas kernels for 23%

profile of v5, /device:TPU:0, one launch (start us, length us, event | category | flops | bytes accessed | tf_op | source)
XLA Modules:
  0.0 372.8 jit_solution(8545418656673783497)
XLA Ops:
  13.3 4.0 %collective-permute-start.2 = (bf16[1,272,512]{2,1,0:T(8,128)(2,1)S(1)}, bf16[1,272,512]{2,1,0:T(8,128)(2,1)S(1)}, u32[]{:S(2)}, u32[]{:S(2)}) collective-permute-start(bf16[1,272,512]{2,1,0:T(8,128)(2,1)S(1)} %fusion.2), channel_id=1, source_target_pairs={{0,2},{1,3},{2,0},{3,1},{4,6},{5,7},{6,4},{7,5},{8,10},{9,11},{10,... | collective-permute-start | bytes 835592 | tf_op jit(solution)/shard_map/ppermute | solution.py:679
  18.6 21.3 %collective-permute-done.2 = bf16[1,272,512]{2,1,0:T(8,128)(2,1)S(1)} collective-permute-done((bf16[1,272,512]{2,1,0:T(8,128)(2,1)S(1)}, bf16[1,272,512]{2,1,0:T(8,128)(2,1)S(1)}, u32[]{:S(2)}, u32[]{:S(2)}) %collective-permute-start.2) | collective-permute-done | bytes 278560 | tf_op jit(solution)/shard_map/ppermute | solution.py:679
  40.0 3.0 collective-permute-start.5
  46.9 19.9 %collective-permute-done.5.b0 = bf16[2,272,512]{2,1,0:T(8,128)(2,1)S(1)} collective-permute-done((bf16[2,272,512]{2,1,0:T(8,128)(2,1)S(1)}, bf16[2,272,512]{2,1,0:T(8,128)(2,1)S(1)}, u32[]{:S(2)}, u32[]{:S(2)}) %collective-permute-start.5) | collective-permute-done | bytes 557088 | tf_op jit(solution)/shard_map/ppermute | solution.py:679
  70.8 11.5 %collective-permute-done.6.by = bf16[2,272,512]{2,1,0:T(8,128)(2,1)S(1)} collective-permute-done((bf16[2,272,512]{2,1,0:T(8,128)(2,1)S(1)}, bf16[2,272,512]{2,1,0:T(8,128)(2,1)S(1)}, u32[]{:S(2)}, u32[]{:S(2)}) %collective-permute-start.6) | collective-permute-done | bytes 557088 | tf_op jit(solution)/shard_map/ppermute | solution.py:679
  91.3 23.7 %collective-permute-done.4.ay = bf16[2,2,272,512]{3,2,1,0:T(8,128)(2,1)} collective-permute-done((bf16[2,2,272,512]{3,2,1,0:T(8,128)(2,1)}, bf16[2,2,272,512]{3,2,1,0:T(8,128)(2,1)}, u32[]{:S(2)}, u32[]{:S(2)}) %collective-permute-start.4) | collective-permute-done | bytes 1114144 | tf_op jit(solution)/shard_map/ppermute | solution.py:679
  115.0 6.9 %collective-permute-done.7.bx = bf16[2,2,272,512]{3,2,1,0:T(8,128)(2,1)} collective-permute-done((bf16[2,2,272,512]{3,2,1,0:T(8,128)(2,1)}, bf16[2,2,272,512]{3,2,1,0:T(8,128)(2,1)}, u32[]{:S(2)}, u32[]{:S(2)}) %collective-permute-start.7) | collective-permute-done | bytes 1114144 | tf_op jit(solution)/shard_map/ppermute | solution.py:679
  121.8 13.3 %attention_forward.1 = (bf16[512,1536]{1,0:T(8,128)(2,1)}, bf16[4,512,128]{2,1,0:T(8,128)(2,1)}, f32[512,1024]{1,0:T(8,128)}, f32[16,1024]{1,0:T(8,128)}) custom-call(s32[6]{0:T(128)} %pad_add_fusion.1.place, bf16[4,512,256]{2,1,0:T(8,128)(2,1)} %pad_maximum_fusion.2.x.x_ref, bf16[2,272,512]{2,1,0:T(8,128)(2,1)} %copy-done.49, ...), custom_call_target="tpu_custom_call" | custom-call | flops 115000000 | bytes 1 | tf_op jit(solution)/shard_map/attention_forward/pallas_call | solution.py:69
  135.7 3.8 %collective-permute-done.9.recv = f32[512,1024]{1,0:T(8,128)S(1)} collective-permute-done((f32[512,1024]{1,0:T(8,128)}, f32[512,1024]{1,0:T(8,128)S(1)}, u32[]{:S(2)}, u32[]{:S(2)}) %collective-permute-start.9) | collective-permute-done | bytes 2097184 | tf_op jit(solution)/shard_map/ppermute | solution.py:679
  145.5 11.8 %all-gather.3.cloned.1.call-done = bf16[34816,256]{1,0:T(8,128)(2,1)} async-done(((bf16[1088,256]{1,0:T(8,128)(2,1)}), bf16[34816,256]{1,0:T(8,128)(2,1)}) %all-gather.3.cloned.1.call-update) | async-done | bytes 17825808 | tf_op jit(solution)/shard_map/all_gather | solution.py:731
  157.2 13.1 %feed_forward.1 = (bf16[4,512,512]{2,1,0:T(8,128)(2,1)}, bf16[4,512,512]{2,1,0:T(8,128)(2,1)}, f32[256,1024]{1,0:T(8,128)}, f32[256,1024]{1,0:T(8,128)}) custom-call(s32[3]{0:T(128)} %pad_add_fusion.3.place.spot_ref.spot, bf16[512,1024]{1,0:T(8,128)(2,1)} %copy-done.46, f32[16,1024]{1,0:T(8,128)} %get-tuple-element.63.vec, ...), custom_call_target="tpu_custom_call" | custom-call | flops 13799999488 | bytes 1 | tf_op jit(solution)/shard_map/feed_forward/pallas_call | solution.py:857
  175.7 5.2 %collective-permute-start.11 = (bf16[288,256]{1,0:T(8,128)(2,1)S(1)}, bf16[288,256]{1,0:T(8,128)(2,1)S(1)}, u32[]{:S(2)}, u32[]{:S(2)}) collective-permute-start(bf16[288,256]{1,0:T(8,128)(2,1)S(1)} %get-tuple-element.69.proj_0), channel_id=1, source_target_pairs={{0,1},{1,0},{2,3},{3,2},{4,5},{5,4},{6,7},{7,6},{8,9},{9,8},{10,11... | collective-permute-start | bytes 442376 | tf_op jit(solution)/shard_map/ppermute | solution.py:679
  184.5 3.3 collective-permute-done.11.proj_1
  187.8 7.1 %collective-permute-done.12.proj_2 = bf16[288,256]{1,0:T(8,128)(2,1)S(1)} collective-permute-done((bf16[288,256]{1,0:T(8,128)(2,1)S(1)}, bf16[288,256]{1,0:T(8,128)(2,1)S(1)}, u32[]{:S(2)}, u32[]{:S(2)}) %collective-permute-start.12) | collective-permute-done | bytes 147488 | tf_op jit(solution)/shard_map/ppermute | solution.py:679
  195.9 5.1 %soft_maxsim.1 = (f32[256,1024]{1,0:T(8,128)S(1)}, bf16[256,1024]{1,0:T(8,128)(2,1)S(1)}, f32[8,304,128]{2,1,0:T(8,128)}, f32[3,1024]{1,0:T(4,128)S(1)}, f32[2,128]{1,0:T(2,128)S(1)}) custom-call(s32[6]{0:T(128)S(1)} %copy-done.41, f32[1]{0:T(128)S(6)} %copy.61.temp, f32[2,128]{1,0:T(2,128)S(1)} %pad_maximum_fusion.10.lanes, ...), custom_call_target="tpu_custom_call" | custom-call | flops 4944999936 | bytes 1 | tf_op jit(solution)/shard_map/soft_maxsim/pallas_call | solution.py:69
  202.9 3.1 down_far.1
  206.8 10.2 %feed_forward_back.1 = (bf16[512,2048]{1,0:T(8,128)(2,1)}, f32[256,1024]{1,0:T(8,128)}, f32[256,1024]{1,0:T(8,128)}, f32[1,2048]{1,0:T(1,128)}) custom-call(s32[3]{0:T(128)} %pad_add_fusion.3.place.spot_ref.spot, bf16[256,1024]{1,0:T(8,128)(2,1)} %copy-done.2, bf16[256,1024]{1,0:T(8,128)(2,1)} %copy-done.4, bf16[4,512,512]{2,1,0:T(8,128)(2,1)} %get-tuple-element.77.slope, ...), custom_call_target="tpu_custom_call" | custom-call | flops 115000000 | bytes 1 | tf_op jit(solution)/shard_map/feed_forward_back/pallas_call | solution.py:956
  218.7 3.0 up_far.1
  227.8 15.3 %attention_backward.1 = (bf16[512,1536]{1,0:T(8,128)(2,1)}, f32[256,1024]{1,0:T(8,128)}, f32[256,1024]{1,0:T(8,128)}, f32[1,1536]{1,0:T(1,128)}) custom-call(s32[6]{0:T(128)} %pad_add_fusion.1.place, bf16[256,1024]{1,0:T(8,128)(2,1)} %copy-done.11, bf16[256,1024]{1,0:T(8,128)(2,1)} %copy-done.13, bf16[512,1536]{1,0:T(8,128)(2,1)} %get-tuple-element.87.qkv, ...), custom_call_target="tpu_custom_call" | custom-call | flops 115000000 | bytes 1 | tf_op jit(solution)/shard_map/attention_backward/pallas_call | solution.py:69
  243.2 4.8 %tail_far.1 = (bf16[2,1,128,2048]{3,2,1,0:T(8,128)(2,1)}, bf16[2,1,128,2048]{3,2,1,0:T(8,128)(2,1)}) custom-call(bf16[4,512,256]{2,1,0:T(8,128)(2,1)} %pad_maximum_fusion.2.x.x_ref, bf16[512,1536]{1,0:T(8,128)(2,1)} %get-tuple-element.108.qkv_ref.refs_0_.refs_5_, bf16[4,512,128]{2,1,0:T(8,128)(2,1)} %get-tuple-element.94.att_ref, ...), custom_call_target="tpu_custom_call" | custom-call | flops 115000000 | bytes 1 | tf_op jit(solution)/shard_map/tail_far/pallas_call | solution.py:586
  251.1 3.7 collective-permute-done.19.refs_4_.refs_5_.refs_2_
  260.6 9.9 %collective-permute-done.20.refs_1_.refs_2_.refs_4_ = bf16[2,256,2048]{2,1,0:T(8,128)(2,1)} collective-permute-done((bf16[2,256,2048]{2,1,0:T(8,128)(2,1)}, bf16[2,256,2048]{2,1,0:T(8,128)(2,1)}, u32[]{:S(2)}, u32[]{:S(2)}) %collective-permute-start.20) | collective-permute-done | bytes 2097184 | tf_op jit(solution)/shard_map/ppermute | solution.py:679
  276.9 5.5 %collective-permute-done.21.refs_3_ = bf16[4,512,256]{2,1,0:T(8,128)(2,1)S(1)} collective-permute-done((bf16[4,512,256]{2,1,0:T(8,128)(2,1)S(1)}, bf16[4,512,256]{2,1,0:T(8,128)(2,1)S(1)}, u32[]{:S(2)}, u32[]{:S(2)}) %collective-permute-start.21) | collective-permute-done | bytes 1048608 | tf_op jit(solution)/shard_map/ppermute | solution.py:679
  285.4 3.2 collective-permute-start.25
  288.5 9.0 %collective-permute-done.22.refs_1_.refs_12_.refs_16_.refs_8_.refs_9_ = bf16[2,1,128,2048]{3,2,1,0:T(8,128)(2,1)} collective-permute-done((bf16[2,1,128,2048]{3,2,1,0:T(8,128)(2,1)}, bf16[2,1,128,2048]{3,2,1,0:T(8,128)(2,1)}, u32[]{:S(2)}, u32[]{:S(2)}) %collective-permute-start.22) | collective-permute-done | bytes 1048608 | tf_op jit(solution)/shard_map/ppermute | solution.py:679
  316.0 4.1 %tail_head.1 = bf16[2,2,128,512]{3,2,1,0:T(8,128)(2,1)} custom-call(s32[3]{0:T(128)} %pad_add_fusion.3.place.spot_ref.spot, bf16[4,512,256]{2,1,0:T(8,128)(2,1)} %pad_maximum_fusion.2.x.x_ref, bf16[4,512,128]{2,1,0:T(8,128)(2,1)} %get-tuple-element.94.att_ref, bf16[512,1536]{1,0:T(8,128)(2,1)} %get-tuple-element.108.qkv_ref.refs_0_.refs_5_, ...), custom_call_target="tpu_custom_call" | custom-call | flops 5750000128 | bytes 1 | tf_op jit(solution)/shard_map/tail_head/pallas_call | solution.py:545
  328.7 3.2 collective-permute-start.32
  336.5 5.3 %collective-permute-done.27.refs_7_.refs_10_.refs_11_ = bf16[2,2,128,512]{3,2,1,0:T(8,128)(2,1)} collective-permute-done((bf16[2,2,128,512]{3,2,1,0:T(8,128)(2,1)}, bf16[2,2,128,512]{3,2,1,0:T(8,128)(2,1)}, u32[]{:S(2)}, u32[]{:S(2)}) %collective-permute-start.27) | collective-permute-done | bytes 524320 | tf_op jit(solution)/shard_map/ppermute | solution.py:679
  341.8 3.3 tail_head_near.1
  345.2 3.1 down_own.1
  354.4 4.2 %collective-permute-done.29.refs_8_.refs_12_ = bf16[1,2,128,512]{3,2,1,0:T(8,128)(2,1)} collective-permute-done((bf16[1,2,128,512]{3,2,1,0:T(8,128)(2,1)}, bf16[1,2,128,512]{3,2,1,0:T(8,128)(2,1)}, u32[]{:S(2)}, u32[]{:S(2)}) %collective-permute-start.29) | collective-permute-done | bytes 262176 | tf_op jit(solution)/shard_map/ppermute | solution.py:679
  358.6 3.4 tail_own.1
  (278 shorter events, 110.1 us)
Async XLA Ops:
  7.2 150.0 %all-gather.3.cloned.1.call-start = ((), (), s32[]{:S(2)}) async-start(), calls=%async_computation.4 | async-start | bytes 18382848 | tf_op jit(solution)/shard_map/all_gather | solution.py:731
  10.8 299.6 %reduce-scatter.3.cloned.1.call-start = ((), (), s32[]{:S(2)}) async-start(), calls=%async_computation.2 | async-start | bytes 1400832 | tf_op jit(solution)/shard_map/reduce_scatter | solution.py:1115
  13.3 26.7 %collective-permute-start.2 = (bf16[1,272,512]{2,1,0:T(8,128)(2,1)S(1)}, bf16[1,272,512]{2,1,0:T(8,128)(2,1)S(1)}, u32[]{:S(2)}, u32[]{:S(2)}) collective-permute-start(bf16[1,272,512]{2,1,0:T(8,128)(2,1)S(1)} %fusion.2), channel_id=1, source_target_pairs={{0,2},{1,3},{2,0},{3,1},{4,6},{5,7},{6,4},{7,5},{8,10},{9,11},{10,... | collective-permute-start | bytes 835592 | tf_op jit(solution)/shard_map/ppermute | solution.py:679
  17.3 71.6 %collective-permute-start = (bf16[256,1024]{1,0:T(8,128)(2,1)}, bf16[256,1024]{1,0:T(8,128)(2,1)}, u32[]{:S(2)}, u32[]{:S(2)}) collective-permute-start(bf16[256,1024]{1,0:T(8,128)(2,1)} %param.14), channel_id=1, source_target_pairs={{0,4},{1,5},{2,6},{3,7},{4,0},{5,1},{6,2},{7,3},{8,12},{9,13},{10,... | collective-permute-start | bytes 1572872 | tf_op jit(solution)/shard_map/ppermute | solution.py:679
  17.4 69.2 %collective-permute-start.8 = (s32[11]{0:T(128)S(1)}, s32[11]{0:T(128)S(1)}, u32[]{:S(2)}, u32[]{:S(2)}) collective-permute-start(s32[11]{0:T(128)S(1)} %pad_add_fusion.2), channel_id=1, source_target_pairs={{0,4},{1,5},{2,6},{3,7},{4,0},{5,1},{6,2},{7,3},{8,12},{9,13},{10,... | collective-permute-start | bytes 140 | tf_op jit(solution)/shard_map/ppermute | solution.py:679
  40.0 26.7 %collective-permute-start.5 = (bf16[2,272,512]{2,1,0:T(8,128)(2,1)S(1)}, bf16[2,272,512]{2,1,0:T(8,128)(2,1)S(1)}, u32[]{:S(2)}, u32[]{:S(2)}) collective-permute-start(bf16[2,272,512]{2,1,0:T(8,128)(2,1)S(1)} %get-tuple-element.142.a0), channel_id=1, source_target_pairs={{0,1},{1,0},{2,3},{3,2},{4,5},{5,4},{6,7},{7,6},{8,9},{9,8},{10,11... | collective-permute-start | bytes 1671176 | tf_op jit(solution)/shard_map/ppermute | solution.py:679
  44.6 24.4 %collective-permute-start.3 = (bf16[2,272,512]{2,1,0:T(8,128)(2,1)S(1)}, bf16[2,272,512]{2,1,0:T(8,128)(2,1)S(1)}, u32[]{:S(2)}, u32[]{:S(2)}) collective-permute-start(bf16[2,272,512]{2,1,0:T(8,128)(2,1)S(1)} %get-tuple-element.142.a0), channel_id=1, source_target_pairs={{0,8},{1,9},{2,10},{3,11},{4,12},{5,13},{6,14},{7,15},{8,0},{9,1},... | collective-permute-start | bytes 1671176 | tf_op jit(solution)/shard_map/ppermute | solution.py:679
  66.7 15.6 %collective-permute-start.6 = (bf16[2,272,512]{2,1,0:T(8,128)(2,1)S(1)}, bf16[2,272,512]{2,1,0:T(8,128)(2,1)S(1)}, u32[]{:S(2)}, u32[]{:S(2)}) collective-permute-start(bf16[2,272,512]{2,1,0:T(8,128)(2,1)S(1)} %collective-permute-done.5.b0), channel_id=1, source_target_pairs={{0,16},{1,17},{2,18},{3,19},{4,20},{5,21},{6,22},{7,23},{8,24},{9,... | collective-permute-start | bytes 1671176 | tf_op jit(solution)/shard_map/ppermute | solution.py:679
  70.2 44.8 %collective-permute-start.4 = (bf16[2,2,272,512]{3,2,1,0:T(8,128)(2,1)}, bf16[2,2,272,512]{3,2,1,0:T(8,128)(2,1)}, u32[]{:S(2)}, u32[]{:S(2)}) collective-permute-start(bf16[2,2,272,512]{3,2,1,0:T(8,128)(2,1)} %pad_maximum_fusion), channel_id=1, source_target_pairs={{0,16},{1,17},{2,18},{3,19},{4,20},{5,21},{6,22},{7,23},{8,24},{9,... | collective-permute-start | bytes 3342344 | tf_op jit(solution)/shard_map/ppermute | solution.py:679
  83.5 38.4 %collective-permute-start.7 = (bf16[2,2,272,512]{3,2,1,0:T(8,128)(2,1)}, bf16[2,2,272,512]{3,2,1,0:T(8,128)(2,1)}, u32[]{:S(2)}, u32[]{:S(2)}) collective-permute-start(bf16[2,2,272,512]{3,2,1,0:T(8,128)(2,1)} %pad_maximum_fusion.1), channel_id=1, source_target_pairs={{0,8},{1,9},{2,10},{3,11},{4,12},{5,13},{6,14},{7,15},{8,0},{9,1},... | collective-permute-start | bytes 3342344 | tf_op jit(solution)/shard_map/ppermute | solution.py:679
  135.1 4.4 %collective-permute-start.9 = (f32[512,1024]{1,0:T(8,128)}, f32[512,1024]{1,0:T(8,128)S(1)}, u32[]{:S(2)}, u32[]{:S(2)}) collective-permute-start(f32[512,1024]{1,0:T(8,128)} %get-tuple-element.62.part), channel_id=1, source_target_pairs={{0,4},{1,5},{2,6},{3,7},{4,0},{5,1},{6,2},{7,3},{8,12},{9,13},{10,... | collective-permute-start | bytes 6291464 | tf_op jit(solution)/shard_map/ppermute | solution.py:679
  170.3 2.9 collective-permute-start.10
  175.7 12.1 %collective-permute-start.11 = (bf16[288,256]{1,0:T(8,128)(2,1)S(1)}, bf16[288,256]{1,0:T(8,128)(2,1)S(1)}, u32[]{:S(2)}, u32[]{:S(2)}) collective-permute-start(bf16[288,256]{1,0:T(8,128)(2,1)S(1)} %get-tuple-element.69.proj_0), channel_id=1, source_target_pairs={{0,1},{1,0},{2,3},{3,2},{4,5},{5,4},{6,7},{7,6},{8,9},{9,8},{10,11... | collective-permute-start | bytes 442376 | tf_op jit(solution)/shard_map/ppermute | solution.py:679
  180.9 13.9 %collective-permute-start.12 = (bf16[288,256]{1,0:T(8,128)(2,1)S(1)}, bf16[288,256]{1,0:T(8,128)(2,1)S(1)}, u32[]{:S(2)}, u32[]{:S(2)}) collective-permute-start(bf16[288,256]{1,0:T(8,128)(2,1)S(1)} %get-tuple-element.69.proj_0), channel_id=1, source_target_pairs={{0,2},{1,3},{2,0},{3,1},{4,6},{5,7},{6,4},{7,5},{8,10},{9,11},{10,... | collective-permute-start | bytes 442376 | tf_op jit(solution)/shard_map/ppermute | solution.py:679
  182.3 12.5 %collective-permute-start.13 = (bf16[288,256]{1,0:T(8,128)(2,1)S(1)}, bf16[288,256]{1,0:T(8,128)(2,1)S(1)}, u32[]{:S(2)}, u32[]{:S(2)}) collective-permute-start(bf16[288,256]{1,0:T(8,128)(2,1)S(1)} %get-tuple-element.69.proj_0), channel_id=1, source_target_pairs={{0,3},{1,2},{2,1},{3,0},{4,7},{5,6},{6,5},{7,4},{8,11},{9,10},{10,... | collective-permute-start | bytes 442376 | tf_op jit(solution)/shard_map/ppermute | solution.py:679
  206.0 48.8 %collective-permute-start.19 = (bf16[2,512,1024]{2,1,0:T(8,128)(2,1)}, bf16[2,512,1024]{2,1,0:T(8,128)(2,1)}, u32[]{:S(2)}, u32[]{:S(2)}) collective-permute-start(bf16[2,512,1024]{2,1,0:T(8,128)(2,1)} %down_far.1), channel_id=1, source_target_pairs={{0,8},{1,9},{2,10},{3,11},{4,12},{5,13},{6,14},{7,15},{8,0},{9,1},... | collective-permute-start | bytes 6291464 | tf_op jit(solution)/shard_map/ppermute | solution.py:679
  217.0 6.4 %collective-permute-start.15 = (f32[256,1024]{1,0:T(8,128)}, f32[256,1024]{1,0:T(8,128)S(1)}, u32[]{:S(2)}, u32[]{:S(2)}) collective-permute-start(f32[256,1024]{1,0:T(8,128)} %get-tuple-element.82), channel_id=1, source_target_pairs={{0,4},{1,5},{2,6},{3,7},{4,0},{5,1},{6,2},{7,3},{8,12},{9,13},{10,... | collective-permute-start | bytes 3145736 | tf_op jit(solution)/shard_map/ppermute | solution.py:679
  221.8 48.7 %collective-permute-start.20 = (bf16[2,256,2048]{2,1,0:T(8,128)(2,1)}, bf16[2,256,2048]{2,1,0:T(8,128)(2,1)}, u32[]{:S(2)}, u32[]{:S(2)}) collective-permute-start(bf16[2,256,2048]{2,1,0:T(8,128)(2,1)} %up_far.1), channel_id=1, source_target_pairs={{0,16},{1,17},{2,18},{3,19},{4,20},{5,21},{6,22},{7,23},{8,24},{9,... | collective-permute-start | bytes 6291464 | tf_op jit(solution)/shard_map/ppermute | solution.py:679
  248.0 49.6 %collective-permute-start.22 = (bf16[2,1,128,2048]{3,2,1,0:T(8,128)(2,1)}, bf16[2,1,128,2048]{3,2,1,0:T(8,128)(2,1)}, u32[]{:S(2)}, u32[]{:S(2)}) collective-permute-start(bf16[2,1,128,2048]{3,2,1,0:T(8,128)(2,1)} %get-tuple-element.97), channel_id=1, source_target_pairs={{0,16},{1,17},{2,18},{3,19},{4,20},{5,21},{6,22},{7,23},{8,24},{9,... | collective-permute-start | bytes 3145736 | tf_op jit(solution)/shard_map/ppermute | solution.py:679
  248.4 40.1 %collective-permute-start.18 = (bf16[2,1,128,2048]{3,2,1,0:T(8,128)(2,1)}, bf16[2,1,128,2048]{3,2,1,0:T(8,128)(2,1)}, u32[]{:S(2)}, u32[]{:S(2)}) collective-permute-start(bf16[2,1,128,2048]{3,2,1,0:T(8,128)(2,1)} %get-tuple-element.96), channel_id=1, source_target_pairs={{0,8},{1,9},{2,10},{3,11},{4,12},{5,13},{6,14},{7,15},{8,0},{9,1},... | collective-permute-start | bytes 3145736 | tf_op jit(solution)/shard_map/ppermute | solution.py:679
  249.7 24.6 %collective-permute-start.17 = (f32[256,1024]{1,0:T(8,128)}, f32[256,1024]{1,0:T(8,128)}, u32[]{:S(2)}, u32[]{:S(2)}) collective-permute-start(f32[256,1024]{1,0:T(8,128)} %get-tuple-element.93), channel_id=1, source_target_pairs={{0,4},{1,5},{2,6},{3,7},{4,0},{5,1},{6,2},{7,3},{8,12},{9,13},{10,... | collective-permute-start | bytes 3145736 | tf_op jit(solution)/shard_map/ppermute | solution.py:679
  251.0 82.1 %reduce-scatter.5.cloned.1.call-start = ((), (), s32[]{:S(2)}) async-start(), calls=%async_computation.3 | async-start | bytes 245760 | tf_op jit(solution)/shard_map/reduce_scatter | solution.py:1122
  257.8 24.6 %collective-permute-start.21 = (bf16[4,512,256]{2,1,0:T(8,128)(2,1)S(1)}, bf16[4,512,256]{2,1,0:T(8,128)(2,1)S(1)}, u32[]{:S(2)}, u32[]{:S(2)}) collective-permute-start(bf16[4,512,256]{2,1,0:T(8,128)(2,1)S(1)} %down_head.1), channel_id=1, source_target_pairs={{0,1},{1,0},{2,3},{3,2},{4,5},{5,4},{6,7},{7,6},{8,9},{9,8},{10,11... | collective-permute-start | bytes 3145736 | tf_op jit(solution)/shard_map/ppermute | solution.py:679
  273.0 31.6 %collective-permute-start.24 = (bf16[1,256,2048]{2,1,0:T(8,128)(2,1)S(1)}, bf16[1,256,2048]{2,1,0:T(8,128)(2,1)S(1)}, u32[]{:S(2)}, u32[]{:S(2)}) collective-permute-start(bf16[1,256,2048]{2,1,0:T(8,128)(2,1)S(1)} %up_near.1), channel_id=1, source_target_pairs={{0,8},{1,9},{2,10},{3,11},{4,12},{5,13},{6,14},{7,15},{8,0},{9,1},... | collective-permute-start | bytes 3145736 | tf_op jit(solution)/shard_map/ppermute | solution.py:679
  285.4 27.4 %collective-permute-start.25 = (bf16[2,512,256]{2,1,0:T(8,128)(2,1)}, bf16[2,512,256]{2,1,0:T(8,128)(2,1)}, u32[]{:S(2)}, u32[]{:S(2)}) collective-permute-start(bf16[2,512,256]{2,1,0:T(8,128)(2,1)} %down_head_near.1), channel_id=1, source_target_pairs={{0,2},{1,3},{2,0},{3,1},{4,6},{5,7},{6,4},{7,5},{8,10},{9,11},{10,... | collective-permute-start | bytes 1572872 | tf_op jit(solution)/shard_map/ppermute | solution.py:679
  300.5 15.4 %collective-permute-start.26 = (bf16[1,1,128,2048]{3,2,1,0:T(8,128)(2,1)}, bf16[1,1,128,2048]{3,2,1,0:T(8,128)(2,1)}, u32[]{:S(2)}, u32[]{:S(2)}) collective-permute-start(bf16[1,1,128,2048]{3,2,1,0:T(8,128)(2,1)} %get-tuple-element.103), channel_id=1, source_target_pairs={{0,8},{1,9},{2,10},{3,11},{4,12},{5,13},{6,14},{7,15},{8,0},{9,1},... | collective-permute-start | bytes 1572872 | tf_op jit(solution)/shard_map/ppermute | solution.py:679
  301.8 14.2 %collective-permute-start.23 = (bf16[1,1,128,2048]{3,2,1,0:T(8,128)(2,1)}, bf16[1,1,128,2048]{3,2,1,0:T(8,128)(2,1)}, u32[]{:S(2)}, u32[]{:S(2)}) collective-permute-start(bf16[1,1,128,2048]{3,2,1,0:T(8,128)(2,1)} %get-tuple-element.102), channel_id=1, source_target_pairs={{0,16},{1,17},{2,18},{3,19},{4,20},{5,21},{6,22},{7,23},{8,24},{9,... | collective-permute-start | bytes 1572872 | tf_op jit(solution)/shard_map/ppermute | solution.py:679
  307.6 15.9 %collective-permute-start.28 = (bf16[2,256,512]{2,1,0:T(8,128)(2,1)}, bf16[2,256,512]{2,1,0:T(8,128)(2,1)}, u32[]{:S(2)}, u32[]{:S(2)}) collective-permute-start(bf16[2,256,512]{2,1,0:T(8,128)(2,1)} %up_head.1), channel_id=1, source_target_pairs={{0,1},{1,0},{2,3},{3,2},{4,5},{5,4},{6,7},{7,6},{8,9},{9,8},{10,11... | collective-permute-start | bytes 1572872 | tf_op jit(solution)/shard_map/ppermute | solution.py:679
  320.0 21.8 %collective-permute-start.27 = (bf16[2,2,128,512]{3,2,1,0:T(8,128)(2,1)}, bf16[2,2,128,512]{3,2,1,0:T(8,128)(2,1)}, u32[]{:S(2)}, u32[]{:S(2)}) collective-permute-start(bf16[2,2,128,512]{3,2,1,0:T(8,128)(2,1)} %tail_head.1), channel_id=1, source_target_pairs={{0,1},{1,0},{2,3},{3,2},{4,5},{5,4},{6,7},{7,6},{8,9},{9,8},{10,11... | collective-permute-start | bytes 1572872 | tf_op jit(solution)/shard_map/ppermute | solution.py:679
  322.0 23.2 %collective-permute-start.31 = (bf16[1,512,256]{2,1,0:T(8,128)(2,1)S(1)}, bf16[1,512,256]{2,1,0:T(8,128)(2,1)}, u32[]{:S(2)}, u32[]{:S(2)}) collective-permute-start(bf16[1,512,256]{2,1,0:T(8,128)(2,1)S(1)} %down_near.1), channel_id=1, source_target_pairs={{0,16},{1,17},{2,18},{3,19},{4,20},{5,21},{6,22},{7,23},{8,24},{9,... | collective-permute-start | bytes 786440 | tf_op jit(solution)/shard_map/ppermute | solution.py:679
  328.7 19.7 %collective-permute-start.32 = (bf16[1,256,512]{2,1,0:T(8,128)(2,1)}, bf16[1,256,512]{2,1,0:T(8,128)(2,1)}, u32[]{:S(2)}, u32[]{:S(2)}) collective-permute-start(bf16[1,256,512]{2,1,0:T(8,128)(2,1)} %up_head_near.1), channel_id=1, source_target_pairs={{0,2},{1,3},{2,0},{3,1},{4,6},{5,7},{6,4},{7,5},{8,10},{9,11},{10,... | collective-permute-start | bytes 786440 | tf_op jit(solution)/shard_map/ppermute | solution.py:679
  345.1 13.4 %collective-permute-start.29 = (bf16[1,2,128,512]{3,2,1,0:T(8,128)(2,1)}, bf16[1,2,128,512]{3,2,1,0:T(8,128)(2,1)}, u32[]{:S(2)}, u32[]{:S(2)}) collective-permute-start(bf16[1,2,128,512]{3,2,1,0:T(8,128)(2,1)} %tail_head_near.1), channel_id=1, source_target_pairs={{0,2},{1,3},{2,0},{3,1},{4,6},{5,7},{6,4},{7,5},{8,10},{9,11},{10,... | collective-permute-start | bytes 786440 | tf_op jit(solution)/shard_map/ppermute | solution.py:679
  (68 other events, 509.7 us)
Sparse Core Ops, SparseCore 0:
  10.9 146.2 all-gather.2
  251.1 43.5 reduce-scatter.2
  312.9 20.1 reduce-scatter.4

commit v6 on v5

--- a/solution.py
+++ b/solution.py
@@ -480,7 +480,7 @@
     )(spot, lhs, *(list(rhs) * count), *([add[0] for add in adds] * count))
 
 
-def tail_grad(spot, x, grad_qkv, att, own, other, halves, blocks, places, adds, name, micros, kind=BF):
+def tail_grad(spot, x, grad_qkv, att, own, other, halves, blocks, places, adds, name, micros, finish=False):
     tokens = x.shape[1]
     whole_cols = places is None
     places = (None,) if whole_cols else places
@@ -498,6 +498,7 @@
 
     def kernel(spot_ref, x_ref, att_ref, *refs):
         out = refs[-1]
+        lefts = []
         at_add = count * (1 + 2 * lane_blocks)
         for c in range(count):
             qkv_ref, *pair = refs[c * (1 + 2 * lane_blocks) : (c + 1) * (1 + 2 * lane_blocks)]
@@ -516,8 +517,16 @@
                     for add in refs[first : first + per]:
                         left += add[0, 0, :, lo : lo + 384].astype(F32)
                         right += add[0, 0, :, lo + 384 : lo + 512].astype(F32)
-                    out[c, k, :, lo : lo + 384] = left.astype(kind)
-                    out[c, k, :, lo + 384 : lo + 512] = right.astype(kind)
+                    if finish:
+                        lefts.append(left)
+                        out[:, half * GROUP : (half + 1) * GROUP] = right
+                        continue
+                    out[c, k, :, lo : lo + 384] = left.astype(BF)
+                    out[c, k, :, lo + 384 : lo + 512] = right.astype(BF)
+        if finish:
+            mine = spot_ref[1] == 0
+            refs[-3][...] = jnp.where(mine, lefts[1], lefts[0]).astype(BF)
+            refs[-2][...] = jnp.where(mine, lefts[0], lefts[1])
 
     specs = [
         pl.BlockSpec((1, tokens, 256), lambda i, s: (blocks[0] + step * i, 0, 0)),
@@ -542,16 +551,23 @@
                 index = lambda i, s, at=at, k=k: (at, k, 0, 0)
             specs.append(pl.BlockSpec((1, 1, GROUP, 512 * heads), index))
             inputs.append(a)
+    out_shape = jax.ShapeDtypeStruct((len(blocks) * count, n_half, GROUP, 512 * heads), BF)
+    out_spec = pl.BlockSpec((count, n_half, GROUP, 512 * heads), lambda i, s: (i, 0, 0, 0))
+    if finish:
+        out_shape = [
+            jax.ShapeDtypeStruct((GROUP, 384), BF),
+            jax.ShapeDtypeStruct((GROUP, 384), F32),
+            jax.ShapeDtypeStruct((GROUP, 2 * GROUP), F32),
+        ]
+        out_spec = [pl.BlockSpec(a.shape, lambda i, s: (0, 0)) for a in out_shape]
     return pl.pallas_call(
         kernel,
-        out_shape=jax.ShapeDtypeStruct((len(blocks) * count, n_half, GROUP, 512 * heads), kind),
+        out_shape=out_shape,
         grid_spec=pltpu.PrefetchScalarGridSpec(
             num_scalar_prefetch=1,
             grid=(len(blocks),),
             in_specs=specs,
-            out_specs=pl.BlockSpec(
-                (count, n_half, GROUP, 512 * heads), lambda i, s: (i, 0, 0, 0)
-            ),
+            out_specs=out_spec,
         ),
         compiler_params=params(58),
         cost_estimate=cost(micros),
@@ -938,7 +954,10 @@
         count = a.shape[0] // 2
         give = lax.dynamic_slice_in_dim(a, (1 - core) * count, count, 0)
         keep = lax.dynamic_slice_in_dim(a, core * count, count, 0)
-        other = swap(give, pair_mask)
+        return joined_columns(keep, swap(give, pair_mask), group)
+
+    def joined_columns(keep, other, group):
+        count = keep.shape[0]
         keep = keep.reshape(count, -1, 1, group)
         other = other.reshape(count, -1, 1, group)
         whole = jnp.where(
@@ -1022,10 +1041,10 @@
         name="pack_sums",
     )(spot, sums_two, sums_one, bias_up_grad, bias_qkv_grad, scalars, grad_heads)
 
-    def tail(after_this, halves, blocks, places, adds, name, micros, kind=BF):
+    def tail(after_this, halves, blocks, places, adds, name, micros, finish=False):
         return tail_grad(
             spot, both_rel, after(grad_qkv, *after_this), att, low_one, low_one_other,
-            halves, blocks, places, adds, name, micros, kind,
+            halves, blocks, places, adds, name, micros, finish,
         )
 
     def second(value, *others):
@@ -1098,19 +1117,16 @@
         spot, low_rel, (after(grad_pre, grad_w_down),), (0,), (0,),
         up_adds + ((up_z1, 0, 0, 0, False), (up_z2, 0, 0, 0, False)), "up_own", 4,
     )[0]
-    kept = tail(
+    give, keep, grad_w_out = tail(
         (up_own,), (0, 1), (0,), (0,),
         a_adds + ((tail_z1, 0, 0, False), (tail_z2, 0, 0, False))
         + b_adds + ((tail_z1, 0, 1, False), (tail_z2, 0, 1, False)),
-        "tail_own", 4,
-    ).reshape(256, 512)
+        "tail_own", 4, True,
+    )
     grad_w_down = scatter_low(grad_w_down).astype(F32)
     grad_w_up = finish_split(up_own, HIDE)
-    grad_w_qkv = finish_split(kept[:, :qkv_cols], GROUP)
-    kept_out = kept[:, qkv_cols:]
-    grad_w_out = scatter_low(
-        jnp.concatenate([kept_out[:GROUP], kept_out[GROUP:]], axis=1)
-    ).astype(F32)
+    grad_w_qkv = joined_columns(keep, swap(give, pair_mask), GROUP)
+    grad_w_out = scatter_low(grad_w_out).astype(F32)
     mixed = jnp.repeat(mixed, low_span, axis=0) if low_span > 1 else mixed
     mixed = lax.psum_scatter(
         mixed.reshape(n_dp * (all_cols + 16), GROUP), "dp", scatter_dimension=0, tiled=True

time: 374 us -> 374 us (level)
    unnamed x132 -> x134, local copies, waits for them, and re-layouts: 19 us -> 19.5 us
  transfers between devices with their start and end apart: 37 -> 37, of which waited for: 22 -> 22; matrix products, arithmetic and copies ran while one was open for 7% -> 7% of each run, Pallas kernels for 23% -> 24%
where the time goes in v6:
time: 374 us; the launch traced here: 372 us
  waiting for transfers between devices  156 us (42%)
  Pallas kernels  111 us (30%)
  starting transfers between devices  45.6 us (12%)
  local copies, waits for them, and re-layouts  31.5 us (8%)
  between operations  15.2 us (4%)
  other arithmetic  13 us (3%)
    ppermute x34, waiting for transfers between devices, swap(): return lax.ppermute(a, ('dp', 'head'), pairs)  143 us
    ppermute x34, starting transfers between devices, swap(): return lax.ppermute(a, ('dp', 'head'), pairs)  45.5 us
    pallas_call x7, Pallas kernels, call(): pl.pallas_call(kernel, out_shape=outs, grid=(1,), in_specs=[SMEM_SPEC] *...  38.3 us
    pallas_call x10, Pallas kernels, weight_grad(): pl.pallas_call(kernel, out_shape=jax.ShapeDtypeStruct((len(blocks) * coun...  27.3 us
    unnamed x134, local copies, waits for them, and re-layouts  19.5 us
    pallas_call x1, Pallas kernels, on_device(): pl.pallas_call(feed_forward, out_shape=[jax.ShapeDtypeStruct((QUADS, toke...  13.1 us
    all_gather x1, waiting for transfers between devices, on_device(): mlp_all = lax.all_gather(packed_mlp, ('dp', 'head'))  11.7 us
    pallas_call x3, Pallas kernels, tail_grad(): pl.pallas_call(kernel, out_shape=out_shape, grid_spec=pltpu.PrefetchScala...  10.9 us
  transfers between devices with their start and end apart: 37, of which 22 were waited for; matrix products, arithmetic and copies ran while one was open for 7% of the time, Pallas kernels for 24%

profile of v6, /device:TPU:0, one launch (start us, length us, event | category | flops | bytes accessed | tf_op | source)
XLA Modules:
  0.0 371.9 jit_solution(12790338082992999264)
XLA Ops:
  13.3 4.0 %collective-permute-start.2 = (bf16[1,272,512]{2,1,0:T(8,128)(2,1)S(1)}, bf16[1,272,512]{2,1,0:T(8,128)(2,1)S(1)}, u32[]{:S(2)}, u32[]{:S(2)}) collective-permute-start(bf16[1,272,512]{2,1,0:T(8,128)(2,1)S(1)} %fusion.2), channel_id=1, source_target_pairs={{0,2},{1,3},{2,0},{3,1},{4,6},{5,7},{6,4},{7,5},{8,10},{9,11},{10,... | collective-permute-start | bytes 835592 | tf_op jit(solution)/shard_map/ppermute | solution.py:695
  18.6 21.3 %collective-permute-done.2 = bf16[1,272,512]{2,1,0:T(8,128)(2,1)S(1)} collective-permute-done((bf16[1,272,512]{2,1,0:T(8,128)(2,1)S(1)}, bf16[1,272,512]{2,1,0:T(8,128)(2,1)S(1)}, u32[]{:S(2)}, u32[]{:S(2)}) %collective-permute-start.2) | collective-permute-done | bytes 278560 | tf_op jit(solution)/shard_map/ppermute | solution.py:695
  40.0 3.0 collective-permute-start.5
  46.9 19.9 %collective-permute-done.5.b0 = bf16[2,272,512]{2,1,0:T(8,128)(2,1)S(1)} collective-permute-done((bf16[2,272,512]{2,1,0:T(8,128)(2,1)S(1)}, bf16[2,272,512]{2,1,0:T(8,128)(2,1)S(1)}, u32[]{:S(2)}, u32[]{:S(2)}) %collective-permute-start.5) | collective-permute-done | bytes 557088 | tf_op jit(solution)/shard_map/ppermute | solution.py:695
  70.7 11.6 %collective-permute-done.6.by = bf16[2,272,512]{2,1,0:T(8,128)(2,1)S(1)} collective-permute-done((bf16[2,272,512]{2,1,0:T(8,128)(2,1)S(1)}, bf16[2,272,512]{2,1,0:T(8,128)(2,1)S(1)}, u32[]{:S(2)}, u32[]{:S(2)}) %collective-permute-start.6) | collective-permute-done | bytes 557088 | tf_op jit(solution)/shard_map/ppermute | solution.py:695
  91.3 23.7 %collective-permute-done.4.ay = bf16[2,2,272,512]{3,2,1,0:T(8,128)(2,1)} collective-permute-done((bf16[2,2,272,512]{3,2,1,0:T(8,128)(2,1)}, bf16[2,2,272,512]{3,2,1,0:T(8,128)(2,1)}, u32[]{:S(2)}, u32[]{:S(2)}) %collective-permute-start.4) | collective-permute-done | bytes 1114144 | tf_op jit(solution)/shard_map/ppermute | solution.py:695
  115.0 6.9 %collective-permute-done.7.bx = bf16[2,2,272,512]{3,2,1,0:T(8,128)(2,1)} collective-permute-done((bf16[2,2,272,512]{3,2,1,0:T(8,128)(2,1)}, bf16[2,2,272,512]{3,2,1,0:T(8,128)(2,1)}, u32[]{:S(2)}, u32[]{:S(2)}) %collective-permute-start.7) | collective-permute-done | bytes 1114144 | tf_op jit(solution)/shard_map/ppermute | solution.py:695
  121.9 13.3 %attention_forward.1 = (bf16[512,1536]{1,0:T(8,128)(2,1)}, bf16[4,512,128]{2,1,0:T(8,128)(2,1)}, f32[512,1024]{1,0:T(8,128)}, f32[16,1024]{1,0:T(8,128)}) custom-call(s32[6]{0:T(128)} %pad_add_fusion.1.place, bf16[4,512,256]{2,1,0:T(8,128)(2,1)} %pad_maximum_fusion.2.x.x_ref, bf16[2,272,512]{2,1,0:T(8,128)(2,1)} %copy-done.49, ...), custom_call_target="tpu_custom_call" | custom-call | flops 115000000 | bytes 1 | tf_op jit(solution)/shard_map/attention_forward/pallas_call | solution.py:69
  135.8 3.7 %collective-permute-done.9.recv = f32[512,1024]{1,0:T(8,128)S(1)} collective-permute-done((f32[512,1024]{1,0:T(8,128)}, f32[512,1024]{1,0:T(8,128)S(1)}, u32[]{:S(2)}, u32[]{:S(2)}) %collective-permute-start.9) | collective-permute-done | bytes 2097184 | tf_op jit(solution)/shard_map/ppermute | solution.py:695
  145.5 11.7 %all-gather.3.cloned.1.call-done = bf16[34816,256]{1,0:T(8,128)(2,1)} async-done(((bf16[1088,256]{1,0:T(8,128)(2,1)}), bf16[34816,256]{1,0:T(8,128)(2,1)}) %all-gather.3.cloned.1.call-update) | async-done | bytes 17825808 | tf_op jit(solution)/shard_map/all_gather | solution.py:747
  157.2 13.1 %feed_forward.1 = (bf16[4,512,512]{2,1,0:T(8,128)(2,1)}, bf16[4,512,512]{2,1,0:T(8,128)(2,1)}, f32[256,1024]{1,0:T(8,128)}, f32[256,1024]{1,0:T(8,128)}) custom-call(s32[3]{0:T(128)} %pad_add_fusion.3.place.spot_ref.spot, bf16[512,1024]{1,0:T(8,128)(2,1)} %copy-done.46, f32[16,1024]{1,0:T(8,128)} %get-tuple-element.66.vec, ...), custom_call_target="tpu_custom_call" | custom-call | flops 13799999488 | bytes 1 | tf_op jit(solution)/shard_map/feed_forward/pallas_call | solution.py:873
  175.7 5.3 %collective-permute-start.11 = (bf16[288,256]{1,0:T(8,128)(2,1)S(1)}, bf16[288,256]{1,0:T(8,128)(2,1)S(1)}, u32[]{:S(2)}, u32[]{:S(2)}) collective-permute-start(bf16[288,256]{1,0:T(8,128)(2,1)S(1)} %get-tuple-element.72.proj_0), channel_id=1, source_target_pairs={{0,1},{1,0},{2,3},{3,2},{4,5},{5,4},{6,7},{7,6},{8,9},{9,8},{10,11... | collective-permute-start | bytes 442376 | tf_op jit(solution)/shard_map/ppermute | solution.py:695
  184.5 3.3 collective-permute-done.11.proj_1
  187.8 7.0 %collective-permute-done.12.proj_2 = bf16[288,256]{1,0:T(8,128)(2,1)S(1)} collective-permute-done((bf16[288,256]{1,0:T(8,128)(2,1)S(1)}, bf16[288,256]{1,0:T(8,128)(2,1)S(1)}, u32[]{:S(2)}, u32[]{:S(2)}) %collective-permute-start.12) | collective-permute-done | bytes 147488 | tf_op jit(solution)/shard_map/ppermute | solution.py:695
  195.9 5.1 %soft_maxsim.1 = (f32[256,1024]{1,0:T(8,128)S(1)}, bf16[256,1024]{1,0:T(8,128)(2,1)S(1)}, f32[8,304,128]{2,1,0:T(8,128)}, f32[3,1024]{1,0:T(4,128)S(1)}, f32[2,128]{1,0:T(2,128)S(1)}) custom-call(s32[6]{0:T(128)S(1)} %copy-done.41, f32[1]{0:T(128)S(6)} %copy.61.temp, f32[2,128]{1,0:T(2,128)S(1)} %pad_maximum_fusion.10.lanes, ...), custom_call_target="tpu_custom_call" | custom-call | flops 4944999936 | bytes 1 | tf_op jit(solution)/shard_map/soft_maxsim/pallas_call | solution.py:69
  203.0 3.1 down_far.1
  206.9 10.2 %feed_forward_back.1 = (bf16[512,2048]{1,0:T(8,128)(2,1)}, f32[256,1024]{1,0:T(8,128)}, f32[256,1024]{1,0:T(8,128)}, f32[1,2048]{1,0:T(1,128)}) custom-call(s32[3]{0:T(128)} %pad_add_fusion.3.place.spot_ref.spot, bf16[256,1024]{1,0:T(8,128)(2,1)} %copy-done.2, bf16[256,1024]{1,0:T(8,128)(2,1)} %copy-done.4, bf16[4,512,512]{2,1,0:T(8,128)(2,1)} %get-tuple-element.80.slope, ...), custom_call_target="tpu_custom_call" | custom-call | flops 115000000 | bytes 1 | tf_op jit(solution)/shard_map/feed_forward_back/pallas_call | solution.py:975
  218.8 3.0 up_far.1
  227.9 15.3 %attention_backward.1 = (bf16[512,1536]{1,0:T(8,128)(2,1)}, f32[256,1024]{1,0:T(8,128)}, f32[256,1024]{1,0:T(8,128)}, f32[1,1536]{1,0:T(1,128)}) custom-call(s32[6]{0:T(128)} %pad_add_fusion.1.place, bf16[256,1024]{1,0:T(8,128)(2,1)} %copy-done.11, bf16[256,1024]{1,0:T(8,128)(2,1)} %copy-done.13, bf16[512,1536]{1,0:T(8,128)(2,1)} %get-tuple-element.90.qkv, ...), custom_call_target="tpu_custom_call" | custom-call | flops 115000000 | bytes 1 | tf_op jit(solution)/shard_map/attention_backward/pallas_call | solution.py:69
  243.2 4.8 %tail_far.1 = (bf16[2,1,128,2048]{3,2,1,0:T(8,128)(2,1)}, bf16[2,1,128,2048]{3,2,1,0:T(8,128)(2,1)}) custom-call(bf16[4,512,256]{2,1,0:T(8,128)(2,1)} %pad_maximum_fusion.2.x.x_ref, bf16[512,1536]{1,0:T(8,128)(2,1)} %get-tuple-element.111.qkv_ref.refs_0_.refs_5_, bf16[4,512,128]{2,1,0:T(8,128)(2,1)} %get-tuple-element.97.att_ref, ...), custom_call_target="tpu_custom_call" | custom-call | flops 115000000 | bytes 1 | tf_op jit(solution)/shard_map/tail_far/pallas_call | solution.py:602
  251.1 3.8 %collective-permute-done.19.refs_4_.refs_5_.refs_2_ = bf16[2,512,1024]{2,1,0:T(8,128)(2,1)} collective-permute-done((bf16[2,512,1024]{2,1,0:T(8,128)(2,1)}, bf16[2,512,1024]{2,1,0:T(8,128)(2,1)}, u32[]{:S(2)}, u32[]{:S(2)}) %collective-permute-start.19) | collective-permute-done | bytes 2097184 | tf_op jit(solution)/shard_map/ppermute | solution.py:695
  260.6 9.9 %collective-permute-done.20.refs_1_.refs_2_.refs_4_ = bf16[2,256,2048]{2,1,0:T(8,128)(2,1)} collective-permute-done((bf16[2,256,2048]{2,1,0:T(8,128)(2,1)}, bf16[2,256,2048]{2,1,0:T(8,128)(2,1)}, u32[]{:S(2)}, u32[]{:S(2)}) %collective-permute-start.20) | collective-permute-done | bytes 2097184 | tf_op jit(solution)/shard_map/ppermute | solution.py:695
  277.0 5.5 %collective-permute-done.21.refs_3_ = bf16[4,512,256]{2,1,0:T(8,128)(2,1)S(1)} collective-permute-done((bf16[4,512,256]{2,1,0:T(8,128)(2,1)S(1)}, bf16[4,512,256]{2,1,0:T(8,128)(2,1)S(1)}, u32[]{:S(2)}, u32[]{:S(2)}) %collective-permute-start.21) | collective-permute-done | bytes 1048608 | tf_op jit(solution)/shard_map/ppermute | solution.py:695
  282.5 3.0 down_head_near.1
  285.5 3.2 collective-permute-start.25
  288.6 9.0 %collective-permute-done.22.refs_1_.refs_12_.refs_16_.refs_8_.refs_9_ = bf16[2,1,128,2048]{3,2,1,0:T(8,128)(2,1)} collective-permute-done((bf16[2,1,128,2048]{3,2,1,0:T(8,128)(2,1)}, bf16[2,1,128,2048]{3,2,1,0:T(8,128)(2,1)}, u32[]{:S(2)}, u32[]{:S(2)}) %collective-permute-start.22) | collective-permute-done | bytes 1048608 | tf_op jit(solution)/shard_map/ppermute | solution.py:695
  315.9 4.0 %tail_head.1 = bf16[2,2,128,512]{3,2,1,0:T(8,128)(2,1)} custom-call(s32[3]{0:T(128)} %pad_add_fusion.3.place.spot_ref.spot, bf16[4,512,256]{2,1,0:T(8,128)(2,1)} %pad_maximum_fusion.2.x.x_ref, bf16[4,512,128]{2,1,0:T(8,128)(2,1)} %get-tuple-element.97.att_ref, bf16[512,1536]{1,0:T(8,128)(2,1)} %get-tuple-element.111.qkv_ref.refs_0_.refs_5_, ...), custom_call_target="tpu_custom_call" | custom-call | flops 5750000128 | bytes 1 | tf_op jit(solution)/shard_map/tail_head/pallas_call | solution.py:563
  328.8 3.1 collective-permute-start.32
  341.9 3.3 tail_head_near.1
  345.3 3.1 down_own.1
  350.7 7.8 %collective-permute-done.29.refs_8_.refs_12_ = bf16[1,2,128,512]{3,2,1,0:T(8,128)(2,1)S(1)} collective-permute-done((bf16[1,2,128,512]{3,2,1,0:T(8,128)(2,1)}, bf16[1,2,128,512]{3,2,1,0:T(8,128)(2,1)S(1)}, u32[]{:S(2)}, u32[]{:S(2)}) %collective-permute-start.29) | collective-permute-done | bytes 262176 | tf_op jit(solution)/shard_map/ppermute | solution.py:695
  359.2 3.5 tail_own.1
  (278 shorter events, 107.9 us)
Async XLA Ops:
  7.2 150.0 %all-gather.3.cloned.1.call-start = ((), (), s32[]{:S(2)}) async-start(), calls=%async_computation.4 | async-start | bytes 18382848 | tf_op jit(solution)/shard_map/all_gather | solution.py:747
  10.8 299.6 %reduce-scatter.3.cloned.1.call-start = ((), (), s32[]{:S(2)}) async-start(), calls=%async_computation.2 | async-start | bytes 1400832 | tf_op jit(solution)/shard_map/reduce_scatter | solution.py:1131
  13.3 26.7 %collective-permute-start.2 = (bf16[1,272,512]{2,1,0:T(8,128)(2,1)S(1)}, bf16[1,272,512]{2,1,0:T(8,128)(2,1)S(1)}, u32[]{:S(2)}, u32[]{:S(2)}) collective-permute-start(bf16[1,272,512]{2,1,0:T(8,128)(2,1)S(1)} %fusion.2), channel_id=1, source_target_pairs={{0,2},{1,3},{2,0},{3,1},{4,6},{5,7},{6,4},{7,5},{8,10},{9,11},{10,... | collective-permute-start | bytes 835592 | tf_op jit(solution)/shard_map/ppermute | solution.py:695
  17.3 71.6 %collective-permute-start = (bf16[256,1024]{1,0:T(8,128)(2,1)}, bf16[256,1024]{1,0:T(8,128)(2,1)}, u32[]{:S(2)}, u32[]{:S(2)}) collective-permute-start(bf16[256,1024]{1,0:T(8,128)(2,1)} %param.14), channel_id=1, source_target_pairs={{0,4},{1,5},{2,6},{3,7},{4,0},{5,1},{6,2},{7,3},{8,12},{9,13},{10,... | collective-permute-start | bytes 1572872 | tf_op jit(solution)/shard_map/ppermute | solution.py:695
  17.4 69.2 %collective-permute-start.8 = (s32[11]{0:T(128)S(1)}, s32[11]{0:T(128)S(1)}, u32[]{:S(2)}, u32[]{:S(2)}) collective-permute-start(s32[11]{0:T(128)S(1)} %pad_add_fusion.2), channel_id=1, source_target_pairs={{0,4},{1,5},{2,6},{3,7},{4,0},{5,1},{6,2},{7,3},{8,12},{9,13},{10,... | collective-permute-start | bytes 140 | tf_op jit(solution)/shard_map/ppermute | solution.py:695
  40.0 26.7 %collective-permute-start.5 = (bf16[2,272,512]{2,1,0:T(8,128)(2,1)S(1)}, bf16[2,272,512]{2,1,0:T(8,128)(2,1)S(1)}, u32[]{:S(2)}, u32[]{:S(2)}) collective-permute-start(bf16[2,272,512]{2,1,0:T(8,128)(2,1)S(1)} %get-tuple-element.148.a0), channel_id=1, source_target_pairs={{0,1},{1,0},{2,3},{3,2},{4,5},{5,4},{6,7},{7,6},{8,9},{9,8},{10,11... | collective-permute-start | bytes 1671176 | tf_op jit(solution)/shard_map/ppermute | solution.py:695
  44.6 24.4 %collective-permute-start.3 = (bf16[2,272,512]{2,1,0:T(8,128)(2,1)S(1)}, bf16[2,272,512]{2,1,0:T(8,128)(2,1)S(1)}, u32[]{:S(2)}, u32[]{:S(2)}) collective-permute-start(bf16[2,272,512]{2,1,0:T(8,128)(2,1)S(1)} %get-tuple-element.148.a0), channel_id=1, source_target_pairs={{0,8},{1,9},{2,10},{3,11},{4,12},{5,13},{6,14},{7,15},{8,0},{9,1},... | collective-permute-start | bytes 1671176 | tf_op jit(solution)/shard_map/ppermute | solution.py:695
  66.7 15.6 %collective-permute-start.6 = (bf16[2,272,512]{2,1,0:T(8,128)(2,1)S(1)}, bf16[2,272,512]{2,1,0:T(8,128)(2,1)S(1)}, u32[]{:S(2)}, u32[]{:S(2)}) collective-permute-start(bf16[2,272,512]{2,1,0:T(8,128)(2,1)S(1)} %collective-permute-done.5.b0), channel_id=1, source_target_pairs={{0,16},{1,17},{2,18},{3,19},{4,20},{5,21},{6,22},{7,23},{8,24},{9,... | collective-permute-start | bytes 1671176 | tf_op jit(solution)/shard_map/ppermute | solution.py:695
  70.2 44.8 %collective-permute-start.4 = (bf16[2,2,272,512]{3,2,1,0:T(8,128)(2,1)}, bf16[2,2,272,512]{3,2,1,0:T(8,128)(2,1)}, u32[]{:S(2)}, u32[]{:S(2)}) collective-permute-start(bf16[2,2,272,512]{3,2,1,0:T(8,128)(2,1)} %pad_maximum_fusion), channel_id=1, source_target_pairs={{0,16},{1,17},{2,18},{3,19},{4,20},{5,21},{6,22},{7,23},{8,24},{9,... | collective-permute-start | bytes 3342344 | tf_op jit(solution)/shard_map/ppermute | solution.py:695
  83.5 38.4 %collective-permute-start.7 = (bf16[2,2,272,512]{3,2,1,0:T(8,128)(2,1)}, bf16[2,2,272,512]{3,2,1,0:T(8,128)(2,1)}, u32[]{:S(2)}, u32[]{:S(2)}) collective-permute-start(bf16[2,2,272,512]{3,2,1,0:T(8,128)(2,1)} %pad_maximum_fusion.1), channel_id=1, source_target_pairs={{0,8},{1,9},{2,10},{3,11},{4,12},{5,13},{6,14},{7,15},{8,0},{9,1},... | collective-permute-start | bytes 3342344 | tf_op jit(solution)/shard_map/ppermute | solution.py:695
  135.2 4.4 %collective-permute-start.9 = (f32[512,1024]{1,0:T(8,128)}, f32[512,1024]{1,0:T(8,128)S(1)}, u32[]{:S(2)}, u32[]{:S(2)}) collective-permute-start(f32[512,1024]{1,0:T(8,128)} %get-tuple-element.65.part), channel_id=1, source_target_pairs={{0,4},{1,5},{2,6},{3,7},{4,0},{5,1},{6,2},{7,3},{8,12},{9,13},{10,... | collective-permute-start | bytes 6291464 | tf_op jit(solution)/shard_map/ppermute | solution.py:695
  175.7 12.2 %collective-permute-start.11 = (bf16[288,256]{1,0:T(8,128)(2,1)S(1)}, bf16[288,256]{1,0:T(8,128)(2,1)S(1)}, u32[]{:S(2)}, u32[]{:S(2)}) collective-permute-start(bf16[288,256]{1,0:T(8,128)(2,1)S(1)} %get-tuple-element.72.proj_0), channel_id=1, source_target_pairs={{0,1},{1,0},{2,3},{3,2},{4,5},{5,4},{6,7},{7,6},{8,9},{9,8},{10,11... | collective-permute-start | bytes 442376 | tf_op jit(solution)/shard_map/ppermute | solution.py:695
  180.9 13.9 %collective-permute-start.12 = (bf16[288,256]{1,0:T(8,128)(2,1)S(1)}, bf16[288,256]{1,0:T(8,128)(2,1)S(1)}, u32[]{:S(2)}, u32[]{:S(2)}) collective-permute-start(bf16[288,256]{1,0:T(8,128)(2,1)S(1)} %get-tuple-element.72.proj_0), channel_id=1, source_target_pairs={{0,2},{1,3},{2,0},{3,1},{4,6},{5,7},{6,4},{7,5},{8,10},{9,11},{10,... | collective-permute-start | bytes 442376 | tf_op jit(solution)/shard_map/ppermute | solution.py:695
  182.4 12.5 %collective-permute-start.13 = (bf16[288,256]{1,0:T(8,128)(2,1)S(1)}, bf16[288,256]{1,0:T(8,128)(2,1)S(1)}, u32[]{:S(2)}, u32[]{:S(2)}) collective-permute-start(bf16[288,256]{1,0:T(8,128)(2,1)S(1)} %get-tuple-element.72.proj_0), channel_id=1, source_target_pairs={{0,3},{1,2},{2,1},{3,0},{4,7},{5,6},{6,5},{7,4},{8,11},{9,10},{10,... | collective-permute-start | bytes 442376 | tf_op jit(solution)/shard_map/ppermute | solution.py:695
  206.1 48.8 %collective-permute-start.19 = (bf16[2,512,1024]{2,1,0:T(8,128)(2,1)}, bf16[2,512,1024]{2,1,0:T(8,128)(2,1)}, u32[]{:S(2)}, u32[]{:S(2)}) collective-permute-start(bf16[2,512,1024]{2,1,0:T(8,128)(2,1)} %down_far.1), channel_id=1, source_target_pairs={{0,8},{1,9},{2,10},{3,11},{4,12},{5,13},{6,14},{7,15},{8,0},{9,1},... | collective-permute-start | bytes 6291464 | tf_op jit(solution)/shard_map/ppermute | solution.py:695
  217.1 6.3 %collective-permute-start.15 = (f32[256,1024]{1,0:T(8,128)}, f32[256,1024]{1,0:T(8,128)S(1)}, u32[]{:S(2)}, u32[]{:S(2)}) collective-permute-start(f32[256,1024]{1,0:T(8,128)} %get-tuple-element.85), channel_id=1, source_target_pairs={{0,4},{1,5},{2,6},{3,7},{4,0},{5,1},{6,2},{7,3},{8,12},{9,13},{10,... | collective-permute-start | bytes 3145736 | tf_op jit(solution)/shard_map/ppermute | solution.py:695
  221.8 48.7 %collective-permute-start.20 = (bf16[2,256,2048]{2,1,0:T(8,128)(2,1)}, bf16[2,256,2048]{2,1,0:T(8,128)(2,1)}, u32[]{:S(2)}, u32[]{:S(2)}) collective-permute-start(bf16[2,256,2048]{2,1,0:T(8,128)(2,1)} %up_far.1), channel_id=1, source_target_pairs={{0,16},{1,17},{2,18},{3,19},{4,20},{5,21},{6,22},{7,23},{8,24},{9,... | collective-permute-start | bytes 6291464 | tf_op jit(solution)/shard_map/ppermute | solution.py:695
  248.0 49.6 %collective-permute-start.22 = (bf16[2,1,128,2048]{3,2,1,0:T(8,128)(2,1)}, bf16[2,1,128,2048]{3,2,1,0:T(8,128)(2,1)}, u32[]{:S(2)}, u32[]{:S(2)}) collective-permute-start(bf16[2,1,128,2048]{3,2,1,0:T(8,128)(2,1)} %get-tuple-element.100), channel_id=1, source_target_pairs={{0,16},{1,17},{2,18},{3,19},{4,20},{5,21},{6,22},{7,23},{8,24},{9,... | collective-permute-start | bytes 3145736 | tf_op jit(solution)/shard_map/ppermute | solution.py:695
  248.5 40.2 %collective-permute-start.18 = (bf16[2,1,128,2048]{3,2,1,0:T(8,128)(2,1)}, bf16[2,1,128,2048]{3,2,1,0:T(8,128)(2,1)}, u32[]{:S(2)}, u32[]{:S(2)}) collective-permute-start(bf16[2,1,128,2048]{3,2,1,0:T(8,128)(2,1)} %get-tuple-element.99), channel_id=1, source_target_pairs={{0,8},{1,9},{2,10},{3,11},{4,12},{5,13},{6,14},{7,15},{8,0},{9,1},... | collective-permute-start | bytes 3145736 | tf_op jit(solution)/shard_map/ppermute | solution.py:695
  249.7 24.7 %collective-permute-start.17 = (f32[256,1024]{1,0:T(8,128)}, f32[256,1024]{1,0:T(8,128)}, u32[]{:S(2)}, u32[]{:S(2)}) collective-permute-start(f32[256,1024]{1,0:T(8,128)} %get-tuple-element.96), channel_id=1, source_target_pairs={{0,4},{1,5},{2,6},{3,7},{4,0},{5,1},{6,2},{7,3},{8,12},{9,13},{10,... | collective-permute-start | bytes 3145736 | tf_op jit(solution)/shard_map/ppermute | solution.py:695
  251.0 82.1 %reduce-scatter.5.cloned.1.call-start = ((), (), s32[]{:S(2)}) async-start(), calls=%async_computation.3 | async-start | bytes 245760 | tf_op jit(solution)/shard_map/reduce_scatter | solution.py:1138
  257.8 24.7 %collective-permute-start.21 = (bf16[4,512,256]{2,1,0:T(8,128)(2,1)S(1)}, bf16[4,512,256]{2,1,0:T(8,128)(2,1)S(1)}, u32[]{:S(2)}, u32[]{:S(2)}) collective-permute-start(bf16[4,512,256]{2,1,0:T(8,128)(2,1)S(1)} %down_head.1), channel_id=1, source_target_pairs={{0,1},{1,0},{2,3},{3,2},{4,5},{5,4},{6,7},{7,6},{8,9},{9,8},{10,11... | collective-permute-start | bytes 3145736 | tf_op jit(solution)/shard_map/ppermute | solution.py:695
  273.1 31.6 %collective-permute-start.24 = (bf16[1,256,2048]{2,1,0:T(8,128)(2,1)S(1)}, bf16[1,256,2048]{2,1,0:T(8,128)(2,1)S(1)}, u32[]{:S(2)}, u32[]{:S(2)}) collective-permute-start(bf16[1,256,2048]{2,1,0:T(8,128)(2,1)S(1)} %up_near.1), channel_id=1, source_target_pairs={{0,8},{1,9},{2,10},{3,11},{4,12},{5,13},{6,14},{7,15},{8,0},{9,1},... | collective-permute-start | bytes 3145736 | tf_op jit(solution)/shard_map/ppermute | solution.py:695
  285.5 27.2 %collective-permute-start.25 = (bf16[2,512,256]{2,1,0:T(8,128)(2,1)}, bf16[2,512,256]{2,1,0:T(8,128)(2,1)}, u32[]{:S(2)}, u32[]{:S(2)}) collective-permute-start(bf16[2,512,256]{2,1,0:T(8,128)(2,1)} %down_head_near.1), channel_id=1, source_target_pairs={{0,2},{1,3},{2,0},{3,1},{4,6},{5,7},{6,4},{7,5},{8,10},{9,11},{10,... | collective-permute-start | bytes 1572872 | tf_op jit(solution)/shard_map/ppermute | solution.py:695
  300.6 15.3 %collective-permute-start.26 = (bf16[1,1,128,2048]{3,2,1,0:T(8,128)(2,1)}, bf16[1,1,128,2048]{3,2,1,0:T(8,128)(2,1)}, u32[]{:S(2)}, u32[]{:S(2)}) collective-permute-start(bf16[1,1,128,2048]{3,2,1,0:T(8,128)(2,1)} %get-tuple-element.106), channel_id=1, source_target_pairs={{0,8},{1,9},{2,10},{3,11},{4,12},{5,13},{6,14},{7,15},{8,0},{9,1},... | collective-permute-start | bytes 1572872 | tf_op jit(solution)/shard_map/ppermute | solution.py:695
  301.9 14.1 %collective-permute-start.23 = (bf16[1,1,128,2048]{3,2,1,0:T(8,128)(2,1)}, bf16[1,1,128,2048]{3,2,1,0:T(8,128)(2,1)}, u32[]{:S(2)}, u32[]{:S(2)}) collective-permute-start(bf16[1,1,128,2048]{3,2,1,0:T(8,128)(2,1)} %get-tuple-element.105), channel_id=1, source_target_pairs={{0,16},{1,17},{2,18},{3,19},{4,20},{5,21},{6,22},{7,23},{8,24},{9,... | collective-permute-start | bytes 1572872 | tf_op jit(solution)/shard_map/ppermute | solution.py:695
  307.6 16.0 %collective-permute-start.28 = (bf16[2,256,512]{2,1,0:T(8,128)(2,1)}, bf16[2,256,512]{2,1,0:T(8,128)(2,1)}, u32[]{:S(2)}, u32[]{:S(2)}) collective-permute-start(bf16[2,256,512]{2,1,0:T(8,128)(2,1)} %up_head.1), channel_id=1, source_target_pairs={{0,1},{1,0},{2,3},{3,2},{4,5},{5,4},{6,7},{7,6},{8,9},{9,8},{10,11... | collective-permute-start | bytes 1572872 | tf_op jit(solution)/shard_map/ppermute | solution.py:695
  320.0 21.9 %collective-permute-start.27 = (bf16[2,2,128,512]{3,2,1,0:T(8,128)(2,1)}, bf16[2,2,128,512]{3,2,1,0:T(8,128)(2,1)}, u32[]{:S(2)}, u32[]{:S(2)}) collective-permute-start(bf16[2,2,128,512]{3,2,1,0:T(8,128)(2,1)} %tail_head.1), channel_id=1, source_target_pairs={{0,1},{1,0},{2,3},{3,2},{4,5},{5,4},{6,7},{7,6},{8,9},{9,8},{10,11... | collective-permute-start | bytes 1572872 | tf_op jit(solution)/shard_map/ppermute | solution.py:695
  322.1 23.2 %collective-permute-start.31 = (bf16[1,512,256]{2,1,0:T(8,128)(2,1)S(1)}, bf16[1,512,256]{2,1,0:T(8,128)(2,1)}, u32[]{:S(2)}, u32[]{:S(2)}) collective-permute-start(bf16[1,512,256]{2,1,0:T(8,128)(2,1)S(1)} %down_near.1), channel_id=1, source_target_pairs={{0,16},{1,17},{2,18},{3,19},{4,20},{5,21},{6,22},{7,23},{8,24},{9,... | collective-permute-start | bytes 786440 | tf_op jit(solution)/shard_map/ppermute | solution.py:695
  328.8 19.7 %collective-permute-start.32 = (bf16[1,256,512]{2,1,0:T(8,128)(2,1)}, bf16[1,256,512]{2,1,0:T(8,128)(2,1)}, u32[]{:S(2)}, u32[]{:S(2)}) collective-permute-start(bf16[1,256,512]{2,1,0:T(8,128)(2,1)} %up_head_near.1), channel_id=1, source_target_pairs={{0,2},{1,3},{2,0},{3,1},{4,6},{5,7},{6,4},{7,5},{8,10},{9,11},{10,... | collective-permute-start | bytes 786440 | tf_op jit(solution)/shard_map/ppermute | solution.py:695
  345.2 13.3 %collective-permute-start.29 = (bf16[1,2,128,512]{3,2,1,0:T(8,128)(2,1)}, bf16[1,2,128,512]{3,2,1,0:T(8,128)(2,1)S(1)}, u32[]{:S(2)}, u32[]{:S(2)}) collective-permute-start(bf16[1,2,128,512]{3,2,1,0:T(8,128)(2,1)} %tail_head_near.1), channel_id=1, source_target_pairs={{0,2},{1,3},{2,0},{3,1},{4,6},{5,7},{6,4},{7,5},{8,10},{9,11},{10,... | collective-permute-start | bytes 786440 | tf_op jit(solution)/shard_map/ppermute | solution.py:695
  350.6 12.2 %collective-permute-start.33 = (bf16[128,512]{1,0:T(8,128)(2,1)S(1)}, bf16[128,512]{1,0:T(8,128)(2,1)S(1)}, u32[]{:S(2)}, u32[]{:S(2)}) collective-permute-start(bf16[128,512]{1,0:T(8,128)(2,1)S(1)} %get-tuple-element.150), channel_id=1, source_target_pairs={{0,4},{1,5},{2,6},{3,7},{4,0},{5,1},{6,2},{7,3},{8,12},{9,13},{10,... | collective-permute-start | bytes 393224 | tf_op jit(solution)/shard_map/ppermute | solution.py:695
  (70 other events, 507.9 us)
Sparse Core Ops, SparseCore 0:
  10.9 146.2 all-gather.2
  251.1 43.5 reduce-scatter.2
  312.8 20.2 reduce-scatter.4

commit v7 on v6

--- a/solution.py
+++ b/solution.py
@@ -569,7 +569,7 @@
             in_specs=specs,
             out_specs=out_spec,
         ),
-        compiler_params=params(58),
+        compiler_params=params(24 if whole_cols or finish else 58),
         cost_estimate=cost(micros),
         name=name,
     )(spot, x, att, *inputs)

time: 374 us -> 372 us (level)
    unnamed x134 -> x140, local copies, waits for them, and re-layouts: 19.5 us -> 18.8 us
  transfers between devices with their start and end apart: 37 -> 37, of which waited for: 22 -> 21; matrix products, arithmetic and copies ran while one was open for 7% -> 7% of each run, Pallas kernels for 24% -> 24%
where the time goes in v7:
time: 372 us; the launch traced here: 370 us
  waiting for transfers between devices  154 us (41%)
  Pallas kernels  111 us (30%)
  starting transfers between devices  46.5 us (12%)
  local copies, waits for them, and re-layouts  30.9 us (8%)
  between operations  15.2 us (4%)
  other arithmetic  13.1 us (4%)
    ppermute x34, waiting for transfers between devices, swap(): return lax.ppermute(a, ('dp', 'head'), pairs)  142 us
    ppermute x34, starting transfers between devices, swap(): return lax.ppermute(a, ('dp', 'head'), pairs)  46.4 us
    pallas_call x7, Pallas kernels, call(): pl.pallas_call(kernel, out_shape=outs, grid=(1,), in_specs=[SMEM_SPEC] *...  38.3 us
    pallas_call x10, Pallas kernels, weight_grad(): pl.pallas_call(kernel, out_shape=jax.ShapeDtypeStruct((len(blocks) * coun...  27.6 us
    unnamed x140, local copies, waits for them, and re-layouts  18.8 us
    pallas_call x1, Pallas kernels, on_device(): pl.pallas_call(feed_forward, out_shape=[jax.ShapeDtypeStruct((QUADS, toke...  13.1 us
    all_gather x1, waiting for transfers between devices, on_device(): mlp_all = lax.all_gather(packed_mlp, ('dp', 'head'))  10.4 us
    pallas_call x1, Pallas kernels, on_device(): pl.pallas_call(feed_forward_back, out_shape=[jax.ShapeDtypeStruct((tokens...  10.2 us
  transfers between devices with their start and end apart: 37, of which 21 were waited for; matrix products, arithmetic and copies ran while one was open for 7% of the time, Pallas kernels for 24%

profile of v7, /device:TPU:0, one launch (start us, length us, event | category | flops | bytes accessed | tf_op | source)
XLA Modules:
  0.0 370.4 jit_solution(12366134493572666293)
XLA Ops:
  13.3 4.0 %collective-permute-start.2 = (bf16[1,272,512]{2,1,0:T(8,128)(2,1)S(1)}, bf16[1,272,512]{2,1,0:T(8,128)(2,1)S(1)}, u32[]{:S(2)}, u32[]{:S(2)}) collective-permute-start(bf16[1,272,512]{2,1,0:T(8,128)(2,1)S(1)} %fusion.2), channel_id=1, source_target_pairs={{0,2},{1,3},{2,0},{3,1},{4,6},{5,7},{6,4},{7,5},{8,10},{9,11},{10,... | collective-permute-start | bytes 835592 | tf_op jit(solution)/shard_map/ppermute | solution.py:695
  18.6 21.3 %collective-permute-done.2 = bf16[1,272,512]{2,1,0:T(8,128)(2,1)S(1)} collective-permute-done((bf16[1,272,512]{2,1,0:T(8,128)(2,1)S(1)}, bf16[1,272,512]{2,1,0:T(8,128)(2,1)S(1)}, u32[]{:S(2)}, u32[]{:S(2)}) %collective-permute-start.2) | collective-permute-done | bytes 278560 | tf_op jit(solution)/shard_map/ppermute | solution.py:695
  40.0 3.0 collective-permute-start.5
  46.9 19.9 %collective-permute-done.5.b0 = bf16[2,272,512]{2,1,0:T(8,128)(2,1)S(1)} collective-permute-done((bf16[2,272,512]{2,1,0:T(8,128)(2,1)S(1)}, bf16[2,272,512]{2,1,0:T(8,128)(2,1)S(1)}, u32[]{:S(2)}, u32[]{:S(2)}) %collective-permute-start.5) | collective-permute-done | bytes 557088 | tf_op jit(solution)/shard_map/ppermute | solution.py:695
  70.8 11.5 %collective-permute-done.6.by = bf16[2,272,512]{2,1,0:T(8,128)(2,1)S(1)} collective-permute-done((bf16[2,272,512]{2,1,0:T(8,128)(2,1)S(1)}, bf16[2,272,512]{2,1,0:T(8,128)(2,1)S(1)}, u32[]{:S(2)}, u32[]{:S(2)}) %collective-permute-start.6) | collective-permute-done | bytes 557088 | tf_op jit(solution)/shard_map/ppermute | solution.py:695
  91.3 23.7 %collective-permute-done.4.ay = bf16[2,2,272,512]{3,2,1,0:T(8,128)(2,1)} collective-permute-done((bf16[2,2,272,512]{3,2,1,0:T(8,128)(2,1)}, bf16[2,2,272,512]{3,2,1,0:T(8,128)(2,1)}, u32[]{:S(2)}, u32[]{:S(2)}) %collective-permute-start.4) | collective-permute-done | bytes 1114144 | tf_op jit(solution)/shard_map/ppermute | solution.py:695
  115.0 6.9 %collective-permute-done.7.bx = bf16[2,2,272,512]{3,2,1,0:T(8,128)(2,1)} collective-permute-done((bf16[2,2,272,512]{3,2,1,0:T(8,128)(2,1)}, bf16[2,2,272,512]{3,2,1,0:T(8,128)(2,1)}, u32[]{:S(2)}, u32[]{:S(2)}) %collective-permute-start.7) | collective-permute-done | bytes 1114144 | tf_op jit(solution)/shard_map/ppermute | solution.py:695
  121.9 13.3 %attention_forward.1 = (bf16[512,1536]{1,0:T(8,128)(2,1)}, bf16[4,512,128]{2,1,0:T(8,128)(2,1)}, f32[512,1024]{1,0:T(8,128)}, f32[16,1024]{1,0:T(8,128)}) custom-call(s32[6]{0:T(128)} %pad_add_fusion.1.place, bf16[4,512,256]{2,1,0:T(8,128)(2,1)} %pad_maximum_fusion.2.x.x_ref, bf16[2,272,512]{2,1,0:T(8,128)(2,1)} %copy-done.54, ...), custom_call_target="tpu_custom_call" | custom-call | flops 115000000 | bytes 1 | tf_op jit(solution)/shard_map/attention_forward/pallas_call | solution.py:69
  135.9 3.7 %collective-permute-done.9.recv = f32[512,1024]{1,0:T(8,128)S(1)} collective-permute-done((f32[512,1024]{1,0:T(8,128)}, f32[512,1024]{1,0:T(8,128)S(1)}, u32[]{:S(2)}, u32[]{:S(2)}) %collective-permute-start.9) | collective-permute-done | bytes 2097184 | tf_op jit(solution)/shard_map/ppermute | solution.py:695
  145.6 10.4 %all-gather.3.cloned.1.call-done = bf16[34816,256]{1,0:T(8,128)(2,1)} async-done(((bf16[1088,256]{1,0:T(8,128)(2,1)}), bf16[34816,256]{1,0:T(8,128)(2,1)}) %all-gather.3.cloned.1.call-update) | async-done | bytes 17825808 | tf_op jit(solution)/shard_map/all_gather | solution.py:747
  155.9 13.1 %feed_forward.1 = (bf16[4,512,512]{2,1,0:T(8,128)(2,1)}, bf16[4,512,512]{2,1,0:T(8,128)(2,1)}, f32[256,1024]{1,0:T(8,128)}, f32[256,1024]{1,0:T(8,128)}) custom-call(s32[3]{0:T(128)} %pad_add_fusion.3.place.spot_ref.spot, bf16[512,1024]{1,0:T(8,128)(2,1)} %copy-done.51, f32[16,1024]{1,0:T(8,128)} %get-tuple-element.66.vec, ...), custom_call_target="tpu_custom_call" | custom-call | flops 13799999488 | bytes 1 | tf_op jit(solution)/shard_map/feed_forward/pallas_call | solution.py:873
  174.3 6.5 %collective-permute-start.11 = (bf16[288,256]{1,0:T(8,128)(2,1)S(1)}, bf16[288,256]{1,0:T(8,128)(2,1)S(1)}, u32[]{:S(2)}, u32[]{:S(2)}) collective-permute-start(bf16[288,256]{1,0:T(8,128)(2,1)S(1)} %get-tuple-element.72.proj_0), channel_id=1, source_target_pairs={{0,1},{1,0},{2,3},{3,2},{4,5},{5,4},{6,7},{7,6},{8,9},{9,8},{10,11... | collective-permute-start | bytes 442376 | tf_op jit(solution)/shard_map/ppermute | solution.py:695
  184.5 3.3 collective-permute-done.11.proj_1
  187.8 7.0 %collective-permute-done.12.proj_2 = bf16[288,256]{1,0:T(8,128)(2,1)S(1)} collective-permute-done((bf16[288,256]{1,0:T(8,128)(2,1)S(1)}, bf16[288,256]{1,0:T(8,128)(2,1)S(1)}, u32[]{:S(2)}, u32[]{:S(2)}) %collective-permute-start.12) | collective-permute-done | bytes 147488 | tf_op jit(solution)/shard_map/ppermute | solution.py:695
  195.9 5.1 %soft_maxsim.1 = (f32[256,1024]{1,0:T(8,128)S(1)}, bf16[256,1024]{1,0:T(8,128)(2,1)S(1)}, f32[8,304,128]{2,1,0:T(8,128)}, f32[3,1024]{1,0:T(4,128)S(1)}, f32[2,128]{1,0:T(2,128)S(1)}) custom-call(s32[6]{0:T(128)S(1)} %copy-done.46, f32[1]{0:T(128)S(6)} %copy.61.temp, f32[2,128]{1,0:T(2,128)S(1)} %pad_maximum_fusion.10.lanes, ...), custom_call_target="tpu_custom_call" | custom-call | flops 4944999936 | bytes 1 | tf_op jit(solution)/shard_map/soft_maxsim/pallas_call | solution.py:69
  202.9 3.1 down_far.1
  206.9 10.2 %feed_forward_back.1 = (bf16[512,2048]{1,0:T(8,128)(2,1)}, f32[256,1024]{1,0:T(8,128)}, f32[256,1024]{1,0:T(8,128)}, f32[1,2048]{1,0:T(1,128)}) custom-call(s32[3]{0:T(128)} %pad_add_fusion.3.place.spot_ref.spot, bf16[256,1024]{1,0:T(8,128)(2,1)} %copy-done.3, bf16[256,1024]{1,0:T(8,128)(2,1)} %copy-done.5, bf16[4,512,512]{2,1,0:T(8,128)(2,1)} %get-tuple-element.80.slope, ...), custom_call_target="tpu_custom_call" | custom-call | flops 115000000 | bytes 1 | tf_op jit(solution)/shard_map/feed_forward_back/pallas_call | solution.py:975
  218.8 3.0 up_far.1
  227.9 15.3 %attention_backward.1 = (bf16[512,1536]{1,0:T(8,128)(2,1)}, f32[256,1024]{1,0:T(8,128)}, f32[256,1024]{1,0:T(8,128)}, f32[1,1536]{1,0:T(1,128)}) custom-call(s32[6]{0:T(128)} %pad_add_fusion.1.place, bf16[256,1024]{1,0:T(8,128)(2,1)} %copy-done.12, bf16[256,1024]{1,0:T(8,128)(2,1)} %copy-done.15, bf16[512,1536]{1,0:T(8,128)(2,1)} %get-tuple-element.90.qkv, ...), custom_call_target="tpu_custom_call" | custom-call | flops 115000000 | bytes 1 | tf_op jit(solution)/shard_map/attention_backward/pallas_call | solution.py:69
  243.2 4.8 %tail_far.1 = (bf16[2,1,128,2048]{3,2,1,0:T(8,128)(2,1)}, bf16[2,1,128,2048]{3,2,1,0:T(8,128)(2,1)}) custom-call(bf16[4,512,256]{2,1,0:T(8,128)(2,1)} %pad_maximum_fusion.2.x.x_ref, bf16[512,1536]{1,0:T(8,128)(2,1)} %get-tuple-element.111.qkv_ref.refs_0_.refs_5_, bf16[4,512,128]{2,1,0:T(8,128)(2,1)} %get-tuple-element.97.att_ref, ...), custom_call_target="tpu_custom_call" | custom-call | flops 115000000 | bytes 1 | tf_op jit(solution)/shard_map/tail_far/pallas_call | solution.py:602
  251.1 3.7 %collective-permute-done.19.refs_4_.refs_5_.refs_2_ = bf16[2,512,1024]{2,1,0:T(8,128)(2,1)} collective-permute-done((bf16[2,512,1024]{2,1,0:T(8,128)(2,1)}, bf16[2,512,1024]{2,1,0:T(8,128)(2,1)}, u32[]{:S(2)}, u32[]{:S(2)}) %collective-permute-start.19) | collective-permute-done | bytes 2097184 | tf_op jit(solution)/shard_map/ppermute | solution.py:695
  260.6 10.0 %collective-permute-done.20.refs_1_.refs_2_.refs_4_ = bf16[2,256,2048]{2,1,0:T(8,128)(2,1)} collective-permute-done((bf16[2,256,2048]{2,1,0:T(8,128)(2,1)}, bf16[2,256,2048]{2,1,0:T(8,128)(2,1)}, u32[]{:S(2)}, u32[]{:S(2)}) %collective-permute-start.20) | collective-permute-done | bytes 2097184 | tf_op jit(solution)/shard_map/ppermute | solution.py:695
  277.0 5.5 %collective-permute-done.21.refs_3_ = bf16[4,512,256]{2,1,0:T(8,128)(2,1)S(1)} collective-permute-done((bf16[4,512,256]{2,1,0:T(8,128)(2,1)S(1)}, bf16[4,512,256]{2,1,0:T(8,128)(2,1)S(1)}, u32[]{:S(2)}, u32[]{:S(2)}) %collective-permute-start.21) | collective-permute-done | bytes 1048608 | tf_op jit(solution)/shard_map/ppermute | solution.py:695
  282.5 3.0 down_head_near.1
  285.4 3.2 collective-permute-start.25
  288.6 9.0 %collective-permute-done.22.refs_1_.refs_12_.refs_16_.refs_8_.refs_9_ = bf16[2,1,128,2048]{3,2,1,0:T(8,128)(2,1)} collective-permute-done((bf16[2,1,128,2048]{3,2,1,0:T(8,128)(2,1)}, bf16[2,1,128,2048]{3,2,1,0:T(8,128)(2,1)}, u32[]{:S(2)}, u32[]{:S(2)}) %collective-permute-start.22) | collective-permute-done | bytes 1048608 | tf_op jit(solution)/shard_map/ppermute | solution.py:695
  297.7 2.9 tail_near.1
  315.9 4.1 %tail_head.1 = bf16[2,2,128,512]{3,2,1,0:T(8,128)(2,1)} custom-call(s32[3]{0:T(128)} %pad_add_fusion.3.place.spot_ref.spot, bf16[4,512,256]{2,1,0:T(8,128)(2,1)} %pad_maximum_fusion.2.x.x_ref, bf16[4,512,128]{2,1,0:T(8,128)(2,1)} %get-tuple-element.97.att_ref, bf16[512,1536]{1,0:T(8,128)(2,1)} %get-tuple-element.111.qkv_ref.refs_0_.refs_5_, ...), custom_call_target="tpu_custom_call" | custom-call | flops 5750000128 | bytes 1 | tf_op jit(solution)/shard_map/tail_head/pallas_call | solution.py:563
  339.0 2.9 collective-permute-done.27.refs_7_.refs_10_.refs_11_
  341.9 3.3 tail_head_near.1
  345.4 3.2 down_own.1
  351.1 7.4 %collective-permute-done.29.refs_8_.refs_12_ = bf16[1,2,128,512]{3,2,1,0:T(8,128)(2,1)S(1)} collective-permute-done((bf16[1,2,128,512]{3,2,1,0:T(8,128)(2,1)}, bf16[1,2,128,512]{3,2,1,0:T(8,128)(2,1)S(1)}, u32[]{:S(2)}, u32[]{:S(2)}) %collective-permute-start.29) | collective-permute-done | bytes 262176 | tf_op jit(solution)/shard_map/ppermute | solution.py:695
  (284 shorter events, 107.5 us)
Async XLA Ops:
  7.2 148.7 %all-gather.3.cloned.1.call-start = ((), (), s32[]{:S(2)}) async-start(), calls=%async_computation.4 | async-start | bytes 18382848 | tf_op jit(solution)/shard_map/all_gather | solution.py:747
  10.8 299.5 %reduce-scatter.3.cloned.1.call-start = ((), (), s32[]{:S(2)}) async-start(), calls=%async_computation.2 | async-start | bytes 1400832 | tf_op jit(solution)/shard_map/reduce_scatter | solution.py:1131
  13.3 26.7 %collective-permute-start.2 = (bf16[1,272,512]{2,1,0:T(8,128)(2,1)S(1)}, bf16[1,272,512]{2,1,0:T(8,128)(2,1)S(1)}, u32[]{:S(2)}, u32[]{:S(2)}) collective-permute-start(bf16[1,272,512]{2,1,0:T(8,128)(2,1)S(1)} %fusion.2), channel_id=1, source_target_pairs={{0,2},{1,3},{2,0},{3,1},{4,6},{5,7},{6,4},{7,5},{8,10},{9,11},{10,... | collective-permute-start | bytes 835592 | tf_op jit(solution)/shard_map/ppermute | solution.py:695
  17.3 71.7 %collective-permute-start = (bf16[256,1024]{1,0:T(8,128)(2,1)}, bf16[256,1024]{1,0:T(8,128)(2,1)}, u32[]{:S(2)}, u32[]{:S(2)}) collective-permute-start(bf16[256,1024]{1,0:T(8,128)(2,1)} %param.14), channel_id=1, source_target_pairs={{0,4},{1,5},{2,6},{3,7},{4,0},{5,1},{6,2},{7,3},{8,12},{9,13},{10,... | collective-permute-start | bytes 1572872 | tf_op jit(solution)/shard_map/ppermute | solution.py:695
  17.4 69.2 %collective-permute-start.8 = (s32[11]{0:T(128)S(1)}, s32[11]{0:T(128)S(1)}, u32[]{:S(2)}, u32[]{:S(2)}) collective-permute-start(s32[11]{0:T(128)S(1)} %pad_add_fusion.2), channel_id=1, source_target_pairs={{0,4},{1,5},{2,6},{3,7},{4,0},{5,1},{6,2},{7,3},{8,12},{9,13},{10,... | collective-permute-start | bytes 140 | tf_op jit(solution)/shard_map/ppermute | solution.py:695
  40.0 26.7 %collective-permute-start.5 = (bf16[2,272,512]{2,1,0:T(8,128)(2,1)S(1)}, bf16[2,272,512]{2,1,0:T(8,128)(2,1)S(1)}, u32[]{:S(2)}, u32[]{:S(2)}) collective-permute-start(bf16[2,272,512]{2,1,0:T(8,128)(2,1)S(1)} %get-tuple-element.148.a0), channel_id=1, source_target_pairs={{0,1},{1,0},{2,3},{3,2},{4,5},{5,4},{6,7},{7,6},{8,9},{9,8},{10,11... | collective-permute-start | bytes 1671176 | tf_op jit(solution)/shard_map/ppermute | solution.py:695
  44.6 24.4 %collective-permute-start.3 = (bf16[2,272,512]{2,1,0:T(8,128)(2,1)S(1)}, bf16[2,272,512]{2,1,0:T(8,128)(2,1)S(1)}, u32[]{:S(2)}, u32[]{:S(2)}) collective-permute-start(bf16[2,272,512]{2,1,0:T(8,128)(2,1)S(1)} %get-tuple-element.148.a0), channel_id=1, source_target_pairs={{0,8},{1,9},{2,10},{3,11},{4,12},{5,13},{6,14},{7,15},{8,0},{9,1},... | collective-permute-start | bytes 1671176 | tf_op jit(solution)/shard_map/ppermute | solution.py:695
  66.7 15.6 %collective-permute-start.6 = (bf16[2,272,512]{2,1,0:T(8,128)(2,1)S(1)}, bf16[2,272,512]{2,1,0:T(8,128)(2,1)S(1)}, u32[]{:S(2)}, u32[]{:S(2)}) collective-permute-start(bf16[2,272,512]{2,1,0:T(8,128)(2,1)S(1)} %collective-permute-done.5.b0), channel_id=1, source_target_pairs={{0,16},{1,17},{2,18},{3,19},{4,20},{5,21},{6,22},{7,23},{8,24},{9,... | collective-permute-start | bytes 1671176 | tf_op jit(solution)/shard_map/ppermute | solution.py:695
  70.2 44.8 %collective-permute-start.4 = (bf16[2,2,272,512]{3,2,1,0:T(8,128)(2,1)}, bf16[2,2,272,512]{3,2,1,0:T(8,128)(2,1)}, u32[]{:S(2)}, u32[]{:S(2)}) collective-permute-start(bf16[2,2,272,512]{3,2,1,0:T(8,128)(2,1)} %pad_maximum_fusion), channel_id=1, source_target_pairs={{0,16},{1,17},{2,18},{3,19},{4,20},{5,21},{6,22},{7,23},{8,24},{9,... | collective-permute-start | bytes 3342344 | tf_op jit(solution)/shard_map/ppermute | solution.py:695
  83.5 38.4 %collective-permute-start.7 = (bf16[2,2,272,512]{3,2,1,0:T(8,128)(2,1)}, bf16[2,2,272,512]{3,2,1,0:T(8,128)(2,1)}, u32[]{:S(2)}, u32[]{:S(2)}) collective-permute-start(bf16[2,2,272,512]{3,2,1,0:T(8,128)(2,1)} %pad_maximum_fusion.1), channel_id=1, source_target_pairs={{0,8},{1,9},{2,10},{3,11},{4,12},{5,13},{6,14},{7,15},{8,0},{9,1},... | collective-permute-start | bytes 3342344 | tf_op jit(solution)/shard_map/ppermute | solution.py:695
  135.2 4.4 %collective-permute-start.9 = (f32[512,1024]{1,0:T(8,128)}, f32[512,1024]{1,0:T(8,128)S(1)}, u32[]{:S(2)}, u32[]{:S(2)}) collective-permute-start(f32[512,1024]{1,0:T(8,128)} %get-tuple-element.65.part), channel_id=1, source_target_pairs={{0,4},{1,5},{2,6},{3,7},{4,0},{5,1},{6,2},{7,3},{8,12},{9,13},{10,... | collective-permute-start | bytes 6291464 | tf_op jit(solution)/shard_map/ppermute | solution.py:695
  174.3 13.5 %collective-permute-start.11 = (bf16[288,256]{1,0:T(8,128)(2,1)S(1)}, bf16[288,256]{1,0:T(8,128)(2,1)S(1)}, u32[]{:S(2)}, u32[]{:S(2)}) collective-permute-start(bf16[288,256]{1,0:T(8,128)(2,1)S(1)} %get-tuple-element.72.proj_0), channel_id=1, source_target_pairs={{0,1},{1,0},{2,3},{3,2},{4,5},{5,4},{6,7},{7,6},{8,9},{9,8},{10,11... | collective-permute-start | bytes 442376 | tf_op jit(solution)/shard_map/ppermute | solution.py:695
  180.9 13.9 %collective-permute-start.12 = (bf16[288,256]{1,0:T(8,128)(2,1)S(1)}, bf16[288,256]{1,0:T(8,128)(2,1)S(1)}, u32[]{:S(2)}, u32[]{:S(2)}) collective-permute-start(bf16[288,256]{1,0:T(8,128)(2,1)S(1)} %get-tuple-element.72.proj_0), channel_id=1, source_target_pairs={{0,2},{1,3},{2,0},{3,1},{4,6},{5,7},{6,4},{7,5},{8,10},{9,11},{10,... | collective-permute-start | bytes 442376 | tf_op jit(solution)/shard_map/ppermute | solution.py:695
  182.4 12.5 %collective-permute-start.13 = (bf16[288,256]{1,0:T(8,128)(2,1)S(1)}, bf16[288,256]{1,0:T(8,128)(2,1)S(1)}, u32[]{:S(2)}, u32[]{:S(2)}) collective-permute-start(bf16[288,256]{1,0:T(8,128)(2,1)S(1)} %get-tuple-element.72.proj_0), channel_id=1, source_target_pairs={{0,3},{1,2},{2,1},{3,0},{4,7},{5,6},{6,5},{7,4},{8,11},{9,10},{10,... | collective-permute-start | bytes 442376 | tf_op jit(solution)/shard_map/ppermute | solution.py:695
  206.1 48.8 %collective-permute-start.19 = (bf16[2,512,1024]{2,1,0:T(8,128)(2,1)}, bf16[2,512,1024]{2,1,0:T(8,128)(2,1)}, u32[]{:S(2)}, u32[]{:S(2)}) collective-permute-start(bf16[2,512,1024]{2,1,0:T(8,128)(2,1)} %down_far.1), channel_id=1, source_target_pairs={{0,8},{1,9},{2,10},{3,11},{4,12},{5,13},{6,14},{7,15},{8,0},{9,1},... | collective-permute-start | bytes 6291464 | tf_op jit(solution)/shard_map/ppermute | solution.py:695
  217.1 6.3 %collective-permute-start.15 = (f32[256,1024]{1,0:T(8,128)}, f32[256,1024]{1,0:T(8,128)S(1)}, u32[]{:S(2)}, u32[]{:S(2)}) collective-permute-start(f32[256,1024]{1,0:T(8,128)} %get-tuple-element.85), channel_id=1, source_target_pairs={{0,4},{1,5},{2,6},{3,7},{4,0},{5,1},{6,2},{7,3},{8,12},{9,13},{10,... | collective-permute-start | bytes 3145736 | tf_op jit(solution)/shard_map/ppermute | solution.py:695
  221.8 48.7 %collective-permute-start.20 = (bf16[2,256,2048]{2,1,0:T(8,128)(2,1)}, bf16[2,256,2048]{2,1,0:T(8,128)(2,1)}, u32[]{:S(2)}, u32[]{:S(2)}) collective-permute-start(bf16[2,256,2048]{2,1,0:T(8,128)(2,1)} %up_far.1), channel_id=1, source_target_pairs={{0,16},{1,17},{2,18},{3,19},{4,20},{5,21},{6,22},{7,23},{8,24},{9,... | collective-permute-start | bytes 6291464 | tf_op jit(solution)/shard_map/ppermute | solution.py:695
  248.1 49.6 %collective-permute-start.22 = (bf16[2,1,128,2048]{3,2,1,0:T(8,128)(2,1)}, bf16[2,1,128,2048]{3,2,1,0:T(8,128)(2,1)}, u32[]{:S(2)}, u32[]{:S(2)}) collective-permute-start(bf16[2,1,128,2048]{3,2,1,0:T(8,128)(2,1)} %get-tuple-element.100), channel_id=1, source_target_pairs={{0,16},{1,17},{2,18},{3,19},{4,20},{5,21},{6,22},{7,23},{8,24},{9,... | collective-permute-start | bytes 3145736 | tf_op jit(solution)/shard_map/ppermute | solution.py:695
  248.5 40.1 %collective-permute-start.18 = (bf16[2,1,128,2048]{3,2,1,0:T(8,128)(2,1)}, bf16[2,1,128,2048]{3,2,1,0:T(8,128)(2,1)}, u32[]{:S(2)}, u32[]{:S(2)}) collective-permute-start(bf16[2,1,128,2048]{3,2,1,0:T(8,128)(2,1)} %get-tuple-element.99), channel_id=1, source_target_pairs={{0,8},{1,9},{2,10},{3,11},{4,12},{5,13},{6,14},{7,15},{8,0},{9,1},... | collective-permute-start | bytes 3145736 | tf_op jit(solution)/shard_map/ppermute | solution.py:695
  249.7 24.7 %collective-permute-start.17 = (f32[256,1024]{1,0:T(8,128)}, f32[256,1024]{1,0:T(8,128)}, u32[]{:S(2)}, u32[]{:S(2)}) collective-permute-start(f32[256,1024]{1,0:T(8,128)} %get-tuple-element.96), channel_id=1, source_target_pairs={{0,4},{1,5},{2,6},{3,7},{4,0},{5,1},{6,2},{7,3},{8,12},{9,13},{10,... | collective-permute-start | bytes 3145736 | tf_op jit(solution)/shard_map/ppermute | solution.py:695
  251.0 82.0 %reduce-scatter.5.cloned.1.call-start = ((), (), s32[]{:S(2)}) async-start(), calls=%async_computation.3 | async-start | bytes 245760 | tf_op jit(solution)/shard_map/reduce_scatter | solution.py:1138
  257.8 24.7 %collective-permute-start.21 = (bf16[4,512,256]{2,1,0:T(8,128)(2,1)S(1)}, bf16[4,512,256]{2,1,0:T(8,128)(2,1)S(1)}, u32[]{:S(2)}, u32[]{:S(2)}) collective-permute-start(bf16[4,512,256]{2,1,0:T(8,128)(2,1)S(1)} %down_head.1), channel_id=1, source_target_pairs={{0,1},{1,0},{2,3},{3,2},{4,5},{5,4},{6,7},{7,6},{8,9},{9,8},{10,11... | collective-permute-start | bytes 3145736 | tf_op jit(solution)/shard_map/ppermute | solution.py:695
  273.1 31.5 %collective-permute-start.24 = (bf16[1,256,2048]{2,1,0:T(8,128)(2,1)S(1)}, bf16[1,256,2048]{2,1,0:T(8,128)(2,1)S(1)}, u32[]{:S(2)}, u32[]{:S(2)}) collective-permute-start(bf16[1,256,2048]{2,1,0:T(8,128)(2,1)S(1)} %up_near.1), channel_id=1, source_target_pairs={{0,8},{1,9},{2,10},{3,11},{4,12},{5,13},{6,14},{7,15},{8,0},{9,1},... | collective-permute-start | bytes 3145736 | tf_op jit(solution)/shard_map/ppermute | solution.py:695
  285.4 27.2 %collective-permute-start.25 = (bf16[2,512,256]{2,1,0:T(8,128)(2,1)}, bf16[2,512,256]{2,1,0:T(8,128)(2,1)}, u32[]{:S(2)}, u32[]{:S(2)}) collective-permute-start(bf16[2,512,256]{2,1,0:T(8,128)(2,1)} %down_head_near.1), channel_id=1, source_target_pairs={{0,2},{1,3},{2,0},{3,1},{4,6},{5,7},{6,4},{7,5},{8,10},{9,11},{10,... | collective-permute-start | bytes 1572872 | tf_op jit(solution)/shard_map/ppermute | solution.py:695
  300.6 15.2 %collective-permute-start.26 = (bf16[1,1,128,2048]{3,2,1,0:T(8,128)(2,1)}, bf16[1,1,128,2048]{3,2,1,0:T(8,128)(2,1)}, u32[]{:S(2)}, u32[]{:S(2)}) collective-permute-start(bf16[1,1,128,2048]{3,2,1,0:T(8,128)(2,1)} %get-tuple-element.106), channel_id=1, source_target_pairs={{0,8},{1,9},{2,10},{3,11},{4,12},{5,13},{6,14},{7,15},{8,0},{9,1},... | collective-permute-start | bytes 1572872 | tf_op jit(solution)/shard_map/ppermute | solution.py:695
  301.9 14.0 %collective-permute-start.23 = (bf16[1,1,128,2048]{3,2,1,0:T(8,128)(2,1)}, bf16[1,1,128,2048]{3,2,1,0:T(8,128)(2,1)}, u32[]{:S(2)}, u32[]{:S(2)}) collective-permute-start(bf16[1,1,128,2048]{3,2,1,0:T(8,128)(2,1)} %get-tuple-element.105), channel_id=1, source_target_pairs={{0,16},{1,17},{2,18},{3,19},{4,20},{5,21},{6,22},{7,23},{8,24},{9,... | collective-permute-start | bytes 1572872 | tf_op jit(solution)/shard_map/ppermute | solution.py:695
  307.5 16.0 %collective-permute-start.28 = (bf16[2,256,512]{2,1,0:T(8,128)(2,1)}, bf16[2,256,512]{2,1,0:T(8,128)(2,1)}, u32[]{:S(2)}, u32[]{:S(2)}) collective-permute-start(bf16[2,256,512]{2,1,0:T(8,128)(2,1)} %up_head.1), channel_id=1, source_target_pairs={{0,1},{1,0},{2,3},{3,2},{4,5},{5,4},{6,7},{7,6},{8,9},{9,8},{10,11... | collective-permute-start | bytes 1572872 | tf_op jit(solution)/shard_map/ppermute | solution.py:695
  319.9 22.0 %collective-permute-start.27 = (bf16[2,2,128,512]{3,2,1,0:T(8,128)(2,1)}, bf16[2,2,128,512]{3,2,1,0:T(8,128)(2,1)}, u32[]{:S(2)}, u32[]{:S(2)}) collective-permute-start(bf16[2,2,128,512]{3,2,1,0:T(8,128)(2,1)} %tail_head.1), channel_id=1, source_target_pairs={{0,1},{1,0},{2,3},{3,2},{4,5},{5,4},{6,7},{7,6},{8,9},{9,8},{10,11... | collective-permute-start | bytes 1572872 | tf_op jit(solution)/shard_map/ppermute | solution.py:695
  322.1 23.3 %collective-permute-start.31 = (bf16[1,512,256]{2,1,0:T(8,128)(2,1)S(1)}, bf16[1,512,256]{2,1,0:T(8,128)(2,1)}, u32[]{:S(2)}, u32[]{:S(2)}) collective-permute-start(bf16[1,512,256]{2,1,0:T(8,128)(2,1)S(1)} %down_near.1), channel_id=1, source_target_pairs={{0,16},{1,17},{2,18},{3,19},{4,20},{5,21},{6,22},{7,23},{8,24},{9,... | collective-permute-start | bytes 786440 | tf_op jit(solution)/shard_map/ppermute | solution.py:695
  328.8 19.8 %collective-permute-start.32 = (bf16[1,256,512]{2,1,0:T(8,128)(2,1)}, bf16[1,256,512]{2,1,0:T(8,128)(2,1)}, u32[]{:S(2)}, u32[]{:S(2)}) collective-permute-start(bf16[1,256,512]{2,1,0:T(8,128)(2,1)} %up_head_near.1), channel_id=1, source_target_pairs={{0,2},{1,3},{2,0},{3,1},{4,6},{5,7},{6,4},{7,5},{8,10},{9,11},{10,... | collective-permute-start | bytes 786440 | tf_op jit(solution)/shard_map/ppermute | solution.py:695
  345.2 13.3 %collective-permute-start.29 = (bf16[1,2,128,512]{3,2,1,0:T(8,128)(2,1)}, bf16[1,2,128,512]{3,2,1,0:T(8,128)(2,1)S(1)}, u32[]{:S(2)}, u32[]{:S(2)}) collective-permute-start(bf16[1,2,128,512]{3,2,1,0:T(8,128)(2,1)} %tail_head_near.1), channel_id=1, source_target_pairs={{0,2},{1,3},{2,0},{3,1},{4,6},{5,7},{6,4},{7,5},{8,10},{9,11},{10,... | collective-permute-start | bytes 786440 | tf_op jit(solution)/shard_map/ppermute | solution.py:695
  351.0 10.4 %collective-permute-start.33 = (bf16[128,512]{1,0:T(8,128)(2,1)S(1)}, bf16[128,512]{1,0:T(8,128)(2,1)S(1)}, u32[]{:S(2)}, u32[]{:S(2)}) collective-permute-start(bf16[128,512]{1,0:T(8,128)(2,1)S(1)} %get-tuple-element.150), channel_id=1, source_target_pairs={{0,4},{1,5},{2,6},{3,7},{4,0},{5,1},{6,2},{7,3},{8,12},{9,13},{10,... | collective-permute-start | bytes 393224 | tf_op jit(solution)/shard_map/ppermute | solution.py:695
  (73 other events, 556.2 us)
Sparse Core Ops, SparseCore 0:
  10.9 144.9 all-gather.2
  251.2 43.5 reduce-scatter.2
  312.8 20.1 reduce-scatter.4
